TPU v7x, 256 devices: a whole 4x4x8 slice. The times are simulated.
256 devices in a mesh: expert: 64 (over y, z, core), half: 4 (over x).
Axes of the slice: x: 4, y: 4, z: 8, core: 2. Of those that a mesh axis runs over, the one named last changes fastest.
Arguments:
- tokens: bfloat16 [8192, 2048], P('expert', 'half'), may hold values from -6 to 6
- cotangent: bfloat16 [8192, 2048], P('expert', 'half'), may hold values from -4 to 4
- route: int32 [8192, 8], P('expert'), may hold values from 0 to 127, all different within a row; in each aligned block of 128 rows (0 to 127, 128 to 255, ...) at most 16 rows name the same one
- prob: bfloat16 [8192, 8], P('expert'), may hold values from 0.19921875 to 1
- w_gate: bfloat16 [128, 768, 2048], P('expert', 'half'), may hold values from -0.125 to 0.125
- w_up: bfloat16 [128, 768, 2048], P('expert', 'half'), may hold values from -0.125 to 0.125
- w_down: bfloat16 [128, 768, 2048], P('expert', 'half'), may hold values from -0.21875 to 0.21875
Outputs:
- grad_tokens: bfloat16 [8192, 2048], P('expert', 'half')
- grad_prob: float32 [8192, 8], P('expert')
- grad_gate: bfloat16 [128, 768, 2048], P('expert', 'half')
- grad_up: bfloat16 [128, 768, 2048], P('expert', 'half')
- grad_down: bfloat16 [128, 768, 2048], P('expert', 'half')
Inputs may be any that keep to these rules, and one draw needn't show every extreme that they name: `route`: each row names 8 different experts; among the rows of one device no expert is named more than 16 times, and that most is reached.
All inputs are finite; a program needn't handle non-finite values.
Results may differ from a plain program's by a relative error of at most 0.013.
Values may be sent and summed in bfloat16 or wider, within the bound.
No kernel may reach another device: no remote copies, remote signals or barrier semaphores. Data moves between devices by JAX's collectives and lax.ppermute only.
A program may use at most 192 MiB of HBM per device.

v0:
```python
import jax
import jax.numpy as jnp
from jax import lax
from jax.sharding import PartitionSpec as P


def per_device(tokens, cotangent, route, prob, w_gate, w_up, w_down):
    tok_rows = route.shape[0]
    top = route.shape[1]
    local_exp = w_gate.shape[0]
    groups = lax.axis_size("expert")
    experts = local_exp * groups
    capacity = 2 * tok_rows * top // experts
    slots = experts * capacity
    flat_route = route.reshape(-1)
    hits = (flat_route[:, None] == jnp.arange(experts, dtype=jnp.int32)[None, :]).astype(jnp.int32)
    rank = jnp.sum((jnp.cumsum(hits, axis=0) - hits) * hits, axis=1)
    slot_of = flat_route * capacity + rank
    source = (
        jnp.zeros((slots,), jnp.int32).at[slot_of].set(jnp.arange(tok_rows * top, dtype=jnp.int32))
    )
    filled = jnp.zeros((slots,), jnp.bool_).at[slot_of].set(True)
    token_of = source // top
    slot_prob = jnp.where(filled, prob.reshape(-1)[source], jnp.zeros((), jnp.bfloat16))
    slot_prob = slot_prob.reshape(groups, local_exp * capacity)

    def pack(rows):
        picked = jnp.where(filled[:, None], rows[token_of], jnp.zeros((), jnp.bfloat16))
        return picked.reshape(groups, local_exp * capacity, rows.shape[1])

    sent_x, sent_d, recv_p = (
        lax.all_to_all(pack(tokens), "expert", split_axis=0, concat_axis=0, tiled=True),
        lax.all_to_all(pack(cotangent), "expert", split_axis=0, concat_axis=0, tiled=True),
        lax.all_to_all(slot_prob, "expert", split_axis=0, concat_axis=0, tiled=True),
    )
    recv_x, recv_d = (
        lax.all_gather(sent_x, "half", axis=2, tiled=True),
        lax.all_gather(sent_d, "half", axis=2, tiled=True),
    )
    width = recv_x.shape[2]
    xin = recv_x.reshape(groups, local_exp, capacity, width)
    dout = recv_d.reshape(groups, local_exp, capacity, width)
    weight = recv_p.reshape(groups, local_exp, capacity).astype(jnp.float32)
    gate = jnp.einsum("gecd,efd->gecf", xin, w_gate, preferred_element_type=jnp.float32)
    upval = jnp.einsum("gecd,efd->gecf", xin, w_up, preferred_element_type=jnp.float32)
    sig = jax.nn.sigmoid(gate)
    act = gate * sig
    hidden = (act * upval).astype(jnp.bfloat16)
    raw = jnp.einsum("gecd,efd->gecf", dout, w_down, preferred_element_type=jnp.float32)
    score = jnp.sum(hidden.astype(jnp.float32) * raw, axis=3)
    scaled = (weight[..., None] * dout.astype(jnp.float32)).astype(jnp.bfloat16)
    dact = weight[..., None] * raw
    dgate = (dact * upval * sig * (1.0 + gate * (1.0 - sig))).astype(jnp.bfloat16)
    dup = (dact * act).astype(jnp.bfloat16)
    grad_down = jnp.einsum(
        "gecf,gecd->efd", hidden, scaled, preferred_element_type=jnp.float32
    ).astype(jnp.bfloat16)
    grad_gate = jnp.einsum("gecf,gecd->efd", dgate, xin, preferred_element_type=jnp.float32).astype(
        jnp.bfloat16
    )
    grad_up = jnp.einsum("gecf,gecd->efd", dup, xin, preferred_element_type=jnp.float32).astype(
        jnp.bfloat16
    )
    part = jnp.einsum("gecf,efd->gecd", dgate, w_gate, preferred_element_type=jnp.float32)
    part = (
        part + jnp.einsum("gecf,efd->gecd", dup, w_up, preferred_element_type=jnp.float32)
    ).astype(jnp.bfloat16)
    summed = lax.psum_scatter(
        part.astype(jnp.float32).astype(jnp.bfloat16), "half", scatter_dimension=3, tiled=True
    ).astype(jnp.float32)
    total_score = lax.psum(score, "half")
    quarter = summed.shape[3]
    back_rows, back_score = (
        lax.all_to_all(
            summed.reshape(groups, local_exp * capacity, quarter).astype(jnp.bfloat16),
            "expert",
            split_axis=0,
            concat_axis=0,
            tiled=True,
        ).astype(jnp.float32),
        lax.all_to_all(
            total_score.reshape(groups, local_exp * capacity).astype(jnp.bfloat16),
            "expert",
            split_axis=0,
            concat_axis=0,
            tiled=True,
        ).astype(jnp.float32),
    )
    picked = back_rows.reshape(slots, quarter)[slot_of].reshape(tok_rows, top, quarter)
    grad_tokens = jnp.sum(picked, axis=1).astype(jnp.bfloat16)
    grad_prob = back_score.reshape(slots)[slot_of].reshape(tok_rows, top)
    return (grad_tokens, grad_prob, grad_gate, grad_up, grad_down)


def solution(mesh):
    in_specs = (
        P("expert", "half"),
        P("expert", "half"),
        P("expert", None),
        P("expert", None),
        P("expert", "half", None),
        P("expert", "half", None),
        P("expert", "half", None),
    )
    out_specs = (
        P("expert", "half"),
        P("expert", None),
        P("expert", "half", None),
        P("expert", "half", None),
        P("expert", "half", None),
    )
    return jax.shard_map(
        per_device, mesh=mesh, in_specs=in_specs, out_specs=out_specs, check_vma=False
    )
```

profile of v0, /device:TPU:1, one launch (start us, length us, event | category | flops | bytes accessed | tf_op | source)
XLA Modules:
  0.0 475.6 jit_solution(6018880050518364092)
XLA Ops:
  10.1 4.3 scatter_custom_fusion.1
  14.5 4.3 scatter_custom_fusion
  18.9 9.2 %gather_fusion.2 = bf16[2048,512]{1,0:T(8,128)(2,1)} fusion(bf16[128,512]{1,0:T(8,128)(2,1)S(1)} %copy-done.2, s32[2048]{0:T(1024)S(1)} %get-tuple-element.25), kind=kCustom, calls=%fused_computation.2 | custom fusion | bytes 4202496 | tf_op jit(solution)/shard_map/gather | solution.py:28
  28.1 9.2 %gather_fusion.1 = bf16[2048,512]{1,0:T(8,128)(2,1)} fusion(bf16[128,512]{1,0:T(8,128)(2,1)S(1)} %copy-done.3, s32[2048]{0:T(1024)S(1)} %get-tuple-element.25), kind=kCustom, calls=%fused_computation.1 | custom fusion | bytes 4202496 | tf_op jit(solution)/shard_map/gather | solution.py:28
  40.8 64.3 %all_to_all.31 = bf16[64,32,512]{2,1,0:T(8,128)(2,1)} all-to-all(bf16[64,32,512]{2,1,0:T(8,128)(2,1)S(1)} %get-tuple-element.27), channel_id=1, replica_groups=mesh['expert'=64,'half'=4] {'expert'}, dimensions={0} | all-to-all | bytes 4194304 | tf_op jit(solution)/shard_map/all_to_all | solution.py:32
  105.1 57.2 %all_to_all.32 = bf16[64,32,512]{2,1,0:T(8,128)(2,1)} all-to-all(bf16[64,32,512]{2,1,0:T(8,128)(2,1)} %get-tuple-element.26), channel_id=1, replica_groups=mesh['expert'=64,'half'=4] {'expert'}, dimensions={0} | all-to-all | bytes 4194304 | tf_op jit(solution)/shard_map/all_to_all | solution.py:33
  163.2 13.1 %gather_fusion = bf16[2048]{0:T(1024)(128)(2,1)S(1)} fusion(bf16[1024]{0:T(1024)(128)(2,1)S(1)} %reshape.125, s32[2048]{0:T(1024)S(1)} %get-tuple-element.24), kind=kCustom, calls=%fused_computation | custom fusion | bytes 16384 | tf_op jit(solution)/shard_map/gather | solution.py:24
  176.4 14.9 %all_to_all.33 = bf16[64,1,32]{2,1,0:T(2,128)(2,1)S(1)} all-to-all(bf16[64,1,32]{2,1,0:T(2,128)(2,1)S(1)} %all_to_all.25), channel_id=1, replica_groups=mesh['expert'=64,'half'=4] {'expert'}, dimensions={0} | all-to-all | bytes 8192 | tf_op jit(solution)/shard_map/all_to_all | solution.py:34
  191.6 7.2 %fusion.9 = f32[2,64,16,192]{3,2,1,0:T(8,128)} fusion(bf16[64,2,16,2048]{3,2,1,0:T(8,128)(2,1)} %bitcast.121, bf16[2,192,2048]{2,1,0:T(8,128)(2,1)S(1)} %copy-done), kind=kOutput, calls=%fused_computation.18 | convolution fusion | flops 1610612736 | bytes 11534336 | tf_op jit(solution)/shard_map/gecd,efd->gecf/dot_general | solution.py:44
  202.5 73.4 %all-gather.3.cloned.1.call-done = bf16[64,32,2048]{2,1,0:T(8,128)(2,1)} async-done(((bf16[64,32,512]{2,1,0:T(8,128)(2,1)}), bf16[64,32,2048]{2,1,0:T(8,128)(2,1)}) %all-gather.3.cloned.1.call-update) | async-done | bytes 8388624 | tf_op jit(solution)/shard_map/all_gather | solution.py:38
  275.8 9.4 %fusion.27 = (f32[64,2,16]{2,0,1:T(8,128)S(1)}, bf16[64,2,16,192]{3,2,0,1:T(8,128)(2,1)}, bf16[64,2,16,192]{3,2,0,1:T(8,128)(2,1)S(1)}, bf16[64,2,16,192]{3,2,0,1:T(8,128)(2,1)S(1)}) fusion(f32[2,64,16,192]{3,2,1,0:T(8,128)} %fusion.11, f32[2,64,16,192]{3,2,1,0:T(8,128)} %fusion.9, f32[64,2,16]{2,0,1:T(8,128)S(1)} %copy.67, ...), kind=kOutput, calls=%fused_computation.42 | convolution fusion | flops 1618081792 | bytes 15482880 | tf_op jit(solution)/shard_map/gecd,efd->gecf/dot_general | solution.py:49
  285.2 8.1 %fusion.28 = f32[2,64,16,2048]{3,2,1,0:T(8,128)} fusion(bf16[64,2,16,192]{3,2,0,1:T(8,128)(2,1)S(1)} %get-tuple-element.22, bf16[2,192,2048]{2,1,0:T(8,128)(2,1)S(1)} %copy-done), kind=kOutput, calls=%fused_computation.46 | convolution fusion | flops 1610612736 | bytes 19136512 | tf_op jit(solution)/shard_map/gecf,efd->gecd/dot_general | solution.py:64
  293.3 11.6 %fusion = bf16[64,2,16,2048]{3,2,0,1:T(8,128)(2,1)} fusion(f32[2,64,16,2048]{3,2,1,0:T(8,128)} %fusion.28, bf16[64,2,16,192]{3,2,0,1:T(8,128)(2,1)S(1)} %get-tuple-element.23, bf16[2,192,2048]{2,1,0:T(8,128)(2,1)S(1)} %copy-done.4), kind=kOutput, calls=%fused_computation.9 | convolution fusion | flops 1619001344 | bytes 27525120 | tf_op jit(solution)/shard_map/gecf,efd->gecd/dot_general | solution.py:66
  305.1 12.0 %psum.7 = bf16[64,2,16]{0,2,1:T(8,128)(2,1)S(1)} all-reduce(f32[64,2,16]{0,2,1:T(8,128)S(1)} %copy.72), channel_id=1, replica_groups=mesh['expert'=64,'half'=4] {'half'}, use_global_device_ids=true, to_apply=%region_8.9 | all-reduce | flops 2048 | bytes 12288 | tf_op jit(solution)/shard_map/psum | solution.py:71
  317.8 14.8 %all-to-all-start.4 = ((bf16[64,1,32]{2,1,0:T(2,128)(2,1)}), bf16[64,1,32]{2,1,0:T(2,128)(2,1)S(1)}, u32[]{:S(2)}, u32[]{:S(2)}) async-start(bf16[64,1,32]{2,1,0:T(2,128)(2,1)} %copy.73), calls=%async_computation.5 | async-start | bytes 65536 | tf_op jit(solution)/shard_map/all_to_all | solution.py:81
  332.6 6.4 %bitcast_convert_fusion.2 = bf16[2,192,2048]{2,1,0:T(8,128)(2,1)} fusion(bf16[64,2,16,192]{3,2,0,1:T(8,128)(2,1)S(1)} %copy-done.6, bf16[64,2,16,2048]{3,2,1,0:T(8,128)(2,1)} %bitcast.122), kind=kOutput, calls=%fused_computation.24 | convolution fusion | flops 1611399168 | bytes 10747904 | tf_op jit(solution)/shard_map/gecf,gecd->efd/dot_general | solution.py:58
  339.0 50.2 %reduce-scatter.2.cloned.1.call-done = bf16[64,2,16,512]{3,2,0,1:T(8,128)(2,1)} async-done(((bf16[64,2,16,2048]{3,2,0,1:T(8,128)(2,1)}), bf16[64,2,16,512]{3,2,0,1:T(8,128)(2,1)}) %reduce-scatter.2.cloned.1.call-update) | async-done | bytes 2097168 | tf_op jit(solution)/shard_map/reduce_scatter | solution.py:68
  392.4 11.0 %all-to-all-start.3 = ((bf16[64,32,512]{2,1,0:T(8,128)(2,1)}), bf16[64,32,512]{2,1,0:T(8,128)(2,1)}, u32[]{:S(2)}, u32[]{:S(2)}) async-start(bf16[64,32,512]{2,1,0:T(8,128)(2,1)} %bitcast.113), calls=%async_computation.4 | async-start | bytes 4194304 | tf_op jit(solution)/shard_map/all_to_all | solution.py:74
  403.4 6.4 %bitcast_convert_fusion.1 = bf16[2,192,2048]{2,1,0:T(8,128)(2,1)} fusion(bf16[64,2,16,192]{3,2,0,1:T(8,128)(2,1)S(1)} %copy-done.8, bf16[64,2,16,2048]{3,2,1,0:T(8,128)(2,1)} %bitcast.123), kind=kOutput, calls=%fused_computation.23 | convolution fusion | flops 1611399168 | bytes 10747904 | tf_op jit(solution)/shard_map/gecf,gecd->efd/dot_general | solution.py:61
  409.8 5.5 %bitcast_convert_fusion = bf16[2,192,2048]{2,1,0:T(8,128)(2,1)} fusion(bf16[64,2,16,192]{3,2,0,1:T(8,128)(2,1)S(1)} %copy-done.11, f32[64,2,16]{2,1,0:T(2,128)S(1)} %copy.76, bf16[64,32,2048]{2,1,0:T(8,128)(2,1)} %all-gather.3.cloned.1.call-done), kind=kOutput, calls=%fused_computation.22 | convolution fusion | flops 1623982080 | bytes 10756096 | tf_op jit(solution)/shard_map/gecf,gecd->efd/dot_general | solution.py:55
  415.5 6.1 %gather_fusion.4 = f32[1024]{0:T(1024)S(1)} fusion(f32[2048]{0:T(1024)S(1)} %reshape.135, s32[1024]{0:T(1024)S(1)} %broadcast_clamp_fusion), kind=kCustom, calls=%fused_computation.4 | custom fusion | bytes 12288 | tf_op jit(solution)/shard_map/gather | solution.py:91
  422.4 32.1 %all-to-all-done.3 = bf16[64,32,512]{2,1,0:T(8,128)(2,1)} async-done(((bf16[64,32,512]{2,1,0:T(8,128)(2,1)}), bf16[64,32,512]{2,1,0:T(8,128)(2,1)}, u32[]{:S(2)}, u32[]{:S(2)}) %all-to-all-start.3) | async-done | bytes 2097184 | tf_op jit(solution)/shard_map/all_to_all | solution.py:74
  454.5 4.1 bitcast_convert_fusion.3
  458.6 7.6 %gather_fusion.3 = f32[1024,512]{1,0:T(8,128)} fusion(f32[2048,512]{1,0:T(8,128)} %bitcast_convert_fusion.3, s32[1024]{0:T(1024)S(1)} %broadcast_clamp_fusion), kind=kCustom, calls=%fused_computation.3 | custom fusion | bytes 4198400 | tf_op jit(solution)/shard_map/gather | solution.py:89
  (69 shorter events, 19.2 us)
Async XLA Ops:
  7.2 184.4 %copy-start = (bf16[2,192,2048]{2,1,0:T(8,128)(2,1)S(1)}, bf16[2,192,2048]{2,1,0:T(8,128)(2,1)}, u32[]{:S(2)}) copy-start(bf16[2,192,2048]{2,1,0:T(8,128)(2,1)} %param.11) | copy-start | bytes 4718596
  7.2 11.7 %copy-start.2 = (bf16[128,512]{1,0:T(8,128)(2,1)S(1)}, bf16[128,512]{1,0:T(8,128)(2,1)}, u32[]{:S(2)}) copy-start(bf16[128,512]{1,0:T(8,128)(2,1)} %param.7) | copy-start | bytes 393220
  7.2 184.3 %all-gather.5.cloned.1.call-start = ((), (), s32[]{:S(2)}) async-start(), calls=%async_computation.7 | async-start | bytes 10485760 | tf_op jit(solution)/shard_map/all_gather | solution.py:37
  18.9 9.2 %copy-start.3 = (bf16[128,512]{1,0:T(8,128)(2,1)S(1)}, bf16[128,512]{1,0:T(8,128)(2,1)}, u32[]{:S(2)}) copy-start(bf16[128,512]{1,0:T(8,128)(2,1)} %param.8) | copy-start | bytes 393220
  105.1 170.7 %all-gather.3.cloned.1.call-start = ((), (), s32[]{:S(2)}) async-start(), calls=%async_computation.6 | async-start | bytes 10485760 | tf_op jit(solution)/shard_map/all_gather | solution.py:38
  162.3 0.7 copy-start.9
  162.3 226.8 %reduce-scatter.2.cloned.1.call-start = ((), (), s32[]{:S(2)}) async-start(), calls=%async_computation.8 | async-start | bytes 10485760 | tf_op jit(solution)/shard_map/reduce_scatter | solution.py:68
  191.5 7.2 %copy-start.4 = (bf16[2,192,2048]{2,1,0:T(8,128)(2,1)S(1)}, bf16[2,192,2048]{2,1,0:T(8,128)(2,1)}, u32[]{:S(2)}) copy-start(bf16[2,192,2048]{2,1,0:T(8,128)(2,1)} %param.12) | copy-start | bytes 4718596
  191.6 7.2 %copy-start.10 = (bf16[64,32,2048]{2,1,0:T(8,128)(2,1)S(1)}, bf16[64,32,2048]{2,1,0:T(8,128)(2,1)}, u32[]{:S(2)}) copy-start(bf16[64,32,2048]{2,1,0:T(8,128)(2,1)} %all-gather.5.cloned.1.call-done) | copy-start | bytes 25165828
  285.2 8.1 %copy-start.5 = (bf16[64,2,16,192]{3,2,0,1:T(8,128)(2,1)}, bf16[64,2,16,192]{3,2,0,1:T(8,128)(2,1)S(1)}, u32[]{:S(2)}) copy-start(bf16[64,2,16,192]{3,2,0,1:T(8,128)(2,1)S(1)} %get-tuple-element.22) | copy-start | bytes 2359300
  285.2 8.1 %copy-start.7 = (bf16[64,2,16,192]{3,2,0,1:T(8,128)(2,1)}, bf16[64,2,16,192]{3,2,0,1:T(8,128)(2,1)S(1)}, u32[]{:S(2)}) copy-start(bf16[64,2,16,192]{3,2,0,1:T(8,128)(2,1)S(1)} %get-tuple-element.23) | copy-start | bytes 2359300
  304.8 27.7 %copy-start.6 = (bf16[64,2,16,192]{3,2,0,1:T(8,128)(2,1)S(1)}, bf16[64,2,16,192]{3,2,0,1:T(8,128)(2,1)}, u32[]{:S(2)}) copy-start(bf16[64,2,16,192]{3,2,0,1:T(8,128)(2,1)} %copy-done.5) | copy-start | bytes 2359300
  317.8 74.6 %all-to-all-start.4 = ((bf16[64,1,32]{2,1,0:T(2,128)(2,1)}), bf16[64,1,32]{2,1,0:T(2,128)(2,1)S(1)}, u32[]{:S(2)}, u32[]{:S(2)}) async-start(bf16[64,1,32]{2,1,0:T(2,128)(2,1)} %copy.73), calls=%async_computation.5 | async-start | bytes 65536 | tf_op jit(solution)/shard_map/all_to_all | solution.py:81
  392.4 11.0 %copy-start.8 = (bf16[64,2,16,192]{3,2,0,1:T(8,128)(2,1)S(1)}, bf16[64,2,16,192]{3,2,0,1:T(8,128)(2,1)}, u32[]{:S(2)}) copy-start(bf16[64,2,16,192]{3,2,0,1:T(8,128)(2,1)} %copy-done.7) | copy-start | bytes 2359300
  392.4 62.1 %all-to-all-start.3 = ((bf16[64,32,512]{2,1,0:T(8,128)(2,1)}), bf16[64,32,512]{2,1,0:T(8,128)(2,1)}, u32[]{:S(2)}, u32[]{:S(2)}) async-start(bf16[64,32,512]{2,1,0:T(8,128)(2,1)} %bitcast.113), calls=%async_computation.4 | async-start | bytes 4194304 | tf_op jit(solution)/shard_map/all_to_all | solution.py:74
  403.4 6.5 %copy-start.11 = (bf16[64,2,16,192]{3,2,0,1:T(8,128)(2,1)S(1)}, bf16[64,2,16,192]{3,2,0,1:T(8,128)(2,1)}, u32[]{:S(2)}) copy-start(bf16[64,2,16,192]{3,2,0,1:T(8,128)(2,1)} %get-tuple-element.21) | copy-start | bytes 2359300
  458.6 10.4 %copy-start.1 = (bf16[2,192,2048]{2,1,0:T(8,128)(2,1)S(1)}, bf16[2,192,2048]{2,1,0:T(8,128)(2,1)}, u32[]{:S(2)}) copy-start(bf16[2,192,2048]{2,1,0:T(8,128)(2,1)} %param.11) | copy-start | bytes 4718596
Sparse Core Ops, SparseCore 0:
  105.2 82.0 all-gather.4
  189.1 86.6 all-gather.2
  305.0 84.1 reduce-scatter.1
where the time goes:
time: 476 us
  waiting for transfers between devices  156 us (33%)
  blocking collectives  148 us (31%)
  local copies, waits for them, and re-layouts  61.4 us (13%)
  matrix products  58.3 us (12%)
  starting transfers between devices  25.9 us (5%)
  between operations  14 us (3%)
  other arithmetic  11.9 us (2%)
    all_gather x1, waiting for transfers between devices, per_device(): lax.all_gather(sent_d, 'half', axis=2, tiled=True)  73.4 us
    all_to_all x1, blocking collectives, per_device(): lax.all_to_all(pack(tokens), 'expert', split_axis=0, concat_axis=0, tiled...  64.3 us
    all_to_all x1, blocking collectives, per_device(): lax.all_to_all(pack(cotangent), 'expert', split_axis=0, concat_axis=0, ti...  57.2 us
    reduce_scatter x1, waiting for transfers between devices, per_device(): lax.psum_scatter(part.astype(jnp.float32).astype(jnp.bfloat16), 'half', s...  50.2 us
    all_to_all x1, waiting for transfers between devices, per_device(): lax.all_to_all(summed.reshape(groups, local_exp * capacity, quarter).asty...  32.1 us
    gather x2, local copies, waits for them, and re-layouts, pack(): rows[token_of]  18.4 us
    all_to_all x1, blocking collectives, per_device(): lax.all_to_all(slot_prob, 'expert', split_axis=0, concat_axis=0, tiled=True)  14.9 us
    all_to_all x1, starting transfers between devices, per_device(): lax.all_to_all(total_score.reshape(groups, local_exp * capacity).astype(j...  14.8 us
  transfers between devices with their start and end apart: 5, of which 3 were waited for; matrix products, arithmetic and copies ran while one was open for 11% of the time, Pallas kernels for 0%

commit v1 on v0

v1 whole, which is shorter than its diff:
```python
import jax
import jax.numpy as jnp
from jax import lax
from jax.sharding import Mesh, PartitionSpec as P

BF = jnp.bfloat16
F32 = jnp.float32
NY, NZ, NC, NX = 4, 8, 2, 4
SLOT = 16


def dot32(spec, a, b):
    return jnp.einsum(spec, a, b, preferred_element_type=F32)


def before(n):
    at = jnp.arange(n)
    return (at[:, None] < at[None, :]).astype(BF)


def weight_pairs(m):
    pairs = []
    for c in range(NC):
        for h in range(NX):
            k = (h + m) % 2
            pairs.append((c * NX + h, (h // 2) * NX + 2 * c + k))
    return pairs


def per_device(tokens, cotangent, route, prob, w_gate, w_up, w_down):
    iy, iz, ic, ix = (lax.axis_index(a) for a in ("y", "z", "c", "x"))
    tok_rows, top = route.shape
    quarter = tokens.shape[1]
    sib = [(0, 1), (1, 0)]

    with jax.named_scope("routing"):
        table = jnp.concatenate([route.T.astype(BF), prob.T], axis=0)
        table = lax.all_gather(table, ("y", "z", "c"), axis=0, tiled=False)
        table = table.reshape(NY, NZ, NC, 2 * top, tok_rows)

    with jax.named_scope("gather_z"):
        xz = lax.all_gather(tokens, "z", axis=0, tiled=False)
        dz = lax.all_gather(cotangent, "z", axis=0, tiled=False)

    with jax.named_scope("weights_out"):
        wparts = []
        for m in range(2):
            k = (ix + m) % 2
            piece = jnp.stack([lax.dynamic_index_in_dim(w, k, 0, keepdims=False) for w in (w_gate, w_up, w_down)])
            wparts.append(lax.ppermute(piece, ("c", "x"), weight_pairs(m)))
        weights = jnp.concatenate(wparts, axis=1)
        wg, wu, wd = weights[0], weights[1], weights[2]

    with jax.named_scope("select"):
        mid = lax.dynamic_index_in_dim(table, iy, 0, keepdims=False)
        mid = lax.dynamic_index_in_dim(mid, ic, 1, keepdims=False)
        ids = 4 * (jnp.arange(NY)[:, None] * NZ + iz) + jnp.arange(NX)[None, :]
        ids = ids.reshape(-1).astype(BF)
        hit = jnp.any(mid[:, None, :top, :] == ids[None, :, None, None], axis=2)
        rank = dot32("zet,tv->zev", hit.astype(BF), before(tok_rows))
        slots = jnp.arange(SLOT, dtype=F32)
        pick = (hit[:, :, None, :] & (rank[:, :, None, :] == slots[None, None, :, None])).astype(BF)

        def route_rows(rows):
            got = dot32("zert,ztf->ezrf", pick, rows).astype(BF)
            got = got.reshape(NY * NX, NZ * SLOT, quarter)
            return lax.all_to_all(got, ("y", "x"), split_axis=0, concat_axis=0, tiled=True)

        x_own = route_rows(xz)
        d_own = route_rows(dz)
        x_sib = lax.ppermute(x_own, "c", sib)
        d_sib = lax.ppermute(d_own, "c", sib)

    with jax.named_scope("slot_weight"):
        mine = (4 * (iy * NZ + iz) + ix).astype(BF)
        on = table[:, :, :, :top, :] == mine
        p_of = jnp.sum(jnp.where(on, table[:, :, :, top:, :], jnp.zeros((), BF)).astype(F32), axis=3)
        hit_e = jnp.any(on, axis=3)
        rank_e = dot32("yzct,tv->yzcv", hit_e.astype(BF), before(tok_rows))
        pick_e = hit_e[..., None, :] & (rank_e[..., None, :] == slots[:, None])
        weight = jnp.sum(jnp.where(pick_e, p_of[..., None, :], 0.0), axis=-1)
        weight = weight.transpose(2, 0, 1, 3)
        weight = jnp.where(ic == 0, weight, weight[::-1]).reshape(-1)

    def rows_of(own, sibling):
        both = jnp.stack([own, sibling]).reshape(NC, NY, NX, NZ * SLOT, quarter)
        return both.transpose(0, 1, 3, 2, 4).reshape(NC * NY * NZ * SLOT, NX * quarter)

    with jax.named_scope("expert"):
        xin = rows_of(x_own, x_sib)
        dout = rows_of(d_own, d_sib)
        gate = dot32("rd,fd->rf", xin, wg)
        upval = dot32("rd,fd->rf", xin, wu)
        raw = dot32("rd,fd->rf", dout, wd)
        sig = jax.nn.sigmoid(gate)
        act = gate * sig
        hidden = (act * upval).astype(BF)
        score = jnp.sum(hidden.astype(F32) * raw, axis=1)
        scaled = (weight[:, None] * dout.astype(F32)).astype(BF)
        dact = weight[:, None] * raw
        dgate = (dact * upval * sig * (1.0 + gate * (1.0 - sig))).astype(BF)
        dup = (dact * act).astype(BF)
        part = dot32("rf,fd->rd", dgate, wg) + dot32("rf,fd->rd", dup, wu)
        part = part.reshape(NC, NY, NZ * SLOT, NX, quarter).transpose(0, 1, 3, 2, 4)
        part = part.reshape(NC, NY * NX, NZ * SLOT, quarter)
        sent = lax.ppermute(part[1].astype(BF), "c", sib)
        grads = jnp.stack(
            [
                dot32("rf,rd->fd", dgate, xin).astype(BF),
                dot32("rf,rd->fd", dup, xin).astype(BF),
                dot32("rf,rd->fd", hidden, scaled).astype(BF),
            ]
        )

    with jax.named_scope("weights_back"):
        half = w_gate.shape[1]
        back = []
        for m in range(2):
            inverse = [(b, a) for a, b in weight_pairs(m)]
            back.append(lax.ppermute(grads[:, m * half : (m + 1) * half], ("c", "x"), inverse))
        even = ix % 2 == 0
        first = jnp.where(even, back[0], back[1])
        second = jnp.where(even, back[1], back[0])
        grad_gate, grad_up, grad_down = (jnp.stack([first[i], second[i]]) for i in range(3))

    with jax.named_scope("score_back"):
        score = jnp.where(ic == 0, score.reshape(NC, -1), score.reshape(NC, -1)[::-1])
        scores = lax.all_gather(score, ("y", "z", "x", "c"), axis=0, tiled=False)
        scores = scores.reshape(NY * NZ * NX, NC, NC, NY, NZ, SLOT)
        scores = scores[:, 0] + scores[:, 1]
        scores = lax.dynamic_index_in_dim(scores, ic, 1, keepdims=False)
        scores = lax.dynamic_index_in_dim(scores, iy, 1, keepdims=False)
        scores = lax.dynamic_index_in_dim(scores, iz, 1, keepdims=False)
        named = route.T[:, None, :] == jnp.arange(NY * NZ * NX, dtype=jnp.int32)[None, :, None]
        hit_s = jnp.any(named, axis=0)
        rank_s = dot32("et,tv->ev", hit_s.astype(BF), before(tok_rows))
        pick_s = hit_s[:, None, :] & (rank_s[:, None, :] == slots[None, :, None])
        of_pair = jnp.sum(jnp.where(pick_s, scores[:, :, None], 0.0), axis=1)
        grad_prob = jnp.sum(jnp.where(named, of_pair[None], 0.0), axis=1).T

    with jax.named_scope("tokens_back"):
        total = (part[0] + sent.astype(F32)).astype(BF)
        home = lax.all_to_all(total, ("y", "x"), split_axis=0, concat_axis=0, tiled=True)
        home = home.reshape(NY * NX, NZ, SLOT, quarter)
        summed = dot32("zert,ezrf->ztf", pick, home).astype(BF)
        grad_tokens = lax.psum_scatter(summed, "z", scatter_dimension=0, tiled=True)[0]
    return (grad_tokens, grad_prob, grad_gate, grad_up, grad_down)


def solution(mesh):
    grid = Mesh(mesh.devices.reshape(NY, NZ, NC, NX), ("y", "z", "c", "x"))
    expert = ("y", "z", "c")
    in_specs = (
        P(expert, "x"),
        P(expert, "x"),
        P(expert, None),
        P(expert, None),
        P(expert, "x", None),
        P(expert, "x", None),
        P(expert, "x", None),
    )
    out_specs = (
        P(expert, "x"),
        P(expert, None),
        P(expert, "x", None),
        P(expert, "x", None),
        P(expert, "x", None),
    )
    return jax.shard_map(per_device, mesh=grid, in_specs=in_specs, out_specs=out_specs, check_vma=False)
```

time: 476 us -> 414 us (0.87)
  the two profiles are of different devices: /device:TPU:1 before, /device:TPU:2 now
where the time goes in v1:
time: 414 us; the launch traced here: 406 us
  waiting for transfers between devices  178 us (43%)
  local copies, waits for them, and re-layouts  61.9 us (15%)
  starting transfers between devices  48.1 us (12%)
  blocking collectives  47.5 us (11%)
  matrix products  31.1 us (8%)
  other arithmetic  25 us (6%)
  between operations  14.4 us (3%)
    all_gather x1, waiting for transfers between devices, per_device(): scores = lax.all_gather(score, ('y', 'z', 'x', 'c'), axis=0, tiled=False)  77.1 us
    all_to_all x2, waiting for transfers between devices, route_rows(): lax.all_to_all(got, ('y', 'x'), split_axis=0, concat_axis=0, tiled=True)  48.5 us
    all_gather x1, blocking collectives, per_device(): table = lax.all_gather(table, ('y', 'z', 'c'), axis=0, tiled=False)  47.5 us
    dot_general x14, matrix products, dot32(): return jnp.einsum(spec, a, b, preferred_element_type=F32)  31.1 us
    reduce_scatter x1, waiting for transfers between devices, per_device(): lax.psum_scatter(summed, 'z', scatter_dimension=0, tiled=True)[0]  28.5 us
    ppermute x2, waiting for transfers between devices, per_device(): wparts.append(lax.ppermute(piece, ('c', 'x'), weight_pairs(m)))  22.4 us
    ppermute x2, starting transfers between devices, per_device(): wparts.append(lax.ppermute(piece, ('c', 'x'), weight_pairs(m)))  19.4 us
    reshape x2, local copies, waits for them, and re-layouts, per_device(): part = part.reshape(NC, NY, NZ * SLOT, NX, quarter).transpose(0, 1, 3, 2, 4)  16.7 us
  transfers between devices with their start and end apart: 14, of which 5 were waited for; matrix products, arithmetic and copies ran while one was open for 18% of the time, Pallas kernels for 0%

profile of v1, /device:TPU:2, one launch (start us, length us, event | category | flops | bytes accessed | tf_op | source)
XLA Modules:
  0.0 406.0 jit_solution(13937376890106360503)
XLA Ops:
  10.0 47.5 %all-gather = bf16[1024,128]{1,0:T(8,128)(2,1)S(1)} all-gather(bf16[16,128]{1,0:T(8,128)(2,1)S(1)} %pad_maximum_fusion.8), channel_id=2, replica_groups=mesh['y'=4,'z'=8,'c'=2,'x'=4] {'y','z','c'}, dimensions={0}, use_global_device_ids=true | all-gather | bytes 266240 | tf_op jit(solution)/shard_map/routing/all_gather | solution.py:38
  61.6 6.5 %all-to-all-start.1 = ((bf16[16,128,512]{2,1,0:T(8,128)(2,1)}), bf16[16,128,512]{2,1,0:T(8,128)(2,1)S(1)}, u32[]{:S(2)}, u32[]{:S(2)}) async-start(bf16[16,128,512]{2,1,0:T(8,128)(2,1)} %bitcast.103), calls=%async_computation.1 | async-start | bytes 4194304 | tf_op jit(solution)/shard_map/select/all_to_all | solution.py:67
  73.6 19.2 %collective-permute-start.1 = (bf16[3,192,2048]{2,1,0:T(8,128)(2,1)}, bf16[3,192,2048]{2,1,0:T(8,128)(2,1)}, u32[]{:S(2)}, u32[]{:S(2)}) collective-permute-start(bf16[3,192,2048]{2,1,0:T(8,128)(2,1)} %pad_maximum_fusion.3), channel_id=1, source_target_pairs={{0,0},{1,1},{2,4},{3,5},{4,2},{5,3},{6,6},{7,7},{8,8},{9,9},{10,12... | collective-permute-start | bytes 7077896 | tf_op jit(solution)/shard_map/weights_out/ppermute | solution.py:50
  96.4 25.4 %all-to-all-done.1 = bf16[16,128,512]{2,1,0:T(8,128)(2,1)S(1)} async-done(((bf16[16,128,512]{2,1,0:T(8,128)(2,1)}), bf16[16,128,512]{2,1,0:T(8,128)(2,1)S(1)}, u32[]{:S(2)}, u32[]{:S(2)}) %all-to-all-start.1) | async-done | bytes 2097184 | tf_op jit(solution)/shard_map/select/all_to_all | solution.py:67
  121.8 7.8 %all-to-all-start = ((bf16[16,128,512]{2,1,0:T(8,128)(2,1)}), bf16[16,128,512]{2,1,0:T(8,128)(2,1)}, u32[]{:S(2)}, u32[]{:S(2)}) async-start(bf16[16,128,512]{2,1,0:T(8,128)(2,1)} %bitcast.104), calls=%async_computation | async-start | bytes 4194304 | tf_op jit(solution)/shard_map/select/all_to_all | solution.py:67
  129.7 3.1 pad_maximum_fusion.4
  135.1 23.1 %all-to-all-done = bf16[16,128,512]{2,1,0:T(8,128)(2,1)} async-done(((bf16[16,128,512]{2,1,0:T(8,128)(2,1)}), bf16[16,128,512]{2,1,0:T(8,128)(2,1)}, u32[]{:S(2)}, u32[]{:S(2)}) %all-to-all-start) | async-done | bytes 2097184 | tf_op jit(solution)/shard_map/select/all_to_all | solution.py:67
  160.3 22.4 %collective-permute-done.2 = bf16[3,192,2048]{2,1,0:T(8,128)(2,1)} collective-permute-done((bf16[3,192,2048]{2,1,0:T(8,128)(2,1)}, bf16[3,192,2048]{2,1,0:T(8,128)(2,1)}, u32[]{:S(2)}, u32[]{:S(2)}) %collective-permute-start.2) | collective-permute-done | bytes 2359328 | tf_op jit(solution)/shard_map/weights_out/ppermute | solution.py:50
  186.1 3.2 copy.50
  189.4 3.2 copy.54
  192.6 3.0 pad_maximum_fusion.2
  201.2 3.2 copy.51
  208.8 3.4 multiply_reduce_fusion
  214.6 6.0 %convolution_add_fusion = f32[1024,2048]{1,0:T(8,128)} fusion(f32[1024,2048]{1,0:T(8,128)S(1)} %fusion.13, bf16[1024,384]{0,1:T(8,128)(2,1)S(1)} %get-tuple-element.13, bf16[3,384,2048]{2,1,0:T(8,128)(2,1)S(1)} %constant_dynamic-update-slice_fusion), kind=kOutput, calls=%fused_computation.3 | convolution fusion | flops 1612709888 | bytes 19136512 | tf_op jit(solution)/shard_map/expert/rf,fd->rd/dot_general | solution.py:13
  220.6 10.8 %reshape.107 = f32[2,4,128,4,512]{4,3,2,1,0:T(4,128)} reshape(f32[1024,2048]{1,0:T(8,128)} %convolution_add_fusion) | data formatting | bytes 16777216 | tf_op jit(solution)/shard_map/expert/reshape | solution.py:104
  231.4 5.9 %copy.71 = f32[2,4,128,4,512]{4,2,3,1,0:T(8,128)S(1)} copy(f32[2,4,128,4,512]{4,3,2,1,0:T(4,128)} %reshape.107) | data formatting | bytes 16777216 | tf_op jit(solution)/shard_map/expert/reshape | solution.py:104
  245.4 4.1 %fusion.5 = bf16[1,384,2048]{2,1,0:T(8,128)(2,1)S(1)} fusion(bf16[1024,384]{0,1:T(8,128)(2,1)S(1)} %get-tuple-element.13, bf16[1024,2048]{1,0:T(8,128)(2,1)} %bitcast.107), kind=kOutput, calls=%fused_computation.15 | convolution fusion | flops 1611399168 | bytes 6553600 | tf_op jit(solution)/shard_map/expert/rf,rd->fd/dot_general | solution.py:13
  259.7 3.8 fusion.1
  263.5 7.8 %all-to-all-start.2 = ((bf16[16,128,512]{2,1,0:T(8,128)(2,1)}), bf16[16,128,512]{2,1,0:T(8,128)(2,1)}, u32[]{:S(2)}, u32[]{:S(2)}) async-start(bf16[16,128,512]{2,1,0:T(8,128)(2,1)} %fusion.1), calls=%async_computation.2 | async-start | bytes 4194304 | tf_op jit(solution)/shard_map/tokens_back/all_to_all | solution.py:143
  272.2 77.1 %all-gather.13.cloned.1.call-done = f32[256,2,512]{2,1,0:T(2,128)} async-done(((f32[1,2,512]{2,1,0:T(2,128)}), f32[256,2,512]{2,1,0:T(2,128)}) %all-gather.13.cloned.1.call-update) | async-done | bytes 1048592 | tf_op jit(solution)/shard_map/score_back/all_gather | solution.py:128
  350.7 4.9 %reshape.110 = f32[128,2,2,4,8,16]{5,4,3,1,0,2:T(8,128)} reshape(f32[256,2,512]{2,0,1:T(8,128)S(1)} %copy.57) | data formatting | bytes 2097152 | tf_op jit(solution)/shard_map/score_back/reshape | solution.py:129
  355.6 4.6 %fusion.38 = (f32[128,1,2,4,8,16]{5,4,3,1,0,2:T(8,128)S(1)}, f32[128,1,2,4,8,16]{5,4,3,1,0,2:T(8,128)S(1)}) fusion(f32[128,2,2,4,8,16]{5,4,3,1,0,2:T(8,128)} %reshape.110), kind=kLoop, calls=%fused_computation.87 | loop fusion | bytes 2097152 | tf_op jit(solution)/shard_map/score_back/slice | solution.py:130
  361.4 3.1 bitcast_convert_fusion
  370.7 28.5 %reduce-scatter.2.cloned.1.call-done = bf16[1,128,512]{2,1,0:T(8,128)(2,1)} async-done(((bf16[8,128,512]{2,1,0:T(8,128)(2,1)}), bf16[1,128,512]{2,1,0:T(8,128)(2,1)}) %reduce-scatter.2.cloned.1.call-update) | async-done | bytes 131088 | tf_op jit(solution)/shard_map/tokens_back/reduce_scatter | solution.py:146
  (102 shorter events, 64.1 us)
Async XLA Ops:
  7.2 50.9 %all-gather.11.cloned.1.call-start = ((), (), s32[]{:S(2)}) async-start(), calls=%async_computation.6 | async-start | bytes 1179648 | tf_op jit(solution)/shard_map/gather_z/all_gather | solution.py:42
  7.9 84.9 %all-gather.9.cloned.1.call-start = ((), (), s32[]{:S(2)}) async-start(), calls=%async_computation.5 | async-start | bytes 1179648 | tf_op jit(solution)/shard_map/gather_z/all_gather | solution.py:43
  61.6 60.2 %all-to-all-start.1 = ((bf16[16,128,512]{2,1,0:T(8,128)(2,1)}), bf16[16,128,512]{2,1,0:T(8,128)(2,1)S(1)}, u32[]{:S(2)}, u32[]{:S(2)}) async-start(bf16[16,128,512]{2,1,0:T(8,128)(2,1)} %bitcast.103), calls=%async_computation.1 | async-start | bytes 4194304 | tf_op jit(solution)/shard_map/select/all_to_all | solution.py:67
  68.1 2.4 copy-start.6
  73.6 84.8 %collective-permute-start.1 = (bf16[3,192,2048]{2,1,0:T(8,128)(2,1)}, bf16[3,192,2048]{2,1,0:T(8,128)(2,1)}, u32[]{:S(2)}, u32[]{:S(2)}) collective-permute-start(bf16[3,192,2048]{2,1,0:T(8,128)(2,1)} %pad_maximum_fusion.3), channel_id=1, source_target_pairs={{0,0},{1,1},{2,4},{3,5},{4,2},{5,3},{6,6},{7,7},{8,8},{9,9},{10,12... | collective-permute-start | bytes 7077896 | tf_op jit(solution)/shard_map/weights_out/ppermute | solution.py:50
  121.8 36.4 %all-to-all-start = ((bf16[16,128,512]{2,1,0:T(8,128)(2,1)}), bf16[16,128,512]{2,1,0:T(8,128)(2,1)}, u32[]{:S(2)}, u32[]{:S(2)}) async-start(bf16[16,128,512]{2,1,0:T(8,128)(2,1)} %bitcast.104), calls=%async_computation | async-start | bytes 4194304 | tf_op jit(solution)/shard_map/select/all_to_all | solution.py:67
  129.6 219.6 %all-gather.13.cloned.1.call-start = ((), (), s32[]{:S(2)}) async-start(), calls=%async_computation.7 | async-start | bytes 1052672 | tf_op jit(solution)/shard_map/score_back/all_gather | solution.py:128
  132.7 49.9 %collective-permute-start.2 = (bf16[3,192,2048]{2,1,0:T(8,128)(2,1)}, bf16[3,192,2048]{2,1,0:T(8,128)(2,1)}, u32[]{:S(2)}, u32[]{:S(2)}) collective-permute-start(bf16[3,192,2048]{2,1,0:T(8,128)(2,1)} %pad_maximum_fusion.4), channel_id=1, source_target_pairs={{0,1},{1,0},{2,5},{3,4},{4,3},{5,2},{6,7},{7,6},{8,9},{9,8},{10,13... | collective-permute-start | bytes 7077896 | tf_op jit(solution)/shard_map/weights_out/ppermute | solution.py:50
  132.9 56.5 %collective-permute-start.3 = (bf16[16,128,512]{2,1,0:T(8,128)(2,1)S(1)}, bf16[16,128,512]{2,1,0:T(8,128)(2,1)}, u32[]{:S(2)}, u32[]{:S(2)}) collective-permute-start(bf16[16,128,512]{2,1,0:T(8,128)(2,1)S(1)} %all-to-all-done.1), channel_id=1, source_target_pairs={{0,4},{4,0},{1,5},{5,1},{2,6},{6,2},{3,7},{7,3},{8,12},{12,8},{9,1... | collective-permute-start | bytes 6291464 | tf_op jit(solution)/shard_map/select/ppermute | solution.py:71
  158.2 43.0 %collective-permute-start = (bf16[16,128,512]{2,1,0:T(8,128)(2,1)}, bf16[16,128,512]{2,1,0:T(8,128)(2,1)}, u32[]{:S(2)}, u32[]{:S(2)}) collective-permute-start(bf16[16,128,512]{2,1,0:T(8,128)(2,1)} %all-to-all-done), channel_id=1, source_target_pairs={{0,4},{4,0},{1,5},{5,1},{2,6},{6,2},{3,7},{7,3},{8,12},{12,8},{9,1... | collective-permute-start | bytes 6291464 | tf_op jit(solution)/shard_map/select/ppermute | solution.py:72
  197.0 2.0 copy-start.1
  208.8 3.4 copy-start.3
  239.8 2.9 copy-start.2
  244.5 15.2 %collective-permute-start.4 = (bf16[16,128,512]{2,1,0:T(8,128)(2,1)}, bf16[16,128,512]{2,1,0:T(8,128)(2,1)}, u32[]{:S(2)}, u32[]{:S(2)}) collective-permute-start(bf16[16,128,512]{2,1,0:T(8,128)(2,1)} %bitcast.29), channel_id=1, source_target_pairs={{0,4},{4,0},{1,5},{5,1},{2,6},{6,2},{3,7},{7,3},{8,12},{12,8},{9,1... | collective-permute-start | bytes 6291464 | tf_op jit(solution)/shard_map/expert/ppermute | solution.py:106
  245.4 4.2 %copy-start.4 = (bf16[128,8,4,512]{3,1,2,0:T(8,128)(2,1)S(1)}, bf16[128,8,4,512]{3,1,2,0:T(8,128)(2,1)}, u32[]{:S(2)}) copy-start(bf16[128,8,4,512]{3,1,2,0:T(8,128)(2,1)} %copy-done.3) | copy-start | bytes 12582916
  245.4 4.2 %copy-start.11 = (bf16[1024,384]{0,1:T(8,128)(2,1)S(1)}, bf16[1024,384]{0,1:T(8,128)(2,1)}, u32[]{:S(2)}) copy-start(bf16[1024,384]{0,1:T(8,128)(2,1)} %get-tuple-element.6) | copy-start | bytes 2359300
  252.1 7.6 %copy-start = (f32[1,4,4,128,512]{4,3,2,1,0:T(8,128)S(1)}, f32[1,4,4,128,512]{4,3,2,1,0:T(8,128)}, u32[]{:S(2)}) copy-start(f32[1,4,4,128,512]{4,3,2,1,0:T(8,128)} %slice.81) | copy-start | bytes 12582916
  254.9 109.7 %collective-permute-start.5 = (bf16[3,192,2048]{2,1,0:T(8,128)(2,1)}, bf16[3,192,2048]{2,1,0:T(8,128)(2,1)S(1)}, u32[]{:S(2)}, u32[]{:S(2)}) collective-permute-start(bf16[3,192,2048]{2,1,0:T(8,128)(2,1)} %get-tuple-element.11), channel_id=1, source_target_pairs={{0,0},{1,1},{4,2},{5,3},{2,4},{3,5},{6,6},{7,7},{8,8},{9,9},{12,10... | collective-permute-start | bytes 7077896 | tf_op jit(solution)/shard_map/weights_back/ppermute | solution.py:120
  257.3 107.3 %collective-permute-start.6 = (bf16[3,192,2048]{2,1,0:T(8,128)(2,1)}, bf16[3,192,2048]{2,1,0:T(8,128)(2,1)}, u32[]{:S(2)}, u32[]{:S(2)}) collective-permute-start(bf16[3,192,2048]{2,1,0:T(8,128)(2,1)} %get-tuple-element.12), channel_id=1, source_target_pairs={{1,0},{0,1},{5,2},{4,3},{3,4},{2,5},{7,6},{6,7},{9,8},{8,9},{13,10... | collective-permute-start | bytes 7077896 | tf_op jit(solution)/shard_map/weights_back/ppermute | solution.py:120
  263.5 7.8 %copy-start.9 = (s32[128,8]{0,1:T(8,128)S(1)}, s32[128,8]{0,1:T(8,128)}, u32[]{:S(2)}) copy-start(s32[128,8]{0,1:T(8,128)} %param.9) | copy-start | bytes 12292
  263.5 97.9 %all-to-all-start.2 = ((bf16[16,128,512]{2,1,0:T(8,128)(2,1)}), bf16[16,128,512]{2,1,0:T(8,128)(2,1)}, u32[]{:S(2)}, u32[]{:S(2)}) async-start(bf16[16,128,512]{2,1,0:T(8,128)(2,1)} %fusion.1), calls=%async_computation.2 | async-start | bytes 4194304 | tf_op jit(solution)/shard_map/tokens_back/all_to_all | solution.py:143
  271.3 128.0 %reduce-scatter.2.cloned.1.call-start = ((), (), s32[]{:S(2)}) async-start(), calls=%async_computation.4 | async-start | bytes 1179648 | tf_op jit(solution)/shard_map/tokens_back/reduce_scatter | solution.py:146
  355.6 4.7 %copy-start.8 = (pred[128,128]{1,0:T(8,128)(4,1)S(1)}, pred[128,128]{1,0:T(8,128)(4,1)}, u32[]{:S(2)}) copy-start(pred[128,128]{1,0:T(8,128)(4,1)} %copy-done.7) | copy-start | bytes 49156
  355.6 5.2 %copy-start.10 = (s32[128,8]{0,1:T(8,128)S(1)}, s32[128,8]{0,1:T(8,128)}, u32[]{:S(2)}) copy-start(s32[128,8]{0,1:T(8,128)} %param.9) | copy-start | bytes 12292
  (2 other events, 2.5 us)
Sparse Core Ops, SparseCore 0:
  9.8 41.7 all-gather.10
  53.4 37.1 all-gather.8
  245.5 103.7 all-gather.12
  364.7 34.4 reduce-scatter.1

commit v2 on v1

v2 whole, which is shorter than its diff:
```python
import jax
import jax.numpy as jnp
from jax import lax
from jax.experimental import pallas as pl
from jax.experimental.pallas import tpu as pltpu
from jax.sharding import Mesh, PartitionSpec as P

BF = jnp.bfloat16
F32 = jnp.float32
NY, NZ, NC, NX = 4, 8, 2, 4
SLOT = 16
TOK = 128
TOP = 8
ROWS = NZ * SLOT
FULL = ROWS + 16
Q = 512
D = NX * Q
FQ = 192
FH = 2 * FQ
DEST = NY * NX
VMEM = pl.BlockSpec(memory_space=pltpu.VMEM)
SMEM = pl.BlockSpec(memory_space=pltpu.SMEM)


def params():
    return pltpu.CompilerParams(vmem_limit_bytes=56 * 1024 * 1024)


def dot(a, b, ca, cb):
    return lax.dot_general(a, b, (((ca,), (cb,)), ((), ())), preferred_element_type=F32)


def iota(shape, axis):
    return lax.broadcasted_iota(jnp.int32, shape, axis)


def expert_of(slot_row, iz, per):
    e = slot_row // per
    return (4 * ((e // NX) * NZ + iz) + e % NX).astype(F32)


def weight_pairs(m):
    pairs = []
    for c in range(NC):
        for h in range(NX):
            k = (h + m) % 2
            pairs.append((c * NX + h, (h // 2) * NX + 2 * c + k))
    return pairs


def select_x(at_ref, g_ref, out_ref, pick_ref):
    iz = at_ref[1]
    before = (iota((TOK, TOK), 0) < iota((TOK, TOK), 1)).astype(BF)
    ids = expert_of(iota((DEST, TOK), 0), iz, 1)
    slot = (iota((DEST * SLOT, TOK), 0) % SLOT).astype(F32)
    lane = iota((DEST * SLOT, TOK), 1)
    carried = jnp.zeros((DEST * SLOT, TOK), F32)
    for z in range(NZ):
        table = g_ref[z, 2 * TOK : 2 * TOK + 2 * TOP, :TOK].astype(F32)
        hit = jnp.zeros((DEST, TOK), F32)
        chance = jnp.zeros((DEST, TOK), F32)
        for k in range(TOP):
            on = table[k : k + 1, :] == ids
            hit = jnp.where(on, 1.0, hit)
            chance = jnp.where(on, table[TOP + k : TOP + k + 1, :], chance)
        rank = dot(hit.astype(BF), before, 1, 0)
        rank = jnp.where(hit > 0.5, rank, -1.0)
        wide = jnp.broadcast_to(rank[:, None, :], (DEST, SLOT, TOK)).reshape(DEST * SLOT, TOK)
        mine = wide == slot
        chance = jnp.broadcast_to(chance[:, None, :], (DEST, SLOT, TOK)).reshape(DEST * SLOT, TOK)
        share = jnp.sum(jnp.where(mine, chance, 0.0), axis=1, keepdims=True)
        carried = jnp.where(lane == z, share, carried)
        pick = jnp.where(mine, 1.0, 0.0).astype(BF)
        pick_ref[z] = pick
        got = dot(pick, g_ref[z, :TOK, :], 1, 0).astype(BF)
        out_ref[:, z * SLOT : (z + 1) * SLOT, :] = got.reshape(DEST, SLOT, Q)
    out_ref[:, ROWS:, :TOK] = carried.astype(BF).reshape(DEST, 16, TOK)
    out_ref[:, ROWS:, TOK:] = jnp.zeros((DEST, 16, Q - TOK), BF)


def select_d(g_ref, pick_ref, out_ref):
    for z in range(NZ):
        got = dot(pick_ref[z], g_ref[z, TOK : 2 * TOK, :], 1, 0).astype(BF)
        out_ref[:, z * SLOT : (z + 1) * SLOT, :] = got.reshape(DEST, SLOT, Q)


def expert(at_ref, x_ref, d_ref, wa_ref, wb_ref, part_ref, keep_ref):
    rows = NY * ROWS

    def take(ref, h):
        return jnp.concatenate([ref[y * NX + h, :ROWS, :] for y in range(NY)], axis=0)

    def project(ref, i):
        halves = []
        for w in (wa_ref, wb_ref):
            total = jnp.zeros((rows, FQ), F32)
            for h in range(NX):
                total = total + dot(take(ref, h), w[i, :, h * Q : (h + 1) * Q], 1, 1)
            halves.append(total)
        return halves

    columns = []
    for y in range(NY):
        carried = x_ref[y * NX, ROWS:, :TOK].astype(F32)
        columns += [carried[:, z : z + 1] for z in range(NZ)]
    weight = jnp.concatenate(columns, axis=0)
    gates = project(x_ref, 0)
    ups = project(x_ref, 1)
    raws = project(d_ref, 2)
    score = jnp.zeros((rows, 1), F32)
    dgates, dups = [], []
    for m in range(2):
        gate, up, raw = gates[m], ups[m], raws[m]
        sig = 1.0 / (1.0 + jnp.exp(-gate))
        act = gate * sig
        hidden = act * up
        score = score + jnp.sum(hidden * raw, axis=1, keepdims=True)
        dact = weight * raw
        dgate = (dact * up * sig * (1.0 + gate * (1.0 - sig))).astype(BF)
        dup = (dact * act).astype(BF)
        keep_ref[m, 0] = dgate
        keep_ref[m, 1] = dup
        keep_ref[m, 2] = (weight * hidden).astype(BF)
        dgates.append(dgate)
        dups.append(dup)
    for h in range(NX):
        cols = slice(h * Q, (h + 1) * Q)
        total = dot(dgates[0], wa_ref[0, :, cols], 1, 0) + dot(dups[0], wa_ref[1, :, cols], 1, 0)
        total = total + dot(dgates[1], wb_ref[0, :, cols], 1, 0) + dot(dups[1], wb_ref[1, :, cols], 1, 0)
        for y in range(NY):
            part_ref[y * NX + h, :ROWS, :] = total[y * ROWS : (y + 1) * ROWS].astype(BF)
    lane = iota((SLOT, TOK), 1) - 2 * NZ * at_ref[2]
    coarse = score.astype(BF).astype(F32)
    fine = score - coarse
    for y in range(NY):
        block = jnp.zeros((SLOT, TOK), F32)
        for z in range(NZ):
            at = (y * NZ + z) * SLOT
            block = jnp.where(lane == z, coarse[at : at + SLOT], block)
            block = jnp.where(lane == NZ + z, fine[at : at + SLOT], block)
        for h in range(NX):
            part_ref[y * NX + h, ROWS:, :TOK] = block.astype(BF)
            part_ref[y * NX + h, ROWS:, TOK:] = jnp.zeros((SLOT, Q - TOK), BF)


def weight_grads(xo_ref, xs_ref, do_ref, ds_ref, ko_ref, ks_ref, a_ref, b_ref, flip):
    @pl.when(pl.program_id(0) == 0)
    def _():
        for i in range(3):
            for m in range(2):
                flip[i, m, :, : NY * ROWS] = ko_ref[m, i].T
                flip[i, m, :, NY * ROWS :] = ks_ref[m, i].T

    def take(own, sibling):
        pieces = [own[y, 0, :ROWS, :] for y in range(NY)] + [sibling[y, 0, :ROWS, :] for y in range(NY)]
        return jnp.concatenate(pieces, axis=0)

    x = take(xo_ref, xs_ref)
    d = take(do_ref, ds_ref)
    for i, rows in ((0, x), (1, x), (2, d)):
        a_ref[i] = dot(flip[i, 0], rows, 1, 0).astype(BF)
        b_ref[i] = dot(flip[i, 1], rows, 1, 0).astype(BF)


def combine(at_ref, g_ref, pick_ref, home_ref, out_ref):
    iz = at_ref[1]
    ids = expert_of(iota((DEST, TOK), 0), iz, 1)
    carried = home_ref[:, ROWS:, :TOK].astype(F32).reshape(DEST * SLOT, TOK)
    for z in range(NZ):
        pick = pick_ref[z]
        rows = home_ref[:, z * SLOT : (z + 1) * SLOT, :].reshape(DEST * SLOT, Q)
        out_ref[z, :TOK, :] = dot(pick, rows, 0, 0).astype(BF)
        score = carried[:, z : z + 1] + carried[:, NZ + z : NZ + z + 1]
        score = score + (carried[:, 2 * NZ + z : 2 * NZ + z + 1] + carried[:, 3 * NZ + z : 3 * NZ + z + 1])
        spread = (pick.astype(F32) * score).reshape(DEST, SLOT, TOK)
        spread = jnp.sum(spread, axis=1)
        table = g_ref[z, 2 * TOK : 2 * TOK + TOP, :TOK].astype(F32)
        lines = [
            jnp.sum(jnp.where(table[k : k + 1, :] == ids, spread, 0.0), axis=0, keepdims=True)
            for k in range(TOP)
        ]
        lines = jnp.concatenate(lines + [jnp.zeros((16 - TOP, TOK), F32)], axis=0)
        coarse = lines.astype(BF)
        out_ref[z, TOK:, :TOK] = coarse
        out_ref[z, TOK:, TOK : 2 * TOK] = (lines - coarse.astype(F32)).astype(BF)
        out_ref[z, TOK:, 2 * TOK :] = jnp.zeros((16, Q - 2 * TOK), BF)


def per_device(tokens, cotangent, route, prob, w_gate, w_up, w_down):
    iy, iz, ic, ix = (lax.axis_index(a) for a in ("y", "z", "c", "x"))
    at = jnp.stack([iy, iz, ic, ix]).astype(jnp.int32)
    sib = [(0, 1), (1, 0)]
    shape = jax.ShapeDtypeStruct

    with jax.named_scope("gather_z"):
        table = jnp.concatenate([route.T.astype(BF), prob.T], axis=0)
        table = jnp.pad(table, ((0, 0), (0, Q - TOK)))
        packed = jnp.concatenate([tokens, cotangent, table], axis=0)
        every = lax.all_gather(packed, "z", axis=0, tiled=False)

    with jax.named_scope("weights_out"):
        weights = []
        for m in range(2):
            k = (ix + m) % 2
            piece = jnp.stack([lax.dynamic_index_in_dim(w, k, 0, keepdims=False) for w in (w_gate, w_up, w_down)])
            weights.append(lax.ppermute(piece, ("c", "x"), weight_pairs(m)))
        wa, wb = weights

    with jax.named_scope("select"):
        every, wa = lax.optimization_barrier((every, wa))
        xs, pick = pl.pallas_call(
            select_x,
            out_shape=(shape((DEST, FULL, Q), BF), shape((NZ, DEST * SLOT, TOK), BF)),
            in_specs=[SMEM, VMEM],
            out_specs=(VMEM, VMEM),
            compiler_params=params(),
            name="select_x",
        )(at, every)
        x_own = lax.all_to_all(xs, ("y", "x"), split_axis=0, concat_axis=0, tiled=True)
        pick_d, wb = lax.optimization_barrier((pick, wb))
        ds = pl.pallas_call(
            select_d,
            out_shape=shape((DEST, ROWS, Q), BF),
            in_specs=[VMEM, VMEM],
            out_specs=VMEM,
            compiler_params=params(),
            name="select_d",
        )(every, pick_d)
        d_own = lax.all_to_all(ds, ("y", "x"), split_axis=0, concat_axis=0, tiled=True)
        x_sib = lax.ppermute(x_own, "c", sib)
        d_sib = lax.ppermute(d_own, "c", sib)

    run = pl.pallas_call(
        expert,
        out_shape=(shape((DEST, FULL, Q), BF), shape((2, 3, NY * ROWS, FQ), BF)),
        in_specs=[SMEM, VMEM, VMEM, VMEM, VMEM],
        out_specs=(VMEM, VMEM),
        compiler_params=params(),
        name="expert",
    )
    with jax.named_scope("expert"):
        part_own, keep_own = run(at, x_own, d_own, wa, wb)
        part_sib, keep_sib = run(at, x_sib, d_sib, wa, wb)
        sent = lax.ppermute(part_sib, "c", sib)

    with jax.named_scope("weights_back"):
        x_spec = pl.BlockSpec((NY, 1, FULL, Q), lambda h: (0, h, 0, 0))
        d_spec = pl.BlockSpec((NY, 1, ROWS, Q), lambda h: (0, h, 0, 0))
        k_spec = pl.BlockSpec((2, 3, NY * ROWS, FQ), lambda h: (0, 0, 0, 0))
        o_spec = pl.BlockSpec((3, FQ, Q), lambda h: (0, 0, h))
        ga, gb = pl.pallas_call(
            weight_grads,
            grid=(NX,),
            out_shape=(shape((3, FQ, D), BF),) * 2,
            in_specs=[x_spec, x_spec, d_spec, d_spec, k_spec, k_spec],
            out_specs=(o_spec, o_spec),
            scratch_shapes=[pltpu.VMEM((3, 2, FQ, 2 * NY * ROWS), BF)],
            compiler_params=params(),
            name="weight_grads",
        )(
            x_own.reshape(NY, NX, FULL, Q),
            x_sib.reshape(NY, NX, FULL, Q),
            d_own.reshape(NY, NX, ROWS, Q),
            d_sib.reshape(NY, NX, ROWS, Q),
            keep_own,
            keep_sib,
        )
        back = []
        for m, g in ((0, ga), (1, gb)):
            inverse = [(b, a) for a, b in weight_pairs(m)]
            back.append(lax.ppermute(g, ("c", "x"), inverse))
        even = ix % 2 == 0
        first = jnp.where(even, back[0], back[1])
        second = jnp.where(even, back[1], back[0])
        grad_gate, grad_up, grad_down = (jnp.stack([first[i], second[i]]) for i in range(3))

    with jax.named_scope("tokens_back"):
        total = (part_own.astype(F32) + sent.astype(F32)).astype(BF)
        home = lax.all_to_all(total, ("y", "x"), split_axis=0, concat_axis=0, tiled=True)
        partial = pl.pallas_call(
            combine,
            out_shape=shape((NZ, TOK + 16, Q), BF),
            in_specs=[SMEM, VMEM, VMEM, VMEM],
            out_specs=VMEM,
            compiler_params=params(),
            name="combine",
        )(at, every, pick, home)
        last = lax.all_to_all(partial, "z", split_axis=0, concat_axis=0, tiled=True).astype(F32)
        grad_tokens = jnp.sum(last[:, :TOK], axis=0).astype(BF)
        lines = jnp.sum(last[:, TOK : TOK + TOP, : 2 * TOK], axis=0)
        grad_prob = (lines[:, :TOK] + lines[:, TOK:]).T
    return (grad_tokens, grad_prob, grad_gate, grad_up, grad_down)


def solution(mesh):
    grid = Mesh(mesh.devices.reshape(NY, NZ, NC, NX), ("y", "z", "c", "x"))
    owner = ("y", "z", "c")
    wide = P(owner, "x")
    thin = P(owner, None)
    deep = P(owner, "x", None)
    return jax.shard_map(
        per_device,
        mesh=grid,
        in_specs=(wide, wide, thin, thin, deep, deep, deep),
        out_specs=(wide, thin, deep, deep, deep),
        check_vma=False,
    )
```

time: 414 us -> 328 us (0.79)
  the two profiles are of different devices: /device:TPU:2 before, /device:TPU:1 now
where the time goes in v2:
time: 328 us; the launch traced here: 326 us
  waiting for transfers between devices  184 us (56%)
  starting transfers between devices  58.1 us (18%)
  Pallas kernels  46.5 us (14%)
  other arithmetic  17.7 us (5%)
  between operations  14.2 us (4%)
  local copies, waits for them, and re-layouts  4.9 us (1%)
    all_to_all x1, waiting for transfers between devices, per_device(): lax.all_to_all(total, ('y', 'x'), split_axis=0, concat_axis=0, tiled=True)  59.8 us
    ppermute x2, waiting for transfers between devices, per_device(): weights.append(lax.ppermute(piece, ('c', 'x'), weight_pairs(m)))  47 us
    all_to_all x1, waiting for transfers between devices, per_device(): lax.all_to_all(xs, ('y', 'x'), split_axis=0, concat_axis=0, tiled=True)  26.6 us
    all_to_all x1, waiting for transfers between devices, per_device(): lax.all_to_all(ds, ('y', 'x'), split_axis=0, concat_axis=0, tiled=True)  24.1 us
    all_to_all x1, waiting for transfers between devices, per_device(): lax.all_to_all(partial, 'z', split_axis=0, concat_axis=0, tiled=True)  22.8 us
    all_to_all x1, starting transfers between devices, per_device(): lax.all_to_all(total, ('y', 'x'), split_axis=0, concat_axis=0, tiled=True)  19.7 us
    pallas_call x1, Pallas kernels, per_device(): part_own, keep_own = run(at, x_own, d_own, wa, wb)  11 us
    pallas_call x1, Pallas kernels, per_device(): part_sib, keep_sib = run(at, x_sib, d_sib, wa, wb)  11 us
  transfers between devices with their start and end apart: 12, of which 6 were waited for; matrix products, arithmetic and copies ran while one was open for 5% of the time, Pallas kernels for 11%

profile of v2, /device:TPU:1, one launch (start us, length us, event | category | flops | bytes accessed | tf_op | source)
XLA Modules:
  0.0 325.8 jit_solution(6790845741969275045)
XLA Ops:
  12.5 1.7 pad_maximum_fusion
  14.2 6.0 %collective-permute-start = (bf16[3,192,2048]{2,1,0:T(8,128)(2,1)}, bf16[3,192,2048]{2,1,0:T(8,128)(2,1)S(1)}, u32[]{:S(2)}, u32[]{:S(2)}) collective-permute-start(bf16[3,192,2048]{2,1,0:T(8,128)(2,1)} %pad_maximum_fusion), channel_id=1, source_target_pairs={{0,0},{1,1},{2,4},{3,5},{4,2},{5,3},{6,6},{7,7},{8,8},{9,9},{10,12... | collective-permute-start | bytes 7077896 | tf_op jit(solution)/shard_map/weights_out/ppermute | solution.py:206
  20.2 1.7 pad_maximum_fusion.1
  23.1 47.0 %collective-permute-done.wa_ref = bf16[3,192,2048]{2,1,0:T(8,128)(2,1)S(1)} collective-permute-done((bf16[3,192,2048]{2,1,0:T(8,128)(2,1)}, bf16[3,192,2048]{2,1,0:T(8,128)(2,1)S(1)}, u32[]{:S(2)}, u32[]{:S(2)}) %collective-permute-start) | collective-permute-done | bytes 2359328 | tf_op jit(solution)/shard_map/weights_out/ppermute | solution.py:206
  70.1 5.8 %select_x.1 = (bf16[16,144,512]{2,1,0:T(8,128)(2,1)}, bf16[8,256,128]{2,1,0:T(8,128)(2,1)}) custom-call(s32[4]{0:T(128)} %pad_add_fusion.at_ref, bf16[8,272,512]{2,1,0:T(8,128)(2,1)} %bitcast.15), custom_call_target="tpu_custom_call" | custom-call | tf_op jit(solution)/shard_map/select/select_x/pallas_call | solution.py:211
  75.9 6.3 %all-to-all-start = ((bf16[16,144,512]{2,1,0:T(8,128)(2,1)}), bf16[16,144,512]{2,1,0:T(8,128)(2,1)S(1)}, u32[]{:S(2)}, u32[]{:S(2)}) async-start(bf16[16,144,512]{2,1,0:T(8,128)(2,1)} %get-tuple-element.19), calls=%async_computation | async-start | bytes 4718592 | tf_op jit(solution)/shard_map/select/all_to_all | solution.py:219
  82.2 3.7 %select_d.1 = bf16[16,128,512]{2,1,0:T(8,128)(2,1)} custom-call(bf16[8,272,512]{2,1,0:T(8,128)(2,1)} %bitcast.16, bf16[8,256,128]{2,1,0:T(8,128)(2,1)} %get-tuple-element.20.pick_ref), custom_call_target="tpu_custom_call" | custom-call | tf_op jit(solution)/shard_map/select/select_d/pallas_call | solution.py:221
  85.9 26.6 %all-to-all-done.x_ref = bf16[16,144,512]{2,1,0:T(8,128)(2,1)S(1)} async-done(((bf16[16,144,512]{2,1,0:T(8,128)(2,1)}), bf16[16,144,512]{2,1,0:T(8,128)(2,1)S(1)}, u32[]{:S(2)}, u32[]{:S(2)}) %all-to-all-start) | async-done | bytes 2359328 | tf_op jit(solution)/shard_map/select/all_to_all | solution.py:219
  112.6 6.6 %all-to-all-start.1 = ((bf16[16,128,512]{2,1,0:T(8,128)(2,1)}), bf16[16,128,512]{2,1,0:T(8,128)(2,1)}, u32[]{:S(2)}, u32[]{:S(2)}) async-start(bf16[16,128,512]{2,1,0:T(8,128)(2,1)} %select_d.1), calls=%async_computation.1 | async-start | bytes 4194304 | tf_op jit(solution)/shard_map/select/all_to_all | solution.py:229
  119.2 2.4 collective-permute-start.2
  121.5 24.1 %all-to-all-done.1.d_ref = bf16[16,128,512]{2,1,0:T(8,128)(2,1)} async-done(((bf16[16,128,512]{2,1,0:T(8,128)(2,1)}), bf16[16,128,512]{2,1,0:T(8,128)(2,1)}, u32[]{:S(2)}, u32[]{:S(2)}) %all-to-all-start.1) | async-done | bytes 2097184 | tf_op jit(solution)/shard_map/select/all_to_all | solution.py:229
  145.6 5.0 %collective-permute-start.3 = (bf16[16,128,512]{2,1,0:T(8,128)(2,1)}, bf16[16,128,512]{2,1,0:T(8,128)(2,1)S(1)}, u32[]{:S(2)}, u32[]{:S(2)}) collective-permute-start(bf16[16,128,512]{2,1,0:T(8,128)(2,1)} %all-to-all-done.1.d_ref), channel_id=1, source_target_pairs={{0,4},{4,0},{1,5},{5,1},{2,6},{6,2},{3,7},{7,3},{8,12},{12,8},{9,1... | collective-permute-start | bytes 6291464 | tf_op jit(solution)/shard_map/select/ppermute | solution.py:231
  150.7 4.0 %collective-permute-done.3.d_ref = bf16[16,128,512]{2,1,0:T(8,128)(2,1)S(1)} collective-permute-done((bf16[16,128,512]{2,1,0:T(8,128)(2,1)}, bf16[16,128,512]{2,1,0:T(8,128)(2,1)S(1)}, u32[]{:S(2)}, u32[]{:S(2)}) %collective-permute-start.3) | collective-permute-done | bytes 2097184 | tf_op jit(solution)/shard_map/select/ppermute | solution.py:231
  156.0 11.0 %expert.3 = (bf16[16,144,512]{2,1,0:T(8,128)(2,1)}, bf16[2,3,512,192]{3,2,1,0:T(8,128)(2,1)}) custom-call(s32[4]{0:T(128)} %pad_add_fusion.at_ref, bf16[16,144,512]{2,1,0:T(8,128)(2,1)} %collective-permute-done.2.x_ref, bf16[16,128,512]{2,1,0:T(8,128)(2,1)} %copy-done.3, bf16[3,192,2048]{2,1,0:T(8,128)(2,1)} %copy-done.1, ...), custom_call_target="tpu_custom_call" | custom-call | tf_op jit(solution)/shard_map/expert/expert/pallas_call | solution.py:243
  167.3 11.0 %expert.2 = (bf16[16,144,512]{2,1,0:T(8,128)(2,1)}, bf16[2,3,512,192]{3,2,1,0:T(8,128)(2,1)}) custom-call(s32[4]{0:T(128)} %pad_add_fusion.at_ref, bf16[16,144,512]{2,1,0:T(8,128)(2,1)} %copy-done, bf16[16,128,512]{2,1,0:T(8,128)(2,1)} %all-to-all-done.1.d_ref, bf16[3,192,2048]{2,1,0:T(8,128)(2,1)} %copy-done.1, ...), custom_call_target="tpu_custom_call" | custom-call | tf_op jit(solution)/shard_map/expert/expert/pallas_call | solution.py:242
  178.4 10.6 %weight_grads.1 = (bf16[3,192,2048]{2,1,0:T(8,128)(2,1)}, bf16[3,192,2048]{2,1,0:T(8,128)(2,1)}) custom-call(bf16[4,4,144,512]{3,2,1,0:T(8,128)(2,1)} %bitcast.14, bf16[4,4,144,512]{3,2,1,0:T(8,128)(2,1)} %bitcast.9.xs_ref, bf16[4,4,128,512]{3,2,1,0:T(8,128)(2,1)} %bitcast.10.do_ref, bf16[4,4,128,512]{3,2,1,0:T(8,128)(2,1)} %bitcast.18, ...), custom_call_target="tpu_custom_call" | custom-call | tf_op jit(solution)/shard_map/weights_back/weight_grads/pallas_call | solution.py:251
  189.0 1.9 collective-permute-start.5
  191.9 2.1 add_convert_fusion
  194.1 19.7 %all-to-all-start.2 = ((bf16[16,144,512]{2,1,0:T(8,128)(2,1)}), bf16[16,144,512]{2,1,0:T(8,128)(2,1)S(1)}, u32[]{:S(2)}, u32[]{:S(2)}) async-start(bf16[16,144,512]{2,1,0:T(8,128)(2,1)} %add_convert_fusion), calls=%async_computation.2 | async-start | bytes 4718592 | tf_op jit(solution)/shard_map/tokens_back/all_to_all | solution.py:279
  213.8 59.8 %all-to-all-done.2.home_ref = bf16[16,144,512]{2,1,0:T(8,128)(2,1)S(1)} async-done(((bf16[16,144,512]{2,1,0:T(8,128)(2,1)}), bf16[16,144,512]{2,1,0:T(8,128)(2,1)S(1)}, u32[]{:S(2)}, u32[]{:S(2)}) %all-to-all-start.2) | async-done | bytes 2359328 | tf_op jit(solution)/shard_map/tokens_back/all_to_all | solution.py:279
  274.9 4.4 %combine.1 = bf16[8,144,512]{2,1,0:T(8,128)(2,1)} custom-call(s32[4]{0:T(128)} %pad_add_fusion.at_ref, bf16[8,272,512]{2,1,0:T(8,128)(2,1)} %bitcast.17, bf16[8,256,128]{2,1,0:T(8,128)(2,1)} %get-tuple-element.20.pick_ref, bf16[16,144,512]{2,1,0:T(8,128)(2,1)} %copy-done.2), custom_call_target="tpu_custom_call" | custom-call | tf_op jit(solution)/shard_map/tokens_back/combine/pallas_call | solution.py:280
  279.3 8.2 %all-to-all-start.3 = ((bf16[8,144,512]{2,1,0:T(8,128)(2,1)}), bf16[8,144,512]{2,1,0:T(8,128)(2,1)S(1)}, u32[]{:S(2)}, u32[]{:S(2)}) async-start(bf16[8,144,512]{2,1,0:T(8,128)(2,1)} %combine.1), calls=%async_computation.3 | async-start | bytes 2359296 | tf_op jit(solution)/shard_map/tokens_back/all_to_all | solution.py:288
  287.5 2.7 broadcast_select_fusion.1
  294.4 22.8 %all-to-all-done.3 = bf16[8,144,512]{2,1,0:T(8,128)(2,1)S(1)} async-done(((bf16[8,144,512]{2,1,0:T(8,128)(2,1)}), bf16[8,144,512]{2,1,0:T(8,128)(2,1)S(1)}, u32[]{:S(2)}, u32[]{:S(2)}) %all-to-all-start.3) | async-done | bytes 1179680 | tf_op jit(solution)/shard_map/tokens_back/all_to_all | solution.py:288
  (40 shorter events, 16.4 us)
Async XLA Ops:
  7.2 4.9 %copy-start.5 = (bf16[2,192,2048]{2,1,0:T(8,128)(2,1)S(1)}, bf16[2,192,2048]{2,1,0:T(8,128)(2,1)}, u32[]{:S(2)}) copy-start(bf16[2,192,2048]{2,1,0:T(8,128)(2,1)} %param.13) | copy-start | bytes 4718596
  7.2 4.9 %copy-start.6 = (bf16[2,192,2048]{2,1,0:T(8,128)(2,1)S(1)}, bf16[2,192,2048]{2,1,0:T(8,128)(2,1)}, u32[]{:S(2)}) copy-start(bf16[2,192,2048]{2,1,0:T(8,128)(2,1)} %param.12) | copy-start | bytes 4718596
  7.2 62.9 %all-gather.3.cloned.1.call-start = ((), (), s32[]{:S(2)}) async-start(), calls=%async_computation.4 | async-start | bytes 2506752 | tf_op jit(solution)/shard_map/gather_z/all_gather | solution.py:199
  14.2 55.9 %collective-permute-start = (bf16[3,192,2048]{2,1,0:T(8,128)(2,1)}, bf16[3,192,2048]{2,1,0:T(8,128)(2,1)S(1)}, u32[]{:S(2)}, u32[]{:S(2)}) collective-permute-start(bf16[3,192,2048]{2,1,0:T(8,128)(2,1)} %pad_maximum_fusion), channel_id=1, source_target_pairs={{0,0},{1,1},{2,4},{3,5},{4,2},{5,3},{6,6},{7,7},{8,8},{9,9},{10,12... | collective-permute-start | bytes 7077896 | tf_op jit(solution)/shard_map/weights_out/ppermute | solution.py:206
  21.9 60.3 %collective-permute-start.1 = (bf16[3,192,2048]{2,1,0:T(8,128)(2,1)}, bf16[3,192,2048]{2,1,0:T(8,128)(2,1)}, u32[]{:S(2)}, u32[]{:S(2)}) collective-permute-start(bf16[3,192,2048]{2,1,0:T(8,128)(2,1)} %pad_maximum_fusion.1), channel_id=1, source_target_pairs={{0,1},{1,0},{2,5},{3,4},{4,3},{5,2},{6,7},{7,6},{8,9},{9,8},{10,13... | collective-permute-start | bytes 7077896 | tf_op jit(solution)/shard_map/weights_out/ppermute | solution.py:206
  70.1 5.8 %copy-start.1 = (bf16[3,192,2048]{2,1,0:T(8,128)(2,1)}, bf16[3,192,2048]{2,1,0:T(8,128)(2,1)S(1)}, u32[]{:S(2)}) copy-start(bf16[3,192,2048]{2,1,0:T(8,128)(2,1)S(1)} %collective-permute-done.wa_ref) | copy-start | bytes 7077892
  75.9 36.6 %all-to-all-start = ((bf16[16,144,512]{2,1,0:T(8,128)(2,1)}), bf16[16,144,512]{2,1,0:T(8,128)(2,1)S(1)}, u32[]{:S(2)}, u32[]{:S(2)}) async-start(bf16[16,144,512]{2,1,0:T(8,128)(2,1)} %get-tuple-element.19), calls=%async_computation | async-start | bytes 4718592 | tf_op jit(solution)/shard_map/select/all_to_all | solution.py:219
  112.6 54.4 %copy-start = (bf16[16,144,512]{2,1,0:T(8,128)(2,1)}, bf16[16,144,512]{2,1,0:T(8,128)(2,1)S(1)}, u32[]{:S(2)}) copy-start(bf16[16,144,512]{2,1,0:T(8,128)(2,1)S(1)} %all-to-all-done.x_ref) | copy-start | bytes 7077892
  112.6 33.1 %all-to-all-start.1 = ((bf16[16,128,512]{2,1,0:T(8,128)(2,1)}), bf16[16,128,512]{2,1,0:T(8,128)(2,1)}, u32[]{:S(2)}, u32[]{:S(2)}) async-start(bf16[16,128,512]{2,1,0:T(8,128)(2,1)} %select_d.1), calls=%async_computation.1 | async-start | bytes 4194304 | tf_op jit(solution)/shard_map/select/all_to_all | solution.py:229
  119.2 35.5 %collective-permute-start.2 = (bf16[16,144,512]{2,1,0:T(8,128)(2,1)S(1)}, bf16[16,144,512]{2,1,0:T(8,128)(2,1)}, u32[]{:S(2)}, u32[]{:S(2)}) collective-permute-start(bf16[16,144,512]{2,1,0:T(8,128)(2,1)S(1)} %all-to-all-done.x_ref), channel_id=1, source_target_pairs={{0,4},{4,0},{1,5},{5,1},{2,6},{6,2},{3,7},{7,3},{8,12},{12,8},{9,1... | collective-permute-start | bytes 7077896 | tf_op jit(solution)/shard_map/select/ppermute | solution.py:230
  145.6 9.0 %collective-permute-start.3 = (bf16[16,128,512]{2,1,0:T(8,128)(2,1)}, bf16[16,128,512]{2,1,0:T(8,128)(2,1)S(1)}, u32[]{:S(2)}, u32[]{:S(2)}) collective-permute-start(bf16[16,128,512]{2,1,0:T(8,128)(2,1)} %all-to-all-done.1.d_ref), channel_id=1, source_target_pairs={{0,4},{4,0},{1,5},{5,1},{2,6},{6,2},{3,7},{7,3},{8,12},{12,8},{9,1... | collective-permute-start | bytes 6291464 | tf_op jit(solution)/shard_map/select/ppermute | solution.py:231
  154.7 1.3 copy-start.3
  167.0 25.0 %collective-permute-start.4 = (bf16[16,144,512]{2,1,0:T(8,128)(2,1)}, bf16[16,144,512]{2,1,0:T(8,128)(2,1)S(1)}, u32[]{:S(2)}, u32[]{:S(2)}) collective-permute-start(bf16[16,144,512]{2,1,0:T(8,128)(2,1)} %get-tuple-element.24), channel_id=1, source_target_pairs={{0,4},{4,0},{1,5},{5,1},{2,6},{6,2},{3,7},{7,3},{8,12},{12,8},{9,1... | collective-permute-start | bytes 7077896 | tf_op jit(solution)/shard_map/expert/ppermute | solution.py:244
  178.4 13.5 %copy-start.4 = (bf16[16,144,512]{2,1,0:T(8,128)(2,1)S(1)}, bf16[16,144,512]{2,1,0:T(8,128)(2,1)}, u32[]{:S(2)}) copy-start(bf16[16,144,512]{2,1,0:T(8,128)(2,1)} %get-tuple-element.23) | copy-start | bytes 7077892
  189.0 98.5 %collective-permute-start.5 = (bf16[3,192,2048]{2,1,0:T(8,128)(2,1)}, bf16[3,192,2048]{2,1,0:T(8,128)(2,1)}, u32[]{:S(2)}, u32[]{:S(2)}) collective-permute-start(bf16[3,192,2048]{2,1,0:T(8,128)(2,1)} %get-tuple-element.27), channel_id=1, source_target_pairs={{0,0},{1,1},{4,2},{5,3},{2,4},{3,5},{6,6},{7,7},{8,8},{9,9},{12,10... | collective-permute-start | bytes 7077896 | tf_op jit(solution)/shard_map/weights_back/ppermute | solution.py:271
  190.9 96.6 %collective-permute-start.6 = (bf16[3,192,2048]{2,1,0:T(8,128)(2,1)}, bf16[3,192,2048]{2,1,0:T(8,128)(2,1)}, u32[]{:S(2)}, u32[]{:S(2)}) collective-permute-start(bf16[3,192,2048]{2,1,0:T(8,128)(2,1)} %get-tuple-element.28), channel_id=1, source_target_pairs={{1,0},{0,1},{5,2},{4,3},{3,4},{2,5},{7,6},{6,7},{9,8},{8,9},{13,10... | collective-permute-start | bytes 7077896 | tf_op jit(solution)/shard_map/weights_back/ppermute | solution.py:271
  194.1 79.5 %all-to-all-start.2 = ((bf16[16,144,512]{2,1,0:T(8,128)(2,1)}), bf16[16,144,512]{2,1,0:T(8,128)(2,1)S(1)}, u32[]{:S(2)}, u32[]{:S(2)}) async-start(bf16[16,144,512]{2,1,0:T(8,128)(2,1)} %add_convert_fusion), calls=%async_computation.2 | async-start | bytes 4718592 | tf_op jit(solution)/shard_map/tokens_back/all_to_all | solution.py:279
  273.5 1.4 copy-start.2
  279.3 37.9 %all-to-all-start.3 = ((bf16[8,144,512]{2,1,0:T(8,128)(2,1)}), bf16[8,144,512]{2,1,0:T(8,128)(2,1)S(1)}, u32[]{:S(2)}, u32[]{:S(2)}) async-start(bf16[8,144,512]{2,1,0:T(8,128)(2,1)} %combine.1), calls=%async_computation.3 | async-start | bytes 2359296 | tf_op jit(solution)/shard_map/tokens_back/all_to_all | solution.py:288
Sparse Core Ops, SparseCore 0:
  10.7 41.4 all-gather.2

commit v3 on v2

--- a/solution.py
+++ b/solution.py
@@ -22,8 +22,8 @@
 SMEM = pl.BlockSpec(memory_space=pltpu.SMEM)
 
 
-def params():
-    return pltpu.CompilerParams(vmem_limit_bytes=56 * 1024 * 1024)
+def params(mib=32):
+    return pltpu.CompilerParams(vmem_limit_bytes=mib * 1024 * 1024)
 
 
 def dot(a, b, ca, cb):
@@ -84,49 +84,50 @@
         out_ref[:, z * SLOT : (z + 1) * SLOT, :] = got.reshape(DEST, SLOT, Q)
 
 
-def expert(at_ref, x_ref, d_ref, wa_ref, wb_ref, part_ref, keep_ref):
-    rows = NY * ROWS
-
-    def take(ref, h):
-        return jnp.concatenate([ref[y * NX + h, :ROWS, :] for y in range(NY)], axis=0)
-
-    def project(ref, i):
-        halves = []
-        for w in (wa_ref, wb_ref):
-            total = jnp.zeros((rows, FQ), F32)
-            for h in range(NX):
-                total = total + dot(take(ref, h), w[i, :, h * Q : (h + 1) * Q], 1, 1)
-            halves.append(total)
-        return halves
-
+def take(ref, h):
+    return jnp.concatenate([ref[y * NX + h, :ROWS, :] for y in range(NY)], axis=0)
+
+
+def both(w, i, h):
+    cols = slice(h * Q, (h + 1) * Q)
+    second = w[1][0, :, cols] if i == 0 else w[2][i - 1, :, cols]
+    return jnp.concatenate([w[0][i, :, cols], second], axis=0)
+
+
+def project(ref, w, i):
+    total = dot(take(ref, 0), both(w, i, 0), 1, 1)
+    for h in range(1, NX):
+        total = total + dot(take(ref, h), both(w, i, h), 1, 1)
+    return total
+
+
+def gates(x_ref, wa_ref, wb_ref, wc_ref, pre_ref, keep_ref):
+    w = (wa_ref, wb_ref, wc_ref)
     columns = []
     for y in range(NY):
         carried = x_ref[y * NX, ROWS:, :TOK].astype(F32)
         columns += [carried[:, z : z + 1] for z in range(NZ)]
     weight = jnp.concatenate(columns, axis=0)
-    gates = project(x_ref, 0)
-    ups = project(x_ref, 1)
-    raws = project(d_ref, 2)
-    score = jnp.zeros((rows, 1), F32)
-    dgates, dups = [], []
-    for m in range(2):
-        gate, up, raw = gates[m], ups[m], raws[m]
-        sig = 1.0 / (1.0 + jnp.exp(-gate))
-        act = gate * sig
-        hidden = act * up
-        score = score + jnp.sum(hidden * raw, axis=1, keepdims=True)
-        dact = weight * raw
-        dgate = (dact * up * sig * (1.0 + gate * (1.0 - sig))).astype(BF)
-        dup = (dact * act).astype(BF)
-        keep_ref[m, 0] = dgate
-        keep_ref[m, 1] = dup
-        keep_ref[m, 2] = (weight * hidden).astype(BF)
-        dgates.append(dgate)
-        dups.append(dup)
+    gate = project(x_ref, w, 0)
+    up = project(x_ref, w, 1)
+    sig = 1.0 / (1.0 + jnp.exp(-gate))
+    act = gate * sig
+    hidden = act * up
+    pre_ref[0] = hidden
+    pre_ref[1] = weight * (up * (sig * (1.0 + gate * (1.0 - sig))))
+    pre_ref[2] = weight * act
+    keep_ref[...] = (weight * hidden).astype(BF)
+
+
+def expert(at_ref, pre_ref, d_ref, wa_ref, wb_ref, wc_ref, part_ref, keep_ref):
+    w = (wa_ref, wb_ref, wc_ref)
+    raw = project(d_ref, w, 2)
+    score = jnp.sum(pre_ref[0] * raw, axis=1, keepdims=True)
+    keep_ref[0] = (raw * pre_ref[1]).astype(BF)
+    keep_ref[1] = (raw * pre_ref[2]).astype(BF)
     for h in range(NX):
-        cols = slice(h * Q, (h + 1) * Q)
-        total = dot(dgates[0], wa_ref[0, :, cols], 1, 0) + dot(dups[0], wa_ref[1, :, cols], 1, 0)
-        total = total + dot(dgates[1], wb_ref[0, :, cols], 1, 0) + dot(dups[1], wb_ref[1, :, cols], 1, 0)
+        total = dot(keep_ref[0], both(w, 0, h), 1, 0)
+        total = total + dot(keep_ref[1], both(w, 1, h), 1, 0)
         for y in range(NY):
             part_ref[y * NX + h, :ROWS, :] = total[y * ROWS : (y + 1) * ROWS].astype(BF)
     lane = iota((SLOT, TOK), 1) - 2 * NZ * at_ref[2]
@@ -143,23 +144,38 @@
             part_ref[y * NX + h, ROWS:, TOK:] = jnp.zeros((SLOT, Q - TOK), BF)
 
 
-def weight_grads(xo_ref, xs_ref, do_ref, ds_ref, ko_ref, ks_ref, a_ref, b_ref, flip):
+def weight_grads(xo_ref, xs_ref, do_ref, ds_ref, ho_ref, hs_ref, ko_ref, ks_ref, a_ref, b_ref, flip):
     @pl.when(pl.program_id(0) == 0)
     def _():
-        for i in range(3):
-            for m in range(2):
-                flip[i, m, :, : NY * ROWS] = ko_ref[m, i].T
-                flip[i, m, :, NY * ROWS :] = ks_ref[m, i].T
-
-    def take(own, sibling):
+        for i in range(2):
+            flip[i, :, : NY * ROWS] = ko_ref[i].T
+            flip[i, :, NY * ROWS :] = ks_ref[i].T
+        flip[2, :, : NY * ROWS] = ho_ref[...].T
+        flip[2, :, NY * ROWS :] = hs_ref[...].T
+
+    def gather(own, sibling):
         pieces = [own[y, 0, :ROWS, :] for y in range(NY)] + [sibling[y, 0, :ROWS, :] for y in range(NY)]
         return jnp.concatenate(pieces, axis=0)
 
-    x = take(xo_ref, xs_ref)
-    d = take(do_ref, ds_ref)
+    x = gather(xo_ref, xs_ref)
+    d = gather(do_ref, ds_ref)
     for i, rows in ((0, x), (1, x), (2, d)):
-        a_ref[i] = dot(flip[i, 0], rows, 1, 0).astype(BF)
-        b_ref[i] = dot(flip[i, 1], rows, 1, 0).astype(BF)
+        grad = dot(flip[i], rows, 1, 0).astype(BF)
+        a_ref[i] = grad[:FQ]
+        b_ref[i] = grad[FQ:]
+
+
+def place(at_ref, a_ref, b_ref, gate_ref, up_ref, down_ref, sem):
+    odd = at_ref[3] % 2
+    copies = []
+    for m, src in ((0, a_ref), (1, b_ref)):
+        k = (odd + m) % 2
+        for i, dst in enumerate((gate_ref, up_ref, down_ref)):
+            copies.append(pltpu.make_async_copy(src.at[i], dst.at[k], sem.at[m, i]))
+    for copy in copies:
+        copy.start()
+    for copy in copies:
+        copy.wait()
 
 
 def combine(at_ref, g_ref, pick_ref, home_ref, out_ref):
@@ -200,14 +216,15 @@
 
     with jax.named_scope("weights_out"):
         weights = []
-        for m in range(2):
+        for m, mats in ((0, (w_gate, w_up, w_down)), (1, (w_gate,)), (1, (w_up, w_down))):
             k = (ix + m) % 2
-            piece = jnp.stack([lax.dynamic_index_in_dim(w, k, 0, keepdims=False) for w in (w_gate, w_up, w_down)])
+            piece = jnp.stack([lax.dynamic_index_in_dim(w, k, 0, keepdims=False) for w in mats])
+            if len(weights) == 2:
+                piece, weights[0] = lax.optimization_barrier((piece, weights[0]))
             weights.append(lax.ppermute(piece, ("c", "x"), weight_pairs(m)))
-        wa, wb = weights
 
     with jax.named_scope("select"):
-        every, wa = lax.optimization_barrier((every, wa))
+        every, *weights[:2] = lax.optimization_barrier((every, *weights[:2]))
         xs, pick = pl.pallas_call(
             select_x,
             out_shape=(shape((DEST, FULL, Q), BF), shape((NZ, DEST * SLOT, TOK), BF)),
@@ -217,7 +234,6 @@
             name="select_x",
         )(at, every)
         x_own = lax.all_to_all(xs, ("y", "x"), split_axis=0, concat_axis=0, tiled=True)
-        pick_d, wb = lax.optimization_barrier((pick, wb))
         ds = pl.pallas_call(
             select_d,
             out_shape=shape((DEST, ROWS, Q), BF),
@@ -225,36 +241,53 @@
             out_specs=VMEM,
             compiler_params=params(),
             name="select_d",
-        )(every, pick_d)
+        )(every, pick)
+        ds, weights[2] = lax.optimization_barrier((ds, weights[2]))
         d_own = lax.all_to_all(ds, ("y", "x"), split_axis=0, concat_axis=0, tiled=True)
         x_sib = lax.ppermute(x_own, "c", sib)
+
+    half = NY * ROWS
+    with jax.named_scope("gates"):
+        ahead = pl.pallas_call(
+            gates,
+            out_shape=(shape((3, half, FH), F32), shape((half, FH), BF)),
+            in_specs=[VMEM] * 4,
+            out_specs=(VMEM, VMEM),
+            compiler_params=params(),
+            name="gates",
+        )
+        pre_own, hid_own = ahead(x_own, *weights)
+        pre_sib, hid_sib = ahead(x_sib, *weights)
+        d_own, pre_own, pre_sib = lax.optimization_barrier((d_own, pre_own, pre_sib))
         d_sib = lax.ppermute(d_own, "c", sib)
-
     run = pl.pallas_call(
         expert,
-        out_shape=(shape((DEST, FULL, Q), BF), shape((2, 3, NY * ROWS, FQ), BF)),
-        in_specs=[SMEM, VMEM, VMEM, VMEM, VMEM],
+        out_shape=(shape((DEST, FULL, Q), BF), shape((2, half, FH), BF)),
+        in_specs=[SMEM] + [VMEM] * 5,
         out_specs=(VMEM, VMEM),
         compiler_params=params(),
         name="expert",
     )
     with jax.named_scope("expert"):
-        part_own, keep_own = run(at, x_own, d_own, wa, wb)
-        part_sib, keep_sib = run(at, x_sib, d_sib, wa, wb)
+        part_sib, keep_sib = run(at, pre_sib, d_sib, *weights)
         sent = lax.ppermute(part_sib, "c", sib)
+        part_own, keep_own = run(at, pre_own, d_own, *weights)
+        total = (part_own.astype(F32) + sent.astype(F32)).astype(BF)
+        total, keep_own, keep_sib = lax.optimization_barrier((total, keep_own, keep_sib))
 
     with jax.named_scope("weights_back"):
         x_spec = pl.BlockSpec((NY, 1, FULL, Q), lambda h: (0, h, 0, 0))
         d_spec = pl.BlockSpec((NY, 1, ROWS, Q), lambda h: (0, h, 0, 0))
-        k_spec = pl.BlockSpec((2, 3, NY * ROWS, FQ), lambda h: (0, 0, 0, 0))
+        h_spec = pl.BlockSpec((half, FH), lambda h: (0, 0))
+        k_spec = pl.BlockSpec((2, half, FH), lambda h: (0, 0, 0))
         o_spec = pl.BlockSpec((3, FQ, Q), lambda h: (0, 0, h))
         ga, gb = pl.pallas_call(
             weight_grads,
             grid=(NX,),
             out_shape=(shape((3, FQ, D), BF),) * 2,
-            in_specs=[x_spec, x_spec, d_spec, d_spec, k_spec, k_spec],
+            in_specs=[x_spec, x_spec, d_spec, d_spec, h_spec, h_spec, k_spec, k_spec],
             out_specs=(o_spec, o_spec),
-            scratch_shapes=[pltpu.VMEM((3, 2, FQ, 2 * NY * ROWS), BF)],
+            scratch_shapes=[pltpu.VMEM((3, FH, 2 * half), BF)],
             compiler_params=params(),
             name="weight_grads",
         )(
@@ -262,6 +295,8 @@
             x_sib.reshape(NY, NX, FULL, Q),
             d_own.reshape(NY, NX, ROWS, Q),
             d_sib.reshape(NY, NX, ROWS, Q),
+            hid_own,
+            hid_sib,
             keep_own,
             keep_sib,
         )
@@ -269,13 +304,18 @@
         for m, g in ((0, ga), (1, gb)):
             inverse = [(b, a) for a, b in weight_pairs(m)]
             back.append(lax.ppermute(g, ("c", "x"), inverse))
-        even = ix % 2 == 0
-        first = jnp.where(even, back[0], back[1])
-        second = jnp.where(even, back[1], back[0])
-        grad_gate, grad_up, grad_down = (jnp.stack([first[i], second[i]]) for i in range(3))
+        anywhere = pl.BlockSpec(memory_space=pl.ANY)
+        grad_gate, grad_up, grad_down = pl.pallas_call(
+            place,
+            out_shape=(shape((2, FQ, D), BF),) * 3,
+            in_specs=[SMEM, anywhere, anywhere],
+            out_specs=(anywhere,) * 3,
+            scratch_shapes=[pltpu.SemaphoreType.DMA((2, 3))],
+            compiler_params=params(),
+            name="place",
+        )(at, back[0], back[1])
 
     with jax.named_scope("tokens_back"):
-        total = (part_own.astype(F32) + sent.astype(F32)).astype(BF)
         home = lax.all_to_all(total, ("y", "x"), split_axis=0, concat_axis=0, tiled=True)
         partial = pl.pallas_call(
             combine,

time: 328 us -> 419 us (1.28)
  Pallas kernels: 46.5 us -> 181 us
  waiting for transfers between devices: 184 us -> 138 us
  local copies, waits for them, and re-layouts: 4.9 us -> 22.5 us
  starting transfers between devices: 58.1 us -> 49.7 us
  other arithmetic: 17.7 us -> 11.7 us
    pallas_call x2 -> x5, Pallas kernels: 22 us -> 165 us  [the longest x1 145 us: per_device(): pl.pallas_call(place, out_shape=(shape((2, FQ, D), BF),) * 3, in_specs=[S...]
    all_to_all x1, waiting for transfers between devices: 59.8 us -> 17.4 us  [per_device(): lax.all_to_all(total, ('y', 'x'), split_axis=0, concat_axis=0, tiled=True)]
    ppermute x2, waiting for transfers between devices: 0.01 us -> 36.4 us  [per_device(): back.append(lax.ppermute(g, ('c', 'x'), inverse))]
    all_to_all x1, waiting for transfers between devices: 22.8 us -> 0.01 us  [per_device(): lax.all_to_all(partial, 'z', split_axis=0, concat_axis=0, tiled=True)]
    unnamed x14 -> x48, local copies, waits for them, and re-layouts: 2.71 us -> 18.6 us
    all_to_all x1, starting transfers between devices: 19.7 us -> 4.59 us  [per_device(): lax.all_to_all(total, ('y', 'x'), split_axis=0, concat_axis=0, tiled=True)]
    all_to_all x1, waiting for transfers between devices: 24.1 us -> 14.5 us  [per_device(): lax.all_to_all(ds, ('y', 'x'), split_axis=0, concat_axis=0, tiled=True)]
    ppermute x2 -> x3, waiting for transfers between devices: 47 us -> 39.2 us  [per_device(): weights.append(lax.ppermute(piece, ('c', 'x'), weight_pairs(m)))]
  transfers between devices with their start and end apart: 12 -> 13, of which waited for: 6 -> 8; matrix products, arithmetic and copies ran while one was open for 5% -> 2% of each run, Pallas kernels for 11% -> 41%
where the time goes in v3:
time: 419 us; the launch traced here: 417 us
  Pallas kernels  181 us (43%)
  waiting for transfers between devices  138 us (33%)
  starting transfers between devices  49.7 us (12%)
  local copies, waits for them, and re-layouts  22.5 us (5%)
  between operations  14.3 us (3%)
  other arithmetic  11.7 us (3%)
    pallas_call x1, Pallas kernels, per_device(): pl.pallas_call(place, out_shape=(shape((2, FQ, D), BF),) * 3, in_specs=[S...  145 us
    ppermute x3, waiting for transfers between devices, per_device(): weights.append(lax.ppermute(piece, ('c', 'x'), weight_pairs(m)))  39.2 us
    ppermute x2, waiting for transfers between devices, per_device(): back.append(lax.ppermute(g, ('c', 'x'), inverse))  36.4 us
    all_to_all x1, waiting for transfers between devices, per_device(): lax.all_to_all(xs, ('y', 'x'), split_axis=0, concat_axis=0, tiled=True)  26.5 us
    unnamed x48, local copies, waits for them, and re-layouts  18.6 us
    all_to_all x1, waiting for transfers between devices, per_device(): lax.all_to_all(total, ('y', 'x'), split_axis=0, concat_axis=0, tiled=True)  17.4 us
    all_to_all x1, waiting for transfers between devices, per_device(): lax.all_to_all(ds, ('y', 'x'), split_axis=0, concat_axis=0, tiled=True)  14.5 us
    ppermute x3, starting transfers between devices, per_device(): weights.append(lax.ppermute(piece, ('c', 'x'), weight_pairs(m)))  11.3 us
  transfers between devices with their start and end apart: 13, of which 8 were waited for; matrix products, arithmetic and copies ran while one was open for 2% of the time, Pallas kernels for 41%

profile of v3, /device:TPU:1, one launch (start us, length us, event | category | flops | bytes accessed | tf_op | source)
XLA Modules:
  0.0 417.3 jit_solution(16465902007957438374)
XLA Ops:
  16.1 6.0 %collective-permute-start = (bf16[3,192,2048]{2,1,0:T(8,128)(2,1)}, bf16[3,192,2048]{2,1,0:T(8,128)(2,1)S(1)}, u32[]{:S(2)}, u32[]{:S(2)}) collective-permute-start(bf16[3,192,2048]{2,1,0:T(8,128)(2,1)} %pad_maximum_fusion), channel_id=1, source_target_pairs={{0,0},{1,1},{2,4},{3,5},{4,2},{5,3},{6,6},{7,7},{8,8},{9,9},{10,12... | collective-permute-start | bytes 7077896 | tf_op jit(solution)/shard_map/weights_out/ppermute | solution.py:224
  22.9 2.7 pad_maximum_fusion.1
  25.6 31.9 %collective-permute-done.wa_ref = bf16[3,192,2048]{2,1,0:T(8,128)(2,1)S(1)} collective-permute-done((bf16[3,192,2048]{2,1,0:T(8,128)(2,1)}, bf16[3,192,2048]{2,1,0:T(8,128)(2,1)S(1)}, u32[]{:S(2)}, u32[]{:S(2)}) %collective-permute-start) | collective-permute-done | bytes 2359328 | tf_op jit(solution)/shard_map/weights_out/ppermute | solution.py:224
  64.9 4.4 %all-to-all-start.1 = ((bf16[16,144,512]{2,1,0:T(8,128)(2,1)}), bf16[16,144,512]{2,1,0:T(8,128)(2,1)}, u32[]{:S(2)}, u32[]{:S(2)}) async-start(bf16[16,144,512]{2,1,0:T(8,128)(2,1)} %copy-done.10), calls=%async_computation.1 | async-start | bytes 4718592 | tf_op jit(solution)/shard_map/select/all_to_all | solution.py:236
  69.3 4.7 %collective-permute-start.2 = (bf16[2,192,2048]{2,1,0:T(8,128)(2,1)}, bf16[2,192,2048]{2,1,0:T(8,128)(2,1)}, u32[]{:S(2)}, u32[]{:S(2)}) collective-permute-start(bf16[2,192,2048]{2,1,0:T(8,128)(2,1)} %pad_maximum_fusion.1), channel_id=1, source_target_pairs={{0,1},{1,0},{2,5},{3,4},{4,3},{5,2},{6,7},{7,6},{8,9},{9,8},{10,13... | collective-permute-start | bytes 4718600 | tf_op jit(solution)/shard_map/weights_out/ppermute | solution.py:224
  74.0 26.5 %all-to-all-done.1.x_ref = bf16[16,144,512]{2,1,0:T(8,128)(2,1)} async-done(((bf16[16,144,512]{2,1,0:T(8,128)(2,1)}), bf16[16,144,512]{2,1,0:T(8,128)(2,1)}, u32[]{:S(2)}, u32[]{:S(2)}) %all-to-all-start.1) | async-done | bytes 2359328 | tf_op jit(solution)/shard_map/select/all_to_all | solution.py:236
  100.5 5.7 %collective-permute-start.3 = (bf16[16,144,512]{2,1,0:T(8,128)(2,1)}, bf16[16,144,512]{2,1,0:T(8,128)(2,1)}, u32[]{:S(2)}, u32[]{:S(2)}) collective-permute-start(bf16[16,144,512]{2,1,0:T(8,128)(2,1)} %all-to-all-done.1.x_ref), channel_id=1, source_target_pairs={{0,4},{4,0},{1,5},{5,1},{2,6},{6,2},{3,7},{7,3},{8,12},{12,8},{9,1... | collective-permute-start | bytes 7077896 | tf_op jit(solution)/shard_map/select/ppermute | solution.py:247
  110.9 6.1 %collective-permute-done.2.wc_ref = bf16[2,192,2048]{2,1,0:T(8,128)(2,1)} collective-permute-done((bf16[2,192,2048]{2,1,0:T(8,128)(2,1)}, bf16[2,192,2048]{2,1,0:T(8,128)(2,1)}, u32[]{:S(2)}, u32[]{:S(2)}) %collective-permute-start.2) | collective-permute-done | bytes 1572896 | tf_op jit(solution)/shard_map/weights_out/ppermute | solution.py:224
  117.0 5.4 %all-to-all-start = ((bf16[16,128,512]{2,1,0:T(8,128)(2,1)}), bf16[16,128,512]{2,1,0:T(8,128)(2,1)}, u32[]{:S(2)}, u32[]{:S(2)}) async-start(bf16[16,128,512]{2,1,0:T(8,128)(2,1)} %copy-done.3), calls=%async_computation | async-start | bytes 4194304 | tf_op jit(solution)/shard_map/select/all_to_all | solution.py:246
  122.3 4.6 %gates.2 = (f32[3,512,384]{2,1,0:T(8,128)S(1)}, bf16[512,384]{1,0:T(8,128)(2,1)S(1)}) custom-call(bf16[16,144,512]{2,1,0:T(8,128)(2,1)} %all-to-all-done.1.x_ref, bf16[3,192,2048]{2,1,0:T(8,128)(2,1)S(1)} %collective-permute-done.wa_ref, bf16[1,192,2048]{2,1,0:T(8,128)(2,1)S(1)} %collective-permute-done.1.wb_ref, ...), custom_call_target="tpu_custom_call" | custom-call | tf_op jit(solution)/shard_map/gates/gates/pallas_call | solution.py:259
  129.1 4.6 %gates.3 = (f32[3,512,384]{2,1,0:T(8,128)S(1)}, bf16[512,384]{1,0:T(8,128)(2,1)S(1)}) custom-call(bf16[16,144,512]{2,1,0:T(8,128)(2,1)} %collective-permute-done.3.x_ref, bf16[3,192,2048]{2,1,0:T(8,128)(2,1)S(1)} %collective-permute-done.wa_ref, bf16[1,192,2048]{2,1,0:T(8,128)(2,1)S(1)} %collective-permute-done.1.wb_ref, ...), custom_call_target="tpu_custom_call" | custom-call | tf_op jit(solution)/shard_map/gates/gates/pallas_call | solution.py:260
  135.9 14.5 %all-to-all-done.d_ref = bf16[16,128,512]{2,1,0:T(8,128)(2,1)} async-done(((bf16[16,128,512]{2,1,0:T(8,128)(2,1)}), bf16[16,128,512]{2,1,0:T(8,128)(2,1)}, u32[]{:S(2)}, u32[]{:S(2)}) %all-to-all-start) | async-done | bytes 2097184 | tf_op jit(solution)/shard_map/select/all_to_all | solution.py:246
  150.4 3.7 collective-permute-start.4
  154.1 4.0 collective-permute-done.4.d_ref
  159.8 5.7 %expert.3 = (bf16[16,144,512]{2,1,0:T(8,128)(2,1)S(1)}, bf16[2,512,384]{2,1,0:T(8,128)(2,1)S(1)}) custom-call(s32[4]{0:T(128)S(1)} %pad_add_fusion.at_ref, f32[3,512,384]{2,1,0:T(8,128)S(1)} %copy-done.9, bf16[16,128,512]{2,1,0:T(8,128)(2,1)S(1)} %collective-permute-done.4.d_ref, bf16[3,192,2048]{2,1,0:T(8,128)(2,1)S(1)} %collective-permute-done.wa_ref, ...), custom_call_target="tpu_custom_call" | custom-call | tf_op jit(solution)/shard_map/expert/expert/pallas_call | solution.py:272
  165.9 5.6 %expert.2 = (bf16[16,144,512]{2,1,0:T(8,128)(2,1)S(1)}, bf16[2,512,384]{2,1,0:T(8,128)(2,1)S(1)}) custom-call(s32[4]{0:T(128)S(1)} %pad_add_fusion.at_ref, f32[3,512,384]{2,1,0:T(8,128)S(1)} %copy-done.7, bf16[16,128,512]{2,1,0:T(8,128)(2,1)} %all-to-all-done.d_ref, bf16[3,192,2048]{2,1,0:T(8,128)(2,1)S(1)} %collective-permute-done.wa_ref, ...), custom_call_target="tpu_custom_call" | custom-call | tf_op jit(solution)/shard_map/expert/expert/pallas_call | solution.py:274
  173.8 4.6 %all-to-all-start.2 = ((bf16[16,144,512]{2,1,0:T(8,128)(2,1)}), bf16[16,144,512]{2,1,0:T(8,128)(2,1)}, u32[]{:S(2)}, u32[]{:S(2)}) async-start(bf16[16,144,512]{2,1,0:T(8,128)(2,1)} %add_convert_fusion), calls=%async_computation.2 | async-start | bytes 4718592 | tf_op jit(solution)/shard_map/tokens_back/all_to_all | solution.py:319
  183.1 9.3 %weight_grads.1 = (bf16[3,192,2048]{2,1,0:T(8,128)(2,1)}, bf16[3,192,2048]{2,1,0:T(8,128)(2,1)}) custom-call(bf16[4,4,144,512]{3,2,1,0:T(8,128)(2,1)} %bitcast.8.xo_ref, bf16[4,4,144,512]{3,2,1,0:T(8,128)(2,1)} %bitcast.9.xs_ref, bf16[4,4,128,512]{3,2,1,0:T(8,128)(2,1)} %bitcast.10.do_ref, bf16[4,4,128,512]{3,2,1,0:T(8,128)(2,1)S(1)} %bitcast.17, ...), custom_call_target="tpu_custom_call" | custom-call | tf_op jit(solution)/shard_map/weights_back/weight_grads/pallas_call | solution.py:284
  192.4 4.9 %collective-permute-start.6 = (bf16[3,192,2048]{2,1,0:T(8,128)(2,1)}, bf16[3,192,2048]{2,1,0:T(8,128)(2,1)}, u32[]{:S(2)}, u32[]{:S(2)}) collective-permute-start(bf16[3,192,2048]{2,1,0:T(8,128)(2,1)} %get-tuple-element.56), channel_id=1, source_target_pairs={{0,0},{1,1},{4,2},{5,3},{2,4},{3,5},{6,6},{7,7},{8,8},{9,9},{12,10... | collective-permute-start | bytes 7077896 | tf_op jit(solution)/shard_map/weights_back/ppermute | solution.py:306
  198.3 17.4 %all-to-all-done.2.home_ref = bf16[16,144,512]{2,1,0:T(8,128)(2,1)} async-done(((bf16[16,144,512]{2,1,0:T(8,128)(2,1)}), bf16[16,144,512]{2,1,0:T(8,128)(2,1)}, u32[]{:S(2)}, u32[]{:S(2)}) %all-to-all-start.2) | async-done | bytes 2359328 | tf_op jit(solution)/shard_map/tokens_back/all_to_all | solution.py:319
  215.7 3.6 combine.1
  219.3 8.2 %all-to-all-start.3 = ((bf16[8,144,512]{2,1,0:T(8,128)(2,1)}), bf16[8,144,512]{2,1,0:T(8,128)(2,1)S(1)}, u32[]{:S(2)}, u32[]{:S(2)}) async-start(bf16[8,144,512]{2,1,0:T(8,128)(2,1)} %combine.1), calls=%async_computation.3 | async-start | bytes 2359296 | tf_op jit(solution)/shard_map/tokens_back/all_to_all | solution.py:328
  227.5 36.4 %collective-permute-done.6.a_ref = bf16[3,192,2048]{2,1,0:T(8,128)(2,1)} collective-permute-done((bf16[3,192,2048]{2,1,0:T(8,128)(2,1)}, bf16[3,192,2048]{2,1,0:T(8,128)(2,1)}, u32[]{:S(2)}, u32[]{:S(2)}) %collective-permute-start.6) | collective-permute-done | bytes 2359328 | tf_op jit(solution)/shard_map/weights_back/ppermute | solution.py:306
  263.9 144.6 %place.1 = (bf16[2,192,2048]{2,1,0:T(8,128)(2,1)}, bf16[2,192,2048]{2,1,0:T(8,128)(2,1)}, bf16[2,192,2048]{2,1,0:T(8,128)(2,1)}) custom-call(s32[4]{0:T(128)S(1)} %pad_add_fusion.at_ref, bf16[3,192,2048]{2,1,0:T(8,128)(2,1)} %collective-permute-done.6.a_ref, bf16[3,192,2048]{2,1,0:T(8,128)(2,1)} %collective-permute-done.7.b_ref), custom_call_target="tpu_custom_call" | custom-call | tf_op jit(solution)/shard_map/weights_back/place/pallas_call | solution.py:308
  (73 shorter events, 37.9 us)
Async XLA Ops:
  7.2 5.8 %copy-start.22 = (bf16[2,192,2048]{2,1,0:T(8,128)(2,1)S(1)}, bf16[2,192,2048]{2,1,0:T(8,128)(2,1)}, u32[]{:S(2)}) copy-start(bf16[2,192,2048]{2,1,0:T(8,128)(2,1)} %param.13) | copy-start | bytes 4718596
  7.2 5.8 %copy-start.23 = (bf16[2,192,2048]{2,1,0:T(8,128)(2,1)S(1)}, bf16[2,192,2048]{2,1,0:T(8,128)(2,1)}, u32[]{:S(2)}) copy-start(bf16[2,192,2048]{2,1,0:T(8,128)(2,1)} %param.12) | copy-start | bytes 4718596
  7.2 51.5 %all-gather.3.cloned.1.call-start = ((), (), s32[]{:S(2)}) async-start(), calls=%async_computation.4 | async-start | bytes 2506752 | tf_op jit(solution)/shard_map/gather_z/all_gather | solution.py:215
  16.1 41.3 %collective-permute-start = (bf16[3,192,2048]{2,1,0:T(8,128)(2,1)}, bf16[3,192,2048]{2,1,0:T(8,128)(2,1)S(1)}, u32[]{:S(2)}, u32[]{:S(2)}) collective-permute-start(bf16[3,192,2048]{2,1,0:T(8,128)(2,1)} %pad_maximum_fusion), channel_id=1, source_target_pairs={{0,0},{1,1},{2,4},{3,5},{4,2},{5,3},{6,6},{7,7},{8,8},{9,9},{10,12... | collective-permute-start | bytes 7077896 | tf_op jit(solution)/shard_map/weights_out/ppermute | solution.py:224
  22.2 36.5 %collective-permute-start.1 = (bf16[1,192,2048]{2,1,0:T(8,128)(2,1)}, bf16[1,192,2048]{2,1,0:T(8,128)(2,1)S(1)}, u32[]{:S(2)}, u32[]{:S(2)}) collective-permute-start(bf16[1,192,2048]{2,1,0:T(8,128)(2,1)} %get-tuple-element.61), channel_id=1, source_target_pairs={{0,1},{1,0},{2,5},{3,4},{4,3},{5,2},{6,7},{7,6},{8,9},{9,8},{10,13... | collective-permute-start | bytes 2359304 | tf_op jit(solution)/shard_map/weights_out/ppermute | solution.py:224
  58.6 1.6 copy-start
  64.9 35.6 %all-to-all-start.1 = ((bf16[16,144,512]{2,1,0:T(8,128)(2,1)}), bf16[16,144,512]{2,1,0:T(8,128)(2,1)}, u32[]{:S(2)}, u32[]{:S(2)}) async-start(bf16[16,144,512]{2,1,0:T(8,128)(2,1)} %copy-done.10), calls=%async_computation.1 | async-start | bytes 4718592 | tf_op jit(solution)/shard_map/select/all_to_all | solution.py:236
  69.3 47.6 %collective-permute-start.2 = (bf16[2,192,2048]{2,1,0:T(8,128)(2,1)}, bf16[2,192,2048]{2,1,0:T(8,128)(2,1)}, u32[]{:S(2)}, u32[]{:S(2)}) collective-permute-start(bf16[2,192,2048]{2,1,0:T(8,128)(2,1)} %pad_maximum_fusion.1), channel_id=1, source_target_pairs={{0,1},{1,0},{2,5},{3,4},{4,3},{5,2},{6,7},{7,6},{8,9},{9,8},{10,13... | collective-permute-start | bytes 4718600 | tf_op jit(solution)/shard_map/weights_out/ppermute | solution.py:224
  100.5 28.6 %collective-permute-start.3 = (bf16[16,144,512]{2,1,0:T(8,128)(2,1)}, bf16[16,144,512]{2,1,0:T(8,128)(2,1)}, u32[]{:S(2)}, u32[]{:S(2)}) collective-permute-start(bf16[16,144,512]{2,1,0:T(8,128)(2,1)} %all-to-all-done.1.x_ref), channel_id=1, source_target_pairs={{0,4},{4,0},{1,5},{5,1},{2,6},{6,2},{3,7},{7,3},{8,12},{12,8},{9,1... | collective-permute-start | bytes 7077896 | tf_op jit(solution)/shard_map/select/ppermute | solution.py:247
  117.0 33.4 %all-to-all-start = ((bf16[16,128,512]{2,1,0:T(8,128)(2,1)}), bf16[16,128,512]{2,1,0:T(8,128)(2,1)}, u32[]{:S(2)}, u32[]{:S(2)}) async-start(bf16[16,128,512]{2,1,0:T(8,128)(2,1)} %copy-done.3), calls=%async_computation | async-start | bytes 4194304 | tf_op jit(solution)/shard_map/select/all_to_all | solution.py:246
  150.4 15.5 %copy-start.7 = (f32[3,512,384]{2,1,0:T(8,128)S(1)}, f32[3,512,384]{2,1,0:T(8,128)}, u32[]{:S(2)}) copy-start(f32[3,512,384]{2,1,0:T(8,128)} %copy-done.6) | copy-start | bytes 7077892
  150.4 7.7 %collective-permute-start.4 = (bf16[16,128,512]{2,1,0:T(8,128)(2,1)}, bf16[16,128,512]{2,1,0:T(8,128)(2,1)S(1)}, u32[]{:S(2)}, u32[]{:S(2)}) collective-permute-start(bf16[16,128,512]{2,1,0:T(8,128)(2,1)} %all-to-all-done.d_ref), channel_id=1, source_target_pairs={{0,4},{4,0},{1,5},{5,1},{2,6},{6,2},{3,7},{7,3},{8,12},{12,8},{9,1... | collective-permute-start | bytes 6291464 | tf_op jit(solution)/shard_map/gates/ppermute | solution.py:262
  158.1 1.7 copy-start.9
  159.8 5.7 %copy-start.4 = (bf16[16,128,512]{2,1,0:T(8,128)(2,1)}, bf16[16,128,512]{2,1,0:T(8,128)(2,1)S(1)}, u32[]{:S(2)}) copy-start(bf16[16,128,512]{2,1,0:T(8,128)(2,1)S(1)} %collective-permute-done.4.d_ref) | copy-start | bytes 6291460
  165.5 6.0 %copy-start.14 = (bf16[2,512,384]{2,1,0:T(8,128)(2,1)}, bf16[2,512,384]{2,1,0:T(8,128)(2,1)S(1)}, u32[]{:S(2)}) copy-start(bf16[2,512,384]{2,1,0:T(8,128)(2,1)S(1)} %get-tuple-element.55.ks_ref) | copy-start | bytes 2359300
  165.5 6.1 %collective-permute-start.5 = (bf16[16,144,512]{2,1,0:T(8,128)(2,1)S(1)}, bf16[16,144,512]{2,1,0:T(8,128)(2,1)S(1)}, u32[]{:S(2)}, u32[]{:S(2)}) collective-permute-start(bf16[16,144,512]{2,1,0:T(8,128)(2,1)S(1)} %get-tuple-element.48), channel_id=1, source_target_pairs={{0,4},{4,0},{1,5},{5,1},{2,6},{6,2},{3,7},{7,3},{8,12},{12,8},{9,1... | collective-permute-start | bytes 7077896 | tf_op jit(solution)/shard_map/expert/ppermute | solution.py:273
  171.5 2.2 copy-start.16
  173.7 4.6 %copy-start.15 = (bf16[2,512,384]{2,1,0:T(8,128)(2,1)S(1)}, bf16[2,512,384]{2,1,0:T(8,128)(2,1)}, u32[]{:S(2)}) copy-start(bf16[2,512,384]{2,1,0:T(8,128)(2,1)} %copy-done.14) | copy-start | bytes 2359300
  173.8 42.0 %all-to-all-start.2 = ((bf16[16,144,512]{2,1,0:T(8,128)(2,1)}), bf16[16,144,512]{2,1,0:T(8,128)(2,1)}, u32[]{:S(2)}, u32[]{:S(2)}) async-start(bf16[16,144,512]{2,1,0:T(8,128)(2,1)} %add_convert_fusion), calls=%async_computation.2 | async-start | bytes 4718592 | tf_op jit(solution)/shard_map/tokens_back/all_to_all | solution.py:319
  183.1 32.6 %copy-start.2 = (bf16[2176,512]{1,0:T(8,128)(2,1)S(1)}, bf16[2176,512]{1,0:T(8,128)(2,1)}, u32[]{:S(2)}) copy-start(bf16[2176,512]{1,0:T(8,128)(2,1)} %all-gather.3.cloned.1.call-done) | copy-start | bytes 6684676
  183.1 32.6 %copy-start.13 = (bf16[8,256,128]{2,1,0:T(8,128)(2,1)S(1)}, bf16[8,256,128]{2,1,0:T(8,128)(2,1)}, u32[]{:S(2)}) copy-start(bf16[8,256,128]{2,1,0:T(8,128)(2,1)} %copy-done.11) | copy-start | bytes 1572868
  192.4 71.5 %collective-permute-start.6 = (bf16[3,192,2048]{2,1,0:T(8,128)(2,1)}, bf16[3,192,2048]{2,1,0:T(8,128)(2,1)}, u32[]{:S(2)}, u32[]{:S(2)}) collective-permute-start(bf16[3,192,2048]{2,1,0:T(8,128)(2,1)} %get-tuple-element.56), channel_id=1, source_target_pairs={{0,0},{1,1},{4,2},{5,3},{2,4},{3,5},{6,6},{7,7},{8,8},{9,9},{12,10... | collective-permute-start | bytes 7077896 | tf_op jit(solution)/shard_map/weights_back/ppermute | solution.py:306
  197.4 66.6 %collective-permute-start.7 = (bf16[3,192,2048]{2,1,0:T(8,128)(2,1)}, bf16[3,192,2048]{2,1,0:T(8,128)(2,1)}, u32[]{:S(2)}, u32[]{:S(2)}) collective-permute-start(bf16[3,192,2048]{2,1,0:T(8,128)(2,1)} %get-tuple-element.57), channel_id=1, source_target_pairs={{1,0},{0,1},{5,2},{4,3},{3,4},{2,5},{7,6},{6,7},{9,8},{8,9},{13,10... | collective-permute-start | bytes 7077896 | tf_op jit(solution)/shard_map/weights_back/ppermute | solution.py:306
  219.3 189.3 %all-to-all-start.3 = ((bf16[8,144,512]{2,1,0:T(8,128)(2,1)}), bf16[8,144,512]{2,1,0:T(8,128)(2,1)S(1)}, u32[]{:S(2)}, u32[]{:S(2)}) async-start(bf16[8,144,512]{2,1,0:T(8,128)(2,1)} %combine.1), calls=%async_computation.3 | async-start | bytes 2359296 | tf_op jit(solution)/shard_map/tokens_back/all_to_all | solution.py:328
  (13 other events, 15.3 us)
Sparse Core Ops, SparseCore 0:
  10.7 41.4 all-gather.2

commit v4 on v3

v4 whole, which is shorter than its diff:
```python
import jax
import jax.numpy as jnp
from jax import lax
from jax.experimental import pallas as pl
from jax.experimental.pallas import tpu as pltpu
from jax.sharding import Mesh, PartitionSpec as P

BF = jnp.bfloat16
F32 = jnp.float32
NY, NZ, NC, NX = 4, 8, 2, 4
SLOT = 16
TOK = 128
TOP = 8
PEER = NY * NZ
ROWS = PEER * SLOT
Q = 512
D = NX * Q
WIDE = D + 128
FQ = 192
FH = 2 * FQ
VMEM = pl.BlockSpec(memory_space=pltpu.VMEM)
SMEM = pl.BlockSpec(memory_space=pltpu.SMEM)


def params(mib=32):
    return pltpu.CompilerParams(vmem_limit_bytes=mib * 1024 * 1024)


def dot(a, b, ca, cb):
    return lax.dot_general(a, b, (((ca,), (cb,)), ((), ())), preferred_element_type=F32)


def iota(shape, axis):
    return lax.broadcasted_iota(jnp.int32, shape, axis)


def weight_pairs(m):
    pairs = []
    for c in range(NC):
        for h in range(NX):
            k = (h + m) % 2
            pairs.append((c * NX + h, (h // 2) * NX + 2 * c + k))
    return pairs


def select_x(at_ref, table_ref, x_ref, out_ref, pick_ref):
    ids = (NX * iota((PEER, TOK), 0) + at_ref[3]).astype(F32)
    before = (iota((TOK, TOK), 0) < iota((TOK, TOK), 1)).astype(BF)
    slot = (iota((ROWS, TOK), 0) % SLOT).astype(F32)
    lane = iota((ROWS, TOK), 1)
    table = table_ref[...]
    hit = jnp.zeros((PEER, TOK), F32)
    chance = jnp.zeros((PEER, TOK), F32)
    for k in range(TOP):
        on = table[k : k + 1, :] == ids
        hit = jnp.where(on, 1.0, hit)
        chance = jnp.where(on, table[TOP + k : TOP + k + 1, :], chance)
    rank = dot(hit.astype(BF), before, 1, 0)
    rank = jnp.where(hit > 0.5, rank, -1.0)
    rank = jnp.broadcast_to(rank[:, None, :], (PEER, SLOT, TOK)).reshape(ROWS, TOK)
    chance = jnp.broadcast_to(chance[:, None, :], (PEER, SLOT, TOK)).reshape(ROWS, TOK)
    mine = rank == slot
    share = jnp.sum(jnp.where(mine, chance, 0.0), axis=1, keepdims=True)
    pick = jnp.where(mine, 1.0, 0.0).astype(BF)
    pick_ref[...] = pick
    for h in range(NX):
        out_ref[:, h * Q : (h + 1) * Q] = dot(pick, x_ref[h], 1, 0).astype(BF)
    out_ref[:, D:] = jnp.where(lane == 0, share, 0.0).astype(BF)


def select_d(pick_ref, d_ref, out_ref):
    for h in range(NX):
        out_ref[:, h * Q : (h + 1) * Q] = dot(pick_ref[...], d_ref[h], 1, 0).astype(BF)


def both(wa_ref, wb_ref, i, h):
    cols = slice(h * Q, (h + 1) * Q)
    return jnp.concatenate([wa_ref[i, :, cols], wb_ref[i, :, cols]], axis=0)


def project(ref, wa_ref, wb_ref, i):
    total = dot(ref[:, :Q], both(wa_ref, wb_ref, i, 0), 1, 1)
    for h in range(1, NX):
        total = total + dot(ref[:, h * Q : (h + 1) * Q], both(wa_ref, wb_ref, i, h), 1, 1)
    return total


def gates(x_ref, wa_ref, wb_ref, pre_ref, keep_ref):
    weight = x_ref[:, D:].astype(F32)[:, :1]
    gate = project(x_ref, wa_ref, wb_ref, 0)
    up = project(x_ref, wa_ref, wb_ref, 1)
    sig = 1.0 / (1.0 + jnp.exp(-gate))
    act = gate * sig
    hidden = act * up
    pre_ref[0] = hidden
    pre_ref[1] = weight * (up * (sig * (1.0 + gate * (1.0 - sig))))
    pre_ref[2] = weight * act
    keep_ref[...] = (weight * hidden).astype(BF)


def expert(at_ref, pre_ref, d_ref, wa_ref, wb_ref, part_ref, keep_ref):
    raw = project(d_ref, wa_ref, wb_ref, 2)
    score = jnp.sum(pre_ref[0] * raw, axis=1, keepdims=True)
    keep_ref[0] = (raw * pre_ref[1]).astype(BF)
    keep_ref[1] = (raw * pre_ref[2]).astype(BF)
    for h in range(NX):
        total = dot(keep_ref[0], both(wa_ref, wb_ref, 0, h), 1, 0)
        total = total + dot(keep_ref[1], both(wa_ref, wb_ref, 1, h), 1, 0)
        part_ref[:, h * Q : (h + 1) * Q] = total.astype(BF)
    lane = iota((ROWS, TOK), 1) - 2 * at_ref[2]
    coarse = score.astype(BF).astype(F32)
    carried = jnp.where(lane == 0, coarse, jnp.where(lane == 1, score - coarse, 0.0))
    part_ref[:, D:] = carried.astype(BF)


def weight_grads(xo_ref, xs_ref, do_ref, ds_ref, ho_ref, hs_ref, ko_ref, ks_ref, a_ref, b_ref, flip):
    @pl.when(pl.program_id(0) == 0)
    def _():
        for i in range(2):
            flip[i, :, :ROWS] = ko_ref[i].T
            flip[i, :, ROWS:] = ks_ref[i].T
        flip[2, :, :ROWS] = ho_ref[...].T
        flip[2, :, ROWS:] = hs_ref[...].T

    x = jnp.concatenate([xo_ref[...], xs_ref[...]], axis=0)
    d = jnp.concatenate([do_ref[...], ds_ref[...]], axis=0)
    for i, rows in ((0, x), (1, x), (2, d)):
        grad = dot(flip[i], rows, 1, 0).astype(BF)
        a_ref[i] = grad[:FQ]
        b_ref[i] = grad[FQ:]


def place(at_ref, a_ref, b_ref, gate_ref, up_ref, down_ref):
    odd = at_ref[3] % 2
    for i, out in enumerate((gate_ref, up_ref, down_ref)):
        out[odd] = a_ref[i]
        out[1 - odd] = b_ref[i]


def combine(at_ref, table_ref, pick_ref, home_ref, out_ref):
    ids = (NX * iota((PEER, TOK), 0) + at_ref[3]).astype(F32)
    pick = pick_ref[...]
    carried = home_ref[:, D:].astype(F32)
    score = (carried[:, 0:1] + carried[:, 1:2]) + (carried[:, 2:3] + carried[:, 3:4])
    spread = jnp.sum((pick.astype(F32) * score).reshape(PEER, SLOT, TOK), axis=1)
    table = table_ref[...]
    lines = [
        jnp.sum(jnp.where(table[k : k + 1, :] == ids, spread, 0.0), axis=0, keepdims=True) for k in range(TOP)
    ]
    lines = jnp.concatenate(lines + [jnp.zeros((16 - TOP, TOK), F32)], axis=0)
    coarse = lines.astype(BF)
    fine = (lines - coarse.astype(F32)).astype(BF)
    for h in range(NX):
        out_ref[h, :TOK, :] = dot(pick, home_ref[:, h * Q : (h + 1) * Q], 0, 0).astype(BF)
        out_ref[h, TOK:, :TOK] = coarse
        out_ref[h, TOK:, TOK : 2 * TOK] = fine
        out_ref[h, TOK:, 2 * TOK :] = jnp.zeros((16, Q - 2 * TOK), BF)


def per_device(tokens, cotangent, route, prob, w_gate, w_up, w_down):
    at = jnp.stack([lax.axis_index(a) for a in ("y", "z", "c", "x")]).astype(jnp.int32)
    ix = lax.axis_index("x")
    sib = [(0, 1), (1, 0)]
    shape = jax.ShapeDtypeStruct

    def to_experts(rows):
        rows = rows.reshape(PEER, SLOT, rows.shape[1])
        rows = lax.all_to_all(rows, ("y", "z"), split_axis=0, concat_axis=0, tiled=True)
        return rows.reshape(ROWS, rows.shape[2])

    with jax.named_scope("select_x"):
        xg = lax.all_gather(tokens, "x", axis=0, tiled=False)
        table = jnp.concatenate([route.T.astype(F32), prob.T.astype(F32)], axis=0)
        xs, pick = pl.pallas_call(
            select_x,
            out_shape=(shape((ROWS, WIDE), BF), shape((ROWS, TOK), BF)),
            in_specs=[SMEM, VMEM, VMEM],
            out_specs=(VMEM, VMEM),
            compiler_params=params(),
            name="select_x",
        )(at, table, xg)
        x_own = to_experts(xs)

    with jax.named_scope("select_d"):
        pick, cotangent = lax.optimization_barrier((pick, cotangent))
        dg = lax.all_gather(cotangent, "x", axis=0, tiled=False)
        ds = pl.pallas_call(
            select_d,
            out_shape=shape((ROWS, D), BF),
            in_specs=[VMEM, VMEM],
            out_specs=VMEM,
            compiler_params=params(),
            name="select_d",
        )(pick, dg)

    with jax.named_scope("weights_out"):
        pick, *mats = lax.optimization_barrier((pick, w_gate, w_up, w_down))
        weights = []
        for m in range(2):
            k = (ix + m) % 2
            piece = jnp.stack([lax.dynamic_index_in_dim(w, k, 0, keepdims=False) for w in mats])
            weights.append(lax.ppermute(piece, ("c", "x"), weight_pairs(m)))

    with jax.named_scope("gates"):
        x_own, ds, *weights = lax.optimization_barrier((x_own, ds, *weights))
        d_own = to_experts(ds)
        x_sib = lax.ppermute(x_own, "c", sib)
        ahead = pl.pallas_call(
            gates,
            out_shape=(shape((3, ROWS, FH), F32), shape((ROWS, FH), BF)),
            in_specs=[VMEM] * 3,
            out_specs=(VMEM, VMEM),
            compiler_params=params(),
            name="gates",
        )
        pre_own, hid_own = ahead(x_own, *weights)
        pre_sib, hid_sib = ahead(x_sib, *weights)
        d_own, pre_own, pre_sib = lax.optimization_barrier((d_own, pre_own, pre_sib))

    with jax.named_scope("expert"):
        d_sib = lax.ppermute(d_own, "c", sib)
        run = pl.pallas_call(
            expert,
            out_shape=(shape((ROWS, WIDE), BF), shape((2, ROWS, FH), BF)),
            in_specs=[SMEM] + [VMEM] * 4,
            out_specs=(VMEM, VMEM),
            compiler_params=params(),
            name="expert",
        )
        part_sib, keep_sib = run(at, pre_sib, d_sib, *weights)
        sent = lax.ppermute(part_sib, "c", sib)
        part_own, keep_own = run(at, pre_own, d_own, *weights)
        total = (part_own.astype(F32) + sent.astype(F32)).astype(BF)
        total, keep_own, keep_sib = lax.optimization_barrier((total, keep_own, keep_sib))

    with jax.named_scope("weights_back"):
        cut = pl.BlockSpec((ROWS, Q), lambda h: (0, h))
        h_spec = pl.BlockSpec((ROWS, FH), lambda h: (0, 0))
        k_spec = pl.BlockSpec((2, ROWS, FH), lambda h: (0, 0, 0))
        o_spec = pl.BlockSpec((3, FQ, Q), lambda h: (0, 0, h))
        pieces = pl.pallas_call(
            weight_grads,
            grid=(NX,),
            out_shape=(shape((3, FQ, D), BF),) * 2,
            in_specs=[cut] * 4 + [h_spec, h_spec, k_spec, k_spec],
            out_specs=(o_spec, o_spec),
            scratch_shapes=[pltpu.VMEM((3, FH, 2 * ROWS), BF)],
            compiler_params=params(),
            name="weight_grads",
        )(x_own, x_sib, d_own, d_sib, hid_own, hid_sib, keep_own, keep_sib)
        back = []
        for m, g in enumerate(pieces):
            inverse = [(b, a) for a, b in weight_pairs(m)]
            back.append(lax.ppermute(g, ("c", "x"), inverse))
        part_rows = FQ // 4
        grad_gate, grad_up, grad_down = pl.pallas_call(
            place,
            grid=(4,),
            out_shape=(shape((2, FQ, D), BF),) * 3,
            in_specs=[SMEM] + [pl.BlockSpec((3, part_rows, D), lambda i: (0, i, 0))] * 2,
            out_specs=(pl.BlockSpec((2, part_rows, D), lambda i: (0, i, 0)),) * 3,
            compiler_params=params(),
            name="place",
        )(at, *back)

    with jax.named_scope("tokens_back"):
        home = to_experts(total)
        partial = pl.pallas_call(
            combine,
            out_shape=shape((NX, TOK + 16, Q), BF),
            in_specs=[SMEM, VMEM, VMEM, VMEM],
            out_specs=VMEM,
            compiler_params=params(),
            name="combine",
        )(at, table, pick, home)
        last = lax.all_to_all(partial, "x", split_axis=0, concat_axis=0, tiled=True).astype(F32)
        grad_tokens = jnp.sum(last[:, :TOK], axis=0).astype(BF)
        lines = jnp.sum(last[:, TOK : TOK + TOP, : 2 * TOK], axis=0)
        grad_prob = (lines[:, :TOK] + lines[:, TOK:]).T
    return (grad_tokens, grad_prob, grad_gate, grad_up, grad_down)


def solution(mesh):
    grid = Mesh(mesh.devices.reshape(NY, NZ, NC, NX), ("y", "z", "c", "x"))
    owner = ("y", "z", "c")
    wide = P(owner, "x")
    thin = P(owner, None)
    deep = P(owner, "x", None)
    return jax.shard_map(
        per_device,
        mesh=grid,
        in_specs=(wide, wide, thin, thin, deep, deep, deep),
        out_specs=(wide, thin, deep, deep, deep),
        check_vma=False,
    )
```

time: 419 us -> 270 us (0.64)
  Pallas kernels: 181 us -> 35 us
  blocking collectives: 0 us -> 70.2 us
  waiting for transfers between devices: 138 us -> 82.9 us
  between operations: 14.3 us -> 0.92 us
  other arithmetic: 11.7 us -> 5.37 us
    pallas_call x4, Pallas kernels: 151 us -> 10.4 us  [the longest x1 5 us: per_device(): pl.pallas_call(place, grid=(4,), out_shape=(shape((2, FQ, D), BF),) * 3,...]
    all_gather x0 -> x2, blocking collectives: none -> 70.2 us  [the longest x1 57.7 us: per_device(): dg = lax.all_gather(cotangent, 'x', axis=0, tiled=False)]
    ppermute x3 -> x2, waiting for transfers between devices: 39.2 us -> 0.01 us  [per_device(): weights.append(lax.ppermute(piece, ('c', 'x'), weight_pairs(m)))]
    ppermute x2, waiting for transfers between devices: 36.4 us -> 17.3 us  [per_device(): back.append(lax.ppermute(g, ('c', 'x'), inverse))]
    all_to_all x4, starting transfers between devices: 22.6 us -> 31.1 us  [the longest x3 26.3 us: to_experts(): lax.all_to_all(rows, ('y', 'z'), split_axis=0, concat_axis=0, tiled=True)]
    ppermute x3 -> x2, starting transfers between devices: 11.3 us -> 7.24 us  [per_device(): weights.append(lax.ppermute(piece, ('c', 'x'), weight_pairs(m)))]
    unnamed x48 -> x46, local copies, waits for them, and re-layouts: 18.6 us -> 20.8 us
  transfers between devices with their start and end apart: 13 -> 11, of which waited for: 8 -> 4; matrix products, arithmetic and copies ran while one was open for 2% -> 0% of each run, Pallas kernels for 41% -> 11%
where the time goes in v4:
time: 270 us; the launch traced here: 268 us
  waiting for transfers between devices  82.9 us (31%)
  blocking collectives  70.2 us (26%)
  starting transfers between devices  52 us (19%)
  Pallas kernels  35 us (13%)
  local copies, waits for them, and re-layouts  21.4 us (8%)
  other arithmetic  5.37 us (2%)
    all_to_all x3, waiting for transfers between devices, to_experts(): lax.all_to_all(rows, ('y', 'z'), split_axis=0, concat_axis=0, tiled=True)  61.5 us
    all_gather x1, blocking collectives, per_device(): dg = lax.all_gather(cotangent, 'x', axis=0, tiled=False)  57.7 us
    all_to_all x3, starting transfers between devices, to_experts(): lax.all_to_all(rows, ('y', 'z'), split_axis=0, concat_axis=0, tiled=True)  26.3 us
    unnamed x46, local copies, waits for them, and re-layouts  20.8 us
    ppermute x2, waiting for transfers between devices, per_device(): back.append(lax.ppermute(g, ('c', 'x'), inverse))  17.3 us
    all_gather x1, blocking collectives, per_device(): xg = lax.all_gather(tokens, 'x', axis=0, tiled=False)  12.5 us
    pallas_call x1, Pallas kernels, per_device(): pl.pallas_call(weight_grads, grid=(NX,), out_shape=(shape((3, FQ, D), BF)...  8.8 us
    ppermute x2, starting transfers between devices, per_device(): weights.append(lax.ppermute(piece, ('c', 'x'), weight_pairs(m)))  7.24 us
  transfers between devices with their start and end apart: 11, of which 4 were waited for; matrix products, arithmetic and copies ran while one was open for 0% of the time, Pallas kernels for 11%

profile of v4, /device:TPU:1, one launch (start us, length us, event | category | flops | bytes accessed | tf_op | source)
XLA Modules:
  0.0 267.8 jit_solution(9218514028655299496)
XLA Ops:
  2.0 12.5 %all-gather = bf16[512,512]{1,0:T(8,128)(2,1)S(1)} all-gather(bf16[128,512]{1,0:T(8,128)(2,1)} %param.7), channel_id=2, replica_groups=mesh['y'=4,'z'=8,'c'=2,'x'=4] {'x'}, dimensions={0}, use_global_device_ids=true | all-gather | bytes 655360 | tf_op jit(solution)/shard_map/select_x/all_gather | solution.py:172
  14.6 2.8 %select_x.1 = (bf16[512,2176]{1,0:T(8,128)(2,1)}, bf16[512,128]{1,0:T(8,128)(2,1)S(1)}) custom-call(s32[4]{0:T(128)S(1)} %pad_add_fusion.at_ref, f32[16,128]{1,0:T(8,128)S(1)} %pad_maximum_fusion.2.table_ref, bf16[4,128,512]{2,1,0:T(8,128)(2,1)S(1)} %bitcast.20), custom_call_target="tpu_custom_call" | custom-call | tf_op jit(solution)/shard_map/select_x/select_x/pallas_call | solution.py:174
  17.5 11.4 %all-to-all-start = ((bf16[32,16,2176]{2,1,0:T(8,128)(2,1)}), bf16[32,16,2176]{2,1,0:T(8,128)(2,1)}, u32[]{:S(2)}, u32[]{:S(2)}) async-start(bf16[32,16,2176]{2,1,0:T(8,128)(2,1)} %bitcast.7), calls=%async_computation | async-start | bytes 4456448 | tf_op jit(solution)/shard_map/select_x/all_to_all | solution.py:168
  31.5 5.6 %collective-permute-start = (bf16[3,192,2048]{2,1,0:T(8,128)(2,1)S(1)}, bf16[3,192,2048]{2,1,0:T(8,128)(2,1)S(1)}, u32[]{:S(2)}, u32[]{:S(2)}) collective-permute-start(bf16[3,192,2048]{2,1,0:T(8,128)(2,1)S(1)} %pad_maximum_fusion), channel_id=1, source_target_pairs={{0,0},{1,1},{2,4},{3,5},{4,2},{5,3},{6,6},{7,7},{8,8},{9,9},{10,12... | collective-permute-start | bytes 7077896 | tf_op jit(solution)/shard_map/weights_out/ppermute | solution.py:202
  39.0 57.7 %all-gather.1 = bf16[512,512]{1,0:T(8,128)(2,1)S(1)} all-gather(bf16[128,512]{1,0:T(8,128)(2,1)S(1)} %copy-done.22), channel_id=3, replica_groups=mesh['y'=4,'z'=8,'c'=2,'x'=4] {'x'}, dimensions={0}, use_global_device_ids=true | all-gather | bytes 655360 | tf_op jit(solution)/shard_map/select_d/all_gather | solution.py:186
  100.2 9.6 %all-to-all-start.1 = ((bf16[32,16,2048]{2,1,0:T(8,128)(2,1)}), bf16[32,16,2048]{2,1,0:T(8,128)(2,1)}, u32[]{:S(2)}, u32[]{:S(2)}) async-start(bf16[32,16,2048]{2,1,0:T(8,128)(2,1)} %bitcast.19), calls=%async_computation.1 | async-start | bytes 4194304 | tf_op jit(solution)/shard_map/gates/all_to_all | solution.py:168
  109.7 3.0 %collective-permute-start.2 = (bf16[512,2176]{1,0:T(8,128)(2,1)}, bf16[512,2176]{1,0:T(8,128)(2,1)S(1)}, u32[]{:S(2)}, u32[]{:S(2)}) collective-permute-start(bf16[512,2176]{1,0:T(8,128)(2,1)} %bitcast.8.x_ref.xo_ref), channel_id=1, source_target_pairs={{0,4},{4,0},{1,5},{5,1},{2,6},{6,2},{3,7},{7,3},{8,12},{12,8},{9,1... | collective-permute-start | bytes 6684680 | tf_op jit(solution)/shard_map/gates/ppermute | solution.py:207
  114.4 4.3 %gates.2 = (f32[3,512,384]{2,1,0:T(8,128)S(1)}, bf16[512,384]{1,0:T(8,128)(2,1)S(1)}) custom-call(bf16[512,2176]{1,0:T(8,128)(2,1)} %bitcast.8.x_ref.xo_ref, bf16[3,192,2048]{2,1,0:T(8,128)(2,1)S(1)} %collective-permute-done.wa_ref, bf16[3,192,2048]{2,1,0:T(8,128)(2,1)S(1)} %copy-done.1), custom_call_target="tpu_custom_call" | custom-call | tf_op jit(solution)/shard_map/gates/gates/pallas_call | solution.py:216
  120.2 2.5 gates.3
  126.2 31.9 %all-to-all-done.1 = bf16[32,16,2048]{2,1,0:T(8,128)(2,1)} async-done(((bf16[32,16,2048]{2,1,0:T(8,128)(2,1)}), bf16[32,16,2048]{2,1,0:T(8,128)(2,1)}, u32[]{:S(2)}, u32[]{:S(2)}) %all-to-all-start.1) | async-done | bytes 2097184 | tf_op jit(solution)/shard_map/gates/all_to_all | solution.py:168
  158.1 3.1 %collective-permute-start.3 = (bf16[512,2048]{1,0:T(8,128)(2,1)}, bf16[512,2048]{1,0:T(8,128)(2,1)S(1)}, u32[]{:S(2)}, u32[]{:S(2)}) collective-permute-start(bf16[512,2048]{1,0:T(8,128)(2,1)} %bitcast.11.d_ref.do_ref), channel_id=1, source_target_pairs={{0,4},{4,0},{1,5},{5,1},{2,6},{6,2},{3,7},{7,3},{8,12},{12,8},{9,1... | collective-permute-start | bytes 6291464 | tf_op jit(solution)/shard_map/expert/ppermute | solution.py:221
  161.2 4.0 %collective-permute-done.3.d_ref.ds_ref = bf16[512,2048]{1,0:T(8,128)(2,1)S(1)} collective-permute-done((bf16[512,2048]{1,0:T(8,128)(2,1)}, bf16[512,2048]{1,0:T(8,128)(2,1)S(1)}, u32[]{:S(2)}, u32[]{:S(2)}) %collective-permute-start.3) | collective-permute-done | bytes 2097184 | tf_op jit(solution)/shard_map/expert/ppermute | solution.py:221
  168.6 4.0 %expert.3 = (bf16[512,2176]{1,0:T(8,128)(2,1)S(1)}, bf16[2,512,384]{2,1,0:T(8,128)(2,1)S(1)}) custom-call(s32[4]{0:T(128)S(1)} %pad_add_fusion.at_ref, f32[3,512,384]{2,1,0:T(8,128)S(1)} %copy-done.12, bf16[512,2048]{1,0:T(8,128)(2,1)S(1)} %collective-permute-done.3.d_ref.ds_ref, bf16[3,192,2048]{2,1,0:T(8,128)(2,1)S(1)} %collective-permute-done.wa_ref, ...), custom_call_target="tpu_custom_call" | custom-call | tf_op jit(solution)/shard_map/expert/expert/pallas_call | solution.py:230
  173.2 5.1 %expert.2 = (bf16[512,2176]{1,0:T(8,128)(2,1)S(1)}, bf16[2,512,384]{2,1,0:T(8,128)(2,1)S(1)}) custom-call(s32[4]{0:T(128)S(1)} %pad_add_fusion.at_ref, f32[3,512,384]{2,1,0:T(8,128)S(1)} %copy-done.10, bf16[512,2048]{1,0:T(8,128)(2,1)} %bitcast.11.d_ref.do_ref, bf16[3,192,2048]{2,1,0:T(8,128)(2,1)S(1)} %collective-permute-done.wa_ref, ...), custom_call_target="tpu_custom_call" | custom-call | tf_op jit(solution)/shard_map/expert/expert/pallas_call | solution.py:232
  178.4 1.9 add_convert_fusion
  180.3 5.3 %all-to-all-start.2 = ((bf16[32,16,2176]{2,1,0:T(8,128)(2,1)}), bf16[32,16,2176]{2,1,0:T(8,128)(2,1)S(1)}, u32[]{:S(2)}, u32[]{:S(2)}) async-start(bf16[32,16,2176]{2,1,0:T(8,128)(2,1)} %bitcast.22), calls=%async_computation.2 | async-start | bytes 4456448 | tf_op jit(solution)/shard_map/tokens_back/all_to_all | solution.py:168
  192.0 8.8 %weight_grads.1 = (bf16[3,192,2048]{2,1,0:T(8,128)(2,1)}, bf16[3,192,2048]{2,1,0:T(8,128)(2,1)}) custom-call(bf16[512,2176]{1,0:T(8,128)(2,1)} %bitcast.8.x_ref.xo_ref, bf16[512,2176]{1,0:T(8,128)(2,1)S(1)} %copy-done.5, bf16[512,2048]{1,0:T(8,128)(2,1)} %bitcast.11.d_ref.do_ref, bf16[512,2048]{1,0:T(8,128)(2,1)S(1)} %copy-done.8, ...), custom_call_target="tpu_custom_call" | custom-call | tf_op jit(solution)/shard_map/weights_back/weight_grads/pallas_call | solution.py:241
  200.8 3.7 %collective-permute-start.5 = (bf16[3,192,2048]{2,1,0:T(8,128)(2,1)}, bf16[3,192,2048]{2,1,0:T(8,128)(2,1)}, u32[]{:S(2)}, u32[]{:S(2)}) collective-permute-start(bf16[3,192,2048]{2,1,0:T(8,128)(2,1)} %get-tuple-element.62), channel_id=1, source_target_pairs={{0,0},{1,1},{4,2},{5,3},{2,4},{3,5},{6,6},{7,7},{8,8},{9,9},{12,10... | collective-permute-start | bytes 7077896 | tf_op jit(solution)/shard_map/weights_back/ppermute | solution.py:254
  204.5 3.2 %collective-permute-start.6 = (bf16[3,192,2048]{2,1,0:T(8,128)(2,1)}, bf16[3,192,2048]{2,1,0:T(8,128)(2,1)}, u32[]{:S(2)}, u32[]{:S(2)}) collective-permute-start(bf16[3,192,2048]{2,1,0:T(8,128)(2,1)} %get-tuple-element.63), channel_id=1, source_target_pairs={{1,0},{0,1},{5,2},{4,3},{3,4},{2,5},{7,6},{6,7},{9,8},{8,9},{13,10... | collective-permute-start | bytes 7077896 | tf_op jit(solution)/shard_map/weights_back/ppermute | solution.py:254
  207.7 29.7 %all-to-all-done.2 = bf16[32,16,2176]{2,1,0:T(8,128)(2,1)S(1)} async-done(((bf16[32,16,2176]{2,1,0:T(8,128)(2,1)}), bf16[32,16,2176]{2,1,0:T(8,128)(2,1)S(1)}, u32[]{:S(2)}, u32[]{:S(2)}) %all-to-all-start.2) | async-done | bytes 2228256 | tf_op jit(solution)/shard_map/tokens_back/all_to_all | solution.py:168
  237.4 1.9 combine.1
  239.2 4.7 %all-to-all-start.3 = ((bf16[4,144,512]{2,1,0:T(8,128)(2,1)}), bf16[4,144,512]{2,1,0:T(8,128)(2,1)S(1)}, u32[]{:S(2)}, u32[]{:S(2)}) async-start(bf16[4,144,512]{2,1,0:T(8,128)(2,1)} %combine.1), calls=%async_computation.3 | async-start | bytes 1179648 | tf_op jit(solution)/shard_map/tokens_back/all_to_all | solution.py:276
  243.9 17.3 %collective-permute-done.6.b_ref = bf16[3,192,2048]{2,1,0:T(8,128)(2,1)} collective-permute-done((bf16[3,192,2048]{2,1,0:T(8,128)(2,1)}, bf16[3,192,2048]{2,1,0:T(8,128)(2,1)}, u32[]{:S(2)}, u32[]{:S(2)}) %collective-permute-start.6) | collective-permute-done | bytes 2359328 | tf_op jit(solution)/shard_map/weights_back/ppermute | solution.py:254
  261.3 5.0 %place.1 = (bf16[2,192,2048]{2,1,0:T(8,128)(2,1)}, bf16[2,192,2048]{2,1,0:T(8,128)(2,1)}, bf16[2,192,2048]{2,1,0:T(8,128)(2,1)}) custom-call(s32[4]{0:T(128)S(1)} %pad_add_fusion.at_ref, bf16[3,192,2048]{2,1,0:T(8,128)(2,1)} %collective-permute-done.5.a_ref, bf16[3,192,2048]{2,1,0:T(8,128)(2,1)} %collective-permute-done.6.b_ref), custom_call_target="tpu_custom_call" | custom-call | tf_op jit(solution)/shard_map/weights_back/place/pallas_call | solution.py:256
  (68 shorter events, 27.9 us)
Async XLA Ops:
  17.5 11.5 %copy-start.19 = (bf16[2,192,2048]{2,1,0:T(8,128)(2,1)S(1)}, bf16[2,192,2048]{2,1,0:T(8,128)(2,1)}, u32[]{:S(2)}) copy-start(bf16[2,192,2048]{2,1,0:T(8,128)(2,1)} %param.11) | copy-start | bytes 4718596
  17.5 82.7 %all-to-all-start = ((bf16[32,16,2176]{2,1,0:T(8,128)(2,1)}), bf16[32,16,2176]{2,1,0:T(8,128)(2,1)}, u32[]{:S(2)}, u32[]{:S(2)}) async-start(bf16[32,16,2176]{2,1,0:T(8,128)(2,1)} %bitcast.7), calls=%async_computation | async-start | bytes 4456448 | tf_op jit(solution)/shard_map/select_x/all_to_all | solution.py:168
  29.0 1.8 copy-start.21
  31.5 67.3 %collective-permute-start = (bf16[3,192,2048]{2,1,0:T(8,128)(2,1)S(1)}, bf16[3,192,2048]{2,1,0:T(8,128)(2,1)S(1)}, u32[]{:S(2)}, u32[]{:S(2)}) collective-permute-start(bf16[3,192,2048]{2,1,0:T(8,128)(2,1)S(1)} %pad_maximum_fusion), channel_id=1, source_target_pairs={{0,0},{1,1},{2,4},{3,5},{4,2},{5,3},{6,6},{7,7},{8,8},{9,9},{10,12... | collective-permute-start | bytes 7077896 | tf_op jit(solution)/shard_map/weights_out/ppermute | solution.py:202
  37.1 2.0 copy-start.22
  37.3 61.4 %collective-permute-start.1 = (bf16[3,192,2048]{2,1,0:T(8,128)(2,1)S(1)}, bf16[3,192,2048]{2,1,0:T(8,128)(2,1)S(1)}, u32[]{:S(2)}, u32[]{:S(2)}) collective-permute-start(bf16[3,192,2048]{2,1,0:T(8,128)(2,1)S(1)} %pad_maximum_fusion.1), channel_id=1, source_target_pairs={{0,1},{1,0},{2,5},{3,4},{4,3},{5,2},{6,7},{7,6},{8,9},{9,8},{10,13... | collective-permute-start | bytes 7077896 | tf_op jit(solution)/shard_map/weights_out/ppermute | solution.py:202
  100.2 58.0 %all-to-all-start.1 = ((bf16[32,16,2048]{2,1,0:T(8,128)(2,1)}), bf16[32,16,2048]{2,1,0:T(8,128)(2,1)}, u32[]{:S(2)}, u32[]{:S(2)}) async-start(bf16[32,16,2048]{2,1,0:T(8,128)(2,1)} %bitcast.19), calls=%async_computation.1 | async-start | bytes 4194304 | tf_op jit(solution)/shard_map/gates/all_to_all | solution.py:168
  109.7 10.4 %collective-permute-start.2 = (bf16[512,2176]{1,0:T(8,128)(2,1)}, bf16[512,2176]{1,0:T(8,128)(2,1)S(1)}, u32[]{:S(2)}, u32[]{:S(2)}) collective-permute-start(bf16[512,2176]{1,0:T(8,128)(2,1)} %bitcast.8.x_ref.xo_ref), channel_id=1, source_target_pairs={{0,4},{4,0},{1,5},{5,1},{2,6},{6,2},{3,7},{7,3},{8,12},{12,8},{9,1... | collective-permute-start | bytes 6684680 | tf_op jit(solution)/shard_map/gates/ppermute | solution.py:207
  112.7 1.7 copy-start.1
  114.4 5.8 %copy-start.2 = (bf16[3,192,2048]{2,1,0:T(8,128)(2,1)S(1)}, bf16[3,192,2048]{2,1,0:T(8,128)(2,1)}, u32[]{:S(2)}) copy-start(bf16[3,192,2048]{2,1,0:T(8,128)(2,1)} %copy-done) | copy-start | bytes 7077892
  120.2 2.5 copy-start.15
  158.1 7.1 %collective-permute-start.3 = (bf16[512,2048]{1,0:T(8,128)(2,1)}, bf16[512,2048]{1,0:T(8,128)(2,1)S(1)}, u32[]{:S(2)}, u32[]{:S(2)}) collective-permute-start(bf16[512,2048]{1,0:T(8,128)(2,1)} %bitcast.11.d_ref.do_ref), channel_id=1, source_target_pairs={{0,4},{4,0},{1,5},{5,1},{2,6},{6,2},{3,7},{7,3},{8,12},{12,8},{9,1... | collective-permute-start | bytes 6291464 | tf_op jit(solution)/shard_map/expert/ppermute | solution.py:221
  165.2 1.7 copy-start.3
  166.9 1.7 copy-start.12
  168.6 4.0 %copy-start.7 = (bf16[512,2048]{1,0:T(8,128)(2,1)}, bf16[512,2048]{1,0:T(8,128)(2,1)S(1)}, u32[]{:S(2)}) copy-start(bf16[512,2048]{1,0:T(8,128)(2,1)S(1)} %collective-permute-done.3.d_ref.ds_ref) | copy-start | bytes 6291460
  168.6 4.7 %copy-start.10 = (f32[3,512,384]{2,1,0:T(8,128)S(1)}, f32[3,512,384]{2,1,0:T(8,128)}, u32[]{:S(2)}) copy-start(f32[3,512,384]{2,1,0:T(8,128)} %copy-done.9) | copy-start | bytes 7077892
  172.6 5.7 %collective-permute-start.4 = (bf16[512,2176]{1,0:T(8,128)(2,1)S(1)}, bf16[512,2176]{1,0:T(8,128)(2,1)S(1)}, u32[]{:S(2)}, u32[]{:S(2)}) collective-permute-start(bf16[512,2176]{1,0:T(8,128)(2,1)S(1)} %get-tuple-element.54), channel_id=1, source_target_pairs={{0,4},{4,0},{1,5},{5,1},{2,6},{6,2},{3,7},{7,3},{8,12},{12,8},{9,1... | collective-permute-start | bytes 6684680 | tf_op jit(solution)/shard_map/expert/ppermute | solution.py:231
  178.3 2.0 copy-start.13
  180.3 57.1 %all-to-all-start.2 = ((bf16[32,16,2176]{2,1,0:T(8,128)(2,1)}), bf16[32,16,2176]{2,1,0:T(8,128)(2,1)S(1)}, u32[]{:S(2)}, u32[]{:S(2)}) async-start(bf16[32,16,2176]{2,1,0:T(8,128)(2,1)} %bitcast.22), calls=%async_computation.2 | async-start | bytes 4456448 | tf_op jit(solution)/shard_map/tokens_back/all_to_all | solution.py:168
  185.6 1.6 copy-start.5
  187.2 1.6 copy-start.8
  200.8 43.2 %collective-permute-start.5 = (bf16[3,192,2048]{2,1,0:T(8,128)(2,1)}, bf16[3,192,2048]{2,1,0:T(8,128)(2,1)}, u32[]{:S(2)}, u32[]{:S(2)}) collective-permute-start(bf16[3,192,2048]{2,1,0:T(8,128)(2,1)} %get-tuple-element.62), channel_id=1, source_target_pairs={{0,0},{1,1},{4,2},{5,3},{2,4},{3,5},{6,6},{7,7},{8,8},{9,9},{12,10... | collective-permute-start | bytes 7077896 | tf_op jit(solution)/shard_map/weights_back/ppermute | solution.py:254
  204.5 56.8 %collective-permute-start.6 = (bf16[3,192,2048]{2,1,0:T(8,128)(2,1)}, bf16[3,192,2048]{2,1,0:T(8,128)(2,1)}, u32[]{:S(2)}, u32[]{:S(2)}) collective-permute-start(bf16[3,192,2048]{2,1,0:T(8,128)(2,1)} %get-tuple-element.63), channel_id=1, source_target_pairs={{1,0},{0,1},{5,2},{4,3},{3,4},{2,5},{7,6},{6,7},{9,8},{8,9},{13,10... | collective-permute-start | bytes 7077896 | tf_op jit(solution)/shard_map/weights_back/ppermute | solution.py:254
  239.2 27.1 %all-to-all-start.3 = ((bf16[4,144,512]{2,1,0:T(8,128)(2,1)}), bf16[4,144,512]{2,1,0:T(8,128)(2,1)S(1)}, u32[]{:S(2)}, u32[]{:S(2)}) async-start(bf16[4,144,512]{2,1,0:T(8,128)(2,1)} %combine.1), calls=%async_computation.3 | async-start | bytes 1179648 | tf_op jit(solution)/shard_map/tokens_back/all_to_all | solution.py:276
  (10 other events, 12.4 us)

commit v5 on v4

--- a/solution.py
+++ b/solution.py
@@ -15,6 +15,8 @@
 ROWS = PEER * SLOT
 Q = 512
 D = NX * Q
+DEST = NY * NX
+PIECE = NZ * SLOT
 WIDE = D + 128
 FQ = 192
 FH = 2 * FQ
@@ -22,7 +24,7 @@
 SMEM = pl.BlockSpec(memory_space=pltpu.SMEM)
 
 
-def params(mib=32):
+def params(mib=20):
     return pltpu.CompilerParams(vmem_limit_bytes=mib * 1024 * 1024)
 
 
@@ -68,9 +70,22 @@
     out_ref[:, D:] = jnp.where(lane == 0, share, 0.0).astype(BF)
 
 
-def select_d(pick_ref, d_ref, out_ref):
-    for h in range(NX):
-        out_ref[:, h * Q : (h + 1) * Q] = dot(pick_ref[...], d_ref[h], 1, 0).astype(BF)
+def select_d(at_ref, g_ref, out_ref):
+    e = iota((DEST, TOK), 0)
+    ids = (NX * ((e // NX) * NZ + at_ref[1]) + e % NX).astype(F32)
+    before = (iota((TOK, TOK), 0) < iota((TOK, TOK), 1)).astype(BF)
+    slot = (iota((DEST * SLOT, TOK), 0) % SLOT).astype(F32)
+    for z in range(NZ):
+        table = g_ref[z, TOK:, :TOK].astype(F32)
+        hit = jnp.zeros((DEST, TOK), F32)
+        for k in range(TOP):
+            hit = jnp.where(table[k : k + 1, :] == ids, 1.0, hit)
+        rank = dot(hit.astype(BF), before, 1, 0)
+        rank = jnp.where(hit > 0.5, rank, -1.0)
+        rank = jnp.broadcast_to(rank[:, None, :], (DEST, SLOT, TOK)).reshape(DEST * SLOT, TOK)
+        pick = jnp.where(rank == slot, 1.0, 0.0).astype(BF)
+        got = dot(pick, g_ref[z, :TOK, :], 1, 0).astype(BF)
+        out_ref[:, z * SLOT : (z + 1) * SLOT, :] = got.reshape(DEST, SLOT, Q)
 
 
 def both(wa_ref, wb_ref, i, h):
@@ -78,17 +93,18 @@
     return jnp.concatenate([wa_ref[i, :, cols], wb_ref[i, :, cols]], axis=0)
 
 
-def project(ref, wa_ref, wb_ref, i):
-    total = dot(ref[:, :Q], both(wa_ref, wb_ref, i, 0), 1, 1)
+def project(rows, wa_ref, wb_ref, i):
+    total = dot(rows[0], both(wa_ref, wb_ref, i, 0), 1, 1)
     for h in range(1, NX):
-        total = total + dot(ref[:, h * Q : (h + 1) * Q], both(wa_ref, wb_ref, i, h), 1, 1)
+        total = total + dot(rows[h], both(wa_ref, wb_ref, i, h), 1, 1)
     return total
 
 
 def gates(x_ref, wa_ref, wb_ref, pre_ref, keep_ref):
     weight = x_ref[:, D:].astype(F32)[:, :1]
-    gate = project(x_ref, wa_ref, wb_ref, 0)
-    up = project(x_ref, wa_ref, wb_ref, 1)
+    rows = [x_ref[:, h * Q : (h + 1) * Q] for h in range(NX)]
+    gate = project(rows, wa_ref, wb_ref, 0)
+    up = project(rows, wa_ref, wb_ref, 1)
     sig = 1.0 / (1.0 + jnp.exp(-gate))
     act = gate * sig
     hidden = act * up
@@ -99,7 +115,8 @@
 
 
 def expert(at_ref, pre_ref, d_ref, wa_ref, wb_ref, part_ref, keep_ref):
-    raw = project(d_ref, wa_ref, wb_ref, 2)
+    rows = [jnp.concatenate([d_ref[y * NX + h] for y in range(NY)], axis=0) for h in range(NX)]
+    raw = project(rows, wa_ref, wb_ref, 2)
     score = jnp.sum(pre_ref[0] * raw, axis=1, keepdims=True)
     keep_ref[0] = (raw * pre_ref[1]).astype(BF)
     keep_ref[1] = (raw * pre_ref[2]).astype(BF)
@@ -113,28 +130,41 @@
     part_ref[:, D:] = carried.astype(BF)
 
 
-def weight_grads(xo_ref, xs_ref, do_ref, ds_ref, ho_ref, hs_ref, ko_ref, ks_ref, a_ref, b_ref, flip):
+def down_grads(do_ref, ds_ref, ho_ref, hs_ref, a_ref, b_ref, flip):
+    @pl.when(pl.program_id(0) == 0)
+    def _():
+        flip[:, :ROWS] = ho_ref[...].T
+        flip[:, ROWS:] = hs_ref[...].T
+
+    d = jnp.concatenate([do_ref[y, 0] for y in range(NY)] + [ds_ref[y, 0] for y in range(NY)], axis=0)
+    grad = dot(flip[...], d, 1, 0).astype(BF)
+    a_ref[0] = grad[:FQ]
+    b_ref[0] = grad[FQ:]
+
+
+def gate_up_grads(xo_ref, xs_ref, ko_ref, ks_ref, a_ref, b_ref, flip):
     @pl.when(pl.program_id(0) == 0)
     def _():
         for i in range(2):
             flip[i, :, :ROWS] = ko_ref[i].T
             flip[i, :, ROWS:] = ks_ref[i].T
-        flip[2, :, :ROWS] = ho_ref[...].T
-        flip[2, :, ROWS:] = hs_ref[...].T
 
     x = jnp.concatenate([xo_ref[...], xs_ref[...]], axis=0)
-    d = jnp.concatenate([do_ref[...], ds_ref[...]], axis=0)
-    for i, rows in ((0, x), (1, x), (2, d)):
-        grad = dot(flip[i], rows, 1, 0).astype(BF)
+    for i in range(2):
+        grad = dot(flip[i], x, 1, 0).astype(BF)
         a_ref[i] = grad[:FQ]
         b_ref[i] = grad[FQ:]
 
 
-def place(at_ref, a_ref, b_ref, gate_ref, up_ref, down_ref):
+def place(at_ref, da_ref, db_ref, a_ref, b_ref, gate_ref, up_ref, down_ref):
     odd = at_ref[3] % 2
-    for i, out in enumerate((gate_ref, up_ref, down_ref)):
-        out[odd] = a_ref[i]
-        out[1 - odd] = b_ref[i]
+    for out, a, b in (
+        (gate_ref, a_ref[0], b_ref[0]),
+        (up_ref, a_ref[1], b_ref[1]),
+        (down_ref, da_ref[0], db_ref[0]),
+    ):
+        out[odd] = a
+        out[1 - odd] = b
 
 
 def combine(at_ref, table_ref, pick_ref, home_ref, out_ref):
@@ -168,9 +198,14 @@
         rows = lax.all_to_all(rows, ("y", "z"), split_axis=0, concat_axis=0, tiled=True)
         return rows.reshape(ROWS, rows.shape[2])
 
+    table = jnp.concatenate([route.T.astype(BF), prob.T], axis=0)
+    with jax.named_scope("gather_d"):
+        packed = jnp.concatenate([cotangent, jnp.pad(table, ((0, 0), (0, Q - TOK)))], axis=0)
+        every = lax.all_gather(packed, "z", axis=0, tiled=False)
+
     with jax.named_scope("select_x"):
         xg = lax.all_gather(tokens, "x", axis=0, tiled=False)
-        table = jnp.concatenate([route.T.astype(F32), prob.T.astype(F32)], axis=0)
+        table = table.astype(F32)
         xs, pick = pl.pallas_call(
             select_x,
             out_shape=(shape((ROWS, WIDE), BF), shape((ROWS, TOK), BF)),
@@ -182,16 +217,14 @@
         x_own = to_experts(xs)
 
     with jax.named_scope("select_d"):
-        pick, cotangent = lax.optimization_barrier((pick, cotangent))
-        dg = lax.all_gather(cotangent, "x", axis=0, tiled=False)
         ds = pl.pallas_call(
             select_d,
-            out_shape=shape((ROWS, D), BF),
-            in_specs=[VMEM, VMEM],
+            out_shape=shape((DEST, PIECE, Q), BF),
+            in_specs=[SMEM, VMEM],
             out_specs=VMEM,
             compiler_params=params(),
             name="select_d",
-        )(pick, dg)
+        )(at, every)
 
     with jax.named_scope("weights_out"):
         pick, *mats = lax.optimization_barrier((pick, w_gate, w_up, w_down))
@@ -202,8 +235,8 @@
             weights.append(lax.ppermute(piece, ("c", "x"), weight_pairs(m)))
 
     with jax.named_scope("gates"):
-        x_own, ds, *weights = lax.optimization_barrier((x_own, ds, *weights))
-        d_own = to_experts(ds)
+        x_own, ds = lax.optimization_barrier((x_own, ds))
+        d_own = lax.all_to_all(ds, ("y", "x"), split_axis=0, concat_axis=0, tiled=True)
         x_sib = lax.ppermute(x_own, "c", sib)
         ahead = pl.pallas_call(
             gates,
@@ -231,40 +264,41 @@
         sent = lax.ppermute(part_sib, "c", sib)
         part_own, keep_own = run(at, pre_own, d_own, *weights)
         total = (part_own.astype(F32) + sent.astype(F32)).astype(BF)
-        total, keep_own, keep_sib = lax.optimization_barrier((total, keep_own, keep_sib))
+        total, hid_own, hid_sib = lax.optimization_barrier((total, hid_own, hid_sib))
 
     with jax.named_scope("weights_back"):
         cut = pl.BlockSpec((ROWS, Q), lambda h: (0, h))
+        cut_d = pl.BlockSpec((NY, 1, PIECE, Q), lambda h: (0, h, 0, 0))
         h_spec = pl.BlockSpec((ROWS, FH), lambda h: (0, 0))
         k_spec = pl.BlockSpec((2, ROWS, FH), lambda h: (0, 0, 0))
-        o_spec = pl.BlockSpec((3, FQ, Q), lambda h: (0, 0, h))
         pieces = pl.pallas_call(
-            weight_grads,
+            down_grads,
             grid=(NX,),
-            out_shape=(shape((3, FQ, D), BF),) * 2,
-            in_specs=[cut] * 4 + [h_spec, h_spec, k_spec, k_spec],
-            out_specs=(o_spec, o_spec),
-            scratch_shapes=[pltpu.VMEM((3, FH, 2 * ROWS), BF)],
-            compiler_params=params(),
-            name="weight_grads",
-        )(x_own, x_sib, d_own, d_sib, hid_own, hid_sib, keep_own, keep_sib)
+            out_shape=(shape((1, FQ, D), BF),) * 2,
+            in_specs=[cut_d, cut_d, h_spec, h_spec],
+            out_specs=(pl.BlockSpec((1, FQ, Q), lambda h: (0, 0, h)),) * 2,
+            scratch_shapes=[pltpu.VMEM((FH, 2 * ROWS), BF)],
+            compiler_params=params(),
+            name="down_grads",
+        )(d_own.reshape(NY, NX, PIECE, Q), d_sib.reshape(NY, NX, PIECE, Q), hid_own, hid_sib)
+        *pieces, keep_own, keep_sib = lax.optimization_barrier((*pieces, keep_own, keep_sib))
+        pieces += pl.pallas_call(
+            gate_up_grads,
+            grid=(NX,),
+            out_shape=(shape((2, FQ, D), BF),) * 2,
+            in_specs=[cut, cut, k_spec, k_spec],
+            out_specs=(pl.BlockSpec((2, FQ, Q), lambda h: (0, 0, h)),) * 2,
+            scratch_shapes=[pltpu.VMEM((2, FH, 2 * ROWS), BF)],
+            compiler_params=params(),
+            name="gate_up_grads",
+        )(x_own, x_sib, keep_own, keep_sib)
         back = []
-        for m, g in enumerate(pieces):
-            inverse = [(b, a) for a, b in weight_pairs(m)]
+        for i, g in enumerate(pieces):
+            inverse = [(b, a) for a, b in weight_pairs(i % 2)]
             back.append(lax.ppermute(g, ("c", "x"), inverse))
-        part_rows = FQ // 4
-        grad_gate, grad_up, grad_down = pl.pallas_call(
-            place,
-            grid=(4,),
-            out_shape=(shape((2, FQ, D), BF),) * 3,
-            in_specs=[SMEM] + [pl.BlockSpec((3, part_rows, D), lambda i: (0, i, 0))] * 2,
-            out_specs=(pl.BlockSpec((2, part_rows, D), lambda i: (0, i, 0)),) * 3,
-            compiler_params=params(),
-            name="place",
-        )(at, *back)
 
     with jax.named_scope("tokens_back"):
-        home = to_experts(total)
+        home, back[0], back[1] = lax.optimization_barrier((to_experts(total), back[0], back[1]))
         partial = pl.pallas_call(
             combine,
             out_shape=shape((NX, TOK + 16, Q), BF),
@@ -277,6 +311,17 @@
         grad_tokens = jnp.sum(last[:, :TOK], axis=0).astype(BF)
         lines = jnp.sum(last[:, TOK : TOK + TOP, : 2 * TOK], axis=0)
         grad_prob = (lines[:, :TOK] + lines[:, TOK:]).T
+    with jax.named_scope("place"):
+        part_rows = FQ // 4
+        grad_gate, grad_up, grad_down = pl.pallas_call(
+            place,
+            grid=(4,),
+            out_shape=(shape((2, FQ, D), BF),) * 3,
+            in_specs=[SMEM] + [pl.BlockSpec((n, part_rows, D), lambda i: (0, i, 0)) for n in (1, 1, 2, 2)],
+            out_specs=(pl.BlockSpec((2, part_rows, D), lambda i: (0, i, 0)),) * 3,
+            compiler_params=params(),
+            name="place",
+        )(at, *back)
     return (grad_tokens, grad_prob, grad_gate, grad_up, grad_down)
 
 

time: 270 us -> 267 us (0.989)
  blocking collectives: 70.2 us -> 12.5 us
  waiting for transfers between devices: 82.9 us -> 126 us
  between operations: 0.92 us -> 14.3 us
  Pallas kernels: 35 us -> 44.1 us
  starting transfers between devices: 52 us -> 44.1 us
  local copies, waits for them, and re-layouts: 21.4 us -> 15.4 us
  other arithmetic: 5.37 us -> 8.87 us
    all_to_all x3 -> x2, waiting for transfers between devices: 61.5 us -> 0.01 us  [to_experts(): lax.all_to_all(rows, ('y', 'z'), split_axis=0, concat_axis=0, tiled=True)]
    all_gather x1 -> x0, blocking collectives: 57.7 us -> none  [per_device(): dg = lax.all_gather(cotangent, 'x', axis=0, tiled=False)]
    all_gather x0 -> x1, waiting for transfers between devices: none -> 49.5 us  [per_device(): every = lax.all_gather(packed, 'z', axis=0, tiled=False)]
    ppermute x2 -> x4, waiting for transfers between devices: 17.3 us -> 47.5 us  [per_device(): back.append(lax.ppermute(g, ('c', 'x'), inverse))]
    all_to_all x0 -> x1, waiting for transfers between devices: none -> 20.1 us  [per_device(): lax.all_to_all(ds, ('y', 'x'), split_axis=0, concat_axis=0, tiled=True)]
    all_to_all x3 -> x2, starting transfers between devices: 26.3 us -> 16.5 us  [to_experts(): lax.all_to_all(rows, ('y', 'z'), split_axis=0, concat_axis=0, tiled=True)]
    unnamed x46 -> x36, local copies, waits for them, and re-layouts: 20.8 us -> 13.1 us
    all_to_all x0 -> x1, starting transfers between devices: none -> 5.05 us  [per_device(): lax.all_to_all(ds, ('y', 'x'), split_axis=0, concat_axis=0, tiled=True)]
  transfers between devices with their start and end apart: 11 -> 14, of which waited for: 4 -> 6; matrix products, arithmetic and copies ran while one was open for 0% -> 2% of each run, Pallas kernels for 11% -> 13%
where the time goes in v5:
time: 267 us; the launch traced here: 265 us
  waiting for transfers between devices  126 us (47%)
  Pallas kernels  44.1 us (17%)
  starting transfers between devices  44.1 us (17%)
  local copies, waits for them, and re-layouts  15.4 us (6%)
  between operations  14.3 us (5%)
  blocking collectives  12.5 us (5%)
  other arithmetic  8.87 us (3%)
    all_gather x1, waiting for transfers between devices, per_device(): every = lax.all_gather(packed, 'z', axis=0, tiled=False)  49.5 us
    ppermute x4, waiting for transfers between devices, per_device(): back.append(lax.ppermute(g, ('c', 'x'), inverse))  47.5 us
    all_to_all x1, waiting for transfers between devices, per_device(): lax.all_to_all(ds, ('y', 'x'), split_axis=0, concat_axis=0, tiled=True)  20.1 us
    all_to_all x2, starting transfers between devices, to_experts(): lax.all_to_all(rows, ('y', 'z'), split_axis=0, concat_axis=0, tiled=True)  16.5 us
    unnamed x36, local copies, waits for them, and re-layouts  13.1 us
    all_gather x1, blocking collectives, per_device(): xg = lax.all_gather(tokens, 'x', axis=0, tiled=False)  12.5 us
    ppermute x4, starting transfers between devices, per_device(): back.append(lax.ppermute(g, ('c', 'x'), inverse))  9.57 us
    ppermute x2, starting transfers between devices, per_device(): weights.append(lax.ppermute(piece, ('c', 'x'), weight_pairs(m)))  7.13 us
  transfers between devices with their start and end apart: 14, of which 6 were waited for; matrix products, arithmetic and copies ran while one was open for 2% of the time, Pallas kernels for 13%

profile of v5, /device:TPU:1, one launch (start us, length us, event | category | flops | bytes accessed | tf_op | source)
XLA Modules:
  0.0 265.1 jit_solution(17697841171194340790)
XLA Ops:
  7.9 12.5 %all-gather = bf16[512,512]{1,0:T(8,128)(2,1)S(1)} all-gather(bf16[128,512]{1,0:T(8,128)(2,1)} %param.7), channel_id=2, replica_groups=mesh['y'=4,'z'=8,'c'=2,'x'=4] {'x'}, dimensions={0}, use_global_device_ids=true | all-gather | bytes 655360 | tf_op jit(solution)/shard_map/select_x/all_gather | solution.py:207
  21.2 2.8 %select_x.1 = (bf16[512,2176]{1,0:T(8,128)(2,1)}, bf16[512,128]{1,0:T(8,128)(2,1)S(1)}) custom-call(s32[4]{0:T(128)S(1)} %pad_add_fusion.at_ref, f32[16,128]{1,0:T(8,128)S(1)} %get-tuple-element.84.table_ref, bf16[4,128,512]{2,1,0:T(8,128)(2,1)S(1)} %bitcast.19), custom_call_target="tpu_custom_call" | custom-call | tf_op jit(solution)/shard_map/select_x/select_x/pallas_call | solution.py:209
  24.6 11.5 %all-to-all-start = ((bf16[32,16,2176]{2,1,0:T(8,128)(2,1)}), bf16[32,16,2176]{2,1,0:T(8,128)(2,1)}, u32[]{:S(2)}, u32[]{:S(2)}) async-start(bf16[32,16,2176]{2,1,0:T(8,128)(2,1)} %bitcast.7), calls=%async_computation | async-start | bytes 4456448 | tf_op jit(solution)/shard_map/select_x/all_to_all | solution.py:198
  37.0 2.1 constant_dynamic-slice_fusion
  40.8 5.5 %collective-permute-start = (bf16[3,192,2048]{2,1,0:T(8,128)(2,1)}, bf16[3,192,2048]{2,1,0:T(8,128)(2,1)S(1)}, u32[]{:S(2)}, u32[]{:S(2)}) collective-permute-start(bf16[3,192,2048]{2,1,0:T(8,128)(2,1)} %pad_maximum_fusion), channel_id=1, source_target_pairs={{0,0},{1,1},{2,4},{3,5},{4,2},{5,3},{6,6},{7,7},{8,8},{9,9},{10,12... | collective-permute-start | bytes 7077896 | tf_op jit(solution)/shard_map/weights_out/ppermute | solution.py:235
  49.6 49.5 %all-gather.4.cloned.1.call-done = bf16[1152,512]{1,0:T(8,128)(2,1)} async-done(((bf16[144,512]{1,0:T(8,128)(2,1)}), bf16[1152,512]{1,0:T(8,128)(2,1)}) %all-gather.4.cloned.1.call-update) | async-done | bytes 1179664 | tf_op jit(solution)/shard_map/gather_d/all_gather | solution.py:204
  100.4 2.3 select_d.1
  104.5 5.1 %all-to-all-start.1 = ((bf16[16,128,512]{2,1,0:T(8,128)(2,1)}), bf16[16,128,512]{2,1,0:T(8,128)(2,1)}, u32[]{:S(2)}, u32[]{:S(2)}) async-start(bf16[16,128,512]{2,1,0:T(8,128)(2,1)} %copy-done), calls=%async_computation.1 | async-start | bytes 4194304 | tf_op jit(solution)/shard_map/gates/all_to_all | solution.py:239
  109.6 4.8 %gates.2 = (f32[3,512,384]{2,1,0:T(8,128)S(1)}, bf16[512,384]{1,0:T(8,128)(2,1)S(1)}) custom-call(bf16[512,2176]{1,0:T(8,128)(2,1)} %bitcast.8.x_ref.xo_ref, bf16[3,192,2048]{2,1,0:T(8,128)(2,1)S(1)} %collective-permute-done.wa_ref, bf16[3,192,2048]{2,1,0:T(8,128)(2,1)} %collective-permute-done.1.wb_ref), custom_call_target="tpu_custom_call" | custom-call | tf_op jit(solution)/shard_map/gates/gates/pallas_call | solution.py:249
  115.8 4.8 %gates.3 = (f32[3,512,384]{2,1,0:T(8,128)S(1)}, bf16[512,384]{1,0:T(8,128)(2,1)S(1)}) custom-call(bf16[512,2176]{1,0:T(8,128)(2,1)} %collective-permute-done.2.x_ref.xs_ref, bf16[3,192,2048]{2,1,0:T(8,128)(2,1)S(1)} %collective-permute-done.wa_ref, bf16[3,192,2048]{2,1,0:T(8,128)(2,1)} %collective-permute-done.1.wb_ref), custom_call_target="tpu_custom_call" | custom-call | tf_op jit(solution)/shard_map/gates/gates/pallas_call | solution.py:250
  122.8 20.1 %all-to-all-done.1.d_ref = bf16[16,128,512]{2,1,0:T(8,128)(2,1)} async-done(((bf16[16,128,512]{2,1,0:T(8,128)(2,1)}), bf16[16,128,512]{2,1,0:T(8,128)(2,1)}, u32[]{:S(2)}, u32[]{:S(2)}) %all-to-all-start.1) | async-done | bytes 2097184 | tf_op jit(solution)/shard_map/gates/all_to_all | solution.py:239
  144.0 4.0 %collective-permute-done.3.d_ref = bf16[16,128,512]{2,1,0:T(8,128)(2,1)S(1)} collective-permute-done((bf16[16,128,512]{2,1,0:T(8,128)(2,1)}, bf16[16,128,512]{2,1,0:T(8,128)(2,1)S(1)}, u32[]{:S(2)}, u32[]{:S(2)}) %collective-permute-start.3) | collective-permute-done | bytes 2097184 | tf_op jit(solution)/shard_map/expert/ppermute | solution.py:254
  149.7 5.9 %expert.3 = (bf16[512,2176]{1,0:T(8,128)(2,1)S(1)}, bf16[2,512,384]{2,1,0:T(8,128)(2,1)S(1)}) custom-call(s32[4]{0:T(128)S(1)} %pad_add_fusion.at_ref, f32[3,512,384]{2,1,0:T(8,128)S(1)} %copy-done.6, bf16[16,128,512]{2,1,0:T(8,128)(2,1)S(1)} %collective-permute-done.3.d_ref, bf16[3,192,2048]{2,1,0:T(8,128)(2,1)S(1)} %collective-permute-done.wa_ref, ...), custom_call_target="tpu_custom_call" | custom-call | tf_op jit(solution)/shard_map/expert/expert/pallas_call | solution.py:263
  156.2 5.8 %expert.2 = (bf16[512,2176]{1,0:T(8,128)(2,1)S(1)}, bf16[2,512,384]{2,1,0:T(8,128)(2,1)S(1)}) custom-call(s32[4]{0:T(128)S(1)} %pad_add_fusion.at_ref, f32[3,512,384]{2,1,0:T(8,128)S(1)} %copy-done.4, bf16[16,128,512]{2,1,0:T(8,128)(2,1)} %all-to-all-done.1.d_ref, bf16[3,192,2048]{2,1,0:T(8,128)(2,1)S(1)} %collective-permute-done.wa_ref, ...), custom_call_target="tpu_custom_call" | custom-call | tf_op jit(solution)/shard_map/expert/expert/pallas_call | solution.py:265
  164.0 5.1 %all-to-all-start.2 = ((bf16[32,16,2176]{2,1,0:T(8,128)(2,1)}), bf16[32,16,2176]{2,1,0:T(8,128)(2,1)S(1)}, u32[]{:S(2)}, u32[]{:S(2)}) async-start(bf16[32,16,2176]{2,1,0:T(8,128)(2,1)} %bitcast.21), calls=%async_computation.2 | async-start | bytes 4456448 | tf_op jit(solution)/shard_map/tokens_back/all_to_all | solution.py:198
  171.6 4.3 %down_grads.1 = (bf16[1,192,2048]{2,1,0:T(8,128)(2,1)S(1)}, bf16[1,192,2048]{2,1,0:T(8,128)(2,1)S(1)}) custom-call(bf16[4,4,128,512]{3,2,1,0:T(8,128)(2,1)} %bitcast.12.do_ref, bf16[4,4,128,512]{3,2,1,0:T(8,128)(2,1)S(1)} %bitcast.18, bf16[512,384]{1,0:T(8,128)(2,1)S(1)} %get-tuple-element.59.ho_ref, bf16[512,384]{1,0:T(8,128)(2,1)S(1)} %copy-done.13), custom_call_target="tpu_custom_call" | custom-call | tf_op jit(solution)/shard_map/weights_back/down_grads/pallas_call | solution.py:274
  176.0 7.1 %gate_up_grads.1 = (bf16[2,192,2048]{2,1,0:T(8,128)(2,1)}, bf16[2,192,2048]{2,1,0:T(8,128)(2,1)}) custom-call(bf16[512,2176]{1,0:T(8,128)(2,1)} %bitcast.8.x_ref.xo_ref, bf16[512,2176]{1,0:T(8,128)(2,1)} %collective-permute-done.2.x_ref.xs_ref, bf16[2,512,384]{2,1,0:T(8,128)(2,1)S(1)} %copy-done.11, bf16[2,512,384]{2,1,0:T(8,128)(2,1)S(1)} %get-tuple-element.71.ks_ref), custom_call_target="tpu_custom_call" | custom-call | tf_op jit(solution)/shard_map/weights_back/gate_up_grads/pallas_call | solution.py:285
  183.0 2.0 collective-permute-start.7
  186.3 4.5 %collective-permute-start.5 = (bf16[1,192,2048]{2,1,0:T(8,128)(2,1)S(1)}, bf16[1,192,2048]{2,1,0:T(8,128)(2,1)S(1)}, u32[]{:S(2)}, u32[]{:S(2)}) collective-permute-start(bf16[1,192,2048]{2,1,0:T(8,128)(2,1)S(1)} %get-tuple-element.65), channel_id=1, source_target_pairs={{0,0},{1,1},{4,2},{5,3},{2,4},{3,5},{6,6},{7,7},{8,8},{9,9},{12,10... | collective-permute-start | bytes 2359304 | tf_op jit(solution)/shard_map/weights_back/ppermute | solution.py:298
  192.6 37.6 %collective-permute-done.5.da_ref = bf16[1,192,2048]{2,1,0:T(8,128)(2,1)S(1)} collective-permute-done((bf16[1,192,2048]{2,1,0:T(8,128)(2,1)S(1)}, bf16[1,192,2048]{2,1,0:T(8,128)(2,1)S(1)}, u32[]{:S(2)}, u32[]{:S(2)}) %collective-permute-start.5) | collective-permute-done | bytes 786464 | tf_op jit(solution)/shard_map/weights_back/ppermute | solution.py:298
  230.3 9.8 %collective-permute-done.6.db_ref = bf16[1,192,2048]{2,1,0:T(8,128)(2,1)S(1)} collective-permute-done((bf16[1,192,2048]{2,1,0:T(8,128)(2,1)S(1)}, bf16[1,192,2048]{2,1,0:T(8,128)(2,1)S(1)}, u32[]{:S(2)}, u32[]{:S(2)}) %collective-permute-start.6) | collective-permute-done | bytes 786464 | tf_op jit(solution)/shard_map/weights_back/ppermute | solution.py:298
  242.8 3.5 %all-to-all-start.3 = ((bf16[4,144,512]{2,1,0:T(8,128)(2,1)}), bf16[4,144,512]{2,1,0:T(8,128)(2,1)S(1)}, u32[]{:S(2)}, u32[]{:S(2)}) async-start(bf16[4,144,512]{2,1,0:T(8,128)(2,1)} %combine.1), calls=%async_computation.3 | async-start | bytes 1179648 | tf_op jit(solution)/shard_map/tokens_back/all_to_all | solution.py:310
  247.4 4.6 %place.1 = (bf16[2,192,2048]{2,1,0:T(8,128)(2,1)}, bf16[2,192,2048]{2,1,0:T(8,128)(2,1)}, bf16[2,192,2048]{2,1,0:T(8,128)(2,1)}) custom-call(s32[4]{0:T(128)S(1)} %pad_add_fusion.at_ref, bf16[1,192,2048]{2,1,0:T(8,128)(2,1)S(1)} %collective-permute-done.5.da_ref, bf16[1,192,2048]{2,1,0:T(8,128)(2,1)S(1)} %copy-done.9, ...), custom_call_target="tpu_custom_call" | custom-call | tf_op jit(solution)/shard_map/place/place/pallas_call | solution.py:316
  252.0 4.7 %all-to-all-done.3 = bf16[4,144,512]{2,1,0:T(8,128)(2,1)S(1)} async-done(((bf16[4,144,512]{2,1,0:T(8,128)(2,1)}), bf16[4,144,512]{2,1,0:T(8,128)(2,1)S(1)}, u32[]{:S(2)}, u32[]{:S(2)}) %all-to-all-start.3) | async-done | bytes 589856 | tf_op jit(solution)/shard_map/tokens_back/all_to_all | solution.py:310
  (65 shorter events, 31.0 us)
Async XLA Ops:
  24.6 11.5 %copy-start.17 = (bf16[128,512]{1,0:T(8,128)(2,1)S(1)}, bf16[128,512]{1,0:T(8,128)(2,1)}, u32[]{:S(2)}) copy-start(bf16[128,512]{1,0:T(8,128)(2,1)} %param.8) | copy-start | bytes 393220
  24.6 12.3 %copy-start.16 = (bf16[2,192,2048]{2,1,0:T(8,128)(2,1)S(1)}, bf16[2,192,2048]{2,1,0:T(8,128)(2,1)}, u32[]{:S(2)}) copy-start(bf16[2,192,2048]{2,1,0:T(8,128)(2,1)} %param.11) | copy-start | bytes 4718596
  24.6 79.4 %all-to-all-start = ((bf16[32,16,2176]{2,1,0:T(8,128)(2,1)}), bf16[32,16,2176]{2,1,0:T(8,128)(2,1)}, u32[]{:S(2)}, u32[]{:S(2)}) async-start(bf16[32,16,2176]{2,1,0:T(8,128)(2,1)} %bitcast.7), calls=%async_computation | async-start | bytes 4456448 | tf_op jit(solution)/shard_map/select_x/all_to_all | solution.py:198
  36.1 63.0 %all-gather.4.cloned.1.call-start = ((), (), s32[]{:S(2)}) async-start(), calls=%async_computation.4 | async-start | bytes 1327104 | tf_op jit(solution)/shard_map/gather_d/all_gather | solution.py:204
  40.8 68.7 %collective-permute-start = (bf16[3,192,2048]{2,1,0:T(8,128)(2,1)}, bf16[3,192,2048]{2,1,0:T(8,128)(2,1)S(1)}, u32[]{:S(2)}, u32[]{:S(2)}) collective-permute-start(bf16[3,192,2048]{2,1,0:T(8,128)(2,1)} %pad_maximum_fusion), channel_id=1, source_target_pairs={{0,0},{1,1},{2,4},{3,5},{4,2},{5,3},{6,6},{7,7},{8,8},{9,9},{10,12... | collective-permute-start | bytes 7077896 | tf_op jit(solution)/shard_map/weights_out/ppermute | solution.py:235
  48.0 61.5 %collective-permute-start.1 = (bf16[3,192,2048]{2,1,0:T(8,128)(2,1)}, bf16[3,192,2048]{2,1,0:T(8,128)(2,1)}, u32[]{:S(2)}, u32[]{:S(2)}) collective-permute-start(bf16[3,192,2048]{2,1,0:T(8,128)(2,1)} %pad_maximum_fusion.1), channel_id=1, source_target_pairs={{0,1},{1,0},{2,5},{3,4},{4,3},{5,2},{6,7},{7,6},{8,9},{9,8},{10,13... | collective-permute-start | bytes 7077896 | tf_op jit(solution)/shard_map/weights_out/ppermute | solution.py:235
  104.0 11.8 %collective-permute-start.2 = (bf16[512,2176]{1,0:T(8,128)(2,1)}, bf16[512,2176]{1,0:T(8,128)(2,1)}, u32[]{:S(2)}, u32[]{:S(2)}) collective-permute-start(bf16[512,2176]{1,0:T(8,128)(2,1)} %bitcast.8.x_ref.xo_ref), channel_id=1, source_target_pairs={{0,4},{4,0},{1,5},{5,1},{2,6},{6,2},{3,7},{7,3},{8,12},{12,8},{9,1... | collective-permute-start | bytes 6684680 | tf_op jit(solution)/shard_map/gates/ppermute | solution.py:240
  104.5 38.4 %all-to-all-start.1 = ((bf16[16,128,512]{2,1,0:T(8,128)(2,1)}), bf16[16,128,512]{2,1,0:T(8,128)(2,1)}, u32[]{:S(2)}, u32[]{:S(2)}) async-start(bf16[16,128,512]{2,1,0:T(8,128)(2,1)} %copy-done), calls=%async_computation.1 | async-start | bytes 4194304 | tf_op jit(solution)/shard_map/gates/all_to_all | solution.py:239
  114.4 1.4 copy-start.3
  142.9 13.4 %copy-start.4 = (f32[3,512,384]{2,1,0:T(8,128)S(1)}, f32[3,512,384]{2,1,0:T(8,128)}, u32[]{:S(2)}) copy-start(f32[3,512,384]{2,1,0:T(8,128)} %copy-done.3) | copy-start | bytes 7077892
  142.9 5.1 %collective-permute-start.3 = (bf16[16,128,512]{2,1,0:T(8,128)(2,1)}, bf16[16,128,512]{2,1,0:T(8,128)(2,1)S(1)}, u32[]{:S(2)}, u32[]{:S(2)}) collective-permute-start(bf16[16,128,512]{2,1,0:T(8,128)(2,1)} %all-to-all-done.1.d_ref), channel_id=1, source_target_pairs={{0,4},{4,0},{1,5},{5,1},{2,6},{6,2},{3,7},{7,3},{8,12},{12,8},{9,1... | collective-permute-start | bytes 6291464 | tf_op jit(solution)/shard_map/expert/ppermute | solution.py:254
  148.0 1.7 copy-start.6
  149.7 5.9 %copy-start.1 = (bf16[16,128,512]{2,1,0:T(8,128)(2,1)}, bf16[16,128,512]{2,1,0:T(8,128)(2,1)S(1)}, u32[]{:S(2)}) copy-start(bf16[16,128,512]{2,1,0:T(8,128)(2,1)S(1)} %collective-permute-done.3.d_ref) | copy-start | bytes 6291460
  155.6 6.4 %collective-permute-start.4 = (bf16[512,2176]{1,0:T(8,128)(2,1)S(1)}, bf16[512,2176]{1,0:T(8,128)(2,1)S(1)}, u32[]{:S(2)}, u32[]{:S(2)}) collective-permute-start(bf16[512,2176]{1,0:T(8,128)(2,1)S(1)} %get-tuple-element.55), channel_id=1, source_target_pairs={{0,4},{4,0},{1,5},{5,1},{2,6},{6,2},{3,7},{7,3},{8,12},{12,8},{9,1... | collective-permute-start | bytes 6684680 | tf_op jit(solution)/shard_map/expert/ppermute | solution.py:264
  162.0 1.9 copy-start.10
  164.0 77.0 %all-to-all-start.2 = ((bf16[32,16,2176]{2,1,0:T(8,128)(2,1)}), bf16[32,16,2176]{2,1,0:T(8,128)(2,1)S(1)}, u32[]{:S(2)}, u32[]{:S(2)}) async-start(bf16[32,16,2176]{2,1,0:T(8,128)(2,1)} %bitcast.21), calls=%async_computation.2 | async-start | bytes 4456448 | tf_op jit(solution)/shard_map/tokens_back/all_to_all | solution.py:198
  169.1 1.6 copy-start.2
  171.6 4.3 %copy-start.11 = (bf16[2,512,384]{2,1,0:T(8,128)(2,1)S(1)}, bf16[2,512,384]{2,1,0:T(8,128)(2,1)}, u32[]{:S(2)}) copy-start(bf16[2,512,384]{2,1,0:T(8,128)(2,1)} %copy-done.10) | copy-start | bytes 2359300
  176.0 65.0 %copy-start.15 = (bf16[512,128]{1,0:T(8,128)(2,1)S(1)}, bf16[512,128]{1,0:T(8,128)(2,1)}, u32[]{:S(2)}) copy-start(bf16[512,128]{1,0:T(8,128)(2,1)} %copy-done.14) | copy-start | bytes 393220
  183.0 63.2 %collective-permute-start.7 = (bf16[2,192,2048]{2,1,0:T(8,128)(2,1)}, bf16[2,192,2048]{2,1,0:T(8,128)(2,1)}, u32[]{:S(2)}, u32[]{:S(2)}) collective-permute-start(bf16[2,192,2048]{2,1,0:T(8,128)(2,1)} %get-tuple-element.72), channel_id=1, source_target_pairs={{0,0},{1,1},{4,2},{5,3},{2,4},{3,5},{6,6},{7,7},{8,8},{9,9},{12,10... | collective-permute-start | bytes 4718600 | tf_op jit(solution)/shard_map/weights_back/ppermute | solution.py:298
  185.0 61.3 %collective-permute-start.8 = (bf16[2,192,2048]{2,1,0:T(8,128)(2,1)}, bf16[2,192,2048]{2,1,0:T(8,128)(2,1)}, u32[]{:S(2)}, u32[]{:S(2)}) collective-permute-start(bf16[2,192,2048]{2,1,0:T(8,128)(2,1)} %get-tuple-element.73), channel_id=1, source_target_pairs={{1,0},{0,1},{5,2},{4,3},{3,4},{2,5},{7,6},{6,7},{9,8},{8,9},{13,10... | collective-permute-start | bytes 4718600 | tf_op jit(solution)/shard_map/weights_back/ppermute | solution.py:298
  186.3 44.0 %collective-permute-start.5 = (bf16[1,192,2048]{2,1,0:T(8,128)(2,1)S(1)}, bf16[1,192,2048]{2,1,0:T(8,128)(2,1)S(1)}, u32[]{:S(2)}, u32[]{:S(2)}) collective-permute-start(bf16[1,192,2048]{2,1,0:T(8,128)(2,1)S(1)} %get-tuple-element.65), channel_id=1, source_target_pairs={{0,0},{1,1},{4,2},{5,3},{2,4},{3,5},{6,6},{7,7},{8,8},{9,9},{12,10... | collective-permute-start | bytes 2359304 | tf_op jit(solution)/shard_map/weights_back/ppermute | solution.py:298
  190.8 49.2 %collective-permute-start.6 = (bf16[1,192,2048]{2,1,0:T(8,128)(2,1)S(1)}, bf16[1,192,2048]{2,1,0:T(8,128)(2,1)S(1)}, u32[]{:S(2)}, u32[]{:S(2)}) collective-permute-start(bf16[1,192,2048]{2,1,0:T(8,128)(2,1)S(1)} %get-tuple-element.66), channel_id=1, source_target_pairs={{1,0},{0,1},{5,2},{4,3},{3,4},{2,5},{7,6},{6,7},{9,8},{8,9},{13,10... | collective-permute-start | bytes 2359304 | tf_op jit(solution)/shard_map/weights_back/ppermute | solution.py:298
  242.8 13.9 %all-to-all-start.3 = ((bf16[4,144,512]{2,1,0:T(8,128)(2,1)}), bf16[4,144,512]{2,1,0:T(8,128)(2,1)S(1)}, u32[]{:S(2)}, u32[]{:S(2)}) async-start(bf16[4,144,512]{2,1,0:T(8,128)(2,1)} %combine.1), calls=%async_computation.3 | async-start | bytes 1179648 | tf_op jit(solution)/shard_map/tokens_back/all_to_all | solution.py:310
  (8 other events, 8.4 us)
Sparse Core Ops, SparseCore 0:
  39.3 59.7 all-gather.3

commit v6 on v5

--- a/solution.py
+++ b/solution.py
@@ -130,41 +130,28 @@
     part_ref[:, D:] = carried.astype(BF)
 
 
-def down_grads(do_ref, ds_ref, ho_ref, hs_ref, a_ref, b_ref, flip):
-    @pl.when(pl.program_id(0) == 0)
-    def _():
-        flip[:, :ROWS] = ho_ref[...].T
-        flip[:, ROWS:] = hs_ref[...].T
-
-    d = jnp.concatenate([do_ref[y, 0] for y in range(NY)] + [ds_ref[y, 0] for y in range(NY)], axis=0)
-    grad = dot(flip[...], d, 1, 0).astype(BF)
-    a_ref[0] = grad[:FQ]
-    b_ref[0] = grad[FQ:]
-
-
-def gate_up_grads(xo_ref, xs_ref, ko_ref, ks_ref, a_ref, b_ref, flip):
+def weight_grads(xo_ref, xs_ref, do_ref, ds_ref, ho_ref, hs_ref, ko_ref, ks_ref, a_ref, b_ref, flip):
     @pl.when(pl.program_id(0) == 0)
     def _():
         for i in range(2):
             flip[i, :, :ROWS] = ko_ref[i].T
             flip[i, :, ROWS:] = ks_ref[i].T
+        flip[2, :, :ROWS] = ho_ref[...].T
+        flip[2, :, ROWS:] = hs_ref[...].T
 
     x = jnp.concatenate([xo_ref[...], xs_ref[...]], axis=0)
-    for i in range(2):
-        grad = dot(flip[i], x, 1, 0).astype(BF)
+    d = jnp.concatenate([do_ref[y, 0] for y in range(NY)] + [ds_ref[y, 0] for y in range(NY)], axis=0)
+    for i, rows in ((0, x), (1, x), (2, d)):
+        grad = dot(flip[i], rows, 1, 0).astype(BF)
         a_ref[i] = grad[:FQ]
         b_ref[i] = grad[FQ:]
 
 
-def place(at_ref, da_ref, db_ref, a_ref, b_ref, gate_ref, up_ref, down_ref):
+def place(at_ref, a_ref, b_ref, gate_ref, up_ref, down_ref):
     odd = at_ref[3] % 2
-    for out, a, b in (
-        (gate_ref, a_ref[0], b_ref[0]),
-        (up_ref, a_ref[1], b_ref[1]),
-        (down_ref, da_ref[0], db_ref[0]),
-    ):
-        out[odd] = a
-        out[1 - odd] = b
+    for i, out in enumerate((gate_ref, up_ref, down_ref)):
+        out[odd] = a_ref[i]
+        out[1 - odd] = b_ref[i]
 
 
 def combine(at_ref, table_ref, pick_ref, home_ref, out_ref):
@@ -216,6 +203,16 @@
         )(at, table, xg)
         x_own = to_experts(xs)
 
+    with jax.named_scope("weights_out"):
+        pick, *mats = lax.optimization_barrier((pick, w_gate, w_up, w_down))
+        weights = []
+        for m in range(2):
+            k = (ix + m) % 2
+            if m == 1:
+                every, *mats = lax.optimization_barrier((every, *mats))
+            piece = jnp.stack([lax.dynamic_index_in_dim(w, k, 0, keepdims=False) for w in mats])
+            weights.append(lax.ppermute(piece, ("c", "x"), weight_pairs(m)))
+
     with jax.named_scope("select_d"):
         ds = pl.pallas_call(
             select_d,
@@ -226,16 +223,8 @@
             name="select_d",
         )(at, every)
 
-    with jax.named_scope("weights_out"):
-        pick, *mats = lax.optimization_barrier((pick, w_gate, w_up, w_down))
-        weights = []
-        for m in range(2):
-            k = (ix + m) % 2
-            piece = jnp.stack([lax.dynamic_index_in_dim(w, k, 0, keepdims=False) for w in mats])
-            weights.append(lax.ppermute(piece, ("c", "x"), weight_pairs(m)))
-
     with jax.named_scope("gates"):
-        x_own, ds = lax.optimization_barrier((x_own, ds))
+        x_own, ds, *weights = lax.optimization_barrier((x_own, ds, *weights))
         d_own = lax.all_to_all(ds, ("y", "x"), split_axis=0, concat_axis=0, tiled=True)
         x_sib = lax.ppermute(x_own, "c", sib)
         ahead = pl.pallas_call(
@@ -264,7 +253,7 @@
         sent = lax.ppermute(part_sib, "c", sib)
         part_own, keep_own = run(at, pre_own, d_own, *weights)
         total = (part_own.astype(F32) + sent.astype(F32)).astype(BF)
-        total, hid_own, hid_sib = lax.optimization_barrier((total, hid_own, hid_sib))
+        total, keep_own, keep_sib = lax.optimization_barrier((total, keep_own, keep_sib))
 
     with jax.named_scope("weights_back"):
         cut = pl.BlockSpec((ROWS, Q), lambda h: (0, h))
@@ -272,33 +261,31 @@
         h_spec = pl.BlockSpec((ROWS, FH), lambda h: (0, 0))
         k_spec = pl.BlockSpec((2, ROWS, FH), lambda h: (0, 0, 0))
         pieces = pl.pallas_call(
-            down_grads,
+            weight_grads,
             grid=(NX,),
-            out_shape=(shape((1, FQ, D), BF),) * 2,
-            in_specs=[cut_d, cut_d, h_spec, h_spec],
-            out_specs=(pl.BlockSpec((1, FQ, Q), lambda h: (0, 0, h)),) * 2,
-            scratch_shapes=[pltpu.VMEM((FH, 2 * ROWS), BF)],
-            compiler_params=params(),
-            name="down_grads",
-        )(d_own.reshape(NY, NX, PIECE, Q), d_sib.reshape(NY, NX, PIECE, Q), hid_own, hid_sib)
-        *pieces, keep_own, keep_sib = lax.optimization_barrier((*pieces, keep_own, keep_sib))
-        pieces += pl.pallas_call(
-            gate_up_grads,
-            grid=(NX,),
-            out_shape=(shape((2, FQ, D), BF),) * 2,
-            in_specs=[cut, cut, k_spec, k_spec],
-            out_specs=(pl.BlockSpec((2, FQ, Q), lambda h: (0, 0, h)),) * 2,
-            scratch_shapes=[pltpu.VMEM((2, FH, 2 * ROWS), BF)],
-            compiler_params=params(),
-            name="gate_up_grads",
-        )(x_own, x_sib, keep_own, keep_sib)
+            out_shape=(shape((3, FQ, D), BF),) * 2,
+            in_specs=[cut, cut, cut_d, cut_d, h_spec, h_spec, k_spec, k_spec],
+            out_specs=(pl.BlockSpec((3, FQ, Q), lambda h: (0, 0, h)),) * 2,
+            scratch_shapes=[pltpu.VMEM((3, FH, 2 * ROWS), BF)],
+            compiler_params=params(28),
+            name="weight_grads",
+        )(
+            x_own,
+            x_sib,
+            d_own.reshape(NY, NX, PIECE, Q),
+            d_sib.reshape(NY, NX, PIECE, Q),
+            hid_own,
+            hid_sib,
+            keep_own,
+            keep_sib,
+        )
         back = []
         for i, g in enumerate(pieces):
-            inverse = [(b, a) for a, b in weight_pairs(i % 2)]
+            inverse = [(b, a) for a, b in weight_pairs(i)]
             back.append(lax.ppermute(g, ("c", "x"), inverse))
 
     with jax.named_scope("tokens_back"):
-        home, back[0], back[1] = lax.optimization_barrier((to_experts(total), back[0], back[1]))
+        home = to_experts(total)
         partial = pl.pallas_call(
             combine,
             out_shape=shape((NX, TOK + 16, Q), BF),
@@ -317,7 +304,7 @@
             place,
             grid=(4,),
             out_shape=(shape((2, FQ, D), BF),) * 3,
-            in_specs=[SMEM] + [pl.BlockSpec((n, part_rows, D), lambda i: (0, i, 0)) for n in (1, 1, 2, 2)],
+            in_specs=[SMEM] + [pl.BlockSpec((n, part_rows, D), lambda i: (0, i, 0)) for n in (3, 3)],
             out_specs=(pl.BlockSpec((2, part_rows, D), lambda i: (0, i, 0)),) * 3,
             compiler_params=params(),
             name="place",

time: 267 us -> 260 us (0.974)
  waiting for transfers between devices: 126 us -> 115 us
  starting transfers between devices: 44.1 us -> 47.7 us
  Pallas kernels: 44.1 us -> 41.1 us
    all_to_all x2, waiting for transfers between devices: 0.01 us -> 51.1 us  [to_experts(): lax.all_to_all(rows, ('y', 'z'), split_axis=0, concat_axis=0, tiled=True)]
    all_gather x1, waiting for transfers between devices: 49.5 us -> 9.84 us  [per_device(): every = lax.all_gather(packed, 'z', axis=0, tiled=False)]
    ppermute x4 -> x2, waiting for transfers between devices: 47.5 us -> 16.1 us  [per_device(): back.append(lax.ppermute(g, ('c', 'x'), inverse))]
    ppermute x2, waiting for transfers between devices: 0.01 us -> 14.2 us  [per_device(): weights.append(lax.ppermute(piece, ('c', 'x'), weight_pairs(m)))]
    ppermute x4 -> x2, starting transfers between devices: 9.57 us -> 3.24 us  [per_device(): back.append(lax.ppermute(g, ('c', 'x'), inverse))]
    ppermute x2, starting transfers between devices: 7.13 us -> 12.3 us  [per_device(): weights.append(lax.ppermute(piece, ('c', 'x'), weight_pairs(m)))]
    all_to_all x1, waiting for transfers between devices: 4.71 us -> 0.01 us  [per_device(): lax.all_to_all(partial, 'x', split_axis=0, concat_axis=0, tiled=True)]
    pallas_call x2 -> x1, Pallas kernels: 11.4 us -> 9.14 us  [per_device(): pl.pallas_call(weight_grads, grid=(NX,), out_shape=(shape((3, FQ, D), BF)...]
  transfers between devices with their start and end apart: 14 -> 12, of which waited for: 6 -> 8; matrix products, arithmetic and copies ran while one was open for 2% -> 3% of each run, Pallas kernels for 13% -> 14%
where the time goes in v6:
time: 260 us; the launch traced here: 257 us
  waiting for transfers between devices  115 us (44%)
  starting transfers between devices  47.7 us (18%)
  Pallas kernels  41.1 us (16%)
  local copies, waits for them, and re-layouts  15.5 us (6%)
  between operations  14.3 us (6%)
  blocking collectives  12.6 us (5%)
  other arithmetic  9.94 us (4%)
    all_to_all x2, waiting for transfers between devices, to_experts(): lax.all_to_all(rows, ('y', 'z'), split_axis=0, concat_axis=0, tiled=True)  51.1 us
    all_to_all x1, waiting for transfers between devices, per_device(): lax.all_to_all(ds, ('y', 'x'), split_axis=0, concat_axis=0, tiled=True)  20.2 us
    all_to_all x2, starting transfers between devices, to_experts(): lax.all_to_all(rows, ('y', 'z'), split_axis=0, concat_axis=0, tiled=True)  19.1 us
    ppermute x2, waiting for transfers between devices, per_device(): back.append(lax.ppermute(g, ('c', 'x'), inverse))  16.1 us
    ppermute x2, waiting for transfers between devices, per_device(): weights.append(lax.ppermute(piece, ('c', 'x'), weight_pairs(m)))  14.2 us
    all_gather x1, blocking collectives, per_device(): xg = lax.all_gather(tokens, 'x', axis=0, tiled=False)  12.6 us
    unnamed x34, local copies, waits for them, and re-layouts  12.4 us
    ppermute x2, starting transfers between devices, per_device(): weights.append(lax.ppermute(piece, ('c', 'x'), weight_pairs(m)))  12.3 us
  transfers between devices with their start and end apart: 12, of which 8 were waited for; matrix products, arithmetic and copies ran while one was open for 3% of the time, Pallas kernels for 14%

profile of v6, /device:TPU:1, one launch (start us, length us, event | category | flops | bytes accessed | tf_op | source)
XLA Modules:
  0.0 256.5 jit_solution(2601731038050778039)
XLA Ops:
  10.4 12.6 %all-gather = bf16[512,512]{1,0:T(8,128)(2,1)S(1)} all-gather(bf16[128,512]{1,0:T(8,128)(2,1)} %param.7), channel_id=2, replica_groups=mesh['y'=4,'z'=8,'c'=2,'x'=4] {'x'}, dimensions={0}, use_global_device_ids=true | all-gather | bytes 655360 | tf_op jit(solution)/shard_map/select_x/all_gather | solution.py:194
  26.4 11.3 %all-to-all-start = ((bf16[32,16,2176]{2,1,0:T(8,128)(2,1)}), bf16[32,16,2176]{2,1,0:T(8,128)(2,1)}, u32[]{:S(2)}, u32[]{:S(2)}) async-start(bf16[32,16,2176]{2,1,0:T(8,128)(2,1)} %bitcast.19), calls=%async_computation | async-start | bytes 4456448 | tf_op jit(solution)/shard_map/select_x/all_to_all | solution.py:185
  41.0 5.6 %collective-permute-start = (bf16[3,192,2048]{2,1,0:T(8,128)(2,1)}, bf16[3,192,2048]{2,1,0:T(8,128)(2,1)}, u32[]{:S(2)}, u32[]{:S(2)}) collective-permute-start(bf16[3,192,2048]{2,1,0:T(8,128)(2,1)} %pad_maximum_fusion), channel_id=1, source_target_pairs={{0,0},{1,1},{2,4},{3,5},{4,2},{5,3},{6,6},{7,7},{8,8},{9,9},{10,12... | collective-permute-start | bytes 7077896 | tf_op jit(solution)/shard_map/weights_out/ppermute | solution.py:214
  46.6 9.8 %all-gather.4.cloned.1.call-done = bf16[1152,512]{1,0:T(8,128)(2,1)} async-done(((bf16[144,512]{1,0:T(8,128)(2,1)}), bf16[1152,512]{1,0:T(8,128)(2,1)}) %all-gather.4.cloned.1.call-update) | async-done | bytes 1179664 | tf_op jit(solution)/shard_map/gather_d/all_gather | solution.py:191
  59.7 6.7 %collective-permute-start.1 = (bf16[3,192,2048]{2,1,0:T(8,128)(2,1)}, bf16[3,192,2048]{2,1,0:T(8,128)(2,1)S(1)}, u32[]{:S(2)}, u32[]{:S(2)}) collective-permute-start(bf16[3,192,2048]{2,1,0:T(8,128)(2,1)} %pad_maximum_fusion.1), channel_id=1, source_target_pairs={{0,1},{1,0},{2,5},{3,4},{4,3},{5,2},{6,7},{7,6},{8,9},{9,8},{10,13... | collective-permute-start | bytes 7077896 | tf_op jit(solution)/shard_map/weights_out/ppermute | solution.py:214
  66.5 2.3 select_d.1
  70.1 10.1 %collective-permute-done.wa_ref = bf16[3,192,2048]{2,1,0:T(8,128)(2,1)} collective-permute-done((bf16[3,192,2048]{2,1,0:T(8,128)(2,1)}, bf16[3,192,2048]{2,1,0:T(8,128)(2,1)}, u32[]{:S(2)}, u32[]{:S(2)}) %collective-permute-start) | collective-permute-done | bytes 2359328 | tf_op jit(solution)/shard_map/weights_out/ppermute | solution.py:214
  80.2 15.4 %all-to-all-done = bf16[32,16,2176]{2,1,0:T(8,128)(2,1)} async-done(((bf16[32,16,2176]{2,1,0:T(8,128)(2,1)}), bf16[32,16,2176]{2,1,0:T(8,128)(2,1)}, u32[]{:S(2)}, u32[]{:S(2)}) %all-to-all-start) | async-done | bytes 2228256 | tf_op jit(solution)/shard_map/select_x/all_to_all | solution.py:185
  95.7 4.1 %collective-permute-done.1.wb_ref = bf16[3,192,2048]{2,1,0:T(8,128)(2,1)S(1)} collective-permute-done((bf16[3,192,2048]{2,1,0:T(8,128)(2,1)}, bf16[3,192,2048]{2,1,0:T(8,128)(2,1)S(1)}, u32[]{:S(2)}, u32[]{:S(2)}) %collective-permute-start.1) | collective-permute-done | bytes 2359328 | tf_op jit(solution)/shard_map/weights_out/ppermute | solution.py:214
  101.1 6.5 %all-to-all-start.1 = ((bf16[16,128,512]{2,1,0:T(8,128)(2,1)}), bf16[16,128,512]{2,1,0:T(8,128)(2,1)}, u32[]{:S(2)}, u32[]{:S(2)}) async-start(bf16[16,128,512]{2,1,0:T(8,128)(2,1)} %copy-done.2), calls=%async_computation.1 | async-start | bytes 4194304 | tf_op jit(solution)/shard_map/gates/all_to_all | solution.py:228
  107.6 4.8 %gates.2 = (f32[3,512,384]{2,1,0:T(8,128)S(1)}, bf16[512,384]{1,0:T(8,128)(2,1)S(1)}) custom-call(bf16[512,2176]{1,0:T(8,128)(2,1)} %bitcast.8.x_ref.xo_ref, bf16[3,192,2048]{2,1,0:T(8,128)(2,1)} %collective-permute-done.wa_ref, bf16[3,192,2048]{2,1,0:T(8,128)(2,1)S(1)} %collective-permute-done.1.wb_ref), custom_call_target="tpu_custom_call" | custom-call | tf_op jit(solution)/shard_map/gates/gates/pallas_call | solution.py:238
  113.8 4.8 %gates.3 = (f32[3,512,384]{2,1,0:T(8,128)S(1)}, bf16[512,384]{1,0:T(8,128)(2,1)S(1)}) custom-call(bf16[512,2176]{1,0:T(8,128)(2,1)} %collective-permute-done.2.x_ref.xs_ref, bf16[3,192,2048]{2,1,0:T(8,128)(2,1)} %collective-permute-done.wa_ref, bf16[3,192,2048]{2,1,0:T(8,128)(2,1)S(1)} %collective-permute-done.1.wb_ref), custom_call_target="tpu_custom_call" | custom-call | tf_op jit(solution)/shard_map/gates/gates/pallas_call | solution.py:239
  120.8 20.2 %all-to-all-done.1.d_ref = bf16[16,128,512]{2,1,0:T(8,128)(2,1)} async-done(((bf16[16,128,512]{2,1,0:T(8,128)(2,1)}), bf16[16,128,512]{2,1,0:T(8,128)(2,1)}, u32[]{:S(2)}, u32[]{:S(2)}) %all-to-all-start.1) | async-done | bytes 2097184 | tf_op jit(solution)/shard_map/gates/all_to_all | solution.py:228
  142.1 4.0 %collective-permute-done.3.d_ref = bf16[16,128,512]{2,1,0:T(8,128)(2,1)S(1)} collective-permute-done((bf16[16,128,512]{2,1,0:T(8,128)(2,1)}, bf16[16,128,512]{2,1,0:T(8,128)(2,1)S(1)}, u32[]{:S(2)}, u32[]{:S(2)}) %collective-permute-start.3) | collective-permute-done | bytes 2097184 | tf_op jit(solution)/shard_map/expert/ppermute | solution.py:243
  147.8 5.9 %expert.3 = (bf16[512,2176]{1,0:T(8,128)(2,1)S(1)}, bf16[2,512,384]{2,1,0:T(8,128)(2,1)S(1)}) custom-call(s32[4]{0:T(128)S(1)} %pad_add_fusion.at_ref, f32[3,512,384]{2,1,0:T(8,128)S(1)} %copy-done.8, bf16[16,128,512]{2,1,0:T(8,128)(2,1)S(1)} %collective-permute-done.3.d_ref, bf16[3,192,2048]{2,1,0:T(8,128)(2,1)} %collective-permute-done.wa_ref, ...), custom_call_target="tpu_custom_call" | custom-call | tf_op jit(solution)/shard_map/expert/expert/pallas_call | solution.py:252
  154.4 5.8 %expert.2 = (bf16[512,2176]{1,0:T(8,128)(2,1)S(1)}, bf16[2,512,384]{2,1,0:T(8,128)(2,1)S(1)}) custom-call(s32[4]{0:T(128)S(1)} %pad_add_fusion.at_ref, f32[3,512,384]{2,1,0:T(8,128)S(1)} %copy-done.6, bf16[16,128,512]{2,1,0:T(8,128)(2,1)} %all-to-all-done.1.d_ref, bf16[3,192,2048]{2,1,0:T(8,128)(2,1)} %collective-permute-done.wa_ref, ...), custom_call_target="tpu_custom_call" | custom-call | tf_op jit(solution)/shard_map/expert/expert/pallas_call | solution.py:254
  160.2 1.9 add_convert_fusion
  162.1 7.8 %all-to-all-start.2 = ((bf16[32,16,2176]{2,1,0:T(8,128)(2,1)}), bf16[32,16,2176]{2,1,0:T(8,128)(2,1)S(1)}, u32[]{:S(2)}, u32[]{:S(2)}) async-start(bf16[32,16,2176]{2,1,0:T(8,128)(2,1)} %bitcast.22), calls=%async_computation.2 | async-start | bytes 4456448 | tf_op jit(solution)/shard_map/tokens_back/all_to_all | solution.py:185
  173.7 9.1 %weight_grads.1 = (bf16[3,192,2048]{2,1,0:T(8,128)(2,1)}, bf16[3,192,2048]{2,1,0:T(8,128)(2,1)}) custom-call(bf16[512,2176]{1,0:T(8,128)(2,1)} %bitcast.8.x_ref.xo_ref, bf16[512,2176]{1,0:T(8,128)(2,1)} %collective-permute-done.2.x_ref.xs_ref, bf16[4,4,128,512]{3,2,1,0:T(8,128)(2,1)} %bitcast.13.do_ref, bf16[4,4,128,512]{3,2,1,0:T(8,128)(2,1)S(1)} %bitcast.18, ...), custom_call_target="tpu_custom_call" | custom-call | tf_op jit(solution)/shard_map/weights_back/weight_grads/pallas_call | solution.py:263
  182.8 1.9 collective-permute-start.5
  186.0 35.6 %all-to-all-done.2 = bf16[32,16,2176]{2,1,0:T(8,128)(2,1)S(1)} async-done(((bf16[32,16,2176]{2,1,0:T(8,128)(2,1)}), bf16[32,16,2176]{2,1,0:T(8,128)(2,1)S(1)}, u32[]{:S(2)}, u32[]{:S(2)}) %all-to-all-start.2) | async-done | bytes 2228256 | tf_op jit(solution)/shard_map/tokens_back/all_to_all | solution.py:185
  223.5 3.5 %all-to-all-start.3 = ((bf16[4,144,512]{2,1,0:T(8,128)(2,1)}), bf16[4,144,512]{2,1,0:T(8,128)(2,1)S(1)}, u32[]{:S(2)}, u32[]{:S(2)}) async-start(bf16[4,144,512]{2,1,0:T(8,128)(2,1)} %combine.1), calls=%async_computation.3 | async-start | bytes 1179648 | tf_op jit(solution)/shard_map/tokens_back/all_to_all | solution.py:297
  227.0 16.1 %collective-permute-done.6.b_ref = bf16[3,192,2048]{2,1,0:T(8,128)(2,1)} collective-permute-done((bf16[3,192,2048]{2,1,0:T(8,128)(2,1)}, bf16[3,192,2048]{2,1,0:T(8,128)(2,1)}, u32[]{:S(2)}, u32[]{:S(2)}) %collective-permute-start.6) | collective-permute-done | bytes 2359328 | tf_op jit(solution)/shard_map/weights_back/ppermute | solution.py:285
  243.1 5.1 %place.1 = (bf16[2,192,2048]{2,1,0:T(8,128)(2,1)}, bf16[2,192,2048]{2,1,0:T(8,128)(2,1)}, bf16[2,192,2048]{2,1,0:T(8,128)(2,1)}) custom-call(s32[4]{0:T(128)S(1)} %pad_add_fusion.at_ref, bf16[3,192,2048]{2,1,0:T(8,128)(2,1)} %collective-permute-done.5.a_ref, bf16[3,192,2048]{2,1,0:T(8,128)(2,1)} %collective-permute-done.6.b_ref), custom_call_target="tpu_custom_call" | custom-call | tf_op jit(solution)/shard_map/place/place/pallas_call | solution.py:303
  (60 shorter events, 31.2 us)
Async XLA Ops:
  7.2 30.5 %copy-start = (bf16[2,192,2048]{2,1,0:T(8,128)(2,1)S(1)}, bf16[2,192,2048]{2,1,0:T(8,128)(2,1)}, u32[]{:S(2)}) copy-start(bf16[2,192,2048]{2,1,0:T(8,128)(2,1)} %param.11) | copy-start | bytes 4718596
  7.2 49.2 %all-gather.4.cloned.1.call-start = ((), (), s32[]{:S(2)}) async-start(), calls=%async_computation.4 | async-start | bytes 1327104 | tf_op jit(solution)/shard_map/gather_d/all_gather | solution.py:191
  26.4 69.3 %all-to-all-start = ((bf16[32,16,2176]{2,1,0:T(8,128)(2,1)}), bf16[32,16,2176]{2,1,0:T(8,128)(2,1)}, u32[]{:S(2)}, u32[]{:S(2)}) async-start(bf16[32,16,2176]{2,1,0:T(8,128)(2,1)} %bitcast.19), calls=%async_computation | async-start | bytes 4456448 | tf_op jit(solution)/shard_map/select_x/all_to_all | solution.py:185
  41.0 39.3 %collective-permute-start = (bf16[3,192,2048]{2,1,0:T(8,128)(2,1)}, bf16[3,192,2048]{2,1,0:T(8,128)(2,1)}, u32[]{:S(2)}, u32[]{:S(2)}) collective-permute-start(bf16[3,192,2048]{2,1,0:T(8,128)(2,1)} %pad_maximum_fusion), channel_id=1, source_target_pairs={{0,0},{1,1},{2,4},{3,5},{4,2},{5,3},{6,6},{7,7},{8,8},{9,9},{10,12... | collective-permute-start | bytes 7077896 | tf_op jit(solution)/shard_map/weights_out/ppermute | solution.py:214
  58.0 8.5 %copy-start.10 = (bf16[1152,512]{1,0:T(8,128)(2,1)S(1)}, bf16[1152,512]{1,0:T(8,128)(2,1)}, u32[]{:S(2)}) copy-start(bf16[1152,512]{1,0:T(8,128)(2,1)} %all-gather.4.cloned.1.call-done) | copy-start | bytes 3538948
  59.7 40.0 %collective-permute-start.1 = (bf16[3,192,2048]{2,1,0:T(8,128)(2,1)}, bf16[3,192,2048]{2,1,0:T(8,128)(2,1)S(1)}, u32[]{:S(2)}, u32[]{:S(2)}) collective-permute-start(bf16[3,192,2048]{2,1,0:T(8,128)(2,1)} %pad_maximum_fusion.1), channel_id=1, source_target_pairs={{0,1},{1,0},{2,5},{3,4},{4,3},{5,2},{6,7},{7,6},{8,9},{9,8},{10,13... | collective-permute-start | bytes 7077896 | tf_op jit(solution)/shard_map/weights_out/ppermute | solution.py:214
  68.7 1.4 copy-start.2
  99.8 14.0 %collective-permute-start.2 = (bf16[512,2176]{1,0:T(8,128)(2,1)}, bf16[512,2176]{1,0:T(8,128)(2,1)}, u32[]{:S(2)}, u32[]{:S(2)}) collective-permute-start(bf16[512,2176]{1,0:T(8,128)(2,1)} %bitcast.8.x_ref.xo_ref), channel_id=1, source_target_pairs={{0,4},{4,0},{1,5},{5,1},{2,6},{6,2},{3,7},{7,3},{8,12},{12,8},{9,1... | collective-permute-start | bytes 6684680 | tf_op jit(solution)/shard_map/gates/ppermute | solution.py:229
  101.1 40.0 %all-to-all-start.1 = ((bf16[16,128,512]{2,1,0:T(8,128)(2,1)}), bf16[16,128,512]{2,1,0:T(8,128)(2,1)}, u32[]{:S(2)}, u32[]{:S(2)}) async-start(bf16[16,128,512]{2,1,0:T(8,128)(2,1)} %copy-done.2), calls=%async_computation.1 | async-start | bytes 4194304 | tf_op jit(solution)/shard_map/gates/all_to_all | solution.py:228
  112.4 1.4 copy-start.5
  118.6 1.4 copy-start.7
  141.0 13.3 %copy-start.6 = (f32[3,512,384]{2,1,0:T(8,128)S(1)}, f32[3,512,384]{2,1,0:T(8,128)}, u32[]{:S(2)}) copy-start(f32[3,512,384]{2,1,0:T(8,128)} %copy-done.5) | copy-start | bytes 7077892
  141.0 5.1 %collective-permute-start.3 = (bf16[16,128,512]{2,1,0:T(8,128)(2,1)}, bf16[16,128,512]{2,1,0:T(8,128)(2,1)S(1)}, u32[]{:S(2)}, u32[]{:S(2)}) collective-permute-start(bf16[16,128,512]{2,1,0:T(8,128)(2,1)} %all-to-all-done.1.d_ref), channel_id=1, source_target_pairs={{0,4},{4,0},{1,5},{5,1},{2,6},{6,2},{3,7},{7,3},{8,12},{12,8},{9,1... | collective-permute-start | bytes 6291464 | tf_op jit(solution)/shard_map/expert/ppermute | solution.py:243
  146.1 1.7 copy-start.8
  147.8 5.9 %copy-start.3 = (bf16[16,128,512]{2,1,0:T(8,128)(2,1)}, bf16[16,128,512]{2,1,0:T(8,128)(2,1)S(1)}, u32[]{:S(2)}) copy-start(bf16[16,128,512]{2,1,0:T(8,128)(2,1)S(1)} %collective-permute-done.3.d_ref) | copy-start | bytes 6291460
  153.7 6.5 %collective-permute-start.4 = (bf16[512,2176]{1,0:T(8,128)(2,1)S(1)}, bf16[512,2176]{1,0:T(8,128)(2,1)S(1)}, u32[]{:S(2)}, u32[]{:S(2)}) collective-permute-start(bf16[512,2176]{1,0:T(8,128)(2,1)S(1)} %get-tuple-element.58), channel_id=1, source_target_pairs={{0,4},{4,0},{1,5},{5,1},{2,6},{6,2},{3,7},{7,3},{8,12},{12,8},{9,1... | collective-permute-start | bytes 6684680 | tf_op jit(solution)/shard_map/expert/ppermute | solution.py:253
  160.2 2.0 copy-start.11
  162.1 59.5 %all-to-all-start.2 = ((bf16[32,16,2176]{2,1,0:T(8,128)(2,1)}), bf16[32,16,2176]{2,1,0:T(8,128)(2,1)S(1)}, u32[]{:S(2)}, u32[]{:S(2)}) async-start(bf16[32,16,2176]{2,1,0:T(8,128)(2,1)} %bitcast.22), calls=%async_computation.2 | async-start | bytes 4456448 | tf_op jit(solution)/shard_map/tokens_back/all_to_all | solution.py:185
  169.9 1.6 copy-start.4
  173.6 48.0 %copy-start.16 = (bf16[512,128]{1,0:T(8,128)(2,1)S(1)}, bf16[512,128]{1,0:T(8,128)(2,1)}, u32[]{:S(2)}) copy-start(bf16[512,128]{1,0:T(8,128)(2,1)} %copy-done.15) | copy-start | bytes 393220
  182.8 44.2 %collective-permute-start.5 = (bf16[3,192,2048]{2,1,0:T(8,128)(2,1)}, bf16[3,192,2048]{2,1,0:T(8,128)(2,1)}, u32[]{:S(2)}, u32[]{:S(2)}) collective-permute-start(bf16[3,192,2048]{2,1,0:T(8,128)(2,1)} %get-tuple-element.66), channel_id=1, source_target_pairs={{0,0},{1,1},{4,2},{5,3},{2,4},{3,5},{6,6},{7,7},{8,8},{9,9},{12,10... | collective-permute-start | bytes 7077896 | tf_op jit(solution)/shard_map/weights_back/ppermute | solution.py:285
  184.7 58.3 %collective-permute-start.6 = (bf16[3,192,2048]{2,1,0:T(8,128)(2,1)}, bf16[3,192,2048]{2,1,0:T(8,128)(2,1)}, u32[]{:S(2)}, u32[]{:S(2)}) collective-permute-start(bf16[3,192,2048]{2,1,0:T(8,128)(2,1)} %get-tuple-element.67), channel_id=1, source_target_pairs={{1,0},{0,1},{5,2},{4,3},{3,4},{2,5},{7,6},{6,7},{9,8},{8,9},{13,10... | collective-permute-start | bytes 7077896 | tf_op jit(solution)/shard_map/weights_back/ppermute | solution.py:285
  223.5 24.7 %all-to-all-start.3 = ((bf16[4,144,512]{2,1,0:T(8,128)(2,1)}), bf16[4,144,512]{2,1,0:T(8,128)(2,1)S(1)}, u32[]{:S(2)}, u32[]{:S(2)}) async-start(bf16[4,144,512]{2,1,0:T(8,128)(2,1)} %combine.1), calls=%async_computation.3 | async-start | bytes 1179648 | tf_op jit(solution)/shard_map/tokens_back/all_to_all | solution.py:297
  243.1 6.6 %copy-start.1 = (bf16[2,192,2048]{2,1,0:T(8,128)(2,1)S(1)}, bf16[2,192,2048]{2,1,0:T(8,128)(2,1)}, u32[]{:S(2)}) copy-start(bf16[2,192,2048]{2,1,0:T(8,128)(2,1)} %param.11) | copy-start | bytes 4718596
  (5 other events, 4.9 us)
Sparse Core Ops, SparseCore 0:
  10.4 45.9 all-gather.3

commit v7 on v4

--- a/solution.py
+++ b/solution.py
@@ -22,7 +22,7 @@
 SMEM = pl.BlockSpec(memory_space=pltpu.SMEM)
 
 
-def params(mib=32):
+def params(mib=20):
     return pltpu.CompilerParams(vmem_limit_bytes=mib * 1024 * 1024)
 
 
@@ -184,6 +184,16 @@
     with jax.named_scope("select_d"):
         pick, cotangent = lax.optimization_barrier((pick, cotangent))
         dg = lax.all_gather(cotangent, "x", axis=0, tiled=False)
+
+    with jax.named_scope("weights_out"):
+        dg, *mats = lax.optimization_barrier((dg, w_gate, w_up, w_down))
+        weights = []
+        for m in range(2):
+            k = (ix + m) % 2
+            piece = jnp.stack([lax.dynamic_index_in_dim(w, k, 0, keepdims=False) for w in mats])
+            weights.append(lax.ppermute(piece, ("c", "x"), weight_pairs(m)))
+
+    with jax.named_scope("select_d"):
         ds = pl.pallas_call(
             select_d,
             out_shape=shape((ROWS, D), BF),
@@ -193,16 +203,8 @@
             name="select_d",
         )(pick, dg)
 
-    with jax.named_scope("weights_out"):
-        pick, *mats = lax.optimization_barrier((pick, w_gate, w_up, w_down))
-        weights = []
-        for m in range(2):
-            k = (ix + m) % 2
-            piece = jnp.stack([lax.dynamic_index_in_dim(w, k, 0, keepdims=False) for w in mats])
-            weights.append(lax.ppermute(piece, ("c", "x"), weight_pairs(m)))
-
     with jax.named_scope("gates"):
-        x_own, ds, *weights = lax.optimization_barrier((x_own, ds, *weights))
+        x_own, ds, weights[0] = lax.optimization_barrier((x_own, ds, weights[0]))
         d_own = to_experts(ds)
         x_sib = lax.ppermute(x_own, "c", sib)
         ahead = pl.pallas_call(
@@ -245,7 +247,7 @@
             in_specs=[cut] * 4 + [h_spec, h_spec, k_spec, k_spec],
             out_specs=(o_spec, o_spec),
             scratch_shapes=[pltpu.VMEM((3, FH, 2 * ROWS), BF)],
-            compiler_params=params(),
+            compiler_params=params(60),
             name="weight_grads",
         )(x_own, x_sib, d_own, d_sib, hid_own, hid_sib, keep_own, keep_sib)
         back = []

time: 270 us -> 243 us (0.900)
  blocking collectives: 70.2 us -> 22.8 us
  waiting for transfers between devices: 82.9 us -> 109 us
  local copies, waits for them, and re-layouts: 21.4 us -> 14.2 us
    ppermute x2, waiting for transfers between devices: 0.01 us -> 51.8 us  [per_device(): weights.append(lax.ppermute(piece, ('c', 'x'), weight_pairs(m)))]
    all_gather x1, blocking collectives: 57.7 us -> 10.3 us  [per_device(): dg = lax.all_gather(cotangent, 'x', axis=0, tiled=False)]
    all_to_all x3, waiting for transfers between devices: 61.5 us -> 39.7 us  [to_experts(): lax.all_to_all(rows, ('y', 'z'), split_axis=0, concat_axis=0, tiled=True)]
    unnamed x46 -> x36, local copies, waits for them, and re-layouts: 20.8 us -> 11.7 us
    ppermute x2, starting transfers between devices: 7.24 us -> 13.8 us  [per_device(): weights.append(lax.ppermute(piece, ('c', 'x'), weight_pairs(m)))]
    ppermute x2, waiting for transfers between devices: 17.3 us -> 13.5 us  [per_device(): back.append(lax.ppermute(g, ('c', 'x'), inverse))]
    ppermute x1, starting transfers between devices: 2.98 us -> 0.01 us  [per_device(): x_sib = lax.ppermute(x_own, 'c', sib)]
  transfers between devices with their start and end apart: 11 -> 11, of which waited for: 4 -> 7; matrix products, arithmetic and copies ran while one was open for 0% -> 2% of each run, Pallas kernels for 11% -> 13%
where the time goes in v7:
time: 243 us; the launch traced here: 241 us
  waiting for transfers between devices  109 us (45%)
  starting transfers between devices  50.2 us (21%)
  Pallas kernels  37.1 us (15%)
  blocking collectives  22.8 us (9%)
  local copies, waits for them, and re-layouts  14.2 us (6%)
  other arithmetic  6.77 us (3%)
    ppermute x2, waiting for transfers between devices, per_device(): weights.append(lax.ppermute(piece, ('c', 'x'), weight_pairs(m)))  51.8 us
    all_to_all x3, waiting for transfers between devices, to_experts(): lax.all_to_all(rows, ('y', 'z'), split_axis=0, concat_axis=0, tiled=True)  39.7 us
    all_to_all x3, starting transfers between devices, to_experts(): lax.all_to_all(rows, ('y', 'z'), split_axis=0, concat_axis=0, tiled=True)  24.2 us
    ppermute x2, starting transfers between devices, per_device(): weights.append(lax.ppermute(piece, ('c', 'x'), weight_pairs(m)))  13.8 us
    ppermute x2, waiting for transfers between devices, per_device(): back.append(lax.ppermute(g, ('c', 'x'), inverse))  13.5 us
    all_gather x1, blocking collectives, per_device(): xg = lax.all_gather(tokens, 'x', axis=0, tiled=False)  12.5 us
    unnamed x36, local copies, waits for them, and re-layouts  11.7 us
    all_gather x1, blocking collectives, per_device(): dg = lax.all_gather(cotangent, 'x', axis=0, tiled=False)  10.3 us
  transfers between devices with their start and end apart: 11, of which 7 were waited for; matrix products, arithmetic and copies ran while one was open for 2% of the time, Pallas kernels for 13%

profile of v7, /device:TPU:1, one launch (start us, length us, event | category | flops | bytes accessed | tf_op | source)
XLA Modules:
  0.0 241.1 jit_solution(5556930673732557193)
XLA Ops:
  2.0 12.5 %all-gather = bf16[512,512]{1,0:T(8,128)(2,1)S(1)} all-gather(bf16[128,512]{1,0:T(8,128)(2,1)} %param.7), channel_id=2, replica_groups=mesh['y'=4,'z'=8,'c'=2,'x'=4] {'x'}, dimensions={0}, use_global_device_ids=true | all-gather | bytes 655360 | tf_op jit(solution)/shard_map/select_x/all_gather | solution.py:172
  14.6 2.8 %select_x.1 = (bf16[512,2176]{1,0:T(8,128)(2,1)}, bf16[512,128]{1,0:T(8,128)(2,1)S(1)}) custom-call(s32[4]{0:T(128)S(1)} %pad_add_fusion.at_ref, f32[16,128]{1,0:T(8,128)S(1)} %pad_maximum_fusion.2.table_ref, bf16[4,128,512]{2,1,0:T(8,128)(2,1)S(1)} %bitcast.20), custom_call_target="tpu_custom_call" | custom-call | tf_op jit(solution)/shard_map/select_x/select_x/pallas_call | solution.py:174
  17.4 11.5 %all-to-all-start = ((bf16[32,16,2176]{2,1,0:T(8,128)(2,1)}), bf16[32,16,2176]{2,1,0:T(8,128)(2,1)}, u32[]{:S(2)}, u32[]{:S(2)}) async-start(bf16[32,16,2176]{2,1,0:T(8,128)(2,1)} %bitcast.7), calls=%async_computation | async-start | bytes 4456448 | tf_op jit(solution)/shard_map/select_x/all_to_all | solution.py:168
  28.9 10.3 %all-gather.1 = bf16[512,512]{1,0:T(8,128)(2,1)S(1)} all-gather(bf16[128,512]{1,0:T(8,128)(2,1)S(1)} %copy-done.17), channel_id=3, replica_groups=mesh['y'=4,'z'=8,'c'=2,'x'=4] {'x'}, dimensions={0}, use_global_device_ids=true | all-gather | bytes 655360 | tf_op jit(solution)/shard_map/select_d/all_gather | solution.py:186
  43.1 8.1 %collective-permute-start = (bf16[3,192,2048]{2,1,0:T(8,128)(2,1)S(1)}, bf16[3,192,2048]{2,1,0:T(8,128)(2,1)S(1)}, u32[]{:S(2)}, u32[]{:S(2)}) collective-permute-start(bf16[3,192,2048]{2,1,0:T(8,128)(2,1)S(1)} %pad_maximum_fusion), channel_id=1, source_target_pairs={{0,0},{1,1},{2,4},{3,5},{4,2},{5,3},{6,6},{7,7},{8,8},{9,9},{10,12... | collective-permute-start | bytes 7077896 | tf_op jit(solution)/shard_map/weights_out/ppermute | solution.py:194
  53.2 24.9 %collective-permute-done.wa_ref = bf16[3,192,2048]{2,1,0:T(8,128)(2,1)S(1)} collective-permute-done((bf16[3,192,2048]{2,1,0:T(8,128)(2,1)S(1)}, bf16[3,192,2048]{2,1,0:T(8,128)(2,1)S(1)}, u32[]{:S(2)}, u32[]{:S(2)}) %collective-permute-start) | collective-permute-done | bytes 2359328 | tf_op jit(solution)/shard_map/weights_out/ppermute | solution.py:194
  78.1 2.1 all-to-all-done
  80.3 7.1 %all-to-all-start.1 = ((bf16[32,16,2048]{2,1,0:T(8,128)(2,1)}), bf16[32,16,2048]{2,1,0:T(8,128)(2,1)}, u32[]{:S(2)}, u32[]{:S(2)}) async-start(bf16[32,16,2048]{2,1,0:T(8,128)(2,1)} %bitcast.19), calls=%async_computation.1 | async-start | bytes 4194304 | tf_op jit(solution)/shard_map/gates/all_to_all | solution.py:168
  89.0 5.6 %collective-permute-start.1 = (bf16[3,192,2048]{2,1,0:T(8,128)(2,1)S(1)}, bf16[3,192,2048]{2,1,0:T(8,128)(2,1)S(1)}, u32[]{:S(2)}, u32[]{:S(2)}) collective-permute-start(bf16[3,192,2048]{2,1,0:T(8,128)(2,1)S(1)} %pad_maximum_fusion.1), channel_id=1, source_target_pairs={{0,1},{1,0},{2,5},{3,4},{4,3},{5,2},{6,7},{7,6},{8,9},{9,8},{10,13... | collective-permute-start | bytes 7077896 | tf_op jit(solution)/shard_map/weights_out/ppermute | solution.py:194
  94.7 26.9 %collective-permute-done.1.wb_ref = bf16[3,192,2048]{2,1,0:T(8,128)(2,1)S(1)} collective-permute-done((bf16[3,192,2048]{2,1,0:T(8,128)(2,1)S(1)}, bf16[3,192,2048]{2,1,0:T(8,128)(2,1)S(1)}, u32[]{:S(2)}, u32[]{:S(2)}) %collective-permute-start.1) | collective-permute-done | bytes 2359328 | tf_op jit(solution)/shard_map/weights_out/ppermute | solution.py:194
  121.6 5.0 %gates.2 = (f32[3,512,384]{2,1,0:T(8,128)S(1)}, bf16[512,384]{1,0:T(8,128)(2,1)S(1)}) custom-call(bf16[512,2176]{1,0:T(8,128)(2,1)} %bitcast.8.x_ref.xo_ref, bf16[3,192,2048]{2,1,0:T(8,128)(2,1)S(1)} %collective-permute-done.wa_ref, bf16[3,192,2048]{2,1,0:T(8,128)(2,1)S(1)} %collective-permute-done.1.wb_ref), custom_call_target="tpu_custom_call" | custom-call | tf_op jit(solution)/shard_map/gates/gates/pallas_call | solution.py:218
  128.1 2.5 %gates.3 = (f32[3,512,384]{2,1,0:T(8,128)S(1)}, bf16[512,384]{1,0:T(8,128)(2,1)S(1)}) custom-call(bf16[512,2176]{1,0:T(8,128)(2,1)S(1)} %collective-permute-done.2.x_ref.xs_ref, bf16[3,192,2048]{2,1,0:T(8,128)(2,1)S(1)} %collective-permute-done.wa_ref, bf16[3,192,2048]{2,1,0:T(8,128)(2,1)S(1)} %collective-permute-done.1.wb_ref), custom_call_target="tpu_custom_call" | custom-call | tf_op jit(solution)/shard_map/gates/gates/pallas_call | solution.py:219
  134.1 2.5 %all-to-all-done.1 = bf16[32,16,2048]{2,1,0:T(8,128)(2,1)} async-done(((bf16[32,16,2048]{2,1,0:T(8,128)(2,1)}), bf16[32,16,2048]{2,1,0:T(8,128)(2,1)}, u32[]{:S(2)}, u32[]{:S(2)}) %all-to-all-start.1) | async-done | bytes 2097184 | tf_op jit(solution)/shard_map/gates/all_to_all | solution.py:168
  138.6 4.0 %collective-permute-done.3.d_ref.ds_ref = bf16[512,2048]{1,0:T(8,128)(2,1)S(1)} collective-permute-done((bf16[512,2048]{1,0:T(8,128)(2,1)}, bf16[512,2048]{1,0:T(8,128)(2,1)S(1)}, u32[]{:S(2)}, u32[]{:S(2)}) %collective-permute-start.3) | collective-permute-done | bytes 2097184 | tf_op jit(solution)/shard_map/expert/ppermute | solution.py:223
  145.9 4.0 %expert.3 = (bf16[512,2176]{1,0:T(8,128)(2,1)S(1)}, bf16[2,512,384]{2,1,0:T(8,128)(2,1)S(1)}) custom-call(s32[4]{0:T(128)S(1)} %pad_add_fusion.at_ref, f32[3,512,384]{2,1,0:T(8,128)S(1)} %copy-done.8, bf16[512,2048]{1,0:T(8,128)(2,1)S(1)} %collective-permute-done.3.d_ref.ds_ref, bf16[3,192,2048]{2,1,0:T(8,128)(2,1)S(1)} %collective-permute-done.wa_ref, ...), custom_call_target="tpu_custom_call" | custom-call | tf_op jit(solution)/shard_map/expert/expert/pallas_call | solution.py:232
  151.2 5.1 %expert.2 = (bf16[512,2176]{1,0:T(8,128)(2,1)S(1)}, bf16[2,512,384]{2,1,0:T(8,128)(2,1)S(1)}) custom-call(s32[4]{0:T(128)S(1)} %pad_add_fusion.at_ref, f32[3,512,384]{2,1,0:T(8,128)S(1)} %copy-done.6, bf16[512,2048]{1,0:T(8,128)(2,1)} %bitcast.11.d_ref.do_ref, bf16[3,192,2048]{2,1,0:T(8,128)(2,1)S(1)} %collective-permute-done.wa_ref, ...), custom_call_target="tpu_custom_call" | custom-call | tf_op jit(solution)/shard_map/expert/expert/pallas_call | solution.py:234
  156.3 2.0 add_convert_fusion
  158.2 5.7 %all-to-all-start.2 = ((bf16[32,16,2176]{2,1,0:T(8,128)(2,1)}), bf16[32,16,2176]{2,1,0:T(8,128)(2,1)S(1)}, u32[]{:S(2)}, u32[]{:S(2)}) async-start(bf16[32,16,2176]{2,1,0:T(8,128)(2,1)} %bitcast.22), calls=%async_computation.2 | async-start | bytes 4456448 | tf_op jit(solution)/shard_map/tokens_back/all_to_all | solution.py:168
  163.9 10.2 %weight_grads.1 = (bf16[3,192,2048]{2,1,0:T(8,128)(2,1)}, bf16[3,192,2048]{2,1,0:T(8,128)(2,1)}) custom-call(bf16[512,2176]{1,0:T(8,128)(2,1)} %bitcast.8.x_ref.xo_ref, bf16[512,2176]{1,0:T(8,128)(2,1)} %copy-done.2, bf16[512,2048]{1,0:T(8,128)(2,1)} %bitcast.11.d_ref.do_ref, bf16[512,2048]{1,0:T(8,128)(2,1)} %copy-done.4, bf16[512,384]{1,0:T(8,128)(2,1)} %copy-done.11, ...), custom_call_target="tpu_custom_call" | custom-call | tf_op jit(solution)/shard_map/weights_back/weight_grads/pallas_call | solution.py:243
  176.1 4.5 %collective-permute-start.6 = (bf16[3,192,2048]{2,1,0:T(8,128)(2,1)}, bf16[3,192,2048]{2,1,0:T(8,128)(2,1)}, u32[]{:S(2)}, u32[]{:S(2)}) collective-permute-start(bf16[3,192,2048]{2,1,0:T(8,128)(2,1)} %get-tuple-element.61), channel_id=1, source_target_pairs={{1,0},{0,1},{5,2},{4,3},{3,4},{2,5},{7,6},{6,7},{9,8},{8,9},{13,10... | collective-permute-start | bytes 7077896 | tf_op jit(solution)/shard_map/weights_back/ppermute | solution.py:256
  180.6 35.0 %all-to-all-done.2 = bf16[32,16,2176]{2,1,0:T(8,128)(2,1)S(1)} async-done(((bf16[32,16,2176]{2,1,0:T(8,128)(2,1)}), bf16[32,16,2176]{2,1,0:T(8,128)(2,1)S(1)}, u32[]{:S(2)}, u32[]{:S(2)}) %all-to-all-start.2) | async-done | bytes 2228256 | tf_op jit(solution)/shard_map/tokens_back/all_to_all | solution.py:168
  217.5 3.5 %all-to-all-start.3 = ((bf16[4,144,512]{2,1,0:T(8,128)(2,1)}), bf16[4,144,512]{2,1,0:T(8,128)(2,1)S(1)}, u32[]{:S(2)}, u32[]{:S(2)}) async-start(bf16[4,144,512]{2,1,0:T(8,128)(2,1)} %combine.1), calls=%async_computation.3 | async-start | bytes 1179648 | tf_op jit(solution)/shard_map/tokens_back/all_to_all | solution.py:278
  221.0 13.5 %collective-permute-done.6.b_ref = bf16[3,192,2048]{2,1,0:T(8,128)(2,1)} collective-permute-done((bf16[3,192,2048]{2,1,0:T(8,128)(2,1)}, bf16[3,192,2048]{2,1,0:T(8,128)(2,1)}, u32[]{:S(2)}, u32[]{:S(2)}) %collective-permute-start.6) | collective-permute-done | bytes 2359328 | tf_op jit(solution)/shard_map/weights_back/ppermute | solution.py:256
  234.6 5.0 %place.1 = (bf16[2,192,2048]{2,1,0:T(8,128)(2,1)}, bf16[2,192,2048]{2,1,0:T(8,128)(2,1)}, bf16[2,192,2048]{2,1,0:T(8,128)(2,1)}) custom-call(s32[4]{0:T(128)S(1)} %pad_add_fusion.at_ref, bf16[3,192,2048]{2,1,0:T(8,128)(2,1)} %collective-permute-done.5.a_ref, bf16[3,192,2048]{2,1,0:T(8,128)(2,1)} %collective-permute-done.6.b_ref), custom_call_target="tpu_custom_call" | custom-call | tf_op jit(solution)/shard_map/weights_back/place/pallas_call | solution.py:258
  (58 shorter events, 25.8 us)
Async XLA Ops:
  17.4 11.5 %copy-start.17 = (bf16[128,512]{1,0:T(8,128)(2,1)S(1)}, bf16[128,512]{1,0:T(8,128)(2,1)}, u32[]{:S(2)}) copy-start(bf16[128,512]{1,0:T(8,128)(2,1)} %param.8) | copy-start | bytes 393220
  17.4 21.8 %copy-start.14 = (bf16[2,192,2048]{2,1,0:T(8,128)(2,1)S(1)}, bf16[2,192,2048]{2,1,0:T(8,128)(2,1)}, u32[]{:S(2)}) copy-start(bf16[2,192,2048]{2,1,0:T(8,128)(2,1)} %param.11) | copy-start | bytes 4718596
  17.4 62.8 %all-to-all-start = ((bf16[32,16,2176]{2,1,0:T(8,128)(2,1)}), bf16[32,16,2176]{2,1,0:T(8,128)(2,1)}, u32[]{:S(2)}, u32[]{:S(2)}) async-start(bf16[32,16,2176]{2,1,0:T(8,128)(2,1)} %bitcast.7), calls=%async_computation | async-start | bytes 4456448 | tf_op jit(solution)/shard_map/select_x/all_to_all | solution.py:168
  39.2 1.7 copy-start.15
  39.2 2.2 copy-start.16
  43.1 35.0 %collective-permute-start = (bf16[3,192,2048]{2,1,0:T(8,128)(2,1)S(1)}, bf16[3,192,2048]{2,1,0:T(8,128)(2,1)S(1)}, u32[]{:S(2)}, u32[]{:S(2)}) collective-permute-start(bf16[3,192,2048]{2,1,0:T(8,128)(2,1)S(1)} %pad_maximum_fusion), channel_id=1, source_target_pairs={{0,0},{1,1},{2,4},{3,5},{4,2},{5,3},{6,6},{7,7},{8,8},{9,9},{10,12... | collective-permute-start | bytes 7077896 | tf_op jit(solution)/shard_map/weights_out/ppermute | solution.py:194
  53.2 34.2 %copy-start.13 = (bf16[1,192,2048]{2,1,0:T(8,128)(2,1)S(1)}, bf16[1,192,2048]{2,1,0:T(8,128)(2,1)}, u32[]{:S(2)}) copy-start(bf16[1,192,2048]{2,1,0:T(8,128)(2,1)} %get-tuple-element.65) | copy-start | bytes 2359300
  80.3 56.4 %all-to-all-start.1 = ((bf16[32,16,2048]{2,1,0:T(8,128)(2,1)}), bf16[32,16,2048]{2,1,0:T(8,128)(2,1)}, u32[]{:S(2)}, u32[]{:S(2)}) async-start(bf16[32,16,2048]{2,1,0:T(8,128)(2,1)} %bitcast.19), calls=%async_computation.1 | async-start | bytes 4194304 | tf_op jit(solution)/shard_map/gates/all_to_all | solution.py:168
  89.0 32.6 %collective-permute-start.1 = (bf16[3,192,2048]{2,1,0:T(8,128)(2,1)S(1)}, bf16[3,192,2048]{2,1,0:T(8,128)(2,1)S(1)}, u32[]{:S(2)}, u32[]{:S(2)}) collective-permute-start(bf16[3,192,2048]{2,1,0:T(8,128)(2,1)S(1)} %pad_maximum_fusion.1), channel_id=1, source_target_pairs={{0,1},{1,0},{2,5},{3,4},{4,3},{5,2},{6,7},{7,6},{8,9},{9,8},{10,13... | collective-permute-start | bytes 7077896 | tf_op jit(solution)/shard_map/weights_out/ppermute | solution.py:194
  94.7 33.4 %collective-permute-start.2 = (bf16[512,2176]{1,0:T(8,128)(2,1)}, bf16[512,2176]{1,0:T(8,128)(2,1)S(1)}, u32[]{:S(2)}, u32[]{:S(2)}) collective-permute-start(bf16[512,2176]{1,0:T(8,128)(2,1)} %bitcast.8.x_ref.xo_ref), channel_id=1, source_target_pairs={{0,4},{4,0},{1,5},{5,1},{2,6},{6,2},{3,7},{7,3},{8,12},{12,8},{9,1... | collective-permute-start | bytes 6684680 | tf_op jit(solution)/shard_map/gates/ppermute | solution.py:209
  121.6 6.5 %copy-start = (bf16[3,192,2048]{2,1,0:T(8,128)(2,1)}, bf16[3,192,2048]{2,1,0:T(8,128)(2,1)S(1)}, u32[]{:S(2)}) copy-start(bf16[3,192,2048]{2,1,0:T(8,128)(2,1)S(1)} %collective-permute-done.1.wb_ref) | copy-start | bytes 7077892
  126.6 1.5 copy-start.5
  128.1 2.5 %copy-start.11 = (bf16[512,384]{1,0:T(8,128)(2,1)}, bf16[512,384]{1,0:T(8,128)(2,1)S(1)}, u32[]{:S(2)}) copy-start(bf16[512,384]{1,0:T(8,128)(2,1)S(1)} %get-tuple-element.56.ho_ref) | copy-start | bytes 1179652
  136.7 5.9 %collective-permute-start.3 = (bf16[512,2048]{1,0:T(8,128)(2,1)}, bf16[512,2048]{1,0:T(8,128)(2,1)S(1)}, u32[]{:S(2)}, u32[]{:S(2)}) collective-permute-start(bf16[512,2048]{1,0:T(8,128)(2,1)} %bitcast.11.d_ref.do_ref), channel_id=1, source_target_pairs={{0,4},{4,0},{1,5},{5,1},{2,6},{6,2},{3,7},{7,3},{8,12},{12,8},{9,1... | collective-permute-start | bytes 6291464 | tf_op jit(solution)/shard_map/expert/ppermute | solution.py:223
  142.6 1.7 copy-start.1
  144.2 1.7 copy-start.8
  145.9 4.0 %copy-start.4 = (bf16[512,2048]{1,0:T(8,128)(2,1)}, bf16[512,2048]{1,0:T(8,128)(2,1)S(1)}, u32[]{:S(2)}) copy-start(bf16[512,2048]{1,0:T(8,128)(2,1)S(1)} %collective-permute-done.3.d_ref.ds_ref) | copy-start | bytes 6291460
  145.9 5.3 %copy-start.6 = (f32[3,512,384]{2,1,0:T(8,128)S(1)}, f32[3,512,384]{2,1,0:T(8,128)}, u32[]{:S(2)}) copy-start(f32[3,512,384]{2,1,0:T(8,128)} %copy-done.5) | copy-start | bytes 7077892
  150.8 5.5 %collective-permute-start.4 = (bf16[512,2176]{1,0:T(8,128)(2,1)S(1)}, bf16[512,2176]{1,0:T(8,128)(2,1)S(1)}, u32[]{:S(2)}, u32[]{:S(2)}) collective-permute-start(bf16[512,2176]{1,0:T(8,128)(2,1)S(1)} %get-tuple-element.52), channel_id=1, source_target_pairs={{0,4},{4,0},{1,5},{5,1},{2,6},{6,2},{3,7},{7,3},{8,12},{12,8},{9,1... | collective-permute-start | bytes 6684680 | tf_op jit(solution)/shard_map/expert/ppermute | solution.py:233
  156.3 2.0 copy-start.10
  158.2 57.4 %all-to-all-start.2 = ((bf16[32,16,2176]{2,1,0:T(8,128)(2,1)}), bf16[32,16,2176]{2,1,0:T(8,128)(2,1)S(1)}, u32[]{:S(2)}, u32[]{:S(2)}) async-start(bf16[32,16,2176]{2,1,0:T(8,128)(2,1)} %bitcast.22), calls=%async_computation.2 | async-start | bytes 4456448 | tf_op jit(solution)/shard_map/tokens_back/all_to_all | solution.py:168
  174.1 46.9 %collective-permute-start.5 = (bf16[3,192,2048]{2,1,0:T(8,128)(2,1)}, bf16[3,192,2048]{2,1,0:T(8,128)(2,1)}, u32[]{:S(2)}, u32[]{:S(2)}) collective-permute-start(bf16[3,192,2048]{2,1,0:T(8,128)(2,1)} %get-tuple-element.60), channel_id=1, source_target_pairs={{0,0},{1,1},{4,2},{5,3},{2,4},{3,5},{6,6},{7,7},{8,8},{9,9},{12,10... | collective-permute-start | bytes 7077896 | tf_op jit(solution)/shard_map/weights_back/ppermute | solution.py:256
  176.1 58.5 %collective-permute-start.6 = (bf16[3,192,2048]{2,1,0:T(8,128)(2,1)}, bf16[3,192,2048]{2,1,0:T(8,128)(2,1)}, u32[]{:S(2)}, u32[]{:S(2)}) collective-permute-start(bf16[3,192,2048]{2,1,0:T(8,128)(2,1)} %get-tuple-element.61), channel_id=1, source_target_pairs={{1,0},{0,1},{5,2},{4,3},{3,4},{2,5},{7,6},{6,7},{9,8},{8,9},{13,10... | collective-permute-start | bytes 7077896 | tf_op jit(solution)/shard_map/weights_back/ppermute | solution.py:256
  217.5 22.0 %all-to-all-start.3 = ((bf16[4,144,512]{2,1,0:T(8,128)(2,1)}), bf16[4,144,512]{2,1,0:T(8,128)(2,1)S(1)}, u32[]{:S(2)}, u32[]{:S(2)}) async-start(bf16[4,144,512]{2,1,0:T(8,128)(2,1)} %combine.1), calls=%async_computation.3 | async-start | bytes 1179648 | tf_op jit(solution)/shard_map/tokens_back/all_to_all | solution.py:278
  (5 other events, 5.8 us)

commit v8 on v7

--- a/solution.py
+++ b/solution.py
@@ -98,8 +98,8 @@
     keep_ref[...] = (weight * hidden).astype(BF)
 
 
-def expert(at_ref, pre_ref, d_ref, wa_ref, wb_ref, part_ref, keep_ref):
-    raw = project(d_ref, wa_ref, wb_ref, 2)
+def expert(at_ref, pre_ref, d_ref, wa_ref, wb_ref, da_ref, db_ref, part_ref, keep_ref):
+    raw = project(d_ref, da_ref, db_ref, 0)
     score = jnp.sum(pre_ref[0] * raw, axis=1, keepdims=True)
     keep_ref[0] = (raw * pre_ref[1]).astype(BF)
     keep_ref[1] = (raw * pre_ref[2]).astype(BF)
@@ -113,28 +113,40 @@
     part_ref[:, D:] = carried.astype(BF)
 
 
-def weight_grads(xo_ref, xs_ref, do_ref, ds_ref, ho_ref, hs_ref, ko_ref, ks_ref, a_ref, b_ref, flip):
+def down_grads(do_ref, ds_ref, ho_ref, hs_ref, a_ref, b_ref, flip):
+    @pl.when(pl.program_id(0) == 0)
+    def _():
+        flip[:, :ROWS] = ho_ref[...].T
+        flip[:, ROWS:] = hs_ref[...].T
+
+    grad = dot(flip[...], jnp.concatenate([do_ref[...], ds_ref[...]], axis=0), 1, 0).astype(BF)
+    a_ref[0] = grad[:FQ]
+    b_ref[0] = grad[FQ:]
+
+
+def gate_up_grads(xo_ref, xs_ref, ko_ref, ks_ref, a_ref, b_ref, flip):
     @pl.when(pl.program_id(0) == 0)
     def _():
         for i in range(2):
             flip[i, :, :ROWS] = ko_ref[i].T
             flip[i, :, ROWS:] = ks_ref[i].T
-        flip[2, :, :ROWS] = ho_ref[...].T
-        flip[2, :, ROWS:] = hs_ref[...].T
 
     x = jnp.concatenate([xo_ref[...], xs_ref[...]], axis=0)
-    d = jnp.concatenate([do_ref[...], ds_ref[...]], axis=0)
-    for i, rows in ((0, x), (1, x), (2, d)):
-        grad = dot(flip[i], rows, 1, 0).astype(BF)
+    for i in range(2):
+        grad = dot(flip[i], x, 1, 0).astype(BF)
         a_ref[i] = grad[:FQ]
         b_ref[i] = grad[FQ:]
 
 
-def place(at_ref, a_ref, b_ref, gate_ref, up_ref, down_ref):
+def place(at_ref, da_ref, db_ref, a_ref, b_ref, gate_ref, up_ref, down_ref):
     odd = at_ref[3] % 2
-    for i, out in enumerate((gate_ref, up_ref, down_ref)):
-        out[odd] = a_ref[i]
-        out[1 - odd] = b_ref[i]
+    for out, a, b in (
+        (gate_ref, a_ref[0], b_ref[0]),
+        (up_ref, a_ref[1], b_ref[1]),
+        (down_ref, da_ref[0], db_ref[0]),
+    ):
+        out[odd] = a
+        out[1 - odd] = b
 
 
 def combine(at_ref, table_ref, pick_ref, home_ref, out_ref):
@@ -188,9 +200,9 @@
     with jax.named_scope("weights_out"):
         dg, *mats = lax.optimization_barrier((dg, w_gate, w_up, w_down))
         weights = []
-        for m in range(2):
+        for m, which in ((0, mats[:2]), (1, mats[:2]), (0, mats[2:]), (1, mats[2:])):
             k = (ix + m) % 2
-            piece = jnp.stack([lax.dynamic_index_in_dim(w, k, 0, keepdims=False) for w in mats])
+            piece = jnp.stack([lax.dynamic_index_in_dim(w, k, 0, keepdims=False) for w in which])
             weights.append(lax.ppermute(piece, ("c", "x"), weight_pairs(m)))
 
     with jax.named_scope("select_d"):
@@ -215,8 +227,9 @@
             compiler_params=params(),
             name="gates",
         )
-        pre_own, hid_own = ahead(x_own, *weights)
-        pre_sib, hid_sib = ahead(x_sib, *weights)
+        pre_own, hid_own = ahead(x_own, *weights[:2])
+        pre_sib, hid_sib = ahead(x_sib, *weights[:2])
+        pre_own, pre_sib, *weights = lax.optimization_barrier((pre_own, pre_sib, *weights))
         d_own, pre_own, pre_sib = lax.optimization_barrier((d_own, pre_own, pre_sib))
 
     with jax.named_scope("expert"):
@@ -224,7 +237,7 @@
         run = pl.pallas_call(
             expert,
             out_shape=(shape((ROWS, WIDE), BF), shape((2, ROWS, FH), BF)),
-            in_specs=[SMEM] + [VMEM] * 4,
+            in_specs=[SMEM] + [VMEM] * 6,
             out_specs=(VMEM, VMEM),
             compiler_params=params(),
             name="expert",
@@ -233,33 +246,48 @@
         sent = lax.ppermute(part_sib, "c", sib)
         part_own, keep_own = run(at, pre_own, d_own, *weights)
         total = (part_own.astype(F32) + sent.astype(F32)).astype(BF)
-        total, keep_own, keep_sib = lax.optimization_barrier((total, keep_own, keep_sib))
+        total, hid_own, hid_sib = lax.optimization_barrier((total, hid_own, hid_sib))
 
     with jax.named_scope("weights_back"):
         cut = pl.BlockSpec((ROWS, Q), lambda h: (0, h))
         h_spec = pl.BlockSpec((ROWS, FH), lambda h: (0, 0))
         k_spec = pl.BlockSpec((2, ROWS, FH), lambda h: (0, 0, 0))
-        o_spec = pl.BlockSpec((3, FQ, Q), lambda h: (0, 0, h))
+        back = []
+
+        def home_again(pieces):
+            for m, piece in enumerate(pieces):
+                back.append(lax.ppermute(piece, ("c", "x"), [(b, a) for a, b in weight_pairs(m)]))
+
         pieces = pl.pallas_call(
-            weight_grads,
+            down_grads,
             grid=(NX,),
-            out_shape=(shape((3, FQ, D), BF),) * 2,
-            in_specs=[cut] * 4 + [h_spec, h_spec, k_spec, k_spec],
-            out_specs=(o_spec, o_spec),
-            scratch_shapes=[pltpu.VMEM((3, FH, 2 * ROWS), BF)],
+            out_shape=(shape((1, FQ, D), BF),) * 2,
+            in_specs=[cut, cut, h_spec, h_spec],
+            out_specs=(pl.BlockSpec((1, FQ, Q), lambda h: (0, 0, h)),) * 2,
+            scratch_shapes=[pltpu.VMEM((FH, 2 * ROWS), BF)],
             compiler_params=params(60),
-            name="weight_grads",
-        )(x_own, x_sib, d_own, d_sib, hid_own, hid_sib, keep_own, keep_sib)
-        back = []
-        for m, g in enumerate(pieces):
-            inverse = [(b, a) for a, b in weight_pairs(m)]
-            back.append(lax.ppermute(g, ("c", "x"), inverse))
+            name="down_grads",
+        )(d_own, d_sib, hid_own, hid_sib)
+        *pieces, keep_own, keep_sib = lax.optimization_barrier((*pieces, keep_own, keep_sib))
+        home_again(pieces)
+        pieces = pl.pallas_call(
+            gate_up_grads,
+            grid=(NX,),
+            out_shape=(shape((2, FQ, D), BF),) * 2,
+            in_specs=[cut, cut, k_spec, k_spec],
+            out_specs=(pl.BlockSpec((2, FQ, Q), lambda h: (0, 0, h)),) * 2,
+            scratch_shapes=[pltpu.VMEM((2, FH, 2 * ROWS), BF)],
+            compiler_params=params(60),
+            name="gate_up_grads",
+        )(x_own, x_sib, keep_own, keep_sib)
+        *pieces, back[0], back[1] = lax.optimization_barrier((*pieces, back[0], back[1]))
+        home_again(pieces)
         part_rows = FQ // 4
         grad_gate, grad_up, grad_down = pl.pallas_call(
             place,
             grid=(4,),
             out_shape=(shape((2, FQ, D), BF),) * 3,
-            in_specs=[SMEM] + [pl.BlockSpec((3, part_rows, D), lambda i: (0, i, 0))] * 2,
+            in_specs=[SMEM] + [pl.BlockSpec((n, part_rows, D), lambda i: (0, i, 0)) for n in (1, 1, 2, 2)],
             out_specs=(pl.BlockSpec((2, part_rows, D), lambda i: (0, i, 0)),) * 3,
             compiler_params=params(),
             name="place",

time: 243 us -> 245 us (level)
    ppermute x2 -> x4, waiting for transfers between devices: 13.5 us -> 29.9 us  [home_again(): lax.ppermute(piece, ('c', 'x'), [(b, a) for a, b in weight_pairs(m)])]
    ppermute x2 -> x4, waiting for transfers between devices: 51.8 us -> 40.8 us  [per_device(): weights.append(lax.ppermute(piece, ('c', 'x'), weight_pairs(m)))]
    all_to_all x3, waiting for transfers between devices: 39.7 us -> 33.5 us  [to_experts(): lax.all_to_all(rows, ('y', 'z'), split_axis=0, concat_axis=0, tiled=True)]
    ppermute x1, starting transfers between devices: 0.01 us -> 3.17 us  [per_device(): x_sib = lax.ppermute(x_own, 'c', sib)]
    pallas_call x3 -> x4, Pallas kernels: 17.7 us -> 19.7 us  [the longest x1 7.54 us: per_device(): pl.pallas_call(gate_up_grads, grid=(NX,), out_shape=(shape((2, FQ, D), BF...]
    ppermute x2 -> x4, starting transfers between devices: 13.8 us -> 12.8 us  [per_device(): weights.append(lax.ppermute(piece, ('c', 'x'), weight_pairs(m)))]
    unnamed x36 -> x40, local copies, waits for them, and re-layouts: 11.7 us -> 12 us
    ppermute x2 -> x4, starting transfers between devices: 6.45 us -> 6.64 us  [home_again(): lax.ppermute(piece, ('c', 'x'), [(b, a) for a, b in weight_pairs(m)])]
  transfers between devices with their start and end apart: 11 -> 15, of which waited for: 7 -> 10; matrix products, arithmetic and copies ran while one was open for 2% -> 1% of each run, Pallas kernels for 13% -> 13%
where the time goes in v8:
time: 245 us; the launch traced here: 243 us
  waiting for transfers between devices  108 us (44%)
  starting transfers between devices  52.2 us (21%)
  Pallas kernels  38.9 us (16%)
  blocking collectives  22.8 us (9%)
  local copies, waits for them, and re-layouts  14.8 us (6%)
  other arithmetic  5.13 us (2%)
    ppermute x4, waiting for transfers between devices, per_device(): weights.append(lax.ppermute(piece, ('c', 'x'), weight_pairs(m)))  40.8 us
    all_to_all x3, waiting for transfers between devices, to_experts(): lax.all_to_all(rows, ('y', 'z'), split_axis=0, concat_axis=0, tiled=True)  33.5 us
    ppermute x4, waiting for transfers between devices, home_again(): lax.ppermute(piece, ('c', 'x'), [(b, a) for a, b in weight_pairs(m)])  29.9 us
    all_to_all x3, starting transfers between devices, to_experts(): lax.all_to_all(rows, ('y', 'z'), split_axis=0, concat_axis=0, tiled=True)  22.4 us
    ppermute x4, starting transfers between devices, per_device(): weights.append(lax.ppermute(piece, ('c', 'x'), weight_pairs(m)))  12.8 us
    all_gather x1, blocking collectives, per_device(): xg = lax.all_gather(tokens, 'x', axis=0, tiled=False)  12.5 us
    unnamed x40, local copies, waits for them, and re-layouts  12 us
    all_gather x1, blocking collectives, per_device(): dg = lax.all_gather(cotangent, 'x', axis=0, tiled=False)  10.3 us
  transfers between devices with their start and end apart: 15, of which 10 were waited for; matrix products, arithmetic and copies ran while one was open for 1% of the time, Pallas kernels for 13%

profile of v8, /device:TPU:1, one launch (start us, length us, event | category | flops | bytes accessed | tf_op | source)
XLA Modules:
  0.0 243.0 jit_solution(18060103039228703505)
XLA Ops:
  2.0 12.5 %all-gather = bf16[512,512]{1,0:T(8,128)(2,1)S(1)} all-gather(bf16[128,512]{1,0:T(8,128)(2,1)} %param.7), channel_id=2, replica_groups=mesh['y'=4,'z'=8,'c'=2,'x'=4] {'x'}, dimensions={0}, use_global_device_ids=true | all-gather | bytes 655360 | tf_op jit(solution)/shard_map/select_x/all_gather | solution.py:184
  17.4 11.5 %all-to-all-start = ((bf16[32,16,2176]{2,1,0:T(8,128)(2,1)}), bf16[32,16,2176]{2,1,0:T(8,128)(2,1)}, u32[]{:S(2)}, u32[]{:S(2)}) async-start(bf16[32,16,2176]{2,1,0:T(8,128)(2,1)} %bitcast.7), calls=%async_computation | async-start | bytes 4456448 | tf_op jit(solution)/shard_map/select_x/all_to_all | solution.py:180
  28.9 10.3 %all-gather.1 = bf16[512,512]{1,0:T(8,128)(2,1)S(1)} all-gather(bf16[128,512]{1,0:T(8,128)(2,1)S(1)} %copy-done.19), channel_id=3, replica_groups=mesh['y'=4,'z'=8,'c'=2,'x'=4] {'x'}, dimensions={0}, use_global_device_ids=true | all-gather | bytes 655360 | tf_op jit(solution)/shard_map/select_d/all_gather | solution.py:198
  42.0 8.1 %collective-permute-start = (bf16[2,192,2048]{2,1,0:T(8,128)(2,1)S(1)}, bf16[2,192,2048]{2,1,0:T(8,128)(2,1)S(1)}, u32[]{:S(2)}, u32[]{:S(2)}) collective-permute-start(bf16[2,192,2048]{2,1,0:T(8,128)(2,1)S(1)} %pad_maximum_fusion), channel_id=1, source_target_pairs={{0,0},{1,1},{2,4},{3,5},{4,2},{5,3},{6,6},{7,7},{8,8},{9,9},{10,12... | collective-permute-start | bytes 4718600 | tf_op jit(solution)/shard_map/weights_out/ppermute | solution.py:206
  52.3 16.0 %collective-permute-done.wa_ref = bf16[2,192,2048]{2,1,0:T(8,128)(2,1)S(1)} collective-permute-done((bf16[2,192,2048]{2,1,0:T(8,128)(2,1)S(1)}, bf16[2,192,2048]{2,1,0:T(8,128)(2,1)S(1)}, u32[]{:S(2)}, u32[]{:S(2)}) %collective-permute-start) | collective-permute-done | bytes 1572896 | tf_op jit(solution)/shard_map/weights_out/ppermute | solution.py:206
  68.2 12.0 %all-to-all-done = bf16[32,16,2176]{2,1,0:T(8,128)(2,1)} async-done(((bf16[32,16,2176]{2,1,0:T(8,128)(2,1)}), bf16[32,16,2176]{2,1,0:T(8,128)(2,1)}, u32[]{:S(2)}, u32[]{:S(2)}) %all-to-all-start) | async-done | bytes 2228256 | tf_op jit(solution)/shard_map/select_x/all_to_all | solution.py:180
  80.3 5.7 %all-to-all-start.1 = ((bf16[32,16,2048]{2,1,0:T(8,128)(2,1)}), bf16[32,16,2048]{2,1,0:T(8,128)(2,1)}, u32[]{:S(2)}, u32[]{:S(2)}) async-start(bf16[32,16,2048]{2,1,0:T(8,128)(2,1)} %bitcast.19), calls=%async_computation.1 | async-start | bytes 4194304 | tf_op jit(solution)/shard_map/gates/all_to_all | solution.py:180
  86.0 3.2 %collective-permute-start.2 = (bf16[512,2176]{1,0:T(8,128)(2,1)}, bf16[512,2176]{1,0:T(8,128)(2,1)S(1)}, u32[]{:S(2)}, u32[]{:S(2)}) collective-permute-start(bf16[512,2176]{1,0:T(8,128)(2,1)} %bitcast.8.x_ref.xo_ref), channel_id=1, source_target_pairs={{0,4},{4,0},{1,5},{5,1},{2,6},{6,2},{3,7},{7,3},{8,12},{12,8},{9,1... | collective-permute-start | bytes 6684680 | tf_op jit(solution)/shard_map/gates/ppermute | solution.py:221
  94.5 24.8 %collective-permute-done.1.wb_ref = bf16[2,192,2048]{2,1,0:T(8,128)(2,1)S(1)} collective-permute-done((bf16[2,192,2048]{2,1,0:T(8,128)(2,1)S(1)}, bf16[2,192,2048]{2,1,0:T(8,128)(2,1)S(1)}, u32[]{:S(2)}, u32[]{:S(2)}) %collective-permute-start.1) | collective-permute-done | bytes 1572896 | tf_op jit(solution)/shard_map/weights_out/ppermute | solution.py:206
  119.3 4.1 %gates.2 = (f32[3,512,384]{2,1,0:T(8,128)S(1)}, bf16[512,384]{1,0:T(8,128)(2,1)S(1)}) custom-call(bf16[512,2176]{1,0:T(8,128)(2,1)} %bitcast.8.x_ref.xo_ref, bf16[2,192,2048]{2,1,0:T(8,128)(2,1)S(1)} %collective-permute-done.wa_ref, bf16[2,192,2048]{2,1,0:T(8,128)(2,1)S(1)} %collective-permute-done.1.wb_ref), custom_call_target="tpu_custom_call" | custom-call | tf_op jit(solution)/shard_map/gates/gates/pallas_call | solution.py:230
  134.2 3.4 %collective-permute-start.5 = (bf16[512,2048]{1,0:T(8,128)(2,1)}, bf16[512,2048]{1,0:T(8,128)(2,1)S(1)}, u32[]{:S(2)}, u32[]{:S(2)}) collective-permute-start(bf16[512,2048]{1,0:T(8,128)(2,1)} %bitcast.11.d_ref.do_ref), channel_id=1, source_target_pairs={{0,4},{4,0},{1,5},{5,1},{2,6},{6,2},{3,7},{7,3},{8,12},{12,8},{9,1... | collective-permute-start | bytes 6291464 | tf_op jit(solution)/shard_map/expert/ppermute | solution.py:236
  137.6 4.0 %collective-permute-done.5.d_ref.ds_ref = bf16[512,2048]{1,0:T(8,128)(2,1)S(1)} collective-permute-done((bf16[512,2048]{1,0:T(8,128)(2,1)}, bf16[512,2048]{1,0:T(8,128)(2,1)S(1)}, u32[]{:S(2)}, u32[]{:S(2)}) %collective-permute-start.5) | collective-permute-done | bytes 2097184 | tf_op jit(solution)/shard_map/expert/ppermute | solution.py:236
  145.5 4.0 %expert.3 = (bf16[512,2176]{1,0:T(8,128)(2,1)S(1)}, bf16[2,512,384]{2,1,0:T(8,128)(2,1)S(1)}) custom-call(s32[4]{0:T(128)S(1)} %pad_add_fusion.at_ref, f32[3,512,384]{2,1,0:T(8,128)S(1)} %copy-done.11, bf16[512,2048]{1,0:T(8,128)(2,1)S(1)} %collective-permute-done.5.d_ref.ds_ref, bf16[2,192,2048]{2,1,0:T(8,128)(2,1)S(1)} %collective-permute-done.wa_ref, ...), custom_call_target="tpu_custom_call" | custom-call | tf_op jit(solution)/shard_map/expert/expert/pallas_call | solution.py:245
  150.8 5.1 %expert.2 = (bf16[512,2176]{1,0:T(8,128)(2,1)S(1)}, bf16[2,512,384]{2,1,0:T(8,128)(2,1)S(1)}) custom-call(s32[4]{0:T(128)S(1)} %pad_add_fusion.at_ref, f32[3,512,384]{2,1,0:T(8,128)S(1)} %copy-done.9, bf16[512,2048]{1,0:T(8,128)(2,1)} %bitcast.11.d_ref.do_ref, bf16[2,192,2048]{2,1,0:T(8,128)(2,1)S(1)} %collective-permute-done.wa_ref, ...), custom_call_target="tpu_custom_call" | custom-call | tf_op jit(solution)/shard_map/expert/expert/pallas_call | solution.py:247
  157.9 5.2 %all-to-all-start.2 = ((bf16[32,16,2176]{2,1,0:T(8,128)(2,1)}), bf16[32,16,2176]{2,1,0:T(8,128)(2,1)S(1)}, u32[]{:S(2)}, u32[]{:S(2)}) async-start(bf16[32,16,2176]{2,1,0:T(8,128)(2,1)} %bitcast.22), calls=%async_computation.2 | async-start | bytes 4456448 | tf_op jit(solution)/shard_map/tokens_back/all_to_all | solution.py:180
  163.1 5.6 %down_grads.1 = (bf16[1,192,2048]{2,1,0:T(8,128)(2,1)}, bf16[1,192,2048]{2,1,0:T(8,128)(2,1)}) custom-call(bf16[512,2048]{1,0:T(8,128)(2,1)} %bitcast.11.d_ref.do_ref, bf16[512,2048]{1,0:T(8,128)(2,1)} %copy-done.2, bf16[512,384]{1,0:T(8,128)(2,1)} %copy-done.14, bf16[512,384]{1,0:T(8,128)(2,1)} %copy-done.15), custom_call_target="tpu_custom_call" | custom-call | tf_op jit(solution)/shard_map/weights_back/down_grads/pallas_call | solution.py:261
  168.7 3.4 %collective-permute-start.7 = (bf16[1,192,2048]{2,1,0:T(8,128)(2,1)}, bf16[1,192,2048]{2,1,0:T(8,128)(2,1)S(1)}, u32[]{:S(2)}, u32[]{:S(2)}) collective-permute-start(bf16[1,192,2048]{2,1,0:T(8,128)(2,1)} %get-tuple-element.88), channel_id=1, source_target_pairs={{0,0},{1,1},{4,2},{5,3},{2,4},{3,5},{6,6},{7,7},{8,8},{9,9},{12,10... | collective-permute-start | bytes 2359304 | tf_op jit(solution)/shard_map/weights_back/ppermute | solution.py:259
  172.2 7.5 %gate_up_grads.1 = (bf16[2,192,2048]{2,1,0:T(8,128)(2,1)}, bf16[2,192,2048]{2,1,0:T(8,128)(2,1)}) custom-call(bf16[512,2176]{1,0:T(8,128)(2,1)} %bitcast.8.x_ref.xo_ref, bf16[512,2176]{1,0:T(8,128)(2,1)} %copy-done, bf16[2,512,384]{2,1,0:T(8,128)(2,1)} %copy-done.13, bf16[2,512,384]{2,1,0:T(8,128)(2,1)} %copy-done.12), custom_call_target="tpu_custom_call" | custom-call | tf_op jit(solution)/shard_map/weights_back/gate_up_grads/pallas_call | solution.py:273
  179.7 10.3 %collective-permute-done.7.da_ref = bf16[1,192,2048]{2,1,0:T(8,128)(2,1)S(1)} collective-permute-done((bf16[1,192,2048]{2,1,0:T(8,128)(2,1)}, bf16[1,192,2048]{2,1,0:T(8,128)(2,1)S(1)}, u32[]{:S(2)}, u32[]{:S(2)}) %collective-permute-start.7) | collective-permute-done | bytes 786464 | tf_op jit(solution)/shard_map/weights_back/ppermute | solution.py:259
  196.3 18.6 %all-to-all-done.2 = bf16[32,16,2176]{2,1,0:T(8,128)(2,1)S(1)} async-done(((bf16[32,16,2176]{2,1,0:T(8,128)(2,1)}), bf16[32,16,2176]{2,1,0:T(8,128)(2,1)S(1)}, u32[]{:S(2)}, u32[]{:S(2)}) %all-to-all-start.2) | async-done | bytes 2228256 | tf_op jit(solution)/shard_map/tokens_back/all_to_all | solution.py:180
  216.7 3.5 %all-to-all-start.3 = ((bf16[4,144,512]{2,1,0:T(8,128)(2,1)}), bf16[4,144,512]{2,1,0:T(8,128)(2,1)S(1)}, u32[]{:S(2)}, u32[]{:S(2)}) async-start(bf16[4,144,512]{2,1,0:T(8,128)(2,1)} %combine.1), calls=%async_computation.3 | async-start | bytes 1179648 | tf_op jit(solution)/shard_map/tokens_back/all_to_all | solution.py:306
  220.2 7.3 %collective-permute-done.9.a_ref = bf16[2,192,2048]{2,1,0:T(8,128)(2,1)} collective-permute-done((bf16[2,192,2048]{2,1,0:T(8,128)(2,1)}, bf16[2,192,2048]{2,1,0:T(8,128)(2,1)}, u32[]{:S(2)}, u32[]{:S(2)}) %collective-permute-start.9) | collective-permute-done | bytes 1572896 | tf_op jit(solution)/shard_map/weights_back/ppermute | solution.py:259
  227.5 9.2 %collective-permute-done.10.b_ref = bf16[2,192,2048]{2,1,0:T(8,128)(2,1)} collective-permute-done((bf16[2,192,2048]{2,1,0:T(8,128)(2,1)}, bf16[2,192,2048]{2,1,0:T(8,128)(2,1)}, u32[]{:S(2)}, u32[]{:S(2)}) %collective-permute-start.10) | collective-permute-done | bytes 1572896 | tf_op jit(solution)/shard_map/weights_back/ppermute | solution.py:259
  236.7 4.8 %place.1 = (bf16[2,192,2048]{2,1,0:T(8,128)(2,1)}, bf16[2,192,2048]{2,1,0:T(8,128)(2,1)}, bf16[2,192,2048]{2,1,0:T(8,128)(2,1)}) custom-call(s32[4]{0:T(128)S(1)} %pad_add_fusion.at_ref, bf16[1,192,2048]{2,1,0:T(8,128)(2,1)S(1)} %collective-permute-done.7.da_ref, bf16[1,192,2048]{2,1,0:T(8,128)(2,1)} %collective-permute-done.8.db_ref, ...), custom_call_target="tpu_custom_call" | custom-call | tf_op jit(solution)/shard_map/weights_back/place/pallas_call | solution.py:286
  (71 shorter events, 42.0 us)
Async XLA Ops:
  17.4 11.5 %copy-start.19 = (bf16[128,512]{1,0:T(8,128)(2,1)S(1)}, bf16[128,512]{1,0:T(8,128)(2,1)}, u32[]{:S(2)}) copy-start(bf16[128,512]{1,0:T(8,128)(2,1)} %param.8) | copy-start | bytes 393220
  17.4 21.8 %copy-start.18 = (bf16[2,192,2048]{2,1,0:T(8,128)(2,1)S(1)}, bf16[2,192,2048]{2,1,0:T(8,128)(2,1)}, u32[]{:S(2)}) copy-start(bf16[2,192,2048]{2,1,0:T(8,128)(2,1)} %param.12) | copy-start | bytes 4718596
  17.4 62.8 %all-to-all-start = ((bf16[32,16,2176]{2,1,0:T(8,128)(2,1)}), bf16[32,16,2176]{2,1,0:T(8,128)(2,1)}, u32[]{:S(2)}, u32[]{:S(2)}) async-start(bf16[32,16,2176]{2,1,0:T(8,128)(2,1)} %bitcast.7), calls=%async_computation | async-start | bytes 4456448 | tf_op jit(solution)/shard_map/select_x/all_to_all | solution.py:180
  42.0 26.2 %collective-permute-start = (bf16[2,192,2048]{2,1,0:T(8,128)(2,1)S(1)}, bf16[2,192,2048]{2,1,0:T(8,128)(2,1)S(1)}, u32[]{:S(2)}, u32[]{:S(2)}) collective-permute-start(bf16[2,192,2048]{2,1,0:T(8,128)(2,1)S(1)} %pad_maximum_fusion), channel_id=1, source_target_pairs={{0,0},{1,1},{2,4},{3,5},{4,2},{5,3},{6,6},{7,7},{8,8},{9,9},{10,12... | collective-permute-start | bytes 4718600 | tf_op jit(solution)/shard_map/weights_out/ppermute | solution.py:206
  80.3 8.9 %copy-start.16 = (bf16[1,192,2048]{2,1,0:T(8,128)(2,1)S(1)}, bf16[1,192,2048]{2,1,0:T(8,128)(2,1)}, u32[]{:S(2)}) copy-start(bf16[1,192,2048]{2,1,0:T(8,128)(2,1)} %get-tuple-element.104) | copy-start | bytes 2359300
  80.3 53.9 %all-to-all-start.1 = ((bf16[32,16,2048]{2,1,0:T(8,128)(2,1)}), bf16[32,16,2048]{2,1,0:T(8,128)(2,1)}, u32[]{:S(2)}, u32[]{:S(2)}) async-start(bf16[32,16,2048]{2,1,0:T(8,128)(2,1)} %bitcast.19), calls=%async_computation.1 | async-start | bytes 4194304 | tf_op jit(solution)/shard_map/gates/all_to_all | solution.py:180
  86.0 38.8 %collective-permute-start.2 = (bf16[512,2176]{1,0:T(8,128)(2,1)}, bf16[512,2176]{1,0:T(8,128)(2,1)S(1)}, u32[]{:S(2)}, u32[]{:S(2)}) collective-permute-start(bf16[512,2176]{1,0:T(8,128)(2,1)} %bitcast.8.x_ref.xo_ref), channel_id=1, source_target_pairs={{0,4},{4,0},{1,5},{5,1},{2,6},{6,2},{3,7},{7,3},{8,12},{12,8},{9,1... | collective-permute-start | bytes 6684680 | tf_op jit(solution)/shard_map/gates/ppermute | solution.py:221
  89.3 30.0 %collective-permute-start.1 = (bf16[2,192,2048]{2,1,0:T(8,128)(2,1)S(1)}, bf16[2,192,2048]{2,1,0:T(8,128)(2,1)S(1)}, u32[]{:S(2)}, u32[]{:S(2)}) collective-permute-start(bf16[2,192,2048]{2,1,0:T(8,128)(2,1)S(1)} %pad_maximum_fusion.1), channel_id=1, source_target_pairs={{0,1},{1,0},{2,5},{3,4},{4,3},{5,2},{6,7},{7,6},{8,9},{9,8},{10,13... | collective-permute-start | bytes 4718600 | tf_op jit(solution)/shard_map/weights_out/ppermute | solution.py:206
  90.7 38.8 %collective-permute-start.4 = (bf16[1,192,2048]{2,1,0:T(8,128)(2,1)S(1)}, bf16[1,192,2048]{2,1,0:T(8,128)(2,1)S(1)}, u32[]{:S(2)}, u32[]{:S(2)}) collective-permute-start(bf16[1,192,2048]{2,1,0:T(8,128)(2,1)S(1)} %get-tuple-element.97), channel_id=1, source_target_pairs={{0,1},{1,0},{2,5},{3,4},{4,3},{5,2},{6,7},{7,6},{8,9},{9,8},{10,13... | collective-permute-start | bytes 2359304 | tf_op jit(solution)/shard_map/weights_out/ppermute | solution.py:206
  92.6 37.8 %collective-permute-start.3 = (bf16[1,192,2048]{2,1,0:T(8,128)(2,1)S(1)}, bf16[1,192,2048]{2,1,0:T(8,128)(2,1)S(1)}, u32[]{:S(2)}, u32[]{:S(2)}) collective-permute-start(bf16[1,192,2048]{2,1,0:T(8,128)(2,1)S(1)} %get-tuple-element.98), channel_id=1, source_target_pairs={{0,0},{1,1},{2,4},{3,5},{4,2},{5,3},{6,6},{7,7},{8,8},{9,9},{10,12... | collective-permute-start | bytes 2359304 | tf_op jit(solution)/shard_map/weights_out/ppermute | solution.py:206
  124.8 2.5 %copy-start.14 = (bf16[512,384]{1,0:T(8,128)(2,1)}, bf16[512,384]{1,0:T(8,128)(2,1)S(1)}, u32[]{:S(2)}) copy-start(bf16[512,384]{1,0:T(8,128)(2,1)S(1)} %get-tuple-element.78.ho_ref) | copy-start | bytes 1179652
  124.8 2.5 %copy-start = (bf16[512,2176]{1,0:T(8,128)(2,1)}, bf16[512,2176]{1,0:T(8,128)(2,1)S(1)}, u32[]{:S(2)}) copy-start(bf16[512,2176]{1,0:T(8,128)(2,1)S(1)} %collective-permute-done.2.x_ref.xs_ref) | copy-start | bytes 6684676
  134.2 7.4 %collective-permute-start.5 = (bf16[512,2048]{1,0:T(8,128)(2,1)}, bf16[512,2048]{1,0:T(8,128)(2,1)S(1)}, u32[]{:S(2)}, u32[]{:S(2)}) collective-permute-start(bf16[512,2048]{1,0:T(8,128)(2,1)} %bitcast.11.d_ref.do_ref), channel_id=1, source_target_pairs={{0,4},{4,0},{1,5},{5,1},{2,6},{6,2},{3,7},{7,3},{8,12},{12,8},{9,1... | collective-permute-start | bytes 6291464 | tf_op jit(solution)/shard_map/expert/ppermute | solution.py:236
  145.5 4.0 %copy-start.2 = (bf16[512,2048]{1,0:T(8,128)(2,1)}, bf16[512,2048]{1,0:T(8,128)(2,1)S(1)}, u32[]{:S(2)}) copy-start(bf16[512,2048]{1,0:T(8,128)(2,1)S(1)} %collective-permute-done.5.d_ref.ds_ref) | copy-start | bytes 6291460
  145.5 5.3 %copy-start.7 = (bf16[1,192,2048]{2,1,0:T(8,128)(2,1)S(1)}, bf16[1,192,2048]{2,1,0:T(8,128)(2,1)}, u32[]{:S(2)}) copy-start(bf16[1,192,2048]{2,1,0:T(8,128)(2,1)} %copy-done.5) | copy-start | bytes 2359300
  145.5 5.3 %copy-start.9 = (f32[3,512,384]{2,1,0:T(8,128)S(1)}, f32[3,512,384]{2,1,0:T(8,128)}, u32[]{:S(2)}) copy-start(f32[3,512,384]{2,1,0:T(8,128)} %copy-done.8) | copy-start | bytes 7077892
  150.5 5.5 %collective-permute-start.6 = (bf16[512,2176]{1,0:T(8,128)(2,1)S(1)}, bf16[512,2176]{1,0:T(8,128)(2,1)S(1)}, u32[]{:S(2)}, u32[]{:S(2)}) collective-permute-start(bf16[512,2176]{1,0:T(8,128)(2,1)S(1)} %get-tuple-element.74), channel_id=1, source_target_pairs={{0,4},{4,0},{1,5},{5,1},{2,6},{6,2},{3,7},{7,3},{8,12},{12,8},{9,1... | collective-permute-start | bytes 6684680 | tf_op jit(solution)/shard_map/expert/ppermute | solution.py:246
  155.9 1.9 copy-start.13
  157.9 57.0 %all-to-all-start.2 = ((bf16[32,16,2176]{2,1,0:T(8,128)(2,1)}), bf16[32,16,2176]{2,1,0:T(8,128)(2,1)S(1)}, u32[]{:S(2)}, u32[]{:S(2)}) async-start(bf16[32,16,2176]{2,1,0:T(8,128)(2,1)} %bitcast.22), calls=%async_computation.2 | async-start | bytes 4456448 | tf_op jit(solution)/shard_map/tokens_back/all_to_all | solution.py:180
  168.7 21.3 %collective-permute-start.7 = (bf16[1,192,2048]{2,1,0:T(8,128)(2,1)}, bf16[1,192,2048]{2,1,0:T(8,128)(2,1)S(1)}, u32[]{:S(2)}, u32[]{:S(2)}) collective-permute-start(bf16[1,192,2048]{2,1,0:T(8,128)(2,1)} %get-tuple-element.88), channel_id=1, source_target_pairs={{0,0},{1,1},{4,2},{5,3},{2,4},{3,5},{6,6},{7,7},{8,8},{9,9},{12,10... | collective-permute-start | bytes 2359304 | tf_op jit(solution)/shard_map/weights_back/ppermute | solution.py:259
  172.1 21.0 %collective-permute-start.8 = (bf16[1,192,2048]{2,1,0:T(8,128)(2,1)}, bf16[1,192,2048]{2,1,0:T(8,128)(2,1)}, u32[]{:S(2)}, u32[]{:S(2)}) collective-permute-start(bf16[1,192,2048]{2,1,0:T(8,128)(2,1)} %get-tuple-element.89), channel_id=1, source_target_pairs={{1,0},{0,1},{5,2},{4,3},{3,4},{2,5},{7,6},{6,7},{9,8},{8,9},{13,10... | collective-permute-start | bytes 2359304 | tf_op jit(solution)/shard_map/weights_back/ppermute | solution.py:259
  193.1 34.3 %collective-permute-start.9 = (bf16[2,192,2048]{2,1,0:T(8,128)(2,1)}, bf16[2,192,2048]{2,1,0:T(8,128)(2,1)}, u32[]{:S(2)}, u32[]{:S(2)}) collective-permute-start(bf16[2,192,2048]{2,1,0:T(8,128)(2,1)} %get-tuple-element.92), channel_id=1, source_target_pairs={{0,0},{1,1},{4,2},{5,3},{2,4},{3,5},{6,6},{7,7},{8,8},{9,9},{12,10... | collective-permute-start | bytes 4718600 | tf_op jit(solution)/shard_map/weights_back/ppermute | solution.py:259
  195.8 40.9 %collective-permute-start.10 = (bf16[2,192,2048]{2,1,0:T(8,128)(2,1)}, bf16[2,192,2048]{2,1,0:T(8,128)(2,1)}, u32[]{:S(2)}, u32[]{:S(2)}) collective-permute-start(bf16[2,192,2048]{2,1,0:T(8,128)(2,1)} %get-tuple-element.93), channel_id=1, source_target_pairs={{1,0},{0,1},{5,2},{4,3},{3,4},{2,5},{7,6},{6,7},{9,8},{8,9},{13,10... | collective-permute-start | bytes 4718600 | tf_op jit(solution)/shard_map/weights_back/ppermute | solution.py:259
  216.7 24.8 %all-to-all-start.3 = ((bf16[4,144,512]{2,1,0:T(8,128)(2,1)}), bf16[4,144,512]{2,1,0:T(8,128)(2,1)S(1)}, u32[]{:S(2)}, u32[]{:S(2)}) async-start(bf16[4,144,512]{2,1,0:T(8,128)(2,1)} %combine.1), calls=%async_computation.3 | async-start | bytes 1179648 | tf_op jit(solution)/shard_map/tokens_back/all_to_all | solution.py:306
  (11 other events, 13.1 us)

commit v9 on v8

--- a/solution.py
+++ b/solution.py
@@ -242,11 +242,11 @@
             compiler_params=params(),
             name="expert",
         )
+        part_own, keep_own = run(at, pre_own, d_own, *weights)
+        part_own, d_sib = lax.optimization_barrier((part_own, d_sib))
         part_sib, keep_sib = run(at, pre_sib, d_sib, *weights)
+        part_sib, hid_own, hid_sib = lax.optimization_barrier((part_sib, hid_own, hid_sib))
         sent = lax.ppermute(part_sib, "c", sib)
-        part_own, keep_own = run(at, pre_own, d_own, *weights)
-        total = (part_own.astype(F32) + sent.astype(F32)).astype(BF)
-        total, hid_own, hid_sib = lax.optimization_barrier((total, hid_own, hid_sib))
 
     with jax.named_scope("weights_back"):
         cut = pl.BlockSpec((ROWS, Q), lambda h: (0, h))
@@ -265,11 +265,13 @@
             in_specs=[cut, cut, h_spec, h_spec],
             out_specs=(pl.BlockSpec((1, FQ, Q), lambda h: (0, 0, h)),) * 2,
             scratch_shapes=[pltpu.VMEM((FH, 2 * ROWS), BF)],
-            compiler_params=params(60),
+            compiler_params=params(),
             name="down_grads",
         )(d_own, d_sib, hid_own, hid_sib)
-        *pieces, keep_own, keep_sib = lax.optimization_barrier((*pieces, keep_own, keep_sib))
+        *pieces, sent = lax.optimization_barrier((*pieces, sent))
         home_again(pieces)
+        total = (part_own.astype(F32) + sent.astype(F32)).astype(BF)
+        total, keep_own, keep_sib = lax.optimization_barrier((total, keep_own, keep_sib))
         pieces = pl.pallas_call(
             gate_up_grads,
             grid=(NX,),

time: 245 us -> 240 us (0.980)
  waiting for transfers between devices: 108 us -> 101 us
    ppermute x4, waiting for transfers between devices: 29.9 us -> 23.2 us  [home_again(): lax.ppermute(piece, ('c', 'x'), [(b, a) for a, b in weight_pairs(m)])]
    ppermute x1, waiting for transfers between devices: 4 us -> 0.01 us  [per_device(): d_sib = lax.ppermute(d_own, 'c', sib)]
    all_to_all x3, waiting for transfers between devices: 33.5 us -> 37.4 us  [to_experts(): lax.all_to_all(rows, ('y', 'z'), split_axis=0, concat_axis=0, tiled=True)]
    unnamed x40 -> x42, local copies, waits for them, and re-layouts: 12 us -> 13.4 us
  transfers between devices with their start and end apart: 15 -> 15, of which waited for: 10 -> 9; matrix products, arithmetic and copies ran while one was open for 1% -> 2% of each run, Pallas kernels for 13% -> 13%
where the time goes in v9:
time: 240 us; the launch traced here: 238 us
  waiting for transfers between devices  101 us (42%)
  starting transfers between devices  52.3 us (22%)
  Pallas kernels  37.9 us (16%)
  blocking collectives  22.8 us (10%)
  local copies, waits for them, and re-layouts  16.1 us (7%)
  other arithmetic  6.38 us (3%)
    ppermute x4, waiting for transfers between devices, per_device(): weights.append(lax.ppermute(piece, ('c', 'x'), weight_pairs(m)))  40.8 us
    all_to_all x3, waiting for transfers between devices, to_experts(): lax.all_to_all(rows, ('y', 'z'), split_axis=0, concat_axis=0, tiled=True)  37.4 us
    ppermute x4, waiting for transfers between devices, home_again(): lax.ppermute(piece, ('c', 'x'), [(b, a) for a, b in weight_pairs(m)])  23.2 us
    all_to_all x3, starting transfers between devices, to_experts(): lax.all_to_all(rows, ('y', 'z'), split_axis=0, concat_axis=0, tiled=True)  22.3 us
    unnamed x42, local copies, waits for them, and re-layouts  13.4 us
    ppermute x4, starting transfers between devices, per_device(): weights.append(lax.ppermute(piece, ('c', 'x'), weight_pairs(m)))  13.1 us
    all_gather x1, blocking collectives, per_device(): xg = lax.all_gather(tokens, 'x', axis=0, tiled=False)  12.5 us
    all_gather x1, blocking collectives, per_device(): dg = lax.all_gather(cotangent, 'x', axis=0, tiled=False)  10.3 us
  transfers between devices with their start and end apart: 15, of which 9 were waited for; matrix products, arithmetic and copies ran while one was open for 2% of the time, Pallas kernels for 13%

profile of v9, /device:TPU:1, one launch (start us, length us, event | category | flops | bytes accessed | tf_op | source)
XLA Modules:
  0.0 237.8 jit_solution(10199806605688314478)
XLA Ops:
  2.0 12.5 %all-gather = bf16[512,512]{1,0:T(8,128)(2,1)S(1)} all-gather(bf16[128,512]{1,0:T(8,128)(2,1)} %param.7), channel_id=2, replica_groups=mesh['y'=4,'z'=8,'c'=2,'x'=4] {'x'}, dimensions={0}, use_global_device_ids=true | all-gather | bytes 655360 | tf_op jit(solution)/shard_map/select_x/all_gather | solution.py:184
  14.6 2.8 %select_x.1 = (bf16[512,2176]{1,0:T(8,128)(2,1)}, bf16[512,128]{1,0:T(8,128)(2,1)S(1)}) custom-call(s32[4]{0:T(128)S(1)} %pad_add_fusion.at_ref, f32[16,128]{1,0:T(8,128)S(1)} %pad_maximum_fusion.2.table_ref, bf16[4,128,512]{2,1,0:T(8,128)(2,1)S(1)} %bitcast.20), custom_call_target="tpu_custom_call" | custom-call | tf_op jit(solution)/shard_map/select_x/select_x/pallas_call | solution.py:186
  17.4 11.5 %all-to-all-start = ((bf16[32,16,2176]{2,1,0:T(8,128)(2,1)}), bf16[32,16,2176]{2,1,0:T(8,128)(2,1)}, u32[]{:S(2)}, u32[]{:S(2)}) async-start(bf16[32,16,2176]{2,1,0:T(8,128)(2,1)} %bitcast.7), calls=%async_computation | async-start | bytes 4456448 | tf_op jit(solution)/shard_map/select_x/all_to_all | solution.py:180
  28.9 10.3 %all-gather.1 = bf16[512,512]{1,0:T(8,128)(2,1)S(1)} all-gather(bf16[128,512]{1,0:T(8,128)(2,1)S(1)} %copy-done.20), channel_id=3, replica_groups=mesh['y'=4,'z'=8,'c'=2,'x'=4] {'x'}, dimensions={0}, use_global_device_ids=true | all-gather | bytes 655360 | tf_op jit(solution)/shard_map/select_d/all_gather | solution.py:198
  42.0 8.1 %collective-permute-start = (bf16[2,192,2048]{2,1,0:T(8,128)(2,1)S(1)}, bf16[2,192,2048]{2,1,0:T(8,128)(2,1)S(1)}, u32[]{:S(2)}, u32[]{:S(2)}) collective-permute-start(bf16[2,192,2048]{2,1,0:T(8,128)(2,1)S(1)} %pad_maximum_fusion), channel_id=1, source_target_pairs={{0,0},{1,1},{2,4},{3,5},{4,2},{5,3},{6,6},{7,7},{8,8},{9,9},{10,12... | collective-permute-start | bytes 4718600 | tf_op jit(solution)/shard_map/weights_out/ppermute | solution.py:206
  52.3 16.0 %collective-permute-done.wa_ref = bf16[2,192,2048]{2,1,0:T(8,128)(2,1)S(1)} collective-permute-done((bf16[2,192,2048]{2,1,0:T(8,128)(2,1)S(1)}, bf16[2,192,2048]{2,1,0:T(8,128)(2,1)S(1)}, u32[]{:S(2)}, u32[]{:S(2)}) %collective-permute-start) | collective-permute-done | bytes 1572896 | tf_op jit(solution)/shard_map/weights_out/ppermute | solution.py:206
  68.2 12.0 %all-to-all-done = bf16[32,16,2176]{2,1,0:T(8,128)(2,1)} async-done(((bf16[32,16,2176]{2,1,0:T(8,128)(2,1)}), bf16[32,16,2176]{2,1,0:T(8,128)(2,1)}, u32[]{:S(2)}, u32[]{:S(2)}) %all-to-all-start) | async-done | bytes 2228256 | tf_op jit(solution)/shard_map/select_x/all_to_all | solution.py:180
  80.3 5.6 %all-to-all-start.1 = ((bf16[32,16,2048]{2,1,0:T(8,128)(2,1)}), bf16[32,16,2048]{2,1,0:T(8,128)(2,1)}, u32[]{:S(2)}, u32[]{:S(2)}) async-start(bf16[32,16,2048]{2,1,0:T(8,128)(2,1)} %bitcast.19), calls=%async_computation.1 | async-start | bytes 4194304 | tf_op jit(solution)/shard_map/gates/all_to_all | solution.py:180
  85.9 3.2 %collective-permute-start.2 = (bf16[512,2176]{1,0:T(8,128)(2,1)}, bf16[512,2176]{1,0:T(8,128)(2,1)S(1)}, u32[]{:S(2)}, u32[]{:S(2)}) collective-permute-start(bf16[512,2176]{1,0:T(8,128)(2,1)} %bitcast.8.x_ref.xo_ref), channel_id=1, source_target_pairs={{0,4},{4,0},{1,5},{5,1},{2,6},{6,2},{3,7},{7,3},{8,12},{12,8},{9,1... | collective-permute-start | bytes 6684680 | tf_op jit(solution)/shard_map/gates/ppermute | solution.py:221
  95.6 24.8 %collective-permute-done.1.wb_ref = bf16[2,192,2048]{2,1,0:T(8,128)(2,1)S(1)} collective-permute-done((bf16[2,192,2048]{2,1,0:T(8,128)(2,1)S(1)}, bf16[2,192,2048]{2,1,0:T(8,128)(2,1)S(1)}, u32[]{:S(2)}, u32[]{:S(2)}) %collective-permute-start.1) | collective-permute-done | bytes 1572896 | tf_op jit(solution)/shard_map/weights_out/ppermute | solution.py:206
  120.4 4.1 %gates.2 = (f32[3,512,384]{2,1,0:T(8,128)S(1)}, bf16[512,384]{1,0:T(8,128)(2,1)S(1)}) custom-call(bf16[512,2176]{1,0:T(8,128)(2,1)} %bitcast.8.x_ref.xo_ref, bf16[2,192,2048]{2,1,0:T(8,128)(2,1)S(1)} %collective-permute-done.wa_ref, bf16[2,192,2048]{2,1,0:T(8,128)(2,1)S(1)} %collective-permute-done.1.wb_ref), custom_call_target="tpu_custom_call" | custom-call | tf_op jit(solution)/shard_map/gates/gates/pallas_call | solution.py:230
  134.1 3.4 %collective-permute-start.5 = (bf16[512,2048]{1,0:T(8,128)(2,1)}, bf16[512,2048]{1,0:T(8,128)(2,1)S(1)}, u32[]{:S(2)}, u32[]{:S(2)}) collective-permute-start(bf16[512,2048]{1,0:T(8,128)(2,1)} %bitcast.11.d_ref.do_ref), channel_id=1, source_target_pairs={{0,4},{4,0},{1,5},{5,1},{2,6},{6,2},{3,7},{7,3},{8,12},{12,8},{9,1... | collective-permute-start | bytes 6291464 | tf_op jit(solution)/shard_map/expert/ppermute | solution.py:236
  141.4 5.2 %expert.2 = (bf16[512,2176]{1,0:T(8,128)(2,1)S(1)}, bf16[2,512,384]{2,1,0:T(8,128)(2,1)S(1)}) custom-call(s32[4]{0:T(128)S(1)} %pad_add_fusion.at_ref, f32[3,512,384]{2,1,0:T(8,128)S(1)} %copy-done.9, bf16[512,2048]{1,0:T(8,128)(2,1)} %bitcast.11.d_ref.do_ref, bf16[2,192,2048]{2,1,0:T(8,128)(2,1)S(1)} %collective-permute-done.wa_ref, ...), custom_call_target="tpu_custom_call" | custom-call | tf_op jit(solution)/shard_map/expert/expert/pallas_call | solution.py:245
  147.5 4.0 %expert.3 = (bf16[512,2176]{1,0:T(8,128)(2,1)S(1)}, bf16[2,512,384]{2,1,0:T(8,128)(2,1)S(1)}) custom-call(s32[4]{0:T(128)S(1)} %pad_add_fusion.at_ref, f32[3,512,384]{2,1,0:T(8,128)S(1)} %copy-done.7, bf16[512,2048]{1,0:T(8,128)(2,1)S(1)} %collective-permute-done.5.d_ref.ds_ref, bf16[2,192,2048]{2,1,0:T(8,128)(2,1)S(1)} %collective-permute-done.wa_ref, ...), custom_call_target="tpu_custom_call" | custom-call | tf_op jit(solution)/shard_map/expert/expert/pallas_call | solution.py:247
  151.7 4.4 %down_grads.1 = (bf16[1,192,2048]{2,1,0:T(8,128)(2,1)S(1)}, bf16[1,192,2048]{2,1,0:T(8,128)(2,1)S(1)}) custom-call(bf16[512,2048]{1,0:T(8,128)(2,1)} %bitcast.11.d_ref.do_ref, bf16[512,2048]{1,0:T(8,128)(2,1)S(1)} %collective-permute-done.5.d_ref.ds_ref, bf16[512,384]{1,0:T(8,128)(2,1)S(1)} %copy-done.13, bf16[512,384]{1,0:T(8,128)(2,1)S(1)} %copy-done.15), custom_call_target="tpu_custom_call" | custom-call | tf_op jit(solution)/shard_map/weights_back/down_grads/pallas_call | solution.py:261
  159.8 5.2 %all-to-all-start.2 = ((bf16[32,16,2176]{2,1,0:T(8,128)(2,1)}), bf16[32,16,2176]{2,1,0:T(8,128)(2,1)S(1)}, u32[]{:S(2)}, u32[]{:S(2)}) async-start(bf16[32,16,2176]{2,1,0:T(8,128)(2,1)} %bitcast.22), calls=%async_computation.2 | async-start | bytes 4456448 | tf_op jit(solution)/shard_map/tokens_back/all_to_all | solution.py:180
  165.0 3.6 %collective-permute-start.7 = (bf16[1,192,2048]{2,1,0:T(8,128)(2,1)}, bf16[1,192,2048]{2,1,0:T(8,128)(2,1)S(1)}, u32[]{:S(2)}, u32[]{:S(2)}) collective-permute-start(bf16[1,192,2048]{2,1,0:T(8,128)(2,1)} %copy-done.17), channel_id=1, source_target_pairs={{0,0},{1,1},{4,2},{5,3},{2,4},{3,5},{6,6},{7,7},{8,8},{9,9},{12,10... | collective-permute-start | bytes 2359304 | tf_op jit(solution)/shard_map/weights_back/ppermute | solution.py:259
  168.7 7.5 %gate_up_grads.1 = (bf16[2,192,2048]{2,1,0:T(8,128)(2,1)}, bf16[2,192,2048]{2,1,0:T(8,128)(2,1)}) custom-call(bf16[512,2176]{1,0:T(8,128)(2,1)} %bitcast.8.x_ref.xo_ref, bf16[512,2176]{1,0:T(8,128)(2,1)} %copy-done, bf16[2,512,384]{2,1,0:T(8,128)(2,1)} %copy-done.10, bf16[2,512,384]{2,1,0:T(8,128)(2,1)} %copy-done.11), custom_call_target="tpu_custom_call" | custom-call | tf_op jit(solution)/shard_map/weights_back/gate_up_grads/pallas_call | solution.py:275
  176.3 10.0 %collective-permute-done.7.da_ref = bf16[1,192,2048]{2,1,0:T(8,128)(2,1)S(1)} collective-permute-done((bf16[1,192,2048]{2,1,0:T(8,128)(2,1)}, bf16[1,192,2048]{2,1,0:T(8,128)(2,1)S(1)}, u32[]{:S(2)}, u32[]{:S(2)}) %collective-permute-start.7) | collective-permute-done | bytes 786464 | tf_op jit(solution)/shard_map/weights_back/ppermute | solution.py:259
  186.2 3.3 %collective-permute-done.8.db_ref = bf16[1,192,2048]{2,1,0:T(8,128)(2,1)} collective-permute-done((bf16[1,192,2048]{2,1,0:T(8,128)(2,1)}, bf16[1,192,2048]{2,1,0:T(8,128)(2,1)}, u32[]{:S(2)}, u32[]{:S(2)}) %collective-permute-start.8) | collective-permute-done | bytes 786464 | tf_op jit(solution)/shard_map/weights_back/ppermute | solution.py:259
  192.6 23.7 %all-to-all-done.2 = bf16[32,16,2176]{2,1,0:T(8,128)(2,1)S(1)} async-done(((bf16[32,16,2176]{2,1,0:T(8,128)(2,1)}), bf16[32,16,2176]{2,1,0:T(8,128)(2,1)S(1)}, u32[]{:S(2)}, u32[]{:S(2)}) %all-to-all-start.2) | async-done | bytes 2228256 | tf_op jit(solution)/shard_map/tokens_back/all_to_all | solution.py:180
  218.2 3.5 %all-to-all-start.3 = ((bf16[4,144,512]{2,1,0:T(8,128)(2,1)}), bf16[4,144,512]{2,1,0:T(8,128)(2,1)S(1)}, u32[]{:S(2)}, u32[]{:S(2)}) async-start(bf16[4,144,512]{2,1,0:T(8,128)(2,1)} %combine.1), calls=%async_computation.3 | async-start | bytes 1179648 | tf_op jit(solution)/shard_map/tokens_back/all_to_all | solution.py:308
  223.9 7.6 %collective-permute-done.10.b_ref = bf16[2,192,2048]{2,1,0:T(8,128)(2,1)} collective-permute-done((bf16[2,192,2048]{2,1,0:T(8,128)(2,1)}, bf16[2,192,2048]{2,1,0:T(8,128)(2,1)}, u32[]{:S(2)}, u32[]{:S(2)}) %collective-permute-start.10) | collective-permute-done | bytes 1572896 | tf_op jit(solution)/shard_map/weights_back/ppermute | solution.py:259
  231.5 4.8 %place.1 = (bf16[2,192,2048]{2,1,0:T(8,128)(2,1)}, bf16[2,192,2048]{2,1,0:T(8,128)(2,1)}, bf16[2,192,2048]{2,1,0:T(8,128)(2,1)}) custom-call(s32[4]{0:T(128)S(1)} %pad_add_fusion.at_ref, bf16[1,192,2048]{2,1,0:T(8,128)(2,1)S(1)} %collective-permute-done.7.da_ref, bf16[1,192,2048]{2,1,0:T(8,128)(2,1)} %collective-permute-done.8.db_ref, ...), custom_call_target="tpu_custom_call" | custom-call | tf_op jit(solution)/shard_map/weights_back/place/pallas_call | solution.py:288
  (73 shorter events, 39.7 us)
Async XLA Ops:
  17.4 11.5 %copy-start.20 = (bf16[128,512]{1,0:T(8,128)(2,1)S(1)}, bf16[128,512]{1,0:T(8,128)(2,1)}, u32[]{:S(2)}) copy-start(bf16[128,512]{1,0:T(8,128)(2,1)} %param.8) | copy-start | bytes 393220
  17.4 21.8 %copy-start.19 = (bf16[2,192,2048]{2,1,0:T(8,128)(2,1)S(1)}, bf16[2,192,2048]{2,1,0:T(8,128)(2,1)}, u32[]{:S(2)}) copy-start(bf16[2,192,2048]{2,1,0:T(8,128)(2,1)} %param.12) | copy-start | bytes 4718596
  17.4 62.8 %all-to-all-start = ((bf16[32,16,2176]{2,1,0:T(8,128)(2,1)}), bf16[32,16,2176]{2,1,0:T(8,128)(2,1)}, u32[]{:S(2)}, u32[]{:S(2)}) async-start(bf16[32,16,2176]{2,1,0:T(8,128)(2,1)} %bitcast.7), calls=%async_computation | async-start | bytes 4456448 | tf_op jit(solution)/shard_map/select_x/all_to_all | solution.py:180
  42.0 26.2 %collective-permute-start = (bf16[2,192,2048]{2,1,0:T(8,128)(2,1)S(1)}, bf16[2,192,2048]{2,1,0:T(8,128)(2,1)S(1)}, u32[]{:S(2)}, u32[]{:S(2)}) collective-permute-start(bf16[2,192,2048]{2,1,0:T(8,128)(2,1)S(1)} %pad_maximum_fusion), channel_id=1, source_target_pairs={{0,0},{1,1},{2,4},{3,5},{4,2},{5,3},{6,6},{7,7},{8,8},{9,9},{10,12... | collective-permute-start | bytes 4718600 | tf_op jit(solution)/shard_map/weights_out/ppermute | solution.py:206
  80.3 53.8 %all-to-all-start.1 = ((bf16[32,16,2048]{2,1,0:T(8,128)(2,1)}), bf16[32,16,2048]{2,1,0:T(8,128)(2,1)}, u32[]{:S(2)}, u32[]{:S(2)}) async-start(bf16[32,16,2048]{2,1,0:T(8,128)(2,1)} %bitcast.19), calls=%async_computation.1 | async-start | bytes 4194304 | tf_op jit(solution)/shard_map/gates/all_to_all | solution.py:180
  85.9 40.1 %collective-permute-start.2 = (bf16[512,2176]{1,0:T(8,128)(2,1)}, bf16[512,2176]{1,0:T(8,128)(2,1)S(1)}, u32[]{:S(2)}, u32[]{:S(2)}) collective-permute-start(bf16[512,2176]{1,0:T(8,128)(2,1)} %bitcast.8.x_ref.xo_ref), channel_id=1, source_target_pairs={{0,4},{4,0},{1,5},{5,1},{2,6},{6,2},{3,7},{7,3},{8,12},{12,8},{9,1... | collective-permute-start | bytes 6684680 | tf_op jit(solution)/shard_map/gates/ppermute | solution.py:221
  89.0 2.3 copy-start.18
  90.4 30.0 %collective-permute-start.1 = (bf16[2,192,2048]{2,1,0:T(8,128)(2,1)S(1)}, bf16[2,192,2048]{2,1,0:T(8,128)(2,1)S(1)}, u32[]{:S(2)}, u32[]{:S(2)}) collective-permute-start(bf16[2,192,2048]{2,1,0:T(8,128)(2,1)S(1)} %pad_maximum_fusion.1), channel_id=1, source_target_pairs={{0,1},{1,0},{2,5},{3,4},{4,3},{5,2},{6,7},{7,6},{8,9},{9,8},{10,13... | collective-permute-start | bytes 4718600 | tf_op jit(solution)/shard_map/weights_out/ppermute | solution.py:206
  91.4 39.2 %collective-permute-start.4 = (bf16[1,192,2048]{2,1,0:T(8,128)(2,1)S(1)}, bf16[1,192,2048]{2,1,0:T(8,128)(2,1)S(1)}, u32[]{:S(2)}, u32[]{:S(2)}) collective-permute-start(bf16[1,192,2048]{2,1,0:T(8,128)(2,1)S(1)} %get-tuple-element.105), channel_id=1, source_target_pairs={{0,1},{1,0},{2,5},{3,4},{4,3},{5,2},{6,7},{7,6},{8,9},{9,8},{10,13... | collective-permute-start | bytes 2359304 | tf_op jit(solution)/shard_map/weights_out/ppermute | solution.py:206
  93.7 37.8 %collective-permute-start.3 = (bf16[1,192,2048]{2,1,0:T(8,128)(2,1)S(1)}, bf16[1,192,2048]{2,1,0:T(8,128)(2,1)S(1)}, u32[]{:S(2)}, u32[]{:S(2)}) collective-permute-start(bf16[1,192,2048]{2,1,0:T(8,128)(2,1)S(1)} %get-tuple-element.106), channel_id=1, source_target_pairs={{0,0},{1,1},{2,4},{3,5},{4,2},{5,3},{6,6},{7,7},{8,8},{9,9},{10,12... | collective-permute-start | bytes 2359304 | tf_op jit(solution)/shard_map/weights_out/ppermute | solution.py:206
  126.0 2.5 %copy-start.12 = (bf16[512,384]{1,0:T(8,128)(2,1)}, bf16[512,384]{1,0:T(8,128)(2,1)S(1)}, u32[]{:S(2)}) copy-start(bf16[512,384]{1,0:T(8,128)(2,1)S(1)} %get-tuple-element.83.ho_ref) | copy-start | bytes 1179652
  126.0 2.5 %copy-start = (bf16[512,2176]{1,0:T(8,128)(2,1)}, bf16[512,2176]{1,0:T(8,128)(2,1)S(1)}, u32[]{:S(2)}) copy-start(bf16[512,2176]{1,0:T(8,128)(2,1)S(1)} %collective-permute-done.2.x_ref.xs_ref) | copy-start | bytes 6684676
  134.1 13.5 %collective-permute-start.5 = (bf16[512,2048]{1,0:T(8,128)(2,1)}, bf16[512,2048]{1,0:T(8,128)(2,1)S(1)}, u32[]{:S(2)}, u32[]{:S(2)}) collective-permute-start(bf16[512,2048]{1,0:T(8,128)(2,1)} %bitcast.11.d_ref.do_ref), channel_id=1, source_target_pairs={{0,4},{4,0},{1,5},{5,1},{2,6},{6,2},{3,7},{7,3},{8,12},{12,8},{9,1... | collective-permute-start | bytes 6291464 | tf_op jit(solution)/shard_map/expert/ppermute | solution.py:236
  141.4 6.1 %copy-start.7 = (f32[3,512,384]{2,1,0:T(8,128)S(1)}, f32[3,512,384]{2,1,0:T(8,128)}, u32[]{:S(2)}) copy-start(f32[3,512,384]{2,1,0:T(8,128)} %copy-done.6) | copy-start | bytes 7077892
  147.5 4.1 %copy-start.13 = (bf16[512,384]{1,0:T(8,128)(2,1)S(1)}, bf16[512,384]{1,0:T(8,128)(2,1)}, u32[]{:S(2)}) copy-start(bf16[512,384]{1,0:T(8,128)(2,1)} %copy-done.12) | copy-start | bytes 1179652
  147.5 4.1 %copy-start.15 = (bf16[512,384]{1,0:T(8,128)(2,1)S(1)}, bf16[512,384]{1,0:T(8,128)(2,1)}, u32[]{:S(2)}) copy-start(bf16[512,384]{1,0:T(8,128)(2,1)} %copy-done.14) | copy-start | bytes 1179652
  151.6 4.5 %copy-start.11 = (bf16[2,512,384]{2,1,0:T(8,128)(2,1)}, bf16[2,512,384]{2,1,0:T(8,128)(2,1)S(1)}, u32[]{:S(2)}) copy-start(bf16[2,512,384]{2,1,0:T(8,128)(2,1)S(1)} %get-tuple-element.93.ks_ref) | copy-start | bytes 2359300
  151.6 6.3 %collective-permute-start.6 = (bf16[512,2176]{1,0:T(8,128)(2,1)S(1)}, bf16[512,2176]{1,0:T(8,128)(2,1)S(1)}, u32[]{:S(2)}, u32[]{:S(2)}) collective-permute-start(bf16[512,2176]{1,0:T(8,128)(2,1)S(1)} %get-tuple-element.87), channel_id=1, source_target_pairs={{0,4},{4,0},{1,5},{5,1},{2,6},{6,2},{3,7},{7,3},{8,12},{12,8},{9,1... | collective-permute-start | bytes 6684680 | tf_op jit(solution)/shard_map/expert/ppermute | solution.py:249
  159.8 56.5 %all-to-all-start.2 = ((bf16[32,16,2176]{2,1,0:T(8,128)(2,1)}), bf16[32,16,2176]{2,1,0:T(8,128)(2,1)S(1)}, u32[]{:S(2)}, u32[]{:S(2)}) async-start(bf16[32,16,2176]{2,1,0:T(8,128)(2,1)} %bitcast.22), calls=%async_computation.2 | async-start | bytes 4456448 | tf_op jit(solution)/shard_map/tokens_back/all_to_all | solution.py:180
  165.0 21.2 %collective-permute-start.7 = (bf16[1,192,2048]{2,1,0:T(8,128)(2,1)}, bf16[1,192,2048]{2,1,0:T(8,128)(2,1)S(1)}, u32[]{:S(2)}, u32[]{:S(2)}) collective-permute-start(bf16[1,192,2048]{2,1,0:T(8,128)(2,1)} %copy-done.17), channel_id=1, source_target_pairs={{0,0},{1,1},{4,2},{5,3},{2,4},{3,5},{6,6},{7,7},{8,8},{9,9},{12,10... | collective-permute-start | bytes 2359304 | tf_op jit(solution)/shard_map/weights_back/ppermute | solution.py:259
  168.6 20.9 %collective-permute-start.8 = (bf16[1,192,2048]{2,1,0:T(8,128)(2,1)}, bf16[1,192,2048]{2,1,0:T(8,128)(2,1)}, u32[]{:S(2)}, u32[]{:S(2)}) collective-permute-start(bf16[1,192,2048]{2,1,0:T(8,128)(2,1)} %copy-done.16), channel_id=1, source_target_pairs={{1,0},{0,1},{5,2},{4,3},{3,4},{2,5},{7,6},{6,7},{9,8},{8,9},{13,10... | collective-permute-start | bytes 2359304 | tf_op jit(solution)/shard_map/weights_back/ppermute | solution.py:259
  189.6 34.4 %collective-permute-start.9 = (bf16[2,192,2048]{2,1,0:T(8,128)(2,1)}, bf16[2,192,2048]{2,1,0:T(8,128)(2,1)}, u32[]{:S(2)}, u32[]{:S(2)}) collective-permute-start(bf16[2,192,2048]{2,1,0:T(8,128)(2,1)} %get-tuple-element.100), channel_id=1, source_target_pairs={{0,0},{1,1},{4,2},{5,3},{2,4},{3,5},{6,6},{7,7},{8,8},{9,9},{12,10... | collective-permute-start | bytes 4718600 | tf_op jit(solution)/shard_map/weights_back/ppermute | solution.py:259
  192.3 39.3 %collective-permute-start.10 = (bf16[2,192,2048]{2,1,0:T(8,128)(2,1)}, bf16[2,192,2048]{2,1,0:T(8,128)(2,1)}, u32[]{:S(2)}, u32[]{:S(2)}) collective-permute-start(bf16[2,192,2048]{2,1,0:T(8,128)(2,1)} %get-tuple-element.101), channel_id=1, source_target_pairs={{1,0},{0,1},{5,2},{4,3},{3,4},{2,5},{7,6},{6,7},{9,8},{8,9},{13,10... | collective-permute-start | bytes 4718600 | tf_op jit(solution)/shard_map/weights_back/ppermute | solution.py:259
  218.2 18.2 %all-to-all-start.3 = ((bf16[4,144,512]{2,1,0:T(8,128)(2,1)}), bf16[4,144,512]{2,1,0:T(8,128)(2,1)S(1)}, u32[]{:S(2)}, u32[]{:S(2)}) async-start(bf16[4,144,512]{2,1,0:T(8,128)(2,1)} %combine.1), calls=%async_computation.3 | async-start | bytes 1179648 | tf_op jit(solution)/shard_map/tokens_back/all_to_all | solution.py:308
  (12 other events, 13.4 us)

commit v10 on v9

--- a/solution.py
+++ b/solution.py
@@ -18,6 +18,7 @@
 WIDE = D + 128
 FQ = 192
 FH = 2 * FQ
+COST = 100_000_000_000
 VMEM = pl.BlockSpec(memory_space=pltpu.VMEM)
 SMEM = pl.BlockSpec(memory_space=pltpu.SMEM)
 
@@ -200,8 +201,11 @@
     with jax.named_scope("weights_out"):
         dg, *mats = lax.optimization_barrier((dg, w_gate, w_up, w_down))
         weights = []
-        for m, which in ((0, mats[:2]), (1, mats[:2]), (0, mats[2:]), (1, mats[2:])):
+        for m in (0, 1, 0, 1):
             k = (ix + m) % 2
+            if len(weights) == 2:
+                *mats, weights[1] = lax.optimization_barrier((*mats, weights[1]))
+            which = mats[2:] if len(weights) > 1 else mats[:2]
             piece = jnp.stack([lax.dynamic_index_in_dim(w, k, 0, keepdims=False) for w in which])
             weights.append(lax.ppermute(piece, ("c", "x"), weight_pairs(m)))
 
@@ -272,6 +276,7 @@
         home_again(pieces)
         total = (part_own.astype(F32) + sent.astype(F32)).astype(BF)
         total, keep_own, keep_sib = lax.optimization_barrier((total, keep_own, keep_sib))
+        back[0], back[1], keep_own, keep_sib = lax.optimization_barrier((back[0], back[1], keep_own, keep_sib))
         pieces = pl.pallas_call(
             gate_up_grads,
             grid=(NX,),
@@ -279,10 +284,10 @@
             in_specs=[cut, cut, k_spec, k_spec],
             out_specs=(pl.BlockSpec((2, FQ, Q), lambda h: (0, 0, h)),) * 2,
             scratch_shapes=[pltpu.VMEM((2, FH, 2 * ROWS), BF)],
+            cost_estimate=pl.CostEstimate(flops=COST, bytes_accessed=COST // 100, transcendentals=0),
             compiler_params=params(60),
             name="gate_up_grads",
         )(x_own, x_sib, keep_own, keep_sib)
-        *pieces, back[0], back[1] = lax.optimization_barrier((*pieces, back[0], back[1]))
         home_again(pieces)
         part_rows = FQ // 4
         grad_gate, grad_up, grad_down = pl.pallas_call(

time: 240 us -> 239 us (level)
    ppermute x4, waiting for transfers between devices: 23.2 us -> 18.1 us  [home_again(): lax.ppermute(piece, ('c', 'x'), [(b, a) for a, b in weight_pairs(m)])]
    all_to_all x3, waiting for transfers between devices: 37.4 us -> 42.1 us  [to_experts(): lax.all_to_all(rows, ('y', 'z'), split_axis=0, concat_axis=0, tiled=True)]
    ppermute x4, starting transfers between devices: 13.1 us -> 16.6 us  [per_device(): weights.append(lax.ppermute(piece, ('c', 'x'), weight_pairs(m)))]
    ppermute x1, starting transfers between devices: 3.17 us -> 0.01 us  [per_device(): x_sib = lax.ppermute(x_own, 'c', sib)]
    unnamed x42 -> x40, local copies, waits for them, and re-layouts: 13.4 us -> 12.4 us
  transfers between devices with their start and end apart: 15 -> 15, of which waited for: 9 -> 10; matrix products, arithmetic and copies ran while one was open for 2% -> 2% of each run, Pallas kernels for 13% -> 13%
where the time goes in v10:
time: 239 us; the launch traced here: 237 us
  waiting for transfers between devices  102 us (43%)
  starting transfers between devices  52.6 us (22%)
  Pallas kernels  38.6 us (16%)
  blocking collectives  22.8 us (10%)
  local copies, waits for them, and re-layouts  15.1 us (6%)
  other arithmetic  5.13 us (2%)
    all_to_all x3, waiting for transfers between devices, to_experts(): lax.all_to_all(rows, ('y', 'z'), split_axis=0, concat_axis=0, tiled=True)  42.1 us
    ppermute x4, waiting for transfers between devices, per_device(): weights.append(lax.ppermute(piece, ('c', 'x'), weight_pairs(m)))  40.2 us
    all_to_all x3, starting transfers between devices, to_experts(): lax.all_to_all(rows, ('y', 'z'), split_axis=0, concat_axis=0, tiled=True)  22.4 us
    ppermute x4, waiting for transfers between devices, home_again(): lax.ppermute(piece, ('c', 'x'), [(b, a) for a, b in weight_pairs(m)])  18.1 us
    ppermute x4, starting transfers between devices, per_device(): weights.append(lax.ppermute(piece, ('c', 'x'), weight_pairs(m)))  16.6 us
    all_gather x1, blocking collectives, per_device(): xg = lax.all_gather(tokens, 'x', axis=0, tiled=False)  12.5 us
    unnamed x40, local copies, waits for them, and re-layouts  12.4 us
    all_gather x1, blocking collectives, per_device(): dg = lax.all_gather(cotangent, 'x', axis=0, tiled=False)  10.3 us
  transfers between devices with their start and end apart: 15, of which 10 were waited for; matrix products, arithmetic and copies ran while one was open for 2% of the time, Pallas kernels for 13%

profile of v10, /device:TPU:1, one launch (start us, length us, event | category | flops | bytes accessed | tf_op | source)
XLA Modules:
  0.0 236.8 jit_solution(7337242598244340857)
XLA Ops:
  2.0 12.5 %all-gather = bf16[512,512]{1,0:T(8,128)(2,1)S(1)} all-gather(bf16[128,512]{1,0:T(8,128)(2,1)} %param.7), channel_id=2, replica_groups=mesh['y'=4,'z'=8,'c'=2,'x'=4] {'x'}, dimensions={0}, use_global_device_ids=true | all-gather | bytes 655360 | tf_op jit(solution)/shard_map/select_x/all_gather | solution.py:185
  17.4 11.5 %all-to-all-start = ((bf16[32,16,2176]{2,1,0:T(8,128)(2,1)}), bf16[32,16,2176]{2,1,0:T(8,128)(2,1)}, u32[]{:S(2)}, u32[]{:S(2)}) async-start(bf16[32,16,2176]{2,1,0:T(8,128)(2,1)} %bitcast.7), calls=%async_computation | async-start | bytes 4456448 | tf_op jit(solution)/shard_map/select_x/all_to_all | solution.py:181
  28.9 10.3 %all-gather.1 = bf16[512,512]{1,0:T(8,128)(2,1)S(1)} all-gather(bf16[128,512]{1,0:T(8,128)(2,1)S(1)} %copy-done.19), channel_id=3, replica_groups=mesh['y'=4,'z'=8,'c'=2,'x'=4] {'x'}, dimensions={0}, use_global_device_ids=true | all-gather | bytes 655360 | tf_op jit(solution)/shard_map/select_d/all_gather | solution.py:199
  42.0 8.1 %collective-permute-start = (bf16[2,192,2048]{2,1,0:T(8,128)(2,1)S(1)}, bf16[2,192,2048]{2,1,0:T(8,128)(2,1)S(1)}, u32[]{:S(2)}, u32[]{:S(2)}) collective-permute-start(bf16[2,192,2048]{2,1,0:T(8,128)(2,1)S(1)} %pad_maximum_fusion), channel_id=1, source_target_pairs={{0,0},{1,1},{2,4},{3,5},{4,2},{5,3},{6,6},{7,7},{8,8},{9,9},{10,12... | collective-permute-start | bytes 4718600 | tf_op jit(solution)/shard_map/weights_out/ppermute | solution.py:210
  52.3 16.0 %collective-permute-done.wa_ref = bf16[2,192,2048]{2,1,0:T(8,128)(2,1)S(1)} collective-permute-done((bf16[2,192,2048]{2,1,0:T(8,128)(2,1)S(1)}, bf16[2,192,2048]{2,1,0:T(8,128)(2,1)S(1)}, u32[]{:S(2)}, u32[]{:S(2)}) %collective-permute-start) | collective-permute-done | bytes 1572896 | tf_op jit(solution)/shard_map/weights_out/ppermute | solution.py:210
  68.2 12.0 %all-to-all-done = bf16[32,16,2176]{2,1,0:T(8,128)(2,1)} async-done(((bf16[32,16,2176]{2,1,0:T(8,128)(2,1)}), bf16[32,16,2176]{2,1,0:T(8,128)(2,1)}, u32[]{:S(2)}, u32[]{:S(2)}) %all-to-all-start) | async-done | bytes 2228256 | tf_op jit(solution)/shard_map/select_x/all_to_all | solution.py:181
  80.3 5.7 %all-to-all-start.1 = ((bf16[32,16,2048]{2,1,0:T(8,128)(2,1)}), bf16[32,16,2048]{2,1,0:T(8,128)(2,1)}, u32[]{:S(2)}, u32[]{:S(2)}) async-start(bf16[32,16,2048]{2,1,0:T(8,128)(2,1)} %bitcast.19), calls=%async_computation.1 | async-start | bytes 4194304 | tf_op jit(solution)/shard_map/gates/all_to_all | solution.py:181
  86.2 3.9 %collective-permute-start.1 = (bf16[2,192,2048]{2,1,0:T(8,128)(2,1)S(1)}, bf16[2,192,2048]{2,1,0:T(8,128)(2,1)S(1)}, u32[]{:S(2)}, u32[]{:S(2)}) collective-permute-start(bf16[2,192,2048]{2,1,0:T(8,128)(2,1)S(1)} %pad_maximum_fusion.1), channel_id=1, source_target_pairs={{0,1},{1,0},{2,5},{3,4},{4,3},{5,2},{6,7},{7,6},{8,9},{9,8},{10,13... | collective-permute-start | bytes 4718600 | tf_op jit(solution)/shard_map/weights_out/ppermute | solution.py:210
  90.1 18.5 %collective-permute-done.1.wb_ref = bf16[2,192,2048]{2,1,0:T(8,128)(2,1)S(1)} collective-permute-done((bf16[2,192,2048]{2,1,0:T(8,128)(2,1)S(1)}, bf16[2,192,2048]{2,1,0:T(8,128)(2,1)S(1)}, u32[]{:S(2)}, u32[]{:S(2)}) %collective-permute-start.1) | collective-permute-done | bytes 1572896 | tf_op jit(solution)/shard_map/weights_out/ppermute | solution.py:210
  113.3 4.1 %gates.2 = (f32[3,512,384]{2,1,0:T(8,128)S(1)}, bf16[512,384]{1,0:T(8,128)(2,1)S(1)}) custom-call(bf16[512,2176]{1,0:T(8,128)(2,1)} %bitcast.8.x_ref.xo_ref, bf16[2,192,2048]{2,1,0:T(8,128)(2,1)S(1)} %collective-permute-done.wa_ref, bf16[2,192,2048]{2,1,0:T(8,128)(2,1)S(1)} %collective-permute-done.1.wb_ref), custom_call_target="tpu_custom_call" | custom-call | tf_op jit(solution)/shard_map/gates/gates/pallas_call | solution.py:234
  124.3 5.8 %collective-permute-done.4.db_ref = bf16[1,192,2048]{2,1,0:T(8,128)(2,1)S(1)} collective-permute-done((bf16[1,192,2048]{2,1,0:T(8,128)(2,1)S(1)}, bf16[1,192,2048]{2,1,0:T(8,128)(2,1)S(1)}, u32[]{:S(2)}, u32[]{:S(2)}) %collective-permute-start.4) | collective-permute-done | bytes 786464 | tf_op jit(solution)/shard_map/weights_out/ppermute | solution.py:210
  134.2 3.4 %collective-permute-start.5 = (bf16[512,2048]{1,0:T(8,128)(2,1)}, bf16[512,2048]{1,0:T(8,128)(2,1)S(1)}, u32[]{:S(2)}, u32[]{:S(2)}) collective-permute-start(bf16[512,2048]{1,0:T(8,128)(2,1)} %bitcast.11.d_ref.do_ref), channel_id=1, source_target_pairs={{0,4},{4,0},{1,5},{5,1},{2,6},{6,2},{3,7},{7,3},{8,12},{12,8},{9,1... | collective-permute-start | bytes 6291464 | tf_op jit(solution)/shard_map/expert/ppermute | solution.py:240
  141.5 5.2 %expert.2 = (bf16[512,2176]{1,0:T(8,128)(2,1)S(1)}, bf16[2,512,384]{2,1,0:T(8,128)(2,1)S(1)}) custom-call(s32[4]{0:T(128)S(1)} %pad_add_fusion.at_ref, f32[3,512,384]{2,1,0:T(8,128)S(1)} %copy-done.8, bf16[512,2048]{1,0:T(8,128)(2,1)} %bitcast.11.d_ref.do_ref, bf16[2,192,2048]{2,1,0:T(8,128)(2,1)S(1)} %collective-permute-done.wa_ref, ...), custom_call_target="tpu_custom_call" | custom-call | tf_op jit(solution)/shard_map/expert/expert/pallas_call | solution.py:249
  147.7 4.0 %expert.3 = (bf16[512,2176]{1,0:T(8,128)(2,1)S(1)}, bf16[2,512,384]{2,1,0:T(8,128)(2,1)S(1)}) custom-call(s32[4]{0:T(128)S(1)} %pad_add_fusion.at_ref, f32[3,512,384]{2,1,0:T(8,128)S(1)} %copy-done.6, bf16[512,2048]{1,0:T(8,128)(2,1)S(1)} %collective-permute-done.5.d_ref.ds_ref, bf16[2,192,2048]{2,1,0:T(8,128)(2,1)S(1)} %collective-permute-done.wa_ref, ...), custom_call_target="tpu_custom_call" | custom-call | tf_op jit(solution)/shard_map/expert/expert/pallas_call | solution.py:251
  151.8 5.1 %down_grads.1 = (bf16[1,192,2048]{2,1,0:T(8,128)(2,1)}, bf16[1,192,2048]{2,1,0:T(8,128)(2,1)}) custom-call(bf16[512,2048]{1,0:T(8,128)(2,1)} %bitcast.11.d_ref.do_ref, bf16[512,2048]{1,0:T(8,128)(2,1)S(1)} %collective-permute-done.5.d_ref.ds_ref, bf16[512,384]{1,0:T(8,128)(2,1)S(1)} %copy-done.11, bf16[512,384]{1,0:T(8,128)(2,1)S(1)} %copy-done.13), custom_call_target="tpu_custom_call" | custom-call | tf_op jit(solution)/shard_map/weights_back/down_grads/pallas_call | solution.py:265
  156.9 3.3 %collective-permute-start.7 = (bf16[1,192,2048]{2,1,0:T(8,128)(2,1)}, bf16[1,192,2048]{2,1,0:T(8,128)(2,1)S(1)}, u32[]{:S(2)}, u32[]{:S(2)}) collective-permute-start(bf16[1,192,2048]{2,1,0:T(8,128)(2,1)} %get-tuple-element.96), channel_id=1, source_target_pairs={{0,0},{1,1},{4,2},{5,3},{2,4},{3,5},{6,6},{7,7},{8,8},{9,9},{12,10... | collective-permute-start | bytes 2359304 | tf_op jit(solution)/shard_map/weights_back/ppermute | solution.py:263
  162.3 5.2 %all-to-all-start.2 = ((bf16[32,16,2176]{2,1,0:T(8,128)(2,1)}), bf16[32,16,2176]{2,1,0:T(8,128)(2,1)S(1)}, u32[]{:S(2)}, u32[]{:S(2)}) async-start(bf16[32,16,2176]{2,1,0:T(8,128)(2,1)} %bitcast.22), calls=%async_computation.2 | async-start | bytes 4456448 | tf_op jit(solution)/shard_map/tokens_back/all_to_all | solution.py:181
  167.5 10.8 %collective-permute-done.7.da_ref = bf16[1,192,2048]{2,1,0:T(8,128)(2,1)S(1)} collective-permute-done((bf16[1,192,2048]{2,1,0:T(8,128)(2,1)}, bf16[1,192,2048]{2,1,0:T(8,128)(2,1)S(1)}, u32[]{:S(2)}, u32[]{:S(2)}) %collective-permute-start.7) | collective-permute-done | bytes 786464 | tf_op jit(solution)/shard_map/weights_back/ppermute | solution.py:263
  178.3 3.1 %collective-permute-done.8.db_ref = bf16[1,192,2048]{2,1,0:T(8,128)(2,1)} collective-permute-done((bf16[1,192,2048]{2,1,0:T(8,128)(2,1)}, bf16[1,192,2048]{2,1,0:T(8,128)(2,1)}, u32[]{:S(2)}, u32[]{:S(2)}) %collective-permute-start.8) | collective-permute-done | bytes 786464 | tf_op jit(solution)/shard_map/weights_back/ppermute | solution.py:263
  181.3 7.5 %gate_up_grads.1 = (bf16[2,192,2048]{2,1,0:T(8,128)(2,1)}, bf16[2,192,2048]{2,1,0:T(8,128)(2,1)}) custom-call(bf16[512,2176]{1,0:T(8,128)(2,1)} %bitcast.8.x_ref.xo_ref, bf16[512,2176]{1,0:T(8,128)(2,1)} %copy-done.9, bf16[2,512,384]{2,1,0:T(8,128)(2,1)} %copy-done.14, bf16[2,512,384]{2,1,0:T(8,128)(2,1)} %copy-done.15), custom_call_target="tpu_custom_call" | custom-call | flops 99999997952 | bytes 1000000000 | tf_op jit(solution)/shard_map/weights_back/gate_up_grads/pallas_call | solution.py:280
  192.1 27.6 %all-to-all-done.2 = bf16[32,16,2176]{2,1,0:T(8,128)(2,1)S(1)} async-done(((bf16[32,16,2176]{2,1,0:T(8,128)(2,1)}), bf16[32,16,2176]{2,1,0:T(8,128)(2,1)S(1)}, u32[]{:S(2)}, u32[]{:S(2)}) %all-to-all-start.2) | async-done | bytes 2228256 | tf_op jit(solution)/shard_map/tokens_back/all_to_all | solution.py:181
  221.6 3.5 %all-to-all-start.3 = ((bf16[4,144,512]{2,1,0:T(8,128)(2,1)}), bf16[4,144,512]{2,1,0:T(8,128)(2,1)S(1)}, u32[]{:S(2)}, u32[]{:S(2)}) async-start(bf16[4,144,512]{2,1,0:T(8,128)(2,1)} %combine.1), calls=%async_computation.3 | async-start | bytes 1179648 | tf_op jit(solution)/shard_map/tokens_back/all_to_all | solution.py:313
  225.1 4.3 %collective-permute-done.10.b_ref = bf16[2,192,2048]{2,1,0:T(8,128)(2,1)} collective-permute-done((bf16[2,192,2048]{2,1,0:T(8,128)(2,1)}, bf16[2,192,2048]{2,1,0:T(8,128)(2,1)}, u32[]{:S(2)}, u32[]{:S(2)}) %collective-permute-start.10) | collective-permute-done | bytes 1572896 | tf_op jit(solution)/shard_map/weights_back/ppermute | solution.py:263
  229.4 4.8 %place.1 = (bf16[2,192,2048]{2,1,0:T(8,128)(2,1)}, bf16[2,192,2048]{2,1,0:T(8,128)(2,1)}, bf16[2,192,2048]{2,1,0:T(8,128)(2,1)}) custom-call(s32[4]{0:T(128)S(1)} %pad_add_fusion.at_ref, bf16[1,192,2048]{2,1,0:T(8,128)(2,1)S(1)} %collective-permute-done.7.da_ref, bf16[1,192,2048]{2,1,0:T(8,128)(2,1)} %collective-permute-done.8.db_ref, ...), custom_call_target="tpu_custom_call" | custom-call | tf_op jit(solution)/shard_map/weights_back/place/pallas_call | solution.py:293
  (71 shorter events, 39.6 us)
Async XLA Ops:
  17.4 11.5 %copy-start.19 = (bf16[128,512]{1,0:T(8,128)(2,1)S(1)}, bf16[128,512]{1,0:T(8,128)(2,1)}, u32[]{:S(2)}) copy-start(bf16[128,512]{1,0:T(8,128)(2,1)} %param.8) | copy-start | bytes 393220
  17.4 21.8 %copy-start.18 = (bf16[2,192,2048]{2,1,0:T(8,128)(2,1)S(1)}, bf16[2,192,2048]{2,1,0:T(8,128)(2,1)}, u32[]{:S(2)}) copy-start(bf16[2,192,2048]{2,1,0:T(8,128)(2,1)} %param.12) | copy-start | bytes 4718596
  17.4 62.8 %all-to-all-start = ((bf16[32,16,2176]{2,1,0:T(8,128)(2,1)}), bf16[32,16,2176]{2,1,0:T(8,128)(2,1)}, u32[]{:S(2)}, u32[]{:S(2)}) async-start(bf16[32,16,2176]{2,1,0:T(8,128)(2,1)} %bitcast.7), calls=%async_computation | async-start | bytes 4456448 | tf_op jit(solution)/shard_map/select_x/all_to_all | solution.py:181
  42.0 26.2 %collective-permute-start = (bf16[2,192,2048]{2,1,0:T(8,128)(2,1)S(1)}, bf16[2,192,2048]{2,1,0:T(8,128)(2,1)S(1)}, u32[]{:S(2)}, u32[]{:S(2)}) collective-permute-start(bf16[2,192,2048]{2,1,0:T(8,128)(2,1)S(1)} %pad_maximum_fusion), channel_id=1, source_target_pairs={{0,0},{1,1},{2,4},{3,5},{4,2},{5,3},{6,6},{7,7},{8,8},{9,9},{10,12... | collective-permute-start | bytes 4718600 | tf_op jit(solution)/shard_map/weights_out/ppermute | solution.py:210
  80.3 5.7 %copy-start.16 = (bf16[1,192,2048]{2,1,0:T(8,128)(2,1)S(1)}, bf16[1,192,2048]{2,1,0:T(8,128)(2,1)}, u32[]{:S(2)}) copy-start(bf16[1,192,2048]{2,1,0:T(8,128)(2,1)} %get-tuple-element.116) | copy-start | bytes 2359300
  80.3 53.9 %all-to-all-start.1 = ((bf16[32,16,2048]{2,1,0:T(8,128)(2,1)}), bf16[32,16,2048]{2,1,0:T(8,128)(2,1)}, u32[]{:S(2)}, u32[]{:S(2)}) async-start(bf16[32,16,2048]{2,1,0:T(8,128)(2,1)} %bitcast.19), calls=%async_computation.1 | async-start | bytes 4194304 | tf_op jit(solution)/shard_map/gates/all_to_all | solution.py:181
  86.0 22.6 %copy-start.17 = (bf16[2,192,2048]{2,1,0:T(8,128)(2,1)S(1)}, bf16[2,192,2048]{2,1,0:T(8,128)(2,1)}, u32[]{:S(2)}) copy-start(bf16[2,192,2048]{2,1,0:T(8,128)(2,1)} %param.13) | copy-start | bytes 4718596
  86.2 22.4 %collective-permute-start.1 = (bf16[2,192,2048]{2,1,0:T(8,128)(2,1)S(1)}, bf16[2,192,2048]{2,1,0:T(8,128)(2,1)S(1)}, u32[]{:S(2)}, u32[]{:S(2)}) collective-permute-start(bf16[2,192,2048]{2,1,0:T(8,128)(2,1)S(1)} %pad_maximum_fusion.1), channel_id=1, source_target_pairs={{0,1},{1,0},{2,5},{3,4},{4,3},{5,2},{6,7},{7,6},{8,9},{9,8},{10,13... | collective-permute-start | bytes 4718600 | tf_op jit(solution)/shard_map/weights_out/ppermute | solution.py:210
  90.1 29.5 %collective-permute-start.2 = (bf16[512,2176]{1,0:T(8,128)(2,1)}, bf16[512,2176]{1,0:T(8,128)(2,1)S(1)}, u32[]{:S(2)}, u32[]{:S(2)}) collective-permute-start(bf16[512,2176]{1,0:T(8,128)(2,1)} %bitcast.8.x_ref.xo_ref), channel_id=1, source_target_pairs={{0,4},{4,0},{1,5},{5,1},{2,6},{6,2},{3,7},{7,3},{8,12},{12,8},{9,1... | collective-permute-start | bytes 6684680 | tf_op jit(solution)/shard_map/gates/ppermute | solution.py:225
  108.7 21.3 %collective-permute-start.4 = (bf16[1,192,2048]{2,1,0:T(8,128)(2,1)S(1)}, bf16[1,192,2048]{2,1,0:T(8,128)(2,1)S(1)}, u32[]{:S(2)}, u32[]{:S(2)}) collective-permute-start(bf16[1,192,2048]{2,1,0:T(8,128)(2,1)S(1)} %get-tuple-element.109), channel_id=1, source_target_pairs={{0,1},{1,0},{2,5},{3,4},{4,3},{5,2},{6,7},{7,6},{8,9},{9,8},{10,13... | collective-permute-start | bytes 2359304 | tf_op jit(solution)/shard_map/weights_out/ppermute | solution.py:210
  111.4 19.5 %collective-permute-start.3 = (bf16[1,192,2048]{2,1,0:T(8,128)(2,1)S(1)}, bf16[1,192,2048]{2,1,0:T(8,128)(2,1)S(1)}, u32[]{:S(2)}, u32[]{:S(2)}) collective-permute-start(bf16[1,192,2048]{2,1,0:T(8,128)(2,1)S(1)} %get-tuple-element.110), channel_id=1, source_target_pairs={{0,0},{1,1},{2,4},{3,5},{4,2},{5,3},{6,6},{7,7},{8,8},{9,9},{10,12... | collective-permute-start | bytes 2359304 | tf_op jit(solution)/shard_map/weights_out/ppermute | solution.py:210
  119.6 2.5 %copy-start.9 = (bf16[512,2176]{1,0:T(8,128)(2,1)}, bf16[512,2176]{1,0:T(8,128)(2,1)S(1)}, u32[]{:S(2)}) copy-start(bf16[512,2176]{1,0:T(8,128)(2,1)S(1)} %collective-permute-done.2.x_ref.xs_ref) | copy-start | bytes 6684676
  134.2 13.4 %collective-permute-start.5 = (bf16[512,2048]{1,0:T(8,128)(2,1)}, bf16[512,2048]{1,0:T(8,128)(2,1)S(1)}, u32[]{:S(2)}, u32[]{:S(2)}) collective-permute-start(bf16[512,2048]{1,0:T(8,128)(2,1)} %bitcast.11.d_ref.do_ref), channel_id=1, source_target_pairs={{0,4},{4,0},{1,5},{5,1},{2,6},{6,2},{3,7},{7,3},{8,12},{12,8},{9,1... | collective-permute-start | bytes 6291464 | tf_op jit(solution)/shard_map/expert/ppermute | solution.py:240
  141.5 6.1 %copy-start.6 = (f32[3,512,384]{2,1,0:T(8,128)S(1)}, f32[3,512,384]{2,1,0:T(8,128)}, u32[]{:S(2)}) copy-start(f32[3,512,384]{2,1,0:T(8,128)} %copy-done.5) | copy-start | bytes 7077892
  147.7 4.1 %copy-start.11 = (bf16[512,384]{1,0:T(8,128)(2,1)S(1)}, bf16[512,384]{1,0:T(8,128)(2,1)}, u32[]{:S(2)}) copy-start(bf16[512,384]{1,0:T(8,128)(2,1)} %copy-done.10) | copy-start | bytes 1179652
  147.7 4.2 %copy-start.13 = (bf16[512,384]{1,0:T(8,128)(2,1)S(1)}, bf16[512,384]{1,0:T(8,128)(2,1)}, u32[]{:S(2)}) copy-start(bf16[512,384]{1,0:T(8,128)(2,1)} %copy-done.12) | copy-start | bytes 1179652
  151.7 5.3 %copy-start.15 = (bf16[2,512,384]{2,1,0:T(8,128)(2,1)}, bf16[2,512,384]{2,1,0:T(8,128)(2,1)S(1)}, u32[]{:S(2)}) copy-start(bf16[2,512,384]{2,1,0:T(8,128)(2,1)S(1)} %get-tuple-element.103.ks_ref) | copy-start | bytes 2359300
  151.7 5.2 %collective-permute-start.6 = (bf16[512,2176]{1,0:T(8,128)(2,1)S(1)}, bf16[512,2176]{1,0:T(8,128)(2,1)S(1)}, u32[]{:S(2)}, u32[]{:S(2)}) collective-permute-start(bf16[512,2176]{1,0:T(8,128)(2,1)S(1)} %get-tuple-element.91), channel_id=1, source_target_pairs={{0,4},{4,0},{1,5},{5,1},{2,6},{6,2},{3,7},{7,3},{8,12},{12,8},{9,1... | collective-permute-start | bytes 6684680 | tf_op jit(solution)/shard_map/expert/ppermute | solution.py:253
  156.9 21.3 %collective-permute-start.7 = (bf16[1,192,2048]{2,1,0:T(8,128)(2,1)}, bf16[1,192,2048]{2,1,0:T(8,128)(2,1)S(1)}, u32[]{:S(2)}, u32[]{:S(2)}) collective-permute-start(bf16[1,192,2048]{2,1,0:T(8,128)(2,1)} %get-tuple-element.96), channel_id=1, source_target_pairs={{0,0},{1,1},{4,2},{5,3},{2,4},{3,5},{6,6},{7,7},{8,8},{9,9},{12,10... | collective-permute-start | bytes 2359304 | tf_op jit(solution)/shard_map/weights_back/ppermute | solution.py:263
  160.3 21.1 %collective-permute-start.8 = (bf16[1,192,2048]{2,1,0:T(8,128)(2,1)}, bf16[1,192,2048]{2,1,0:T(8,128)(2,1)}, u32[]{:S(2)}, u32[]{:S(2)}) collective-permute-start(bf16[1,192,2048]{2,1,0:T(8,128)(2,1)} %get-tuple-element.97), channel_id=1, source_target_pairs={{1,0},{0,1},{5,2},{4,3},{3,4},{2,5},{7,6},{6,7},{9,8},{8,9},{13,10... | collective-permute-start | bytes 2359304 | tf_op jit(solution)/shard_map/weights_back/ppermute | solution.py:263
  162.3 57.5 %all-to-all-start.2 = ((bf16[32,16,2176]{2,1,0:T(8,128)(2,1)}), bf16[32,16,2176]{2,1,0:T(8,128)(2,1)S(1)}, u32[]{:S(2)}, u32[]{:S(2)}) async-start(bf16[32,16,2176]{2,1,0:T(8,128)(2,1)} %bitcast.22), calls=%async_computation.2 | async-start | bytes 4456448 | tf_op jit(solution)/shard_map/tokens_back/all_to_all | solution.py:181
  188.8 36.3 %collective-permute-start.9 = (bf16[2,192,2048]{2,1,0:T(8,128)(2,1)}, bf16[2,192,2048]{2,1,0:T(8,128)(2,1)}, u32[]{:S(2)}, u32[]{:S(2)}) collective-permute-start(bf16[2,192,2048]{2,1,0:T(8,128)(2,1)} %get-tuple-element.104), channel_id=1, source_target_pairs={{0,0},{1,1},{4,2},{5,3},{2,4},{3,5},{6,6},{7,7},{8,8},{9,9},{12,10... | collective-permute-start | bytes 4718600 | tf_op jit(solution)/shard_map/weights_back/ppermute | solution.py:263
  191.5 37.9 %collective-permute-start.10 = (bf16[2,192,2048]{2,1,0:T(8,128)(2,1)}, bf16[2,192,2048]{2,1,0:T(8,128)(2,1)}, u32[]{:S(2)}, u32[]{:S(2)}) collective-permute-start(bf16[2,192,2048]{2,1,0:T(8,128)(2,1)} %get-tuple-element.105), channel_id=1, source_target_pairs={{1,0},{0,1},{5,2},{4,3},{3,4},{2,5},{7,6},{6,7},{9,8},{8,9},{13,10... | collective-permute-start | bytes 4718600 | tf_op jit(solution)/shard_map/weights_back/ppermute | solution.py:263
  221.6 13.7 %all-to-all-start.3 = ((bf16[4,144,512]{2,1,0:T(8,128)(2,1)}), bf16[4,144,512]{2,1,0:T(8,128)(2,1)S(1)}, u32[]{:S(2)}, u32[]{:S(2)}) async-start(bf16[4,144,512]{2,1,0:T(8,128)(2,1)} %combine.1), calls=%async_computation.3 | async-start | bytes 1179648 | tf_op jit(solution)/shard_map/tokens_back/all_to_all | solution.py:313
  (11 other events, 12.4 us)

commit v11 on v10

--- a/solution.py
+++ b/solution.py
@@ -220,7 +220,7 @@
         )(pick, dg)
 
     with jax.named_scope("gates"):
-        x_own, ds, weights[0] = lax.optimization_barrier((x_own, ds, weights[0]))
+        x_own, ds = lax.optimization_barrier((x_own, ds))
         d_own = to_experts(ds)
         x_sib = lax.ppermute(x_own, "c", sib)
         ahead = pl.pallas_call(
@@ -228,6 +228,7 @@
             out_shape=(shape((3, ROWS, FH), F32), shape((ROWS, FH), BF)),
             in_specs=[VMEM] * 3,
             out_specs=(VMEM, VMEM),
+            cost_estimate=pl.CostEstimate(flops=COST, bytes_accessed=COST // 100, transcendentals=0),
             compiler_params=params(),
             name="gates",
         )

time: 239 us -> 253 us (1.059)
  waiting for transfers between devices: 102 us -> 114 us
  local copies, waits for them, and re-layouts: 15.1 us -> 7.22 us
  starting transfers between devices: 52.6 us -> 57.5 us
  Pallas kernels: 38.6 us -> 41.4 us
    all_to_all x3, waiting for transfers between devices: 42.1 us -> 69.2 us  [to_experts(): lax.all_to_all(rows, ('y', 'z'), split_axis=0, concat_axis=0, tiled=True)]
    ppermute x4, waiting for transfers between devices: 40.2 us -> 28.7 us  [per_device(): weights.append(lax.ppermute(piece, ('c', 'x'), weight_pairs(m)))]
    unnamed x40, local copies, waits for them, and re-layouts: 12.4 us -> 5.52 us
    all_to_all x3, starting transfers between devices: 22.4 us -> 28.4 us  [to_experts(): lax.all_to_all(rows, ('y', 'z'), split_axis=0, concat_axis=0, tiled=True)]
    ppermute x4, waiting for transfers between devices: 18.1 us -> 12.4 us  [home_again(): lax.ppermute(piece, ('c', 'x'), [(b, a) for a, b in weight_pairs(m)])]
  transfers between devices with their start and end apart: 15 -> 15, of which waited for: 10 -> 7; matrix products, arithmetic and copies ran while one was open for 2% -> 2% of each run, Pallas kernels for 13% -> 13%
where the time goes in v11:
time: 253 us; the launch traced here: 250 us
  waiting for transfers between devices  114 us (45%)
  starting transfers between devices  57.5 us (23%)
  Pallas kernels  41.4 us (16%)
  blocking collectives  23.5 us (9%)
  local copies, waits for them, and re-layouts  7.22 us (3%)
  other arithmetic  6.26 us (2%)
    all_to_all x3, waiting for transfers between devices, to_experts(): lax.all_to_all(rows, ('y', 'z'), split_axis=0, concat_axis=0, tiled=True)  69.2 us
    ppermute x4, waiting for transfers between devices, per_device(): weights.append(lax.ppermute(piece, ('c', 'x'), weight_pairs(m)))  28.7 us
    all_to_all x3, starting transfers between devices, to_experts(): lax.all_to_all(rows, ('y', 'z'), split_axis=0, concat_axis=0, tiled=True)  28.4 us
    ppermute x4, starting transfers between devices, per_device(): weights.append(lax.ppermute(piece, ('c', 'x'), weight_pairs(m)))  15.5 us
    all_gather x1, blocking collectives, per_device(): xg = lax.all_gather(tokens, 'x', axis=0, tiled=False)  12.5 us
    ppermute x4, waiting for transfers between devices, home_again(): lax.ppermute(piece, ('c', 'x'), [(b, a) for a, b in weight_pairs(m)])  12.4 us
    all_gather x1, blocking collectives, per_device(): dg = lax.all_gather(cotangent, 'x', axis=0, tiled=False)  10.9 us
    ppermute x4, starting transfers between devices, home_again(): lax.ppermute(piece, ('c', 'x'), [(b, a) for a, b in weight_pairs(m)])  8.31 us
  transfers between devices with their start and end apart: 15, of which 7 were waited for; matrix products, arithmetic and copies ran while one was open for 2% of the time, Pallas kernels for 13%

profile of v11, /device:TPU:1, one launch (start us, length us, event | category | flops | bytes accessed | tf_op | source)
XLA Modules:
  0.0 250.4 jit_solution(15038460082051079183)
XLA Ops:
  2.0 12.5 %all-gather = bf16[512,512]{1,0:T(8,128)(2,1)S(1)} all-gather(bf16[128,512]{1,0:T(8,128)(2,1)} %param.7), channel_id=2, replica_groups=mesh['y'=4,'z'=8,'c'=2,'x'=4] {'x'}, dimensions={0}, use_global_device_ids=true | all-gather | bytes 655360 | tf_op jit(solution)/shard_map/select_x/all_gather | solution.py:185
  14.6 2.8 %select_x.1 = (bf16[512,2176]{1,0:T(8,128)(2,1)}, bf16[512,128]{1,0:T(8,128)(2,1)S(1)}) custom-call(s32[4]{0:T(128)S(1)} %pad_add_fusion.at_ref, f32[16,128]{1,0:T(8,128)S(1)} %pad_maximum_fusion.2.table_ref, bf16[4,128,512]{2,1,0:T(8,128)(2,1)S(1)} %bitcast.19), custom_call_target="tpu_custom_call" | custom-call | tf_op jit(solution)/shard_map/select_x/select_x/pallas_call | solution.py:187
  17.4 11.6 %all-to-all-start = ((bf16[32,16,2176]{2,1,0:T(8,128)(2,1)}), bf16[32,16,2176]{2,1,0:T(8,128)(2,1)}, u32[]{:S(2)}, u32[]{:S(2)}) async-start(bf16[32,16,2176]{2,1,0:T(8,128)(2,1)} %bitcast.7), calls=%async_computation | async-start | bytes 4456448 | tf_op jit(solution)/shard_map/select_x/all_to_all | solution.py:181
  29.1 10.9 %all-gather.1 = bf16[512,512]{1,0:T(8,128)(2,1)} all-gather(bf16[128,512]{1,0:T(8,128)(2,1)S(1)} %copy-done.19), channel_id=3, replica_groups=mesh['y'=4,'z'=8,'c'=2,'x'=4] {'x'}, dimensions={0}, use_global_device_ids=true | all-gather | bytes 655360 | tf_op jit(solution)/shard_map/select_d/all_gather | solution.py:199
  40.6 7.9 %collective-permute-start.1 = (bf16[2,192,2048]{2,1,0:T(8,128)(2,1)S(1)}, bf16[2,192,2048]{2,1,0:T(8,128)(2,1)S(1)}, u32[]{:S(2)}, u32[]{:S(2)}) collective-permute-start(bf16[2,192,2048]{2,1,0:T(8,128)(2,1)S(1)} %pad_maximum_fusion.1), channel_id=1, source_target_pairs={{0,1},{1,0},{2,5},{3,4},{4,3},{5,2},{6,7},{7,6},{8,9},{9,8},{10,13... | collective-permute-start | bytes 4718600 | tf_op jit(solution)/shard_map/weights_out/ppermute | solution.py:210
  54.0 28.7 %collective-permute-done.1.wb_ref = bf16[2,192,2048]{2,1,0:T(8,128)(2,1)S(1)} collective-permute-done((bf16[2,192,2048]{2,1,0:T(8,128)(2,1)S(1)}, bf16[2,192,2048]{2,1,0:T(8,128)(2,1)S(1)}, u32[]{:S(2)}, u32[]{:S(2)}) %collective-permute-start.1) | collective-permute-done | bytes 1572896 | tf_op jit(solution)/shard_map/weights_out/ppermute | solution.py:210
  84.0 3.7 %collective-permute-start.4 = (bf16[1,192,2048]{2,1,0:T(8,128)(2,1)}, bf16[1,192,2048]{2,1,0:T(8,128)(2,1)}, u32[]{:S(2)}, u32[]{:S(2)}) collective-permute-start(bf16[1,192,2048]{2,1,0:T(8,128)(2,1)} %get-tuple-element.107), channel_id=1, source_target_pairs={{0,1},{1,0},{2,5},{3,4},{4,3},{5,2},{6,7},{7,6},{8,9},{9,8},{10,13... | collective-permute-start | bytes 2359304 | tf_op jit(solution)/shard_map/weights_out/ppermute | solution.py:210
  89.6 9.7 %all-to-all-start.1 = ((bf16[32,16,2048]{2,1,0:T(8,128)(2,1)}), bf16[32,16,2048]{2,1,0:T(8,128)(2,1)}, u32[]{:S(2)}, u32[]{:S(2)}) async-start(bf16[32,16,2048]{2,1,0:T(8,128)(2,1)} %bitcast.10), calls=%async_computation.1 | async-start | bytes 4194304 | tf_op jit(solution)/shard_map/gates/all_to_all | solution.py:181
  99.5 4.1 %gates.2 = (f32[3,512,384]{2,1,0:T(8,128)S(1)}, bf16[512,384]{1,0:T(8,128)(2,1)S(1)}) custom-call(bf16[512,2176]{1,0:T(8,128)(2,1)} %bitcast.8.x_ref.xo_ref, bf16[2,192,2048]{2,1,0:T(8,128)(2,1)S(1)} %collective-permute-done.wa_ref, bf16[2,192,2048]{2,1,0:T(8,128)(2,1)S(1)} %collective-permute-done.1.wb_ref), custom_call_target="tpu_custom_call" | custom-call | flops 99999997952 | bytes 1000000000 | tf_op jit(solution)/shard_map/gates/gates/pallas_call | solution.py:235
  104.4 2.5 gates.3
  109.1 40.0 %all-to-all-done.1 = bf16[32,16,2048]{2,1,0:T(8,128)(2,1)} async-done(((bf16[32,16,2048]{2,1,0:T(8,128)(2,1)}), bf16[32,16,2048]{2,1,0:T(8,128)(2,1)}, u32[]{:S(2)}, u32[]{:S(2)}) %all-to-all-start.1) | async-done | bytes 2097184 | tf_op jit(solution)/shard_map/gates/all_to_all | solution.py:181
  152.2 5.6 %expert.2 = (bf16[512,2176]{1,0:T(8,128)(2,1)S(1)}, bf16[2,512,384]{2,1,0:T(8,128)(2,1)S(1)}) custom-call(s32[4]{0:T(128)S(1)} %copy-done.12, f32[3,512,384]{2,1,0:T(8,128)S(1)} %copy-done.3, bf16[512,2048]{1,0:T(8,128)(2,1)} %bitcast.11.d_ref.do_ref, bf16[2,192,2048]{2,1,0:T(8,128)(2,1)S(1)} %collective-permute-done.wa_ref, ...), custom_call_target="tpu_custom_call" | custom-call | tf_op jit(solution)/shard_map/expert/expert/pallas_call | solution.py:250
  158.8 4.9 %expert.3 = (bf16[512,2176]{1,0:T(8,128)(2,1)S(1)}, bf16[2,512,384]{2,1,0:T(8,128)(2,1)S(1)}) custom-call(s32[4]{0:T(128)S(1)} %copy-done.12, f32[3,512,384]{2,1,0:T(8,128)S(1)} %copy-done.1, bf16[512,2048]{1,0:T(8,128)(2,1)S(1)} %collective-permute-done.5.d_ref.ds_ref, bf16[2,192,2048]{2,1,0:T(8,128)(2,1)S(1)} %collective-permute-done.wa_ref, ...), custom_call_target="tpu_custom_call" | custom-call | tf_op jit(solution)/shard_map/expert/expert/pallas_call | solution.py:252
  163.9 5.1 %down_grads.1 = (bf16[1,192,2048]{2,1,0:T(8,128)(2,1)}, bf16[1,192,2048]{2,1,0:T(8,128)(2,1)}) custom-call(bf16[512,2048]{1,0:T(8,128)(2,1)} %bitcast.11.d_ref.do_ref, bf16[512,2048]{1,0:T(8,128)(2,1)S(1)} %collective-permute-done.5.d_ref.ds_ref, bf16[512,384]{1,0:T(8,128)(2,1)S(1)} %copy-done.6, bf16[512,384]{1,0:T(8,128)(2,1)S(1)} %copy-done.8), custom_call_target="tpu_custom_call" | custom-call | tf_op jit(solution)/shard_map/weights_back/down_grads/pallas_call | solution.py:266
  170.9 2.2 collective-permute-start.8
  175.0 7.1 %all-to-all-start.2 = ((bf16[32,16,2176]{2,1,0:T(8,128)(2,1)}), bf16[32,16,2176]{2,1,0:T(8,128)(2,1)S(1)}, u32[]{:S(2)}, u32[]{:S(2)}) async-start(bf16[32,16,2176]{2,1,0:T(8,128)(2,1)} %bitcast.21), calls=%async_computation.2 | async-start | bytes 4456448 | tf_op jit(solution)/shard_map/tokens_back/all_to_all | solution.py:181
  182.1 6.2 %collective-permute-done.7.da_ref = bf16[1,192,2048]{2,1,0:T(8,128)(2,1)S(1)} collective-permute-done((bf16[1,192,2048]{2,1,0:T(8,128)(2,1)}, bf16[1,192,2048]{2,1,0:T(8,128)(2,1)S(1)}, u32[]{:S(2)}, u32[]{:S(2)}) %collective-permute-start.7) | collective-permute-done | bytes 786464 | tf_op jit(solution)/shard_map/weights_back/ppermute | solution.py:264
  188.3 4.3 %collective-permute-done.8.db_ref = bf16[1,192,2048]{2,1,0:T(8,128)(2,1)} collective-permute-done((bf16[1,192,2048]{2,1,0:T(8,128)(2,1)}, bf16[1,192,2048]{2,1,0:T(8,128)(2,1)}, u32[]{:S(2)}, u32[]{:S(2)}) %collective-permute-start.8) | collective-permute-done | bytes 786464 | tf_op jit(solution)/shard_map/weights_back/ppermute | solution.py:264
  192.6 7.5 %gate_up_grads.1 = (bf16[2,192,2048]{2,1,0:T(8,128)(2,1)}, bf16[2,192,2048]{2,1,0:T(8,128)(2,1)}) custom-call(bf16[512,2176]{1,0:T(8,128)(2,1)} %bitcast.8.x_ref.xo_ref, bf16[512,2176]{1,0:T(8,128)(2,1)} %copy-done.13, bf16[2,512,384]{2,1,0:T(8,128)(2,1)} %copy-done.14, bf16[2,512,384]{2,1,0:T(8,128)(2,1)} %copy-done.15), custom_call_target="tpu_custom_call" | custom-call | flops 99999997952 | bytes 1000000000 | tf_op jit(solution)/shard_map/weights_back/gate_up_grads/pallas_call | solution.py:281
  200.1 2.7 %collective-permute-start.9 = (bf16[2,192,2048]{2,1,0:T(8,128)(2,1)}, bf16[2,192,2048]{2,1,0:T(8,128)(2,1)}, u32[]{:S(2)}, u32[]{:S(2)}) collective-permute-start(bf16[2,192,2048]{2,1,0:T(8,128)(2,1)} %get-tuple-element.102), channel_id=1, source_target_pairs={{0,0},{1,1},{4,2},{5,3},{2,4},{3,5},{6,6},{7,7},{8,8},{9,9},{12,10... | collective-permute-start | bytes 4718600 | tf_op jit(solution)/shard_map/weights_back/ppermute | solution.py:264
  204.3 29.2 %all-to-all-done.2 = bf16[32,16,2176]{2,1,0:T(8,128)(2,1)S(1)} async-done(((bf16[32,16,2176]{2,1,0:T(8,128)(2,1)}), bf16[32,16,2176]{2,1,0:T(8,128)(2,1)S(1)}, u32[]{:S(2)}, u32[]{:S(2)}) %all-to-all-start.2) | async-done | bytes 2228256 | tf_op jit(solution)/shard_map/tokens_back/all_to_all | solution.py:181
  235.4 3.5 %all-to-all-start.3 = ((bf16[4,144,512]{2,1,0:T(8,128)(2,1)}), bf16[4,144,512]{2,1,0:T(8,128)(2,1)S(1)}, u32[]{:S(2)}, u32[]{:S(2)}) async-start(bf16[4,144,512]{2,1,0:T(8,128)(2,1)} %combine.1), calls=%async_computation.3 | async-start | bytes 1179648 | tf_op jit(solution)/shard_map/tokens_back/all_to_all | solution.py:314
  240.8 4.8 %place.1 = (bf16[2,192,2048]{2,1,0:T(8,128)(2,1)}, bf16[2,192,2048]{2,1,0:T(8,128)(2,1)}, bf16[2,192,2048]{2,1,0:T(8,128)(2,1)}) custom-call(s32[4]{0:T(128)S(1)} %copy-done.12, bf16[1,192,2048]{2,1,0:T(8,128)(2,1)S(1)} %collective-permute-done.7.da_ref, bf16[1,192,2048]{2,1,0:T(8,128)(2,1)} %collective-permute-done.8.db_ref, ...), custom_call_target="tpu_custom_call" | custom-call | tf_op jit(solution)/shard_map/weights_back/place/pallas_call | solution.py:294
  245.6 3.3 %all-to-all-done.3 = bf16[4,144,512]{2,1,0:T(8,128)(2,1)S(1)} async-done(((bf16[4,144,512]{2,1,0:T(8,128)(2,1)}), bf16[4,144,512]{2,1,0:T(8,128)(2,1)S(1)}, u32[]{:S(2)}, u32[]{:S(2)}) %all-to-all-start.3) | async-done | bytes 589856 | tf_op jit(solution)/shard_map/tokens_back/all_to_all | solution.py:314
  (71 shorter events, 28.6 us)
Async XLA Ops:
  17.4 11.7 %copy-start.19 = (bf16[128,512]{1,0:T(8,128)(2,1)S(1)}, bf16[128,512]{1,0:T(8,128)(2,1)}, u32[]{:S(2)}) copy-start(bf16[128,512]{1,0:T(8,128)(2,1)} %param.8) | copy-start | bytes 393220
  17.4 22.6 %copy-start.17 = (bf16[2,192,2048]{2,1,0:T(8,128)(2,1)S(1)}, bf16[2,192,2048]{2,1,0:T(8,128)(2,1)}, u32[]{:S(2)}) copy-start(bf16[2,192,2048]{2,1,0:T(8,128)(2,1)} %param.12) | copy-start | bytes 4718596
  17.4 22.6 %copy-start.18 = (bf16[2,192,2048]{2,1,0:T(8,128)(2,1)S(1)}, bf16[2,192,2048]{2,1,0:T(8,128)(2,1)}, u32[]{:S(2)}) copy-start(bf16[2,192,2048]{2,1,0:T(8,128)(2,1)} %param.11) | copy-start | bytes 4718596
  17.4 72.2 %all-to-all-start = ((bf16[32,16,2176]{2,1,0:T(8,128)(2,1)}), bf16[32,16,2176]{2,1,0:T(8,128)(2,1)}, u32[]{:S(2)}, u32[]{:S(2)}) async-start(bf16[32,16,2176]{2,1,0:T(8,128)(2,1)} %bitcast.7), calls=%async_computation | async-start | bytes 4456448 | tf_op jit(solution)/shard_map/select_x/all_to_all | solution.py:181
  40.6 42.1 %collective-permute-start.1 = (bf16[2,192,2048]{2,1,0:T(8,128)(2,1)S(1)}, bf16[2,192,2048]{2,1,0:T(8,128)(2,1)S(1)}, u32[]{:S(2)}, u32[]{:S(2)}) collective-permute-start(bf16[2,192,2048]{2,1,0:T(8,128)(2,1)S(1)} %pad_maximum_fusion.1), channel_id=1, source_target_pairs={{0,1},{1,0},{2,5},{3,4},{4,3},{5,2},{6,7},{7,6},{8,9},{9,8},{10,13... | collective-permute-start | bytes 4718600 | tf_op jit(solution)/shard_map/weights_out/ppermute | solution.py:210
  49.8 32.9 %copy-start.16 = (bf16[2,192,2048]{2,1,0:T(8,128)(2,1)S(1)}, bf16[2,192,2048]{2,1,0:T(8,128)(2,1)}, u32[]{:S(2)}) copy-start(bf16[2,192,2048]{2,1,0:T(8,128)(2,1)} %param.13) | copy-start | bytes 4718596
  49.8 49.8 %collective-permute-start = (bf16[2,192,2048]{2,1,0:T(8,128)(2,1)}, bf16[2,192,2048]{2,1,0:T(8,128)(2,1)S(1)}, u32[]{:S(2)}, u32[]{:S(2)}) collective-permute-start(bf16[2,192,2048]{2,1,0:T(8,128)(2,1)} %pad_maximum_fusion), channel_id=1, source_target_pairs={{0,0},{1,1},{2,4},{3,5},{4,2},{5,3},{6,6},{7,7},{8,8},{9,9},{10,12... | collective-permute-start | bytes 4718600 | tf_op jit(solution)/shard_map/weights_out/ppermute | solution.py:210
  84.0 25.1 %collective-permute-start.4 = (bf16[1,192,2048]{2,1,0:T(8,128)(2,1)}, bf16[1,192,2048]{2,1,0:T(8,128)(2,1)}, u32[]{:S(2)}, u32[]{:S(2)}) collective-permute-start(bf16[1,192,2048]{2,1,0:T(8,128)(2,1)} %get-tuple-element.107), channel_id=1, source_target_pairs={{0,1},{1,0},{2,5},{3,4},{4,3},{5,2},{6,7},{7,6},{8,9},{9,8},{10,13... | collective-permute-start | bytes 2359304 | tf_op jit(solution)/shard_map/weights_out/ppermute | solution.py:210
  87.7 21.4 %collective-permute-start.3 = (bf16[1,192,2048]{2,1,0:T(8,128)(2,1)}, bf16[1,192,2048]{2,1,0:T(8,128)(2,1)}, u32[]{:S(2)}, u32[]{:S(2)}) collective-permute-start(bf16[1,192,2048]{2,1,0:T(8,128)(2,1)} %get-tuple-element.108), channel_id=1, source_target_pairs={{0,0},{1,1},{2,4},{3,5},{4,2},{5,3},{6,6},{7,7},{8,8},{9,9},{10,12... | collective-permute-start | bytes 2359304 | tf_op jit(solution)/shard_map/weights_out/ppermute | solution.py:210
  89.6 59.4 %all-to-all-start.1 = ((bf16[32,16,2048]{2,1,0:T(8,128)(2,1)}), bf16[32,16,2048]{2,1,0:T(8,128)(2,1)}, u32[]{:S(2)}, u32[]{:S(2)}) async-start(bf16[32,16,2048]{2,1,0:T(8,128)(2,1)} %bitcast.10), calls=%async_computation.1 | async-start | bytes 4194304 | tf_op jit(solution)/shard_map/gates/all_to_all | solution.py:181
  99.3 5.0 %collective-permute-start.2 = (bf16[512,2176]{1,0:T(8,128)(2,1)}, bf16[512,2176]{1,0:T(8,128)(2,1)S(1)}, u32[]{:S(2)}, u32[]{:S(2)}) collective-permute-start(bf16[512,2176]{1,0:T(8,128)(2,1)} %bitcast.8.x_ref.xo_ref), channel_id=1, source_target_pairs={{0,4},{4,0},{1,5},{5,1},{2,6},{6,2},{3,7},{7,3},{8,12},{12,8},{9,1... | collective-permute-start | bytes 6684680 | tf_op jit(solution)/shard_map/gates/ppermute | solution.py:225
  104.4 46.2 %copy-start.12 = (s32[4]{0:T(128)S(1)}, s32[4]{0:T(128)}, u32[]{:S(2)}) copy-start(s32[4]{0:T(128)} %copy-done.11) | copy-start | bytes 52
  149.1 9.7 %collective-permute-start.5 = (bf16[512,2048]{1,0:T(8,128)(2,1)}, bf16[512,2048]{1,0:T(8,128)(2,1)S(1)}, u32[]{:S(2)}, u32[]{:S(2)}) collective-permute-start(bf16[512,2048]{1,0:T(8,128)(2,1)} %bitcast.11.d_ref.do_ref), channel_id=1, source_target_pairs={{0,4},{4,0},{1,5},{5,1},{2,6},{6,2},{3,7},{7,3},{8,12},{12,8},{9,1... | collective-permute-start | bytes 6291464 | tf_op jit(solution)/shard_map/expert/ppermute | solution.py:241
  152.2 6.5 %copy-start.1 = (f32[3,512,384]{2,1,0:T(8,128)S(1)}, f32[3,512,384]{2,1,0:T(8,128)}, u32[]{:S(2)}) copy-start(f32[3,512,384]{2,1,0:T(8,128)} %copy-done) | copy-start | bytes 7077892
  158.8 5.1 %copy-start.8 = (bf16[512,384]{1,0:T(8,128)(2,1)S(1)}, bf16[512,384]{1,0:T(8,128)(2,1)}, u32[]{:S(2)}) copy-start(bf16[512,384]{1,0:T(8,128)(2,1)} %copy-done.7) | copy-start | bytes 1179652
  163.7 5.3 %copy-start.15 = (bf16[2,512,384]{2,1,0:T(8,128)(2,1)}, bf16[2,512,384]{2,1,0:T(8,128)(2,1)S(1)}, u32[]{:S(2)}) copy-start(bf16[2,512,384]{2,1,0:T(8,128)(2,1)S(1)} %get-tuple-element.101.ks_ref) | copy-start | bytes 2359300
  163.7 5.2 %collective-permute-start.6 = (bf16[512,2176]{1,0:T(8,128)(2,1)S(1)}, bf16[512,2176]{1,0:T(8,128)(2,1)S(1)}, u32[]{:S(2)}, u32[]{:S(2)}) collective-permute-start(bf16[512,2176]{1,0:T(8,128)(2,1)S(1)} %get-tuple-element.89), channel_id=1, source_target_pairs={{0,4},{4,0},{1,5},{5,1},{2,6},{6,2},{3,7},{7,3},{8,12},{12,8},{9,1... | collective-permute-start | bytes 6684680 | tf_op jit(solution)/shard_map/expert/ppermute | solution.py:254
  169.0 19.3 %collective-permute-start.7 = (bf16[1,192,2048]{2,1,0:T(8,128)(2,1)}, bf16[1,192,2048]{2,1,0:T(8,128)(2,1)S(1)}, u32[]{:S(2)}, u32[]{:S(2)}) collective-permute-start(bf16[1,192,2048]{2,1,0:T(8,128)(2,1)} %get-tuple-element.94), channel_id=1, source_target_pairs={{0,0},{1,1},{4,2},{5,3},{2,4},{3,5},{6,6},{7,7},{8,8},{9,9},{12,10... | collective-permute-start | bytes 2359304 | tf_op jit(solution)/shard_map/weights_back/ppermute | solution.py:264
  170.9 21.6 %collective-permute-start.8 = (bf16[1,192,2048]{2,1,0:T(8,128)(2,1)}, bf16[1,192,2048]{2,1,0:T(8,128)(2,1)}, u32[]{:S(2)}, u32[]{:S(2)}) collective-permute-start(bf16[1,192,2048]{2,1,0:T(8,128)(2,1)} %get-tuple-element.95), channel_id=1, source_target_pairs={{1,0},{0,1},{5,2},{4,3},{3,4},{2,5},{7,6},{6,7},{9,8},{8,9},{13,10... | collective-permute-start | bytes 2359304 | tf_op jit(solution)/shard_map/weights_back/ppermute | solution.py:264
  175.0 58.6 %all-to-all-start.2 = ((bf16[32,16,2176]{2,1,0:T(8,128)(2,1)}), bf16[32,16,2176]{2,1,0:T(8,128)(2,1)S(1)}, u32[]{:S(2)}, u32[]{:S(2)}) async-start(bf16[32,16,2176]{2,1,0:T(8,128)(2,1)} %bitcast.21), calls=%async_computation.2 | async-start | bytes 4456448 | tf_op jit(solution)/shard_map/tokens_back/all_to_all | solution.py:181
  182.1 51.5 %copy-start.10 = (f32[16,128]{1,0:T(8,128)S(1)}, f32[16,128]{1,0:T(8,128)}, u32[]{:S(2)}) copy-start(f32[16,128]{1,0:T(8,128)} %copy-done.9) | copy-start | bytes 24580
  200.1 38.8 %collective-permute-start.9 = (bf16[2,192,2048]{2,1,0:T(8,128)(2,1)}, bf16[2,192,2048]{2,1,0:T(8,128)(2,1)}, u32[]{:S(2)}, u32[]{:S(2)}) collective-permute-start(bf16[2,192,2048]{2,1,0:T(8,128)(2,1)} %get-tuple-element.102), channel_id=1, source_target_pairs={{0,0},{1,1},{4,2},{5,3},{2,4},{3,5},{6,6},{7,7},{8,8},{9,9},{12,10... | collective-permute-start | bytes 4718600 | tf_op jit(solution)/shard_map/weights_back/ppermute | solution.py:264
  202.7 38.0 %collective-permute-start.10 = (bf16[2,192,2048]{2,1,0:T(8,128)(2,1)}, bf16[2,192,2048]{2,1,0:T(8,128)(2,1)}, u32[]{:S(2)}, u32[]{:S(2)}) collective-permute-start(bf16[2,192,2048]{2,1,0:T(8,128)(2,1)} %get-tuple-element.103), channel_id=1, source_target_pairs={{1,0},{0,1},{5,2},{4,3},{3,4},{2,5},{7,6},{6,7},{9,8},{8,9},{13,10... | collective-permute-start | bytes 4718600 | tf_op jit(solution)/shard_map/weights_back/ppermute | solution.py:264
  235.4 13.5 %all-to-all-start.3 = ((bf16[4,144,512]{2,1,0:T(8,128)(2,1)}), bf16[4,144,512]{2,1,0:T(8,128)(2,1)S(1)}, u32[]{:S(2)}, u32[]{:S(2)}) async-start(bf16[4,144,512]{2,1,0:T(8,128)(2,1)} %combine.1), calls=%async_computation.3 | async-start | bytes 1179648 | tf_op jit(solution)/shard_map/tokens_back/all_to_all | solution.py:314
  (11 other events, 24.6 us)

commit v12 on v11

--- a/solution.py
+++ b/solution.py
@@ -203,8 +203,6 @@
         weights = []
         for m in (0, 1, 0, 1):
             k = (ix + m) % 2
-            if len(weights) == 2:
-                *mats, weights[1] = lax.optimization_barrier((*mats, weights[1]))
             which = mats[2:] if len(weights) > 1 else mats[:2]
             piece = jnp.stack([lax.dynamic_index_in_dim(w, k, 0, keepdims=False) for w in which])
             weights.append(lax.ppermute(piece, ("c", "x"), weight_pairs(m)))

time: 253 us -> 238 us (0.941)
  waiting for transfers between devices: 114 us -> 101 us
  starting transfers between devices: 57.5 us -> 54.2 us
    ppermute x4, waiting for transfers between devices: 28.7 us -> 5.68 us  [per_device(): weights.append(lax.ppermute(piece, ('c', 'x'), weight_pairs(m)))]
    all_to_all x3, waiting for transfers between devices: 69.2 us -> 76.5 us  [to_experts(): lax.all_to_all(rows, ('y', 'z'), split_axis=0, concat_axis=0, tiled=True)]
    all_to_all x3, starting transfers between devices: 28.4 us -> 22.5 us  [to_experts(): lax.all_to_all(rows, ('y', 'z'), split_axis=0, concat_axis=0, tiled=True)]
    ppermute x4, waiting for transfers between devices: 12.4 us -> 18.1 us  [home_again(): lax.ppermute(piece, ('c', 'x'), [(b, a) for a, b in weight_pairs(m)])]
    ppermute x1, starting transfers between devices: 0.18 us -> 3.17 us  [per_device(): x_sib = lax.ppermute(x_own, 'c', sib)]
  transfers between devices with their start and end apart: 15 -> 15, of which waited for: 7 -> 9; matrix products, arithmetic and copies ran while one was open for 2% -> 3% of each run, Pallas kernels for 13% -> 14%
where the time goes in v12:
time: 238 us; the launch traced here: 236 us
  waiting for transfers between devices  101 us (42%)
  starting transfers between devices  54.2 us (23%)
  Pallas kernels  41.4 us (17%)
  blocking collectives  23.5 us (10%)
  other arithmetic  7.4 us (3%)
  local copies, waits for them, and re-layouts  7.17 us (3%)
    all_to_all x3, waiting for transfers between devices, to_experts(): lax.all_to_all(rows, ('y', 'z'), split_axis=0, concat_axis=0, tiled=True)  76.5 us
    all_to_all x3, starting transfers between devices, to_experts(): lax.all_to_all(rows, ('y', 'z'), split_axis=0, concat_axis=0, tiled=True)  22.5 us
    ppermute x4, waiting for transfers between devices, home_again(): lax.ppermute(piece, ('c', 'x'), [(b, a) for a, b in weight_pairs(m)])  18.1 us
    ppermute x4, starting transfers between devices, per_device(): weights.append(lax.ppermute(piece, ('c', 'x'), weight_pairs(m)))  14.9 us
    all_gather x1, blocking collectives, per_device(): xg = lax.all_gather(tokens, 'x', axis=0, tiled=False)  12.5 us
    all_gather x1, blocking collectives, per_device(): dg = lax.all_gather(cotangent, 'x', axis=0, tiled=False)  10.9 us
    pallas_call x1, Pallas kernels, per_device(): pl.pallas_call(gate_up_grads, grid=(NX,), out_shape=(shape((2, FQ, D), BF...  7.51 us
    ppermute x4, starting transfers between devices, home_again(): lax.ppermute(piece, ('c', 'x'), [(b, a) for a, b in weight_pairs(m)])  6.66 us
  transfers between devices with their start and end apart: 15, of which 9 were waited for; matrix products, arithmetic and copies ran while one was open for 3% of the time, Pallas kernels for 14%

profile of v12, /device:TPU:1, one launch (start us, length us, event | category | flops | bytes accessed | tf_op | source)
XLA Modules:
  0.0 235.9 jit_solution(2373014587566269086)
XLA Ops:
  2.0 12.5 %all-gather = bf16[512,512]{1,0:T(8,128)(2,1)S(1)} all-gather(bf16[128,512]{1,0:T(8,128)(2,1)} %param.7), channel_id=2, replica_groups=mesh['y'=4,'z'=8,'c'=2,'x'=4] {'x'}, dimensions={0}, use_global_device_ids=true | all-gather | bytes 655360 | tf_op jit(solution)/shard_map/select_x/all_gather | solution.py:185
  17.4 11.6 %all-to-all-start = ((bf16[32,16,2176]{2,1,0:T(8,128)(2,1)}), bf16[32,16,2176]{2,1,0:T(8,128)(2,1)}, u32[]{:S(2)}, u32[]{:S(2)}) async-start(bf16[32,16,2176]{2,1,0:T(8,128)(2,1)} %bitcast.7), calls=%async_computation | async-start | bytes 4456448 | tf_op jit(solution)/shard_map/select_x/all_to_all | solution.py:181
  29.1 10.9 %all-gather.1 = bf16[512,512]{1,0:T(8,128)(2,1)} all-gather(bf16[128,512]{1,0:T(8,128)(2,1)S(1)} %copy-done.19), channel_id=3, replica_groups=mesh['y'=4,'z'=8,'c'=2,'x'=4] {'x'}, dimensions={0}, use_global_device_ids=true | all-gather | bytes 655360 | tf_op jit(solution)/shard_map/select_d/all_gather | solution.py:199
  41.7 8.1 %collective-permute-start = (bf16[2,192,2048]{2,1,0:T(8,128)(2,1)}, bf16[2,192,2048]{2,1,0:T(8,128)(2,1)S(1)}, u32[]{:S(2)}, u32[]{:S(2)}) collective-permute-start(bf16[2,192,2048]{2,1,0:T(8,128)(2,1)} %pad_maximum_fusion), channel_id=1, source_target_pairs={{0,0},{1,1},{2,4},{3,5},{4,2},{5,3},{6,6},{7,7},{8,8},{9,9},{10,12... | collective-permute-start | bytes 4718600 | tf_op jit(solution)/shard_map/weights_out/ppermute | solution.py:208
  55.4 3.8 %collective-permute-start.3 = (bf16[1,192,2048]{2,1,0:T(8,128)(2,1)}, bf16[1,192,2048]{2,1,0:T(8,128)(2,1)}, u32[]{:S(2)}, u32[]{:S(2)}) collective-permute-start(bf16[1,192,2048]{2,1,0:T(8,128)(2,1)} %get-tuple-element.104), channel_id=1, source_target_pairs={{0,0},{1,1},{2,4},{3,5},{4,2},{5,3},{6,6},{7,7},{8,8},{9,9},{10,12... | collective-permute-start | bytes 2359304 | tf_op jit(solution)/shard_map/weights_out/ppermute | solution.py:208
  61.4 19.1 %all-to-all-done = bf16[32,16,2176]{2,1,0:T(8,128)(2,1)} async-done(((bf16[32,16,2176]{2,1,0:T(8,128)(2,1)}), bf16[32,16,2176]{2,1,0:T(8,128)(2,1)}, u32[]{:S(2)}, u32[]{:S(2)}) %all-to-all-start) | async-done | bytes 2228256 | tf_op jit(solution)/shard_map/select_x/all_to_all | solution.py:181
  80.4 5.6 %all-to-all-start.1 = ((bf16[32,16,2048]{2,1,0:T(8,128)(2,1)}), bf16[32,16,2048]{2,1,0:T(8,128)(2,1)}, u32[]{:S(2)}, u32[]{:S(2)}) async-start(bf16[32,16,2048]{2,1,0:T(8,128)(2,1)} %bitcast.10), calls=%async_computation.1 | async-start | bytes 4194304 | tf_op jit(solution)/shard_map/gates/all_to_all | solution.py:181
  86.0 3.2 %collective-permute-start.2 = (bf16[512,2176]{1,0:T(8,128)(2,1)}, bf16[512,2176]{1,0:T(8,128)(2,1)S(1)}, u32[]{:S(2)}, u32[]{:S(2)}) collective-permute-start(bf16[512,2176]{1,0:T(8,128)(2,1)} %bitcast.8.x_ref.xo_ref), channel_id=1, source_target_pairs={{0,4},{4,0},{1,5},{5,1},{2,6},{6,2},{3,7},{7,3},{8,12},{12,8},{9,1... | collective-permute-start | bytes 6684680 | tf_op jit(solution)/shard_map/gates/ppermute | solution.py:223
  89.3 4.1 %gates.2 = (f32[3,512,384]{2,1,0:T(8,128)S(1)}, bf16[512,384]{1,0:T(8,128)(2,1)S(1)}) custom-call(bf16[512,2176]{1,0:T(8,128)(2,1)} %bitcast.8.x_ref.xo_ref, bf16[2,192,2048]{2,1,0:T(8,128)(2,1)S(1)} %collective-permute-done.wa_ref, bf16[2,192,2048]{2,1,0:T(8,128)(2,1)S(1)} %collective-permute-done.1.wb_ref), custom_call_target="tpu_custom_call" | custom-call | flops 99999997952 | bytes 1000000000 | tf_op jit(solution)/shard_map/gates/gates/pallas_call | solution.py:233
  98.8 5.6 %collective-permute-done.4.db_ref = bf16[1,192,2048]{2,1,0:T(8,128)(2,1)} collective-permute-done((bf16[1,192,2048]{2,1,0:T(8,128)(2,1)}, bf16[1,192,2048]{2,1,0:T(8,128)(2,1)}, u32[]{:S(2)}, u32[]{:S(2)}) %collective-permute-start.4) | collective-permute-done | bytes 786464 | tf_op jit(solution)/shard_map/weights_out/ppermute | solution.py:208
  104.4 29.8 %all-to-all-done.1 = bf16[32,16,2048]{2,1,0:T(8,128)(2,1)} async-done(((bf16[32,16,2048]{2,1,0:T(8,128)(2,1)}), bf16[32,16,2048]{2,1,0:T(8,128)(2,1)}, u32[]{:S(2)}, u32[]{:S(2)}) %all-to-all-start.1) | async-done | bytes 2097184 | tf_op jit(solution)/shard_map/gates/all_to_all | solution.py:181
  134.2 3.4 %collective-permute-start.5 = (bf16[512,2048]{1,0:T(8,128)(2,1)}, bf16[512,2048]{1,0:T(8,128)(2,1)S(1)}, u32[]{:S(2)}, u32[]{:S(2)}) collective-permute-start(bf16[512,2048]{1,0:T(8,128)(2,1)} %bitcast.11.d_ref.do_ref), channel_id=1, source_target_pairs={{0,4},{4,0},{1,5},{5,1},{2,6},{6,2},{3,7},{7,3},{8,12},{12,8},{9,1... | collective-permute-start | bytes 6291464 | tf_op jit(solution)/shard_map/expert/ppermute | solution.py:239
  139.3 5.6 %expert.2 = (bf16[512,2176]{1,0:T(8,128)(2,1)S(1)}, bf16[2,512,384]{2,1,0:T(8,128)(2,1)S(1)}) custom-call(s32[4]{0:T(128)S(1)} %copy-done.12, f32[3,512,384]{2,1,0:T(8,128)S(1)} %copy-done.3, bf16[512,2048]{1,0:T(8,128)(2,1)} %bitcast.11.d_ref.do_ref, bf16[2,192,2048]{2,1,0:T(8,128)(2,1)S(1)} %collective-permute-done.wa_ref, ...), custom_call_target="tpu_custom_call" | custom-call | tf_op jit(solution)/shard_map/expert/expert/pallas_call | solution.py:248
  145.8 4.9 %expert.3 = (bf16[512,2176]{1,0:T(8,128)(2,1)S(1)}, bf16[2,512,384]{2,1,0:T(8,128)(2,1)S(1)}) custom-call(s32[4]{0:T(128)S(1)} %copy-done.12, f32[3,512,384]{2,1,0:T(8,128)S(1)} %copy-done.1, bf16[512,2048]{1,0:T(8,128)(2,1)S(1)} %collective-permute-done.5.d_ref.ds_ref, bf16[2,192,2048]{2,1,0:T(8,128)(2,1)S(1)} %collective-permute-done.wa_ref, ...), custom_call_target="tpu_custom_call" | custom-call | tf_op jit(solution)/shard_map/expert/expert/pallas_call | solution.py:250
  150.9 5.1 %down_grads.1 = (bf16[1,192,2048]{2,1,0:T(8,128)(2,1)}, bf16[1,192,2048]{2,1,0:T(8,128)(2,1)}) custom-call(bf16[512,2048]{1,0:T(8,128)(2,1)} %bitcast.11.d_ref.do_ref, bf16[512,2048]{1,0:T(8,128)(2,1)S(1)} %collective-permute-done.5.d_ref.ds_ref, bf16[512,384]{1,0:T(8,128)(2,1)S(1)} %copy-done.6, bf16[512,384]{1,0:T(8,128)(2,1)S(1)} %copy-done.8), custom_call_target="tpu_custom_call" | custom-call | tf_op jit(solution)/shard_map/weights_back/down_grads/pallas_call | solution.py:264
  156.0 3.3 %collective-permute-start.7 = (bf16[1,192,2048]{2,1,0:T(8,128)(2,1)}, bf16[1,192,2048]{2,1,0:T(8,128)(2,1)S(1)}, u32[]{:S(2)}, u32[]{:S(2)}) collective-permute-start(bf16[1,192,2048]{2,1,0:T(8,128)(2,1)} %get-tuple-element.90), channel_id=1, source_target_pairs={{0,0},{1,1},{4,2},{5,3},{2,4},{3,5},{6,6},{7,7},{8,8},{9,9},{12,10... | collective-permute-start | bytes 2359304 | tf_op jit(solution)/shard_map/weights_back/ppermute | solution.py:262
  161.3 5.2 %all-to-all-start.2 = ((bf16[32,16,2176]{2,1,0:T(8,128)(2,1)}), bf16[32,16,2176]{2,1,0:T(8,128)(2,1)S(1)}, u32[]{:S(2)}, u32[]{:S(2)}) async-start(bf16[32,16,2176]{2,1,0:T(8,128)(2,1)} %bitcast.21), calls=%async_computation.2 | async-start | bytes 4456448 | tf_op jit(solution)/shard_map/tokens_back/all_to_all | solution.py:181
  166.6 10.7 %collective-permute-done.7.da_ref = bf16[1,192,2048]{2,1,0:T(8,128)(2,1)S(1)} collective-permute-done((bf16[1,192,2048]{2,1,0:T(8,128)(2,1)}, bf16[1,192,2048]{2,1,0:T(8,128)(2,1)S(1)}, u32[]{:S(2)}, u32[]{:S(2)}) %collective-permute-start.7) | collective-permute-done | bytes 786464 | tf_op jit(solution)/shard_map/weights_back/ppermute | solution.py:262
  177.4 3.1 %collective-permute-done.8.db_ref = bf16[1,192,2048]{2,1,0:T(8,128)(2,1)} collective-permute-done((bf16[1,192,2048]{2,1,0:T(8,128)(2,1)}, bf16[1,192,2048]{2,1,0:T(8,128)(2,1)}, u32[]{:S(2)}, u32[]{:S(2)}) %collective-permute-start.8) | collective-permute-done | bytes 786464 | tf_op jit(solution)/shard_map/weights_back/ppermute | solution.py:262
  180.4 7.5 %gate_up_grads.1 = (bf16[2,192,2048]{2,1,0:T(8,128)(2,1)}, bf16[2,192,2048]{2,1,0:T(8,128)(2,1)}) custom-call(bf16[512,2176]{1,0:T(8,128)(2,1)} %bitcast.8.x_ref.xo_ref, bf16[512,2176]{1,0:T(8,128)(2,1)} %copy-done.13, bf16[2,512,384]{2,1,0:T(8,128)(2,1)} %copy-done.14, bf16[2,512,384]{2,1,0:T(8,128)(2,1)} %copy-done.15), custom_call_target="tpu_custom_call" | custom-call | flops 99999997952 | bytes 1000000000 | tf_op jit(solution)/shard_map/weights_back/gate_up_grads/pallas_call | solution.py:279
  191.2 27.6 %all-to-all-done.2 = bf16[32,16,2176]{2,1,0:T(8,128)(2,1)S(1)} async-done(((bf16[32,16,2176]{2,1,0:T(8,128)(2,1)}), bf16[32,16,2176]{2,1,0:T(8,128)(2,1)S(1)}, u32[]{:S(2)}, u32[]{:S(2)}) %all-to-all-start.2) | async-done | bytes 2228256 | tf_op jit(solution)/shard_map/tokens_back/all_to_all | solution.py:181
  220.7 3.5 %all-to-all-start.3 = ((bf16[4,144,512]{2,1,0:T(8,128)(2,1)}), bf16[4,144,512]{2,1,0:T(8,128)(2,1)S(1)}, u32[]{:S(2)}, u32[]{:S(2)}) async-start(bf16[4,144,512]{2,1,0:T(8,128)(2,1)} %combine.1), calls=%async_computation.3 | async-start | bytes 1179648 | tf_op jit(solution)/shard_map/tokens_back/all_to_all | solution.py:312
  224.2 4.3 %collective-permute-done.10.b_ref = bf16[2,192,2048]{2,1,0:T(8,128)(2,1)} collective-permute-done((bf16[2,192,2048]{2,1,0:T(8,128)(2,1)}, bf16[2,192,2048]{2,1,0:T(8,128)(2,1)}, u32[]{:S(2)}, u32[]{:S(2)}) %collective-permute-start.10) | collective-permute-done | bytes 1572896 | tf_op jit(solution)/shard_map/weights_back/ppermute | solution.py:262
  228.5 4.8 %place.1 = (bf16[2,192,2048]{2,1,0:T(8,128)(2,1)}, bf16[2,192,2048]{2,1,0:T(8,128)(2,1)}, bf16[2,192,2048]{2,1,0:T(8,128)(2,1)}) custom-call(s32[4]{0:T(128)S(1)} %copy-done.12, bf16[1,192,2048]{2,1,0:T(8,128)(2,1)S(1)} %collective-permute-done.7.da_ref, bf16[1,192,2048]{2,1,0:T(8,128)(2,1)} %collective-permute-done.8.db_ref, ...), custom_call_target="tpu_custom_call" | custom-call | tf_op jit(solution)/shard_map/weights_back/place/pallas_call | solution.py:292
  (71 shorter events, 31.5 us)
Async XLA Ops:
  17.4 11.7 %copy-start.19 = (bf16[128,512]{1,0:T(8,128)(2,1)S(1)}, bf16[128,512]{1,0:T(8,128)(2,1)}, u32[]{:S(2)}) copy-start(bf16[128,512]{1,0:T(8,128)(2,1)} %param.8) | copy-start | bytes 393220
  17.4 22.6 %copy-start.17 = (bf16[2,192,2048]{2,1,0:T(8,128)(2,1)S(1)}, bf16[2,192,2048]{2,1,0:T(8,128)(2,1)}, u32[]{:S(2)}) copy-start(bf16[2,192,2048]{2,1,0:T(8,128)(2,1)} %param.12) | copy-start | bytes 4718596
  17.4 22.6 %copy-start.18 = (bf16[2,192,2048]{2,1,0:T(8,128)(2,1)S(1)}, bf16[2,192,2048]{2,1,0:T(8,128)(2,1)}, u32[]{:S(2)}) copy-start(bf16[2,192,2048]{2,1,0:T(8,128)(2,1)} %param.11) | copy-start | bytes 4718596
  17.4 63.0 %all-to-all-start = ((bf16[32,16,2176]{2,1,0:T(8,128)(2,1)}), bf16[32,16,2176]{2,1,0:T(8,128)(2,1)}, u32[]{:S(2)}, u32[]{:S(2)}) async-start(bf16[32,16,2176]{2,1,0:T(8,128)(2,1)} %bitcast.7), calls=%async_computation | async-start | bytes 4456448 | tf_op jit(solution)/shard_map/select_x/all_to_all | solution.py:181
  41.7 47.5 %collective-permute-start = (bf16[2,192,2048]{2,1,0:T(8,128)(2,1)}, bf16[2,192,2048]{2,1,0:T(8,128)(2,1)S(1)}, u32[]{:S(2)}, u32[]{:S(2)}) collective-permute-start(bf16[2,192,2048]{2,1,0:T(8,128)(2,1)} %pad_maximum_fusion), channel_id=1, source_target_pairs={{0,0},{1,1},{2,4},{3,5},{4,2},{5,3},{6,6},{7,7},{8,8},{9,9},{10,12... | collective-permute-start | bytes 4718600 | tf_op jit(solution)/shard_map/weights_out/ppermute | solution.py:208
  51.1 8.1 %copy-start.4 = (bf16[512,512]{1,0:T(8,128)(2,1)S(1)}, bf16[512,512]{1,0:T(8,128)(2,1)}, u32[]{:S(2)}) copy-start(bf16[512,512]{1,0:T(8,128)(2,1)} %all-gather.1) | copy-start | bytes 1572868
  51.1 38.1 %collective-permute-start.1 = (bf16[2,192,2048]{2,1,0:T(8,128)(2,1)}, bf16[2,192,2048]{2,1,0:T(8,128)(2,1)S(1)}, u32[]{:S(2)}, u32[]{:S(2)}) collective-permute-start(bf16[2,192,2048]{2,1,0:T(8,128)(2,1)} %pad_maximum_fusion.1), channel_id=1, source_target_pairs={{0,1},{1,0},{2,5},{3,4},{4,3},{5,2},{6,7},{7,6},{8,9},{9,8},{10,13... | collective-permute-start | bytes 4718600 | tf_op jit(solution)/shard_map/weights_out/ppermute | solution.py:208
  54.0 50.4 %collective-permute-start.4 = (bf16[1,192,2048]{2,1,0:T(8,128)(2,1)}, bf16[1,192,2048]{2,1,0:T(8,128)(2,1)}, u32[]{:S(2)}, u32[]{:S(2)}) collective-permute-start(bf16[1,192,2048]{2,1,0:T(8,128)(2,1)} %get-tuple-element.103), channel_id=1, source_target_pairs={{0,1},{1,0},{2,5},{3,4},{4,3},{5,2},{6,7},{7,6},{8,9},{9,8},{10,13... | collective-permute-start | bytes 2359304 | tf_op jit(solution)/shard_map/weights_out/ppermute | solution.py:208
  55.4 49.0 %collective-permute-start.3 = (bf16[1,192,2048]{2,1,0:T(8,128)(2,1)}, bf16[1,192,2048]{2,1,0:T(8,128)(2,1)}, u32[]{:S(2)}, u32[]{:S(2)}) collective-permute-start(bf16[1,192,2048]{2,1,0:T(8,128)(2,1)} %get-tuple-element.104), channel_id=1, source_target_pairs={{0,0},{1,1},{2,4},{3,5},{4,2},{5,3},{6,6},{7,7},{8,8},{9,9},{10,12... | collective-permute-start | bytes 2359304 | tf_op jit(solution)/shard_map/weights_out/ppermute | solution.py:208
  80.4 53.8 %all-to-all-start.1 = ((bf16[32,16,2048]{2,1,0:T(8,128)(2,1)}), bf16[32,16,2048]{2,1,0:T(8,128)(2,1)}, u32[]{:S(2)}, u32[]{:S(2)}) async-start(bf16[32,16,2048]{2,1,0:T(8,128)(2,1)} %bitcast.10), calls=%async_computation.1 | async-start | bytes 4194304 | tf_op jit(solution)/shard_map/gates/all_to_all | solution.py:181
  86.0 8.1 %collective-permute-start.2 = (bf16[512,2176]{1,0:T(8,128)(2,1)}, bf16[512,2176]{1,0:T(8,128)(2,1)S(1)}, u32[]{:S(2)}, u32[]{:S(2)}) collective-permute-start(bf16[512,2176]{1,0:T(8,128)(2,1)} %bitcast.8.x_ref.xo_ref), channel_id=1, source_target_pairs={{0,4},{4,0},{1,5},{5,1},{2,6},{6,2},{3,7},{7,3},{8,12},{12,8},{9,1... | collective-permute-start | bytes 6684680 | tf_op jit(solution)/shard_map/gates/ppermute | solution.py:223
  94.1 43.5 %copy-start.12 = (s32[4]{0:T(128)S(1)}, s32[4]{0:T(128)}, u32[]{:S(2)}) copy-start(s32[4]{0:T(128)} %copy-done.11) | copy-start | bytes 52
  134.2 11.6 %collective-permute-start.5 = (bf16[512,2048]{1,0:T(8,128)(2,1)}, bf16[512,2048]{1,0:T(8,128)(2,1)S(1)}, u32[]{:S(2)}, u32[]{:S(2)}) collective-permute-start(bf16[512,2048]{1,0:T(8,128)(2,1)} %bitcast.11.d_ref.do_ref), channel_id=1, source_target_pairs={{0,4},{4,0},{1,5},{5,1},{2,6},{6,2},{3,7},{7,3},{8,12},{12,8},{9,1... | collective-permute-start | bytes 6291464 | tf_op jit(solution)/shard_map/expert/ppermute | solution.py:239
  139.3 6.5 %copy-start.1 = (f32[3,512,384]{2,1,0:T(8,128)S(1)}, f32[3,512,384]{2,1,0:T(8,128)}, u32[]{:S(2)}) copy-start(f32[3,512,384]{2,1,0:T(8,128)} %copy-done) | copy-start | bytes 7077892
  145.8 5.1 %copy-start.8 = (bf16[512,384]{1,0:T(8,128)(2,1)S(1)}, bf16[512,384]{1,0:T(8,128)(2,1)}, u32[]{:S(2)}) copy-start(bf16[512,384]{1,0:T(8,128)(2,1)} %copy-done.7) | copy-start | bytes 1179652
  150.8 5.3 %copy-start.15 = (bf16[2,512,384]{2,1,0:T(8,128)(2,1)}, bf16[2,512,384]{2,1,0:T(8,128)(2,1)S(1)}, u32[]{:S(2)}) copy-start(bf16[2,512,384]{2,1,0:T(8,128)(2,1)S(1)} %get-tuple-element.97.ks_ref) | copy-start | bytes 2359300
  150.8 5.2 %collective-permute-start.6 = (bf16[512,2176]{1,0:T(8,128)(2,1)S(1)}, bf16[512,2176]{1,0:T(8,128)(2,1)S(1)}, u32[]{:S(2)}, u32[]{:S(2)}) collective-permute-start(bf16[512,2176]{1,0:T(8,128)(2,1)S(1)} %get-tuple-element.85), channel_id=1, source_target_pairs={{0,4},{4,0},{1,5},{5,1},{2,6},{6,2},{3,7},{7,3},{8,12},{12,8},{9,1... | collective-permute-start | bytes 6684680 | tf_op jit(solution)/shard_map/expert/ppermute | solution.py:252
  156.0 21.3 %collective-permute-start.7 = (bf16[1,192,2048]{2,1,0:T(8,128)(2,1)}, bf16[1,192,2048]{2,1,0:T(8,128)(2,1)S(1)}, u32[]{:S(2)}, u32[]{:S(2)}) collective-permute-start(bf16[1,192,2048]{2,1,0:T(8,128)(2,1)} %get-tuple-element.90), channel_id=1, source_target_pairs={{0,0},{1,1},{4,2},{5,3},{2,4},{3,5},{6,6},{7,7},{8,8},{9,9},{12,10... | collective-permute-start | bytes 2359304 | tf_op jit(solution)/shard_map/weights_back/ppermute | solution.py:262
  159.3 21.1 %collective-permute-start.8 = (bf16[1,192,2048]{2,1,0:T(8,128)(2,1)}, bf16[1,192,2048]{2,1,0:T(8,128)(2,1)}, u32[]{:S(2)}, u32[]{:S(2)}) collective-permute-start(bf16[1,192,2048]{2,1,0:T(8,128)(2,1)} %get-tuple-element.91), channel_id=1, source_target_pairs={{1,0},{0,1},{5,2},{4,3},{3,4},{2,5},{7,6},{6,7},{9,8},{8,9},{13,10... | collective-permute-start | bytes 2359304 | tf_op jit(solution)/shard_map/weights_back/ppermute | solution.py:262
  161.3 57.5 %all-to-all-start.2 = ((bf16[32,16,2176]{2,1,0:T(8,128)(2,1)}), bf16[32,16,2176]{2,1,0:T(8,128)(2,1)S(1)}, u32[]{:S(2)}, u32[]{:S(2)}) async-start(bf16[32,16,2176]{2,1,0:T(8,128)(2,1)} %bitcast.21), calls=%async_computation.2 | async-start | bytes 4456448 | tf_op jit(solution)/shard_map/tokens_back/all_to_all | solution.py:181
  166.6 52.2 %copy-start.10 = (f32[16,128]{1,0:T(8,128)S(1)}, f32[16,128]{1,0:T(8,128)}, u32[]{:S(2)}) copy-start(f32[16,128]{1,0:T(8,128)} %copy-done.9) | copy-start | bytes 24580
  187.9 36.3 %collective-permute-start.9 = (bf16[2,192,2048]{2,1,0:T(8,128)(2,1)}, bf16[2,192,2048]{2,1,0:T(8,128)(2,1)}, u32[]{:S(2)}, u32[]{:S(2)}) collective-permute-start(bf16[2,192,2048]{2,1,0:T(8,128)(2,1)} %get-tuple-element.98), channel_id=1, source_target_pairs={{0,0},{1,1},{4,2},{5,3},{2,4},{3,5},{6,6},{7,7},{8,8},{9,9},{12,10... | collective-permute-start | bytes 4718600 | tf_op jit(solution)/shard_map/weights_back/ppermute | solution.py:262
  190.6 37.8 %collective-permute-start.10 = (bf16[2,192,2048]{2,1,0:T(8,128)(2,1)}, bf16[2,192,2048]{2,1,0:T(8,128)(2,1)}, u32[]{:S(2)}, u32[]{:S(2)}) collective-permute-start(bf16[2,192,2048]{2,1,0:T(8,128)(2,1)} %get-tuple-element.99), channel_id=1, source_target_pairs={{1,0},{0,1},{5,2},{4,3},{3,4},{2,5},{7,6},{6,7},{9,8},{8,9},{13,10... | collective-permute-start | bytes 4718600 | tf_op jit(solution)/shard_map/weights_back/ppermute | solution.py:262
  220.7 13.7 %all-to-all-start.3 = ((bf16[4,144,512]{2,1,0:T(8,128)(2,1)}), bf16[4,144,512]{2,1,0:T(8,128)(2,1)S(1)}, u32[]{:S(2)}, u32[]{:S(2)}) async-start(bf16[4,144,512]{2,1,0:T(8,128)(2,1)} %combine.1), calls=%async_computation.3 | async-start | bytes 1179648 | tf_op jit(solution)/shard_map/tokens_back/all_to_all | solution.py:312
  (11 other events, 24.1 us)
